TPU v7x, 128 devices: a whole 4x4x4 slice. The times are simulated.
128 devices in a mesh: rows: 8 (over z, core), tensor: 16 (over y, x).
Axes of the slice: x: 4, y: 4, z: 4, core: 2. Of those that a mesh axis runs over, the one named last changes fastest.
Arguments:
- base_hidden: bfloat16 [512, 8192], P('rows', 'tensor'), may hold values from -360 to 360
- expert_hidden: bfloat16 [512, 4096], P('rows', 'tensor'), may hold values from -360 to 360
- anti_hidden: bfloat16 [512, 4096], P('rows', 'tensor'), may hold values from -360 to 360
- base_gain: bfloat16 [8192], P('tensor'), may hold values from 0.5 to 1.5
- expert_gain: bfloat16 [4096], P('tensor'), may hold values from 0.5 to 1.5
- anti_gain: bfloat16 [4096], P('tensor'), may hold values from 0.5 to 1.5
- base_head: bfloat16 [8192, 16, 4096], P('tensor', None, 'rows'), may hold values from -60 to 60
- expert_head: bfloat16 [4096, 16, 4096], P('tensor', None, 'rows'), may hold values from -0.09375 to 0.09375
- anti_head: bfloat16 [4096, 16, 4096], P('tensor', None, 'rows'), may hold values from -0.09375 to 0.09375
- strength: float32 [1], replicated, may hold values from 0.5 to 2
- token_ids: int32 [512], P('rows'), may hold values from 0 to 65535
Outputs:
- log_probs: float32 [512, 65536], P('rows', 'tensor')
- picked: float32 [512], P('rows')
All inputs are finite; a program needn't handle non-finite values.
Results may differ from a plain program's by a relative error of at most 0.0022.
Values may be sent and summed in bfloat16 or wider, within the bound.
No kernel may reach another device: no remote copies, remote signals or barrier semaphores. Data moves between devices by JAX's collectives and lax.ppermute only.
A program may use at most 384 MiB of HBM per device.

v0:
```python
import jax
import jax.numpy as jnp
from jax import lax
from jax.sharding import PartitionSpec as P

D = 8192
DE = 4096


def combined_all(value, axis, join):
    pieces = jax.tree.map(lambda part: lax.all_gather(part, axis), value)
    head = jax.tree.map(lambda part: part[0], pieces)
    tail = jax.tree.map(lambda part: part[1:], pieces)
    so_far, _ = lax.scan(lambda so_far, section: (join(so_far, section), None), head, tail)
    return so_far


def scaled(hidden, gain, total, width):
    values = hidden.astype(jnp.float32)
    return (values * lax.rsqrt(total / width + 1e-05)[:, None] * gain.astype(jnp.float32)).astype(
        jnp.bfloat16
    )


def project(normed, weights):
    return jnp.einsum("td,dac->atc", normed, weights, preferred_element_type=jnp.float32)


def combine_stats(first, second):
    top = jnp.maximum(first[0], second[0])
    total = first[1] * jnp.exp(first[0] - top) + second[1] * jnp.exp(second[0] - top)
    return (top, total, first[2] + second[2])


def shards(
    base_hidden,
    expert_hidden,
    anti_hidden,
    base_gain,
    expert_gain,
    anti_gain,
    base_head,
    expert_head,
    anti_head,
    strength,
    token_ids,
):
    alpha = strength[0]
    base_vals = base_hidden.astype(jnp.float32)
    expert_vals = expert_hidden.astype(jnp.float32)
    anti_vals = anti_hidden.astype(jnp.float32)
    base_sq, expert_sq, anti_sq = lax.psum(
        (
            jnp.sum(base_vals * base_vals, axis=1),
            jnp.sum(expert_vals * expert_vals, axis=1),
            jnp.sum(anti_vals * anti_vals, axis=1),
        ),
        "tensor",
    )
    normed_base = scaled(base_hidden, base_gain, base_sq, D)
    normed_expert = scaled(expert_hidden, expert_gain, expert_sq, DE)
    normed_anti = scaled(anti_hidden, anti_gain, anti_sq, DE)
    all_base, all_expert, all_anti = (
        lax.all_gather(normed_base, "rows", axis=0, tiled=True),
        lax.all_gather(normed_expert, "rows", axis=0, tiled=True),
        lax.all_gather(normed_anti, "rows", axis=0, tiled=True),
    )
    base_part = lax.psum_scatter(
        project(all_base, base_head), "tensor", scatter_dimension=0, tiled=True
    )[0]
    expert_part = lax.psum_scatter(
        project(all_expert, expert_head).astype(jnp.bfloat16),
        "tensor",
        scatter_dimension=0,
        tiled=True,
    ).astype(jnp.float32)[0]
    anti_part = lax.psum_scatter(
        project(all_anti, anti_head).astype(jnp.bfloat16), "tensor", scatter_dimension=0, tiled=True
    ).astype(jnp.float32)[0]
    base_logits, expert_logits, anti_logits = (
        lax.all_to_all(base_part, "rows", split_axis=0, concat_axis=1, tiled=True),
        lax.all_to_all(expert_part, "rows", split_axis=0, concat_axis=1, tiled=True),
        lax.all_to_all(anti_part, "rows", split_axis=0, concat_axis=1, tiled=True),
    )
    logits = base_logits + alpha * (expert_logits - anti_logits)
    local_top = jnp.max(logits, axis=1)
    local_total = jnp.sum(jnp.exp(logits - local_top[:, None]), axis=1)
    offset = lax.axis_index("tensor") * logits.shape[1]
    positions = lax.broadcasted_iota(jnp.int32, logits.shape, 1)
    chosen = positions == (token_ids - offset)[:, None]
    local_pick = jnp.sum(jnp.where(chosen, logits, 0.0), axis=1)
    top, total, pick = combined_all((local_top, local_total, local_pick), "tensor", combine_stats)
    logz = top + jnp.log(total)
    return (logits - logz[:, None], pick - logz)


def solution(mesh):
    return jax.shard_map(
        shards,
        mesh=mesh,
        in_specs=(
            P("rows", "tensor"),
            P("rows", "tensor"),
            P("rows", "tensor"),
            P("tensor"),
            P("tensor"),
            P("tensor"),
            P("tensor", None, "rows"),
            P("tensor", None, "rows"),
            P("tensor", None, "rows"),
            P(),
            P("rows"),
        ),
        out_specs=(P("rows", "tensor"), P("rows")),
        check_vma=False,
    )
```

profile of v0, /device:TPU:0, one launch (start us, length us, event | category | flops | bytes accessed | tf_op | source)
XLA Modules:
  0.0 464.4 jit_solution(13236237539045816971)
XLA Ops:
  7.2 0.0 reduce-scatter.12.cloned.1.call-start
  7.2 1.0 fusion.16
  8.2 0.9 fusion.19
  9.1 40.7 %all-reduce.7 = (f32[64]{0:T(128)S(1)}, f32[64]{0:T(128)S(1)}, f32[64]{0:T(128)S(1)}) all-reduce(f32[64]{0:T(128)S(1)} %fusion.16, f32[64]{0:T(128)S(1)} %get-tuple-element.73, f32[64]{0:T(128)S(1)} %get-tuple-element.74), channel_id=1, replica_groups=mesh['rows'=8,'tensor'=16] {'tensor'}, use_global_device_ids=true, to_apply=%region_1.0 | all-reduce | flops 192 | bytes 1536 | tf_op jit(solution)/shard_map/psum | solution.py:52
  49.8 0.7 convert_element_type.48
  50.5 0.8 fusion.21
  51.3 14.0 %all_gather.28 = bf16[512,256]{1,0:T(8,128)(2,1)S(1)} all-gather(bf16[64,256]{1,0:T(8,128)(2,1)S(1)} %fusion.21), channel_id=1, replica_groups=mesh['rows'=8,'tensor'=16] {'rows'}, dimensions={0}, use_global_device_ids=true | all-gather | bytes 294912 | tf_op jit(solution)/shard_map/all_gather | solution.py:65
  65.4 0.0 copy-start.4
  65.4 0.0 copy-start.2
  65.4 11.2 %convert_bitcast_fusion.1 = bf16[16,512,512]{2,1,0:T(8,128)(2,1)} fusion(bf16[256,16,512]{2,1,0:T(8,128)(2,1)} %param.20, bf16[512,256]{1,0:T(8,128)(2,1)S(1)} %all_gather.28), kind=kOutput, calls=%fused_computation.13 | convolution fusion | flops 2151677952 | bytes 12845056 | tf_op jit(solution)/shard_map/td,dac->atc/dot_general | solution.py:26
  76.6 0.0 reduce-scatter.12.cloned.1.call-update
  76.6 0.0 reduce-scatter.14.cloned.1.call-start
  76.6 0.0 copy-done.4
  76.7 0.0 copy-done.2
  76.7 0.1 fusion.24
  76.8 13.0 %all_gather.29 = bf16[512,256]{1,0:T(8,128)(2,1)S(1)} all-gather(bf16[64,256]{1,0:T(8,128)(2,1)S(1)} %fusion.24), channel_id=1, replica_groups=mesh['rows'=8,'tensor'=16] {'rows'}, dimensions={0}, use_global_device_ids=true | all-gather | bytes 294912 | tf_op jit(solution)/shard_map/all_gather | solution.py:66
  89.8 0.0 copy-start.3
  89.8 0.0 copy-start.1
  89.8 11.2 %convert_bitcast_fusion = bf16[16,512,512]{2,1,0:T(8,128)(2,1)} fusion(bf16[256,16,512]{2,1,0:T(8,128)(2,1)} %param.21, bf16[512,256]{1,0:T(8,128)(2,1)S(1)} %all_gather.29), kind=kOutput, calls=%fused_computation.12 | convolution fusion | flops 2151677952 | bytes 12845056 | tf_op jit(solution)/shard_map/td,dac->atc/dot_general | solution.py:26
  101.0 0.0 reduce-scatter.14.cloned.1.call-update
  101.0 0.0 reduce-scatter.10.cloned.1.call-start
  101.0 0.0 copy-done.3
  101.1 0.0 copy-done.1
  101.1 0.1 fusion.18
  101.2 13.3 %all_gather.27 = bf16[512,512]{1,0:T(8,128)(2,1)S(1)} all-gather(bf16[64,512]{1,0:T(8,128)(2,1)S(1)} %fusion.18), channel_id=1, replica_groups=mesh['rows'=8,'tensor'=16] {'rows'}, dimensions={0}, use_global_device_ids=true | all-gather | bytes 589824 | tf_op jit(solution)/shard_map/all_gather | solution.py:64
  114.5 27.1 %convolution_bitcast_fusion = f32[16,512,512]{2,1,0:T(8,128)} fusion(bf16[512,16,512]{2,1,0:T(8,128)(2,1)} %param.19, bf16[512,512]{1,0:T(8,128)(2,1)S(1)} %all_gather.27), kind=kOutput, calls=%fused_computation.10 | convolution fusion | flops 4294967296 | bytes 25690112 | tf_op jit(solution)/shard_map/td,dac->atc/dot_general | solution.py:26
  141.6 0.0 reduce-scatter.10.cloned.1.call-update
  141.6 0.0 copy-start.6
  141.6 0.0 copy-start.5
  141.6 16.1 %reduce-scatter.12.cloned.1.call-done = bf16[1,512,512]{2,1,0:T(8,128)(2,1)} async-done(((bf16[16,512,512]{2,1,0:T(8,128)(2,1)}), bf16[1,512,512]{2,1,0:T(8,128)(2,1)}) %reduce-scatter.12.cloned.1.call-update) | async-done | bytes 524304
  157.7 2.1 convert.2
  159.9 4.4 all-to-all-start.1
  164.3 81.1 %reduce-scatter.14.cloned.1.call-done = bf16[1,512,512]{2,1,0:T(8,128)(2,1)} async-done(((bf16[16,512,512]{2,1,0:T(8,128)(2,1)}), bf16[1,512,512]{2,1,0:T(8,128)(2,1)}) %reduce-scatter.14.cloned.1.call-update) | async-done | bytes 524304
  245.5 1.2 convert.3
  246.6 0.0 all-to-all-done.1
  246.6 20.3 %all_to_all.47 = f32[8,64,512]{2,1,0:T(8,128)S(1)} all-to-all(f32[8,64,512]{2,1,0:T(8,128)S(1)} %convert.3), channel_id=1, replica_groups=mesh['rows'=8,'tensor'=16] {'rows'}, dimensions={0} | all-to-all | bytes 2097152 | tf_op jit(solution)/shard_map/all_to_all | solution.py:83
  266.9 91.8 %reduce-scatter.10.cloned.1.call-done = f32[1,512,512]{2,1,0:T(8,128)} async-done(((f32[16,512,512]{2,1,0:T(8,128)}), f32[1,512,512]{2,1,0:T(8,128)}) %reduce-scatter.10.cloned.1.call-update) | async-done | bytes 1048592
  358.8 4.4 all-to-all-start
  363.8 0.0 copy-done.6
  363.8 0.6 dynamic-slice
  365.1 0.0 copy-done.5
  365.1 14.0 %all-to-all-done = f32[8,64,512]{2,1,0:T(8,128)S(1)} async-done(((f32[8,64,512]{2,1,0:T(8,128)}), f32[8,64,512]{2,1,0:T(8,128)S(1)}, u32[]{:S(2)}, u32[]{:S(2)}) %all-to-all-start) | async-done | bytes 1048608 | tf_op jit(solution)/shard_map/all_to_all | solution.py:81
  379.1 0.0 copy-start
  379.1 1.0 copy-done
  380.1 1.6 fusion.27
  381.7 0.2 dynamic-update-slice
  381.9 0.4 fusion.10
  382.4 0.2 dynamic-update-slice.2
  382.6 0.2 dynamic-update-slice.1
  382.8 72.3 %all-reduce.6 = (f32[1024]{0:T(1024)S(1)}, f32[1024]{0:T(1024)S(1)}, f32[1024]{0:T(1024)S(1)}) all-reduce(f32[1024]{0:T(1024)S(1)} %dynamic-update-slice, f32[1024]{0:T(1024)S(1)} %dynamic-update-slice.1, f32[1024]{0:T(1024)S(1)} %dynamic-update-slice.2), channel_id=2, replica_groups=mesh['rows'=8,'tensor'=16] {'tensor'}, use_global_device_ids=true, to_apply=%add | all-reduce | flops 3072 | bytes 24576
  455.1 0.1 slice.27
  455.2 0.1 slice.28
  455.3 0.1 slice.29
  455.3 0.1 reshape.61
  455.4 0.1 reshape.62
  455.5 0.1 reshape.63
  455.5 0.6 while.14
  456.2 0.1 copy.21
  456.3 0.5 fusion.26
  456.8 1.1 broadcast_subtract_fusion
  (28 shorter events, 0.5 us)
Async XLA Ops:
  7.2 150.6 %reduce-scatter.12.cloned.1.call-start = ((), (), s32[]{:S(2)}) async-start(), calls=%async_computation.7 | async-start | bytes 8912896
  65.4 11.3 %copy-start.4 = (bf16[256]{0:T(256)(128)(2,1)S(1)}, bf16[256]{0:T(256)(128)(2,1)}, u32[]{:S(2)}) copy-start(bf16[256]{0:T(256)(128)(2,1)} %param.18) | copy-start | bytes 1540
  65.4 11.3 %copy-start.2 = (bf16[64,256]{1,0:T(8,128)(2,1)S(1)}, bf16[64,256]{1,0:T(8,128)(2,1)}, u32[]{:S(2)}) copy-start(bf16[64,256]{1,0:T(8,128)(2,1)} %param.15) | copy-start | bytes 98308
  76.6 168.9 %reduce-scatter.14.cloned.1.call-start = ((), (), s32[]{:S(2)}) async-start(), calls=%async_computation.8 | async-start | bytes 8912896
  89.8 11.3 %copy-start.3 = (bf16[512]{0:T(512)(128)(2,1)S(1)}, bf16[512]{0:T(512)(128)(2,1)}, u32[]{:S(2)}) copy-start(bf16[512]{0:T(512)(128)(2,1)} %param.16) | copy-start | bytes 3076
  89.8 11.3 %copy-start.1 = (bf16[64,512]{1,0:T(8,128)(2,1)S(1)}, bf16[64,512]{1,0:T(8,128)(2,1)}, u32[]{:S(2)}) copy-start(bf16[64,512]{1,0:T(8,128)(2,1)} %param.13) | copy-start | bytes 196612
  101.0 257.8 %reduce-scatter.10.cloned.1.call-start = ((), (), s32[]{:S(2)}) async-start(), calls=%async_computation.6 | async-start | bytes 17825792
  141.6 222.2 %copy-start.6 = (u32[128]{0:T(128)S(1)}, u32[128]{0:T(128)}, u32[]{:S(2)}) copy-start(u32[128]{0:T(128)} %constant.34) | copy-start | bytes 1540
  141.6 223.5 %copy-start.5 = (s32[64]{0:T(128)S(1)}, s32[64]{0:T(128)}, u32[]{:S(2)}) copy-start(s32[64]{0:T(128)} %param.23) | copy-start | bytes 772
  159.9 86.7 %all-to-all-start.1 = ((f32[8,64,512]{2,1,0:T(8,128)}), f32[8,64,512]{2,1,0:T(8,128)S(1)}, u32[]{:S(2)}, u32[]{:S(2)}) async-start(f32[8,64,512]{2,1,0:T(8,128)} %convert.2), calls=%async_computation.1 | async-start | bytes 2097152 | tf_op jit(solution)/shard_map/all_to_all | solution.py:82
  358.8 20.4 %all-to-all-start = ((f32[8,64,512]{2,1,0:T(8,128)}), f32[8,64,512]{2,1,0:T(8,128)S(1)}, u32[]{:S(2)}, u32[]{:S(2)}) async-start(f32[8,64,512]{2,1,0:T(8,128)} %bitcast.56), calls=%async_computation | async-start | bytes 2097152 | tf_op jit(solution)/shard_map/all_to_all | solution.py:81
  379.1 1.0 copy-start
Sparse Core Ops, SparseCore 0:
  76.7 81.0 reduce-scatter.11
  161.2 84.2 reduce-scatter.13
  248.9 109.8 reduce-scatter.9
where the time goes:
time: 465 us; the launch traced here: 464 us
  waiting for transfers between devices  203 us (44%)
  blocking collectives  174 us (37%)
  matrix products  49.4 us (11%)
  between operations  15.2 us (3%)
  other arithmetic  10.9 us (2%)
  starting transfers between devices  8.93 us (2%)
    unnamed x6, waiting for transfers between devices  189 us
    unnamed x1, blocking collectives  72.3 us
    dot_general x3, matrix products, project(): jnp.einsum('td,dac->atc', normed, weights, preferred_element_type=jnp.flo...  49.4 us
    psum x1, blocking collectives, shards(): lax.psum((jnp.sum(base_vals * base_vals, axis=1), jnp.sum(expert_vals * e...  40.7 us
    all_to_all x1, blocking collectives, shards(): lax.all_to_all(anti_part, 'rows', split_axis=0, concat_axis=1, tiled=True)  20.3 us
    all_gather x1, blocking collectives, shards(): lax.all_gather(normed_expert, 'rows', axis=0, tiled=True)  14 us
    all_to_all x1, waiting for transfers between devices, shards(): lax.all_to_all(base_part, 'rows', split_axis=0, concat_axis=1, tiled=True)  14 us
    all_gather x1, blocking collectives, shards(): lax.all_gather(normed_base, 'rows', axis=0, tiled=True)  13.3 us
  transfers between devices with their start and end apart: 5, of which 4 were waited for; matrix products, arithmetic and copies ran while one was open for 9% of the time, Pallas kernels for 0%

commit v1 on v0

v1 whole, which is shorter than its diff:
```python
import jax
import jax.numpy as jnp
import numpy as np
from jax import lax
from jax.experimental import pallas as pl
from jax.experimental.pallas import tpu as pltpu
from jax.sharding import PartitionSpec as P

D = 8192
DE = 4096
NZ, NC, NY, NX = 4, 2, 4, 4
AXES = ("rows", "tensor")
BF = jnp.bfloat16
F16 = jnp.float16
F32 = jnp.float32
DOWN, UP = 0.0625, 16.0


def device(z, c, y, x):
    return (z * NC + c) * (NY * NX) + y * NX + x


def exchange(value, axis, stage):
    pairs = []
    for z in range(NZ):
        for c in range(NC):
            u = 1 if (stage + c) % 2 == 0 else 3
            for y in range(NY):
                for x in range(NX):
                    to = {
                        "z": (z ^ u, c, y, x),
                        "y": (z, c, y ^ u, x),
                        "x": (z, c, y, x ^ u),
                        "core": (z, 1 - c, y, x),
                    }[axis]
                    pairs.append((device(z, c, y, x), device(*to)))
    return lax.ppermute(value, AXES, pairs)


def tables():
    out = np.zeros((NZ * NC * NY * NX, 48), np.int32)
    for z in range(NZ):
        for c in range(NC):
            u, v = (1, 3) if c == 0 else (3, 1)
            first, second = (2, u, v, 0), (u, 2, 0, v)
            for y in range(NY):
                for x in range(NX):
                    row = [(y ^ j) * NX + (x ^ i) for i in first for j in second]
                    row += [(y ^ i) * NX + (x ^ j) for i in first for j in second]
                    row += [(z ^ i) * NC + k for i in (0, u, v, 2) for k in (c, 1 - c)]
                    out[device(z, c, y, x), : len(row)] = row
    return out


def relay_kernel(head, out):
    out[...] = jnp.swapaxes(head[...], 0, 1)


def relay(head, start, count, step=64):
    _, n_a, c = head.shape
    out = pl.pallas_call(
        relay_kernel,
        grid=(count // step,),
        in_specs=[pl.BlockSpec((step, n_a, c), lambda i: (start // step + i, 0, 0))],
        out_specs=pl.BlockSpec((n_a, step, c), lambda i: (0, i, 0)),
        out_shape=jax.ShapeDtypeStruct((n_a, count, c), head.dtype),
        cost_estimate=pl.CostEstimate(flops=10**10, bytes_accessed=2**24, transcendentals=0),
    )(head)
    return pltpu.with_memory_space_constraint(out, pltpu.HBM)


def matmul_kernel(table, alpha, *refs):
    xs, ws, out = refs[:8], refs[8:12], refs[12]
    tokens = xs[0].shape[0]
    for i in range(2):
        base0, base1, expert, anti = [
            jnp.dot(x[...], w[0], preferred_element_type=F32) for x, w in zip(xs[i::2], ws)
        ]
        total = base0 + base1 + alpha[0] * (expert - anti)
        out[0, i * tokens : (i + 1) * tokens] = total.astype(out.dtype)


def project(table, alpha, acts, heads, first, half, dtype):
    tokens = acts[0].shape[0]
    half_c = heads[0].shape[2] // 2
    quarter = heads[0].shape[1]

    def features(i):
        return pl.BlockSpec((tokens, quarter), lambda _, tab: (0, i))

    def weights():
        return pl.BlockSpec((1, quarter, half_c), lambda i, tab: (tab[first + i], 0, half))

    return pl.pallas_call(
        matmul_kernel,
        grid_spec=pltpu.PrefetchScalarGridSpec(
            num_scalar_prefetch=1,
            grid=(4,),
            in_specs=[pl.BlockSpec(memory_space=pltpu.SMEM)]
            + [features(i) for i in range(4) for _ in acts]
            + [weights() for _ in heads],
            out_specs=pl.BlockSpec((1, 2 * tokens, half_c), lambda i, tab: (i, 0, 0)),
        ),
        out_shape=jax.ShapeDtypeStruct((4, 2 * tokens, half_c), dtype),
        compiler_params=pltpu.CompilerParams(vmem_limit_bytes=32 << 20),
        cost_estimate=pl.CostEstimate(flops=1, bytes_accessed=1, transcendentals=0),
    )(table, alpha, *acts * 4, *heads)


def wide(value):
    return value.astype(F32) * UP if value.dtype == F16 else value.astype(F32)


def narrow(value):
    return (value * DOWN).astype(F16)


def together(*values):
    return lax.optimization_barrier(values)


def merge(stats):
    top = jnp.max(stats[:, 0], axis=0)
    total = jnp.sum(stats[:, 1] * jnp.exp(stats[:, 0] - top[None]), axis=0)
    return top + jnp.log(total), jnp.sum(stats[:, 2], axis=0)


def final_kernel(source, logits, logz, out):
    width = logits.shape[2]
    for i in range(logits.shape[0]):
        at = pl.multiple_of(source[i] * width, width)
        out[:, pl.ds(at, width)] = logits[i] - logz[...]


def shards(
    base_hidden,
    expert_hidden,
    anti_hidden,
    base_gain,
    expert_gain,
    anti_gain,
    base_head,
    expert_head,
    anti_head,
    strength,
    token_ids,
):
    r = lax.axis_index("rows")
    t = lax.axis_index("tensor")
    rows, c_width = token_ids.shape[0], base_head.shape[2]
    mine = lax.dynamic_slice(jnp.asarray(tables()), (r * (NY * NX) + t, 0), (1, 48))[0]
    table, source = mine[:32], mine[32:40]

    values = [h.astype(F32) for h in (base_hidden, expert_hidden, anti_hidden)]
    sq = jnp.stack([jnp.sum(h * h, axis=1) for h in values])
    quarter = expert_head.shape[0]
    raw = ((base_head, 0), (base_head, quarter), (expert_head, 0), (anti_head, 0))
    heads = []
    for i, (axis, stage) in enumerate((("x", 0), ("x", 1), ("y", 0), ("y", 1))):
        head, start = raw[i]
        sq, head = together(sq, head)
        got, head = together(exchange(sq, axis, stage), relay(head, start, quarter))
        heads.append(head)
        sq = sq + got
    widths = (D, DE, DE)
    gains = (base_gain, expert_gain, anti_gain)
    normed = jnp.concatenate(
        [
            h * lax.rsqrt(sq[i] / widths[i] + 1e-05)[:, None] * gains[i].astype(F32)
            for i, h in enumerate(values)
        ],
        axis=1,
    ).astype(BF)

    pair = exchange(normed, "z", 0)
    far = exchange(jnp.stack([normed, pair]), "z", 1)
    mine = jnp.concatenate([pair, far[1], normed, far[0]])
    acts = [mine, exchange(mine, "core", 0)]

    axes = (("x", "y"), ("y", "x"))
    kept = [[], []]
    moved = [[], []]
    for i in range(4):
        for half in range(2):
            part = project(table, strength, acts, heads, 16 * half + 4 * i, half, BF if i < 2 else F32)
            table, part = together(table, part)
            if i < 2:
                moved[half].append(exchange(part, axes[half][0], 0))
            else:
                kept[half].append(part)
    second_step = [
        exchange(narrow(kept[h][0] + wide(moved[h][0])), axes[h][0], 1) for h in range(2)
    ]
    sums = [kept[h][1] + wide(moved[h][1]) + wide(second_step[h]) for h in range(2)]
    moved = [exchange(narrow(sums[h][:2]), axes[h][1], 0) for h in range(2)]
    second_step = [
        exchange(narrow(sums[h][3] + wide(moved[h][1])), axes[h][1], 1) for h in range(2)
    ]
    logits = jnp.concatenate(
        [narrow(sums[h][2] + wide(moved[h][0]) + wide(second_step[h])) for h in range(2)], axis=1
    ).reshape(NC, NZ, rows, c_width)

    other = exchange(logits[1], "core", 0)
    both = jnp.stack([logits[0], other], axis=1)
    near = exchange(both[:2], "z", 0)
    last = exchange(jnp.stack([both[3], near[1]]), "z", 1)
    home = jnp.concatenate([both[2], near[0], last[0], last[1]]).astype(F32) * UP
    top = jnp.max(home, axis=(0, 2))
    total = jnp.sum(jnp.exp(home - top[None, :, None]), axis=(0, 2))
    column = source[:, None, None] * c_width + lax.broadcasted_iota(jnp.int32, (8, 1, c_width), 2)
    wanted = (token_ids - t * (8 * c_width))[None, :, None]
    pick = jnp.sum(jnp.where(column == wanted, home, 0.0), axis=(0, 2))
    stats = jnp.stack([top, total, pick])
    stats = lax.all_to_all(
        jnp.broadcast_to(stats[None], (NY * NX, 3, rows)), "tensor", 0, 0, tiled=True
    )
    logz, pick = merge(stats)

    log_probs = pl.pallas_call(
        final_kernel,
        in_specs=[
            pl.BlockSpec(memory_space=pltpu.SMEM),
            pl.BlockSpec(memory_space=pltpu.VMEM),
            pl.BlockSpec(memory_space=pltpu.VMEM),
        ],
        out_specs=pl.BlockSpec(memory_space=pltpu.VMEM),
        out_shape=jax.ShapeDtypeStruct((rows, 8 * c_width), F32),
    )(source, home, logz[:, None])
    return log_probs, pick - logz


def solution(mesh):
    return jax.shard_map(
        shards,
        mesh=mesh,
        in_specs=(
            P("rows", "tensor"),
            P("rows", "tensor"),
            P("rows", "tensor"),
            P("tensor"),
            P("tensor"),
            P("tensor"),
            P("tensor", None, "rows"),
            P("tensor", None, "rows"),
            P("tensor", None, "rows"),
            P(),
            P("rows"),
        ),
        out_specs=(P("rows", "tensor"), P("rows")),
        check_vma=False,
    )
```

time: 465 us -> 160 us (0.34)
  blocking collectives: 174 us -> 0 us
  waiting for transfers between devices: 203 us -> 48.6 us
  Pallas kernels: 0 us -> 57.3 us
  matrix products: 49.4 us -> 0 us
  starting transfers between devices: 8.93 us -> 38.9 us
  between operations: 15.2 us -> 1.7 us
    unnamed x6 -> x0, waiting for transfers between devices: 189 us -> none
    unnamed x1 -> x0, blocking collectives: 72.3 us -> none
    pallas_call x0 -> x13, Pallas kernels: none -> 57.3 us  [the longest x8 34.5 us: project(): pl.pallas_call(matmul_kernel, grid_spec=pltpu.PrefetchScalarGridSpec(num_...]
    dot_general x3 -> x0, matrix products: 49.4 us -> none  [project(): jnp.einsum('td,dac->atc', normed, weights, preferred_element_type=jnp.flo...]
    ppermute x0 -> x20, waiting for transfers between devices: none -> 41.6 us  [exchange(): return lax.ppermute(value, AXES, pairs)]
    psum x1 -> x0, blocking collectives: 40.7 us -> none  [shards(): lax.psum((jnp.sum(base_vals * base_vals, axis=1), jnp.sum(expert_vals * e...]
    all_gather x3 -> x0, blocking collectives: 40.4 us -> none  [the longest x1 14 us: shards(): lax.all_gather(normed_expert, 'rows', axis=0, tiled=True)]
    ppermute x0 -> x20, starting transfers between devices: none -> 31.4 us  [exchange(): return lax.ppermute(value, AXES, pairs)]
  transfers between devices with their start and end apart: 5 -> 21, of which waited for: 4 -> 13; matrix products, arithmetic and copies ran while one was open for 9% -> 2% of each run, Pallas kernels for 0% -> 32%
where the time goes in v1:
time: 160 us; the launch traced here: 159 us
  Pallas kernels  57.3 us (36%)
  waiting for transfers between devices  48.6 us (30%)
  starting transfers between devices  38.9 us (24%)
  other arithmetic  9.06 us (6%)
  local copies, waits for them, and re-layouts  3.47 us (2%)
  between operations  1.7 us (1%)
    ppermute x20, waiting for transfers between devices, exchange(): return lax.ppermute(value, AXES, pairs)  41.6 us
    pallas_call x8, Pallas kernels, project(): pl.pallas_call(matmul_kernel, grid_spec=pltpu.PrefetchScalarGridSpec(num_...  34.5 us
    ppermute x20, starting transfers between devices, exchange(): return lax.ppermute(value, AXES, pairs)  31.4 us
    pallas_call x4, Pallas kernels, relay(): pl.pallas_call(relay_kernel, grid=(count // step,), in_specs=[pl.BlockSpe...  20.4 us
    all_to_all x1, starting transfers between devices, shards(): lax.all_to_all(jnp.broadcast_to(stats[None], (NY * NX, 3, rows)), 'tensor...  7.56 us
    all_to_all x1, waiting for transfers between devices, shards(): lax.all_to_all(jnp.broadcast_to(stats[None], (NY * NX, 3, rows)), 'tensor...  6.98 us
  transfers between devices with their start and end apart: 21, of which 13 were waited for; matrix products, arithmetic and copies ran while one was open for 2% of the time, Pallas kernels for 32%

profile of v1, /device:TPU:0, one launch (start us, length us, event | category | flops | bytes accessed | tf_op | source)
XLA Modules:
  0.0 159.0 jit_solution(1299260446042952561)
XLA Ops:
  0.6 0.9 fusion.23
  1.5 0.9 fusion.26
  2.4 1.0 fusion.20
  3.4 1.7 %collective-permute-start = (f32[3,64]{1,0:T(4,128)S(1)}, f32[3,64]{1,0:T(4,128)S(1)}, u32[]{:S(2)}, u32[]{:S(2)}) collective-permute-start(f32[3,64]{1,0:T(4,128)S(1)} %pad_maximum_fusion.6), channel_id=1, source_target_pairs={{0,1},{1,0},{2,3},{3,2},{4,5},{5,4},{6,7},{7,6},{8,9},{9,8},{10,11... | collective-permute-start | bytes 2312 | tf_op jit(solution)/shard_map/ppermute | solution.py:37
  5.0 5.1 %shard_map.131.refs_8_ = bf16[16,256,512]{2,1,0:T(8,128)(2,1)} custom-call(bf16[512,16,512]{2,1,0:T(8,128)(2,1)} %head.1), custom_call_target="tpu_custom_call" | custom-call | flops 10000000000 | bytes 16777216 | tf_op jit(solution)/shard_map/pallas_call | solution.py:61
  10.2 2.2 %collective-permute-start.1 = (f32[3,64]{1,0:T(4,128)S(1)}, f32[3,64]{1,0:T(4,128)S(1)}, u32[]{:S(2)}, u32[]{:S(2)}) collective-permute-start(f32[3,64]{1,0:T(4,128)S(1)} %add.114), channel_id=1, source_target_pairs={{0,3},{1,2},{2,1},{3,0},{4,7},{5,6},{6,5},{7,4},{8,11},{9,10},{10,... | collective-permute-start | bytes 2312 | tf_op jit(solution)/shard_map/ppermute | solution.py:37
  12.4 5.1 %shard_map.132.refs_9_ = bf16[16,256,512]{2,1,0:T(8,128)(2,1)} custom-call(bf16[512,16,512]{2,1,0:T(8,128)(2,1)} %head.1), custom_call_target="tpu_custom_call" | custom-call | flops 10000000000 | bytes 16777216 | tf_op jit(solution)/shard_map/pallas_call | solution.py:61
  17.5 1.7 %collective-permute-start.2 = (f32[3,64]{1,0:T(4,128)S(1)}, f32[3,64]{1,0:T(4,128)S(1)}, u32[]{:S(2)}, u32[]{:S(2)}) collective-permute-start(f32[3,64]{1,0:T(4,128)S(1)} %add.115), channel_id=1, source_target_pairs={{0,4},{1,5},{2,6},{3,7},{4,0},{5,1},{6,2},{7,3},{8,12},{9,13},{10,... | collective-permute-start | bytes 2312 | tf_op jit(solution)/shard_map/ppermute | solution.py:37
  19.2 5.1 %shard_map.133.refs_10_ = bf16[16,256,512]{2,1,0:T(8,128)(2,1)} custom-call(bf16[256,16,512]{2,1,0:T(8,128)(2,1)} %head.2), custom_call_target="tpu_custom_call" | custom-call | flops 10000000000 | bytes 16777216 | tf_op jit(solution)/shard_map/pallas_call | solution.py:61
  24.3 2.3 %collective-permute-start.3 = (f32[3,64]{1,0:T(4,128)S(1)}, f32[3,64]{1,0:T(4,128)S(1)}, u32[]{:S(2)}, u32[]{:S(2)}) collective-permute-start(f32[3,64]{1,0:T(4,128)S(1)} %add.116), channel_id=1, source_target_pairs={{0,12},{1,13},{2,14},{3,15},{4,8},{5,9},{6,10},{7,11},{8,4},{9,5},... | collective-permute-start | bytes 2312 | tf_op jit(solution)/shard_map/ppermute | solution.py:37
  26.6 5.1 %shard_map.134.refs_11_ = bf16[16,256,512]{2,1,0:T(8,128)(2,1)} custom-call(bf16[256,16,512]{2,1,0:T(8,128)(2,1)} %head.3), custom_call_target="tpu_custom_call" | custom-call | flops 10000000000 | bytes 16777216 | tf_op jit(solution)/shard_map/pallas_call | solution.py:61
  31.9 2.0 %collective-permute-start.4 = (bf16[64,1024]{1,0:T(8,128)(2,1)S(1)}, bf16[64,1024]{1,0:T(8,128)(2,1)S(1)}, u32[]{:S(2)}, u32[]{:S(2)}) collective-permute-start(bf16[64,1024]{1,0:T(8,128)(2,1)S(1)} %pad_maximum_fusion.5), channel_id=1, source_target_pairs={{0,32},{1,33},{2,34},{3,35},{4,36},{5,37},{6,38},{7,39},{8,40},{9,... | collective-permute-start | bytes 393224 | tf_op jit(solution)/shard_map/ppermute | solution.py:37
  34.0 3.0 %collective-permute-done.4 = bf16[64,1024]{1,0:T(8,128)(2,1)S(1)} collective-permute-done((bf16[64,1024]{1,0:T(8,128)(2,1)S(1)}, bf16[64,1024]{1,0:T(8,128)(2,1)S(1)}, u32[]{:S(2)}, u32[]{:S(2)}) %collective-permute-start.4) | collective-permute-done | bytes 131104 | tf_op jit(solution)/shard_map/ppermute | solution.py:37
  37.0 4.1 %collective-permute-start.5 = (bf16[2,64,1024]{2,1,0:T(8,128)(2,1)S(1)}, bf16[2,64,1024]{2,1,0:T(8,128)(2,1)S(1)}, u32[]{:S(2)}, u32[]{:S(2)}) collective-permute-start(bf16[2,64,1024]{2,1,0:T(8,128)(2,1)S(1)} %pad_maximum_fusion.4), channel_id=1, source_target_pairs={{0,96},{1,97},{2,98},{3,99},{4,100},{5,101},{6,102},{7,103},{8,104... | collective-permute-start | bytes 786440 | tf_op jit(solution)/shard_map/ppermute | solution.py:37
  41.1 4.4 %collective-permute-done.5 = bf16[2,64,1024]{2,1,0:T(8,128)(2,1)S(1)} collective-permute-done((bf16[2,64,1024]{2,1,0:T(8,128)(2,1)S(1)}, bf16[2,64,1024]{2,1,0:T(8,128)(2,1)S(1)}, u32[]{:S(2)}, u32[]{:S(2)}) %collective-permute-start.5) | collective-permute-done | bytes 262176 | tf_op jit(solution)/shard_map/ppermute | solution.py:37
  46.3 0.7 constant_dynamic-slice_fusion
  47.0 0.5 collective-permute-done.6.refs_1_.refs_3_.refs_5_.refs_7_
  47.5 4.3 %shard_map.135 = bf16[4,512,256]{2,1,0:T(8,128)(2,1)S(1)} custom-call(s32[32]{0:T(128)S(1)} %slice_bitcast_fusion.5.table, f32[1]{0:T(128)S(6)} %copy.21.alpha, bf16[256,1024]{1,0:T(8,128)(2,1)S(1)} %pad_maximum_fusion.refs_0_.refs_2_.refs_4_.refs_6_, bf16[256,1024]{1,0:T(8,128)(2,1)S(1)} %collective-permute-done.6.refs_1_.refs_3_.refs_5_.refs_7_, ...), custom_call_target="tpu_custom_call" | custom-call | flops 1 | bytes 1 | tf_op jit(solution)/shard_map/pallas_call | solution.py:94
  51.9 0.7 collective-permute-start.8
  52.5 4.3 %shard_map.136 = bf16[4,512,256]{2,1,0:T(8,128)(2,1)S(1)} custom-call(s32[32]{0:T(128)S(1)} %slice_bitcast_fusion.5.table, f32[1]{0:T(128)S(6)} %copy.21.alpha, bf16[256,1024]{1,0:T(8,128)(2,1)S(1)} %pad_maximum_fusion.refs_0_.refs_2_.refs_4_.refs_6_, bf16[256,1024]{1,0:T(8,128)(2,1)S(1)} %collective-permute-done.6.refs_1_.refs_3_.refs_5_.refs_7_, ...), custom_call_target="tpu_custom_call" | custom-call | flops 1 | bytes 1 | tf_op jit(solution)/shard_map/pallas_call | solution.py:94
  56.9 0.8 collective-permute-start.13
  57.6 4.3 %shard_map.137 = bf16[4,512,256]{2,1,0:T(8,128)(2,1)S(1)} custom-call(s32[32]{0:T(128)S(1)} %slice_bitcast_fusion.5.table, f32[1]{0:T(128)S(6)} %copy.21.alpha, bf16[256,1024]{1,0:T(8,128)(2,1)S(1)} %pad_maximum_fusion.refs_0_.refs_2_.refs_4_.refs_6_, bf16[256,1024]{1,0:T(8,128)(2,1)S(1)} %collective-permute-done.6.refs_1_.refs_3_.refs_5_.refs_7_, ...), custom_call_target="tpu_custom_call" | custom-call | flops 1 | bytes 1 | tf_op jit(solution)/shard_map/pallas_call | solution.py:94
  61.9 4.3 %shard_map.138 = bf16[4,512,256]{2,1,0:T(8,128)(2,1)S(1)} custom-call(s32[32]{0:T(128)S(1)} %slice_bitcast_fusion.5.table, f32[1]{0:T(128)S(6)} %copy.21.alpha, bf16[256,1024]{1,0:T(8,128)(2,1)S(1)} %pad_maximum_fusion.refs_0_.refs_2_.refs_4_.refs_6_, bf16[256,1024]{1,0:T(8,128)(2,1)S(1)} %collective-permute-done.6.refs_1_.refs_3_.refs_5_.refs_7_, ...), custom_call_target="tpu_custom_call" | custom-call | flops 1 | bytes 1 | tf_op jit(solution)/shard_map/pallas_call | solution.py:94
  66.3 1.5 collective-permute-start.7
  67.8 4.3 %shard_map.139 = f32[4,512,256]{2,1,0:T(8,128)S(1)} custom-call(s32[32]{0:T(128)S(1)} %slice_bitcast_fusion.5.table, f32[1]{0:T(128)S(6)} %copy.21.alpha, bf16[256,1024]{1,0:T(8,128)(2,1)S(1)} %pad_maximum_fusion.refs_0_.refs_2_.refs_4_.refs_6_, bf16[256,1024]{1,0:T(8,128)(2,1)S(1)} %collective-permute-done.6.refs_1_.refs_3_.refs_5_.refs_7_, ...), custom_call_target="tpu_custom_call" | custom-call | flops 1 | bytes 1 | tf_op jit(solution)/shard_map/pallas_call | solution.py:94
  72.1 0.4 multiply_convert_fusion.1
  72.5 1.2 collective-permute-start.9
  73.7 1.4 collective-permute-start.12
  75.1 4.3 %shard_map.140 = f32[4,512,256]{2,1,0:T(8,128)S(1)} custom-call(s32[32]{0:T(128)S(1)} %slice_bitcast_fusion.5.table, f32[1]{0:T(128)S(6)} %copy.21.alpha, bf16[256,1024]{1,0:T(8,128)(2,1)S(1)} %pad_maximum_fusion.refs_0_.refs_2_.refs_4_.refs_6_, bf16[256,1024]{1,0:T(8,128)(2,1)S(1)} %collective-permute-done.6.refs_1_.refs_3_.refs_5_.refs_7_, ...), custom_call_target="tpu_custom_call" | custom-call | flops 1 | bytes 1 | tf_op jit(solution)/shard_map/pallas_call | solution.py:94
  79.4 0.4 multiply_convert_fusion
  79.9 1.1 collective-permute-start.14
  81.0 4.3 %shard_map.141 = f32[4,512,256]{2,1,0:T(8,128)S(1)} custom-call(s32[32]{0:T(128)S(1)} %slice_bitcast_fusion.5.table, f32[1]{0:T(128)S(6)} %copy.21.alpha, bf16[256,1024]{1,0:T(8,128)(2,1)S(1)} %pad_maximum_fusion.refs_0_.refs_2_.refs_4_.refs_6_, bf16[256,1024]{1,0:T(8,128)(2,1)S(1)} %collective-permute-done.6.refs_1_.refs_3_.refs_5_.refs_7_, ...), custom_call_target="tpu_custom_call" | custom-call | flops 1 | bytes 1 | tf_op jit(solution)/shard_map/pallas_call | solution.py:94
  85.3 4.3 %shard_map.142 = f32[4,512,256]{2,1,0:T(8,128)S(1)} custom-call(s32[32]{0:T(128)S(1)} %slice_bitcast_fusion.5.table, f32[1]{0:T(128)S(6)} %copy.21.alpha, bf16[256,1024]{1,0:T(8,128)(2,1)S(1)} %pad_maximum_fusion.refs_0_.refs_2_.refs_4_.refs_6_, bf16[256,1024]{1,0:T(8,128)(2,1)S(1)} %collective-permute-done.6.refs_1_.refs_3_.refs_5_.refs_7_, ...), custom_call_target="tpu_custom_call" | custom-call | flops 1 | bytes 1 | tf_op jit(solution)/shard_map/pallas_call | solution.py:94
  89.7 3.5 %collective-permute-done.9 = f16[4,512,256]{2,1,0:T(8,128)(2,1)S(1)} collective-permute-done((f16[4,512,256]{2,1,0:T(8,128)(2,1)S(1)}, f16[4,512,256]{2,1,0:T(8,128)(2,1)S(1)}, u32[]{:S(2)}, u32[]{:S(2)}) %collective-permute-start.9) | collective-permute-done | bytes 1048608 | tf_op jit(solution)/shard_map/ppermute | solution.py:37
  93.1 0.4 multiply_add_fusion.1
  93.7 0.3 collective-permute-start.10
  93.9 0.2 collective-permute-done.12
  94.1 8.5 %collective-permute-done.14 = f16[4,512,256]{2,1,0:T(8,128)(2,1)S(1)} collective-permute-done((f16[4,512,256]{2,1,0:T(8,128)(2,1)S(1)}, f16[4,512,256]{2,1,0:T(8,128)(2,1)S(1)}, u32[]{:S(2)}, u32[]{:S(2)}) %collective-permute-start.14) | collective-permute-done | bytes 1048608 | tf_op jit(solution)/shard_map/ppermute | solution.py:37
  102.6 0.4 multiply_add_fusion
  103.1 1.9 %collective-permute-start.15 = (f16[2,512,256]{2,1,0:T(8,128)(2,1)S(1)}, f16[2,512,256]{2,1,0:T(8,128)(2,1)S(1)}, u32[]{:S(2)}, u32[]{:S(2)}) collective-permute-start(f16[2,512,256]{2,1,0:T(8,128)(2,1)S(1)} %fusion), channel_id=1, source_target_pairs={{0,1},{1,0},{2,3},{3,2},{4,5},{5,4},{6,7},{7,6},{8,9},{9,8},{10,11... | collective-permute-start | bytes 1572872 | tf_op jit(solution)/shard_map/ppermute | solution.py:37
  105.1 0.3 collective-permute-done.10
  105.5 3.2 %collective-permute-start.11 = (f16[512,256]{1,0:T(8,128)(2,1)S(1)}, f16[512,256]{1,0:T(8,128)(2,1)S(1)}, u32[]{:S(2)}, u32[]{:S(2)}) collective-permute-start(f16[512,256]{1,0:T(8,128)(2,1)S(1)} %fusion.17), channel_id=1, source_target_pairs={{0,12},{1,13},{2,14},{3,15},{4,8},{5,9},{6,10},{7,11},{8,4},{9,5},... | collective-permute-start | bytes 786440 | tf_op jit(solution)/shard_map/ppermute | solution.py:37
  108.7 3.7 %collective-permute-done.15 = f16[2,512,256]{2,1,0:T(8,128)(2,1)S(1)} collective-permute-done((f16[2,512,256]{2,1,0:T(8,128)(2,1)S(1)}, f16[2,512,256]{2,1,0:T(8,128)(2,1)S(1)}, u32[]{:S(2)}, u32[]{:S(2)}) %collective-permute-start.15) | collective-permute-done | bytes 524320 | tf_op jit(solution)/shard_map/ppermute | solution.py:37
  112.5 1.7 %collective-permute-start.16 = (f16[512,256]{1,0:T(8,128)(2,1)S(1)}, f16[512,256]{1,0:T(8,128)(2,1)S(1)}, u32[]{:S(2)}, u32[]{:S(2)}) collective-permute-start(f16[512,256]{1,0:T(8,128)(2,1)S(1)} %fusion.18), channel_id=1, source_target_pairs={{0,3},{1,2},{2,1},{3,0},{4,7},{5,6},{6,5},{7,4},{8,11},{9,10},{10,... | collective-permute-start | bytes 786440 | tf_op jit(solution)/shard_map/ppermute | solution.py:37
  114.3 0.2 fusion.14
  114.4 5.7 %collective-permute-done.16 = f16[512,256]{1,0:T(8,128)(2,1)S(1)} collective-permute-done((f16[512,256]{1,0:T(8,128)(2,1)S(1)}, f16[512,256]{1,0:T(8,128)(2,1)S(1)}, u32[]{:S(2)}, u32[]{:S(2)}) %collective-permute-start.16) | collective-permute-done | bytes 262176 | tf_op jit(solution)/shard_map/ppermute | solution.py:37
  120.2 0.2 fusion.8
  120.3 0.1 fusion.16
  120.6 1.5 collective-permute-done.17
  122.2 0.3 collective-permute-start.18
  122.6 6.0 %collective-permute-done.18 = f16[2,2,64,512]{3,2,1,0:T(8,128)(2,1)S(1)} collective-permute-done((f16[2,2,64,512]{3,2,1,0:T(8,128)(2,1)S(1)}, f16[2,2,64,512]{3,2,1,0:T(8,128)(2,1)S(1)}, u32[]{:S(2)}, u32[]{:S(2)}) %collective-permute-start.18) | collective-permute-done | bytes 262176 | tf_op jit(solution)/shard_map/ppermute | solution.py:37
  128.7 3.3 %collective-permute-start.19 = (f16[2,2,64,512]{3,2,1,0:T(8,128)(2,1)S(1)}, f16[2,2,64,512]{3,2,1,0:T(8,128)(2,1)S(1)}, u32[]{:S(2)}, u32[]{:S(2)}) collective-permute-start(f16[2,2,64,512]{3,2,1,0:T(8,128)(2,1)S(1)} %fusion.19), channel_id=1, source_target_pairs={{0,96},{1,97},{2,98},{3,99},{4,100},{5,101},{6,102},{7,103},{8,104... | collective-permute-start | bytes 786440 | tf_op jit(solution)/shard_map/ppermute | solution.py:37
  132.1 4.3 %collective-permute-done.19 = f16[2,2,64,512]{3,2,1,0:T(8,128)(2,1)S(1)} collective-permute-done((f16[2,2,64,512]{3,2,1,0:T(8,128)(2,1)S(1)}, f16[2,2,64,512]{3,2,1,0:T(8,128)(2,1)S(1)}, u32[]{:S(2)}, u32[]{:S(2)}) %collective-permute-start.19) | collective-permute-done | bytes 262176 | tf_op jit(solution)/shard_map/ppermute | solution.py:37
  136.5 0.3 fusion.2
  136.7 1.5 exponential_reduce_fusion
  138.2 0.7 reshape.164
  138.9 7.6 %all-to-all-start = ((f32[16,1,192]{2,1,0:T(1,128)}), f32[16,1,192]{2,1,0:T(1,128)S(1)}, u32[]{:S(2)}, u32[]{:S(2)}) async-start(f32[16,1,192]{2,1,0:T(1,128)} %reshape.164), calls=%async_computation | async-start | bytes 32768 | tf_op jit(solution)/shard_map/all_to_all | solution.py:214
  146.5 0.6 slice_bitcast_fusion.6.source
  147.1 7.0 %all-to-all-done = f32[16,1,192]{2,1,0:T(1,128)S(1)} async-done(((f32[16,1,192]{2,1,0:T(1,128)}), f32[16,1,192]{2,1,0:T(1,128)S(1)}, u32[]{:S(2)}, u32[]{:S(2)}) %all-to-all-start) | async-done | bytes 12320 | tf_op jit(solution)/shard_map/all_to_all | solution.py:214
  154.1 0.5 broadcast.125
  154.6 0.7 reduce.2
  155.5 0.5 fusion.29
  156.0 0.7 copy.18.logz
  156.7 2.3 %shard_map.143 = f32[64,4096]{1,0:T(8,128)} custom-call(s32[8]{0:T(128)} %slice_bitcast_fusion.6.source, f32[8,64,512]{2,1,0:T(8,128)} %get-tuple-element.66.logits, f32[64,1]{1,0:T(8,128)} %copy.18.logz), custom_call_target="tpu_custom_call" | custom-call | tf_op jit(solution)/shard_map/pallas_call | solution.py:219
  (60 shorter events, 1.7 us)
Async XLA Ops:
  3.4 6.8 %copy-start.4 = (bf16[256]{0:T(256)(128)(2,1)S(1)}, bf16[256]{0:T(256)(128)(2,1)}, u32[]{:S(2)}) copy-start(bf16[256]{0:T(256)(128)(2,1)} %param.16) | copy-start | bytes 1540
  3.4 6.8 %copy-start.5 = (bf16[256]{0:T(256)(128)(2,1)S(1)}, bf16[256]{0:T(256)(128)(2,1)}, u32[]{:S(2)}) copy-start(bf16[256]{0:T(256)(128)(2,1)} %param.17) | copy-start | bytes 1540
  3.4 6.8 %copy-start.3 = (bf16[512]{0:T(512)(128)(2,1)S(1)}, bf16[512]{0:T(512)(128)(2,1)}, u32[]{:S(2)}) copy-start(bf16[512]{0:T(512)(128)(2,1)} %param.15) | copy-start | bytes 3076
  3.4 6.8 %collective-permute-start = (f32[3,64]{1,0:T(4,128)S(1)}, f32[3,64]{1,0:T(4,128)S(1)}, u32[]{:S(2)}, u32[]{:S(2)}) collective-permute-start(f32[3,64]{1,0:T(4,128)S(1)} %pad_maximum_fusion.6), channel_id=1, source_target_pairs={{0,1},{1,0},{2,3},{3,2},{4,5},{5,4},{6,7},{7,6},{8,9},{9,8},{10,11... | collective-permute-start | bytes 2312 | tf_op jit(solution)/shard_map/ppermute | solution.py:37
  10.2 7.3 %collective-permute-start.1 = (f32[3,64]{1,0:T(4,128)S(1)}, f32[3,64]{1,0:T(4,128)S(1)}, u32[]{:S(2)}, u32[]{:S(2)}) collective-permute-start(f32[3,64]{1,0:T(4,128)S(1)} %add.114), channel_id=1, source_target_pairs={{0,3},{1,2},{2,1},{3,0},{4,7},{5,6},{6,5},{7,4},{8,11},{9,10},{10,... | collective-permute-start | bytes 2312 | tf_op jit(solution)/shard_map/ppermute | solution.py:37
  17.5 6.8 %collective-permute-start.2 = (f32[3,64]{1,0:T(4,128)S(1)}, f32[3,64]{1,0:T(4,128)S(1)}, u32[]{:S(2)}, u32[]{:S(2)}) collective-permute-start(f32[3,64]{1,0:T(4,128)S(1)} %add.115), channel_id=1, source_target_pairs={{0,4},{1,5},{2,6},{3,7},{4,0},{5,1},{6,2},{7,3},{8,12},{9,13},{10,... | collective-permute-start | bytes 2312 | tf_op jit(solution)/shard_map/ppermute | solution.py:37
  24.3 7.4 %copy-start = (bf16[64,512]{1,0:T(8,128)(2,1)S(1)}, bf16[64,512]{1,0:T(8,128)(2,1)}, u32[]{:S(2)}) copy-start(bf16[64,512]{1,0:T(8,128)(2,1)} %param.12) | copy-start | bytes 196612
  24.3 7.5 %copy-start.1 = (bf16[64,256]{1,0:T(8,128)(2,1)S(1)}, bf16[64,256]{1,0:T(8,128)(2,1)}, u32[]{:S(2)}) copy-start(bf16[64,256]{1,0:T(8,128)(2,1)} %param.13) | copy-start | bytes 98308
  24.3 7.5 %copy-start.2 = (bf16[64,256]{1,0:T(8,128)(2,1)S(1)}, bf16[64,256]{1,0:T(8,128)(2,1)}, u32[]{:S(2)}) copy-start(bf16[64,256]{1,0:T(8,128)(2,1)} %param.14) | copy-start | bytes 98308
  24.3 7.4 %collective-permute-start.3 = (f32[3,64]{1,0:T(4,128)S(1)}, f32[3,64]{1,0:T(4,128)S(1)}, u32[]{:S(2)}, u32[]{:S(2)}) collective-permute-start(f32[3,64]{1,0:T(4,128)S(1)} %add.116), channel_id=1, source_target_pairs={{0,12},{1,13},{2,14},{3,15},{4,8},{5,9},{6,10},{7,11},{8,4},{9,5},... | collective-permute-start | bytes 2312 | tf_op jit(solution)/shard_map/ppermute | solution.py:37
  31.9 5.0 %collective-permute-start.4 = (bf16[64,1024]{1,0:T(8,128)(2,1)S(1)}, bf16[64,1024]{1,0:T(8,128)(2,1)S(1)}, u32[]{:S(2)}, u32[]{:S(2)}) collective-permute-start(bf16[64,1024]{1,0:T(8,128)(2,1)S(1)} %pad_maximum_fusion.5), channel_id=1, source_target_pairs={{0,32},{1,33},{2,34},{3,35},{4,36},{5,37},{6,38},{7,39},{8,40},{9,... | collective-permute-start | bytes 393224 | tf_op jit(solution)/shard_map/ppermute | solution.py:37
  37.0 8.5 %collective-permute-start.5 = (bf16[2,64,1024]{2,1,0:T(8,128)(2,1)S(1)}, bf16[2,64,1024]{2,1,0:T(8,128)(2,1)S(1)}, u32[]{:S(2)}, u32[]{:S(2)}) collective-permute-start(bf16[2,64,1024]{2,1,0:T(8,128)(2,1)S(1)} %pad_maximum_fusion.4), channel_id=1, source_target_pairs={{0,96},{1,97},{2,98},{3,99},{4,100},{5,101},{6,102},{7,103},{8,104... | collective-permute-start | bytes 786440 | tf_op jit(solution)/shard_map/ppermute | solution.py:37
  45.6 2.0 %collective-permute-start.6 = (bf16[256,1024]{1,0:T(8,128)(2,1)S(1)}, bf16[256,1024]{1,0:T(8,128)(2,1)S(1)}, u32[]{:S(2)}, u32[]{:S(2)}) collective-permute-start(bf16[256,1024]{1,0:T(8,128)(2,1)S(1)} %pad_maximum_fusion.refs_0_.refs_2_.refs_4_.refs_6_), channel_id=1, source_target_pairs={{0,16},{1,17},{2,18},{3,19},{4,20},{5,21},{6,22},{7,23},{8,24},{9,... | collective-permute-start | bytes 1572872 | tf_op jit(solution)/shard_map/ppermute | solution.py:37
  51.9 20.2 %collective-permute-start.8 = (bf16[4,512,256]{2,1,0:T(8,128)(2,1)S(1)}, bf16[4,512,256]{2,1,0:T(8,128)(2,1)S(1)}, u32[]{:S(2)}, u32[]{:S(2)}) collective-permute-start(bf16[4,512,256]{2,1,0:T(8,128)(2,1)S(1)} %shard_map.135), channel_id=1, source_target_pairs={{0,1},{1,0},{2,3},{3,2},{4,5},{5,4},{6,7},{7,6},{8,9},{9,8},{10,11... | collective-permute-start | bytes 3145736 | tf_op jit(solution)/shard_map/ppermute | solution.py:37
  56.9 22.6 %collective-permute-start.13 = (bf16[4,512,256]{2,1,0:T(8,128)(2,1)S(1)}, bf16[4,512,256]{2,1,0:T(8,128)(2,1)S(1)}, u32[]{:S(2)}, u32[]{:S(2)}) collective-permute-start(bf16[4,512,256]{2,1,0:T(8,128)(2,1)S(1)} %shard_map.136), channel_id=1, source_target_pairs={{0,4},{1,5},{2,6},{3,7},{4,0},{5,1},{6,2},{7,3},{8,12},{9,13},{10,... | collective-permute-start | bytes 3145736 | tf_op jit(solution)/shard_map/ppermute | solution.py:37
  66.3 23.4 %collective-permute-start.7 = (bf16[4,512,256]{2,1,0:T(8,128)(2,1)S(1)}, bf16[4,512,256]{2,1,0:T(8,128)(2,1)S(1)}, u32[]{:S(2)}, u32[]{:S(2)}) collective-permute-start(bf16[4,512,256]{2,1,0:T(8,128)(2,1)S(1)} %shard_map.137), channel_id=1, source_target_pairs={{0,1},{1,0},{2,3},{3,2},{4,5},{5,4},{6,7},{7,6},{8,9},{9,8},{10,11... | collective-permute-start | bytes 3145736 | tf_op jit(solution)/shard_map/ppermute | solution.py:37
  72.5 20.6 %collective-permute-start.9 = (f16[4,512,256]{2,1,0:T(8,128)(2,1)S(1)}, f16[4,512,256]{2,1,0:T(8,128)(2,1)S(1)}, u32[]{:S(2)}, u32[]{:S(2)}) collective-permute-start(f16[4,512,256]{2,1,0:T(8,128)(2,1)S(1)} %multiply_convert_fusion.1), channel_id=1, source_target_pairs={{0,3},{1,2},{2,1},{3,0},{4,7},{5,6},{6,5},{7,4},{8,11},{9,10},{10,... | collective-permute-start | bytes 3145736 | tf_op jit(solution)/shard_map/ppermute | solution.py:37
  73.7 20.4 %collective-permute-start.12 = (bf16[4,512,256]{2,1,0:T(8,128)(2,1)S(1)}, bf16[4,512,256]{2,1,0:T(8,128)(2,1)S(1)}, u32[]{:S(2)}, u32[]{:S(2)}) collective-permute-start(bf16[4,512,256]{2,1,0:T(8,128)(2,1)S(1)} %shard_map.138), channel_id=1, source_target_pairs={{0,4},{1,5},{2,6},{3,7},{4,0},{5,1},{6,2},{7,3},{8,12},{9,13},{10,... | collective-permute-start | bytes 3145736 | tf_op jit(solution)/shard_map/ppermute | solution.py:37
  79.9 22.7 %collective-permute-start.14 = (f16[4,512,256]{2,1,0:T(8,128)(2,1)S(1)}, f16[4,512,256]{2,1,0:T(8,128)(2,1)S(1)}, u32[]{:S(2)}, u32[]{:S(2)}) collective-permute-start(f16[4,512,256]{2,1,0:T(8,128)(2,1)S(1)} %multiply_convert_fusion), channel_id=1, source_target_pairs={{0,12},{1,13},{2,14},{3,15},{4,8},{5,9},{6,10},{7,11},{8,4},{9,5},... | collective-permute-start | bytes 3145736 | tf_op jit(solution)/shard_map/ppermute | solution.py:37
  93.7 11.7 %collective-permute-start.10 = (f16[2,512,256]{2,1,0:T(8,128)(2,1)S(1)}, f16[2,512,256]{2,1,0:T(8,128)(2,1)S(1)}, u32[]{:S(2)}, u32[]{:S(2)}) collective-permute-start(f16[2,512,256]{2,1,0:T(8,128)(2,1)S(1)} %fusion.1), channel_id=1, source_target_pairs={{0,4},{1,5},{2,6},{3,7},{4,0},{5,1},{6,2},{7,3},{8,12},{9,13},{10,... | collective-permute-start | bytes 1572872 | tf_op jit(solution)/shard_map/ppermute | solution.py:37
  103.1 9.3 %collective-permute-start.15 = (f16[2,512,256]{2,1,0:T(8,128)(2,1)S(1)}, f16[2,512,256]{2,1,0:T(8,128)(2,1)S(1)}, u32[]{:S(2)}, u32[]{:S(2)}) collective-permute-start(f16[2,512,256]{2,1,0:T(8,128)(2,1)S(1)} %fusion), channel_id=1, source_target_pairs={{0,1},{1,0},{2,3},{3,2},{4,5},{5,4},{6,7},{7,6},{8,9},{9,8},{10,11... | collective-permute-start | bytes 1572872 | tf_op jit(solution)/shard_map/ppermute | solution.py:37
  105.5 8.8 %collective-permute-start.11 = (f16[512,256]{1,0:T(8,128)(2,1)S(1)}, f16[512,256]{1,0:T(8,128)(2,1)S(1)}, u32[]{:S(2)}, u32[]{:S(2)}) collective-permute-start(f16[512,256]{1,0:T(8,128)(2,1)S(1)} %fusion.17), channel_id=1, source_target_pairs={{0,12},{1,13},{2,14},{3,15},{4,8},{5,9},{6,10},{7,11},{8,4},{9,5},... | collective-permute-start | bytes 786440 | tf_op jit(solution)/shard_map/ppermute | solution.py:37
  112.5 7.7 %collective-permute-start.16 = (f16[512,256]{1,0:T(8,128)(2,1)S(1)}, f16[512,256]{1,0:T(8,128)(2,1)S(1)}, u32[]{:S(2)}, u32[]{:S(2)}) collective-permute-start(f16[512,256]{1,0:T(8,128)(2,1)S(1)} %fusion.18), channel_id=1, source_target_pairs={{0,3},{1,2},{2,1},{3,0},{4,7},{5,6},{6,5},{7,4},{8,11},{9,10},{10,... | collective-permute-start | bytes 786440 | tf_op jit(solution)/shard_map/ppermute | solution.py:37
  114.4 17.6 %copy-start.6 = (s32[64]{0:T(128)S(1)}, s32[64]{0:T(128)}, u32[]{:S(2)}) copy-start(s32[64]{0:T(128)} %param.22) | copy-start | bytes 772
  120.5 1.6 %collective-permute-start.17 = (f16[4,64,512]{2,1,0:T(8,128)(2,1)S(1)}, f16[4,64,512]{2,1,0:T(8,128)(2,1)S(1)}, u32[]{:S(2)}, u32[]{:S(2)}) collective-permute-start(f16[4,64,512]{2,1,0:T(8,128)(2,1)S(1)} %bitcast.74), channel_id=1, source_target_pairs={{0,16},{1,17},{2,18},{3,19},{4,20},{5,21},{6,22},{7,23},{8,24},{9,... | collective-permute-start | bytes 786440 | tf_op jit(solution)/shard_map/ppermute | solution.py:37
  122.2 6.5 %collective-permute-start.18 = (f16[2,2,64,512]{3,2,1,0:T(8,128)(2,1)S(1)}, f16[2,2,64,512]{3,2,1,0:T(8,128)(2,1)S(1)}, u32[]{:S(2)}, u32[]{:S(2)}) collective-permute-start(f16[2,2,64,512]{3,2,1,0:T(8,128)(2,1)S(1)} %fusion.15), channel_id=1, source_target_pairs={{0,32},{1,33},{2,34},{3,35},{4,36},{5,37},{6,38},{7,39},{8,40},{9,... | collective-permute-start | bytes 786440 | tf_op jit(solution)/shard_map/ppermute | solution.py:37
  128.7 7.7 %collective-permute-start.19 = (f16[2,2,64,512]{3,2,1,0:T(8,128)(2,1)S(1)}, f16[2,2,64,512]{3,2,1,0:T(8,128)(2,1)S(1)}, u32[]{:S(2)}, u32[]{:S(2)}) collective-permute-start(f16[2,2,64,512]{3,2,1,0:T(8,128)(2,1)S(1)} %fusion.19), channel_id=1, source_target_pairs={{0,96},{1,97},{2,98},{3,99},{4,100},{5,101},{6,102},{7,103},{8,104... | collective-permute-start | bytes 786440 | tf_op jit(solution)/shard_map/ppermute | solution.py:37
  138.9 15.1 %all-to-all-start = ((f32[16,1,192]{2,1,0:T(1,128)}), f32[16,1,192]{2,1,0:T(1,128)S(1)}, u32[]{:S(2)}, u32[]{:S(2)}) async-start(f32[16,1,192]{2,1,0:T(1,128)} %reshape.164), calls=%async_computation | async-start | bytes 32768 | tf_op jit(solution)/shard_map/all_to_all | solution.py:214

commit v2 on v1

--- a/solution.py
+++ b/solution.py
@@ -1,3 +1,5 @@
+import functools
+
 import jax
 import jax.numpy as jnp
 import numpy as np
@@ -58,30 +60,27 @@
 
 def relay(head, start, count, step=64):
     _, n_a, c = head.shape
-    out = pl.pallas_call(
+    return pl.pallas_call(
         relay_kernel,
         grid=(count // step,),
         in_specs=[pl.BlockSpec((step, n_a, c), lambda i: (start // step + i, 0, 0))],
         out_specs=pl.BlockSpec((n_a, step, c), lambda i: (0, i, 0)),
         out_shape=jax.ShapeDtypeStruct((n_a, count, c), head.dtype),
+        compiler_params=pltpu.CompilerParams(vmem_limit_bytes=12 << 20),
         cost_estimate=pl.CostEstimate(flops=10**10, bytes_accessed=2**24, transcendentals=0),
     )(head)
-    return pltpu.with_memory_space_constraint(out, pltpu.HBM)
-
-
-def matmul_kernel(table, alpha, *refs):
-    xs, ws, out = refs[:8], refs[8:12], refs[12]
-    tokens = xs[0].shape[0]
-    for i in range(2):
-        base0, base1, expert, anti = [
-            jnp.dot(x[...], w[0], preferred_element_type=F32) for x, w in zip(xs[i::2], ws)
-        ]
-        total = base0 + base1 + alpha[0] * (expert - anti)
-        out[0, i * tokens : (i + 1) * tokens] = total.astype(out.dtype)
+
+
+def matmul_kernel(table, alpha, xb0, xb1, xe, xa, wb0, wb1, we, wa, out):
+    base0, base1, expert, anti = [
+        jnp.dot(x[...], w[0], preferred_element_type=F32)
+        for x, w in ((xb0, wb0), (xb1, wb1), (xe, we), (xa, wa))
+    ]
+    out[0] = (base0 + base1 + alpha[0] * (expert - anti)).astype(out.dtype)
 
 
 def project(table, alpha, acts, heads, first, half, dtype):
-    tokens = acts[0].shape[0]
+    tokens = acts.shape[0]
     half_c = heads[0].shape[2] // 2
     quarter = heads[0].shape[1]
 
@@ -97,14 +96,14 @@
             num_scalar_prefetch=1,
             grid=(4,),
             in_specs=[pl.BlockSpec(memory_space=pltpu.SMEM)]
-            + [features(i) for i in range(4) for _ in acts]
+            + [features(i) for i in range(4)]
             + [weights() for _ in heads],
-            out_specs=pl.BlockSpec((1, 2 * tokens, half_c), lambda i, tab: (i, 0, 0)),
+            out_specs=pl.BlockSpec((1, tokens, half_c), lambda i, tab: (i, 0, 0)),
         ),
-        out_shape=jax.ShapeDtypeStruct((4, 2 * tokens, half_c), dtype),
-        compiler_params=pltpu.CompilerParams(vmem_limit_bytes=32 << 20),
+        out_shape=jax.ShapeDtypeStruct((4, tokens, half_c), dtype),
+        compiler_params=pltpu.CompilerParams(vmem_limit_bytes=12 << 20),
         cost_estimate=pl.CostEstimate(flops=1, bytes_accessed=1, transcendentals=0),
-    )(table, alpha, *acts * 4, *heads)
+    )(table, alpha, *[acts] * 4, *heads)
 
 
 def wide(value):
@@ -115,21 +114,85 @@
     return (value * DOWN).astype(F16)
 
 
+def in_hbm(value):
+    return pltpu.with_memory_space_constraint(value, pltpu.HBM)
+
+
 def together(*values):
     return lax.optimization_barrier(values)
 
 
-def merge(stats):
-    top = jnp.max(stats[:, 0], axis=0)
-    total = jnp.sum(stats[:, 1] * jnp.exp(stats[:, 0] - top[None]), axis=0)
-    return top + jnp.log(total), jnp.sum(stats[:, 2], axis=0)
-
-
-def final_kernel(source, logits, logz, out):
-    width = logits.shape[2]
-    for i in range(logits.shape[0]):
+def lanes(columns, rows):
+    lane = lax.broadcasted_iota(jnp.int32, (rows, 128), 1)
+    out = jnp.zeros((rows, 128), F32)
+    for i, column in enumerate(columns):
+        out = jnp.where(lane == i, column, out)
+    return out
+
+
+def square_kernel(*refs):
+    values = [h[...].astype(F32) for h in refs[:-1]]
+    sums = [jnp.sum(h * h, axis=1, keepdims=True) for h in values]
+    refs[-1][...] = lanes(sums, refs[-1].shape[0])
+
+
+def norm_kernel(widths, *refs):
+    hidden, gains, sq, got, out = refs[:3], refs[3:6], refs[6], refs[7], refs[8]
+    total = sq[...] + got[...]
+    at = 0
+    for i, h in enumerate(hidden):
+        scale = lax.rsqrt(total[:, i : i + 1] / widths[i] + 1e-05)
+        value = h[...].astype(F32) * scale * gains[i][...].astype(F32)
+        out[:, at : at + h.shape[1]] = value.astype(out.dtype)
+        at += h.shape[1]
+
+
+def stats_kernel(source, home, wanted, out):
+    pieces, rows, width = home.shape
+    top = jnp.max(home[...], axis=(0,))
+    top = jnp.max(top, axis=1, keepdims=True)
+    total = jnp.zeros((rows, width), F32)
+    pick = jnp.zeros((rows, width), F32)
+    lane = lax.broadcasted_iota(jnp.int32, (rows, width), 1)
+    for i in range(pieces):
+        value = home[i]
+        total += jnp.exp(value - top)
+        pick += jnp.where(lane == wanted[...] - source[i] * width, value, 0.0)
+    total = jnp.sum(total, axis=1, keepdims=True)
+    pick = jnp.sum(pick, axis=1, keepdims=True)
+    square = jnp.concatenate([lanes([top, total, pick], rows), jnp.zeros((128 - rows, 128), F32)])
+    out[...] = jnp.broadcast_to(square.T[None, :8], out.shape)
+
+
+def final_kernel(source, home, stats, out, picked):
+    pieces, rows, width = home.shape
+    tops, totals, picks = [stats[:, i, :rows] for i in range(3)]
+    top = jnp.max(tops, axis=0, keepdims=True)
+    logz = top + jnp.log(jnp.sum(totals * jnp.exp(tops - top), axis=0, keepdims=True))
+    picked[...] = jnp.sum(picks, axis=0, keepdims=True) - logz
+    square = jnp.concatenate(
+        [jnp.broadcast_to(logz, (128, rows)), jnp.zeros((128, 128 - rows), F32)], axis=1
+    )
+    column = square.T[:rows, :1]
+    for i in range(pieces):
         at = pl.multiple_of(source[i] * width, width)
-        out[:, pl.ds(at, width)] = logits[i] - logz[...]
+        out[:, pl.ds(at, width)] = home[i] - column
+
+
+def call(kernel, shapes, *args):
+    def spec(v):
+        small = v.ndim == 1 and v.dtype == jnp.int32
+        return pl.BlockSpec(memory_space=pltpu.SMEM) if small else pl.BlockSpec()
+
+    outs = [jax.ShapeDtypeStruct(s, d) for s, d in shapes]
+    result = pl.pallas_call(
+        kernel,
+        in_specs=[spec(v) for v in args],
+        out_specs=[pl.BlockSpec() for _ in outs],
+        out_shape=outs,
+        compiler_params=pltpu.CompilerParams(vmem_limit_bytes=16 << 20),
+    )(*args)
+    return result if len(outs) > 1 else result[0]
 
 
 def shards(
@@ -151,31 +214,35 @@
     mine = lax.dynamic_slice(jnp.asarray(tables()), (r * (NY * NX) + t, 0), (1, 48))[0]
     table, source = mine[:32], mine[32:40]
 
-    values = [h.astype(F32) for h in (base_hidden, expert_hidden, anti_hidden)]
-    sq = jnp.stack([jnp.sum(h * h, axis=1) for h in values])
     quarter = expert_head.shape[0]
-    raw = ((base_head, 0), (base_head, quarter), (expert_head, 0), (anti_head, 0))
+    base = in_hbm(base_head)
+    raw = [(base, 0), (base, quarter), (expert_head, 0), (anti_head, 0)]
     heads = []
-    for i, (axis, stage) in enumerate((("x", 0), ("x", 1), ("y", 0), ("y", 1))):
-        head, start = raw[i]
-        sq, head = together(sq, head)
-        got, head = together(exchange(sq, axis, stage), relay(head, start, quarter))
+
+    def swap(value, axis, stage, beside):
+        if not beside:
+            return exchange(value, axis, stage)
+        head, start = raw[len(heads)]
+        value, head = together(value, head)
+        got, head = together(exchange(value, axis, stage), relay(head, start, quarter))
         heads.append(head)
-        sq = sq + got
-    widths = (D, DE, DE)
-    gains = (base_gain, expert_gain, anti_gain)
-    normed = jnp.concatenate(
-        [
-            h * lax.rsqrt(sq[i] / widths[i] + 1e-05)[:, None] * gains[i].astype(F32)
-            for i, h in enumerate(values)
-        ],
-        axis=1,
-    ).astype(BF)
-
-    pair = exchange(normed, "z", 0)
-    far = exchange(jnp.stack([normed, pair]), "z", 1)
+        return got
+
+    hidden = (base_hidden, expert_hidden, anti_hidden)
+    gains = [g[None] for g in (base_gain, expert_gain, anti_gain)]
+    sq = call(square_kernel, [((rows, 128), F32)], *[in_hbm(h) for h in hidden])
+    sq += swap(sq, "x", 0, False)
+    sq += swap(sq, "x", 1, True)
+    sq += swap(sq, "y", 0, False)
+    got = swap(sq, "y", 1, True)
+    width = sum(h.shape[1] for h in hidden)
+    normed = call(
+        functools.partial(norm_kernel, (D, DE, DE)), [((rows, width), BF)], *hidden, *gains, sq, got
+    )
+    pair = swap(normed, "z", 0, True)
+    far = swap(jnp.stack([normed, pair]), "z", 1, True)
     mine = jnp.concatenate([pair, far[1], normed, far[0]])
-    acts = [mine, exchange(mine, "core", 0)]
+    acts = jnp.concatenate([mine, exchange(mine, "core", 0)])
 
     axes = (("x", "y"), ("y", "x"))
     kept = [[], []]
@@ -205,28 +272,13 @@
     near = exchange(both[:2], "z", 0)
     last = exchange(jnp.stack([both[3], near[1]]), "z", 1)
     home = jnp.concatenate([both[2], near[0], last[0], last[1]]).astype(F32) * UP
-    top = jnp.max(home, axis=(0, 2))
-    total = jnp.sum(jnp.exp(home - top[None, :, None]), axis=(0, 2))
-    column = source[:, None, None] * c_width + lax.broadcasted_iota(jnp.int32, (8, 1, c_width), 2)
-    wanted = (token_ids - t * (8 * c_width))[None, :, None]
-    pick = jnp.sum(jnp.where(column == wanted, home, 0.0), axis=(0, 2))
-    stats = jnp.stack([top, total, pick])
-    stats = lax.all_to_all(
-        jnp.broadcast_to(stats[None], (NY * NX, 3, rows)), "tensor", 0, 0, tiled=True
+    wanted = (token_ids - t * (8 * c_width))[:, None]
+    stats = call(stats_kernel, [((NY * NX, 8, 128), F32)], source, home, wanted)
+    stats = lax.all_to_all(stats, "tensor", 0, 0, tiled=True)
+    log_probs, picked = call(
+        final_kernel, [((rows, 8 * c_width), F32), ((1, rows), F32)], source, home, stats
     )
-    logz, pick = merge(stats)
-
-    log_probs = pl.pallas_call(
-        final_kernel,
-        in_specs=[
-            pl.BlockSpec(memory_space=pltpu.SMEM),
-            pl.BlockSpec(memory_space=pltpu.VMEM),
-            pl.BlockSpec(memory_space=pltpu.VMEM),
-        ],
-        out_specs=pl.BlockSpec(memory_space=pltpu.VMEM),
-        out_shape=jax.ShapeDtypeStruct((rows, 8 * c_width), F32),
-    )(source, home, logz[:, None])
-    return log_probs, pick - logz
+    return log_probs, picked[0]
 
 
 def solution(mesh):

time: 160 us -> 139 us (0.87)
  Pallas kernels: 57.3 us -> 36.8 us
  blocking collectives: 0 us -> 14 us
  starting transfers between devices: 38.9 us -> 30.1 us
  other arithmetic: 9.06 us -> 2.9 us
  waiting for transfers between devices: 48.6 us -> 51.6 us
  local copies, waits for them, and re-layouts: 3.47 us -> 1.11 us
    all_to_all x0 -> x1, blocking collectives: none -> 14 us  [shards(): stats = lax.all_to_all(stats, 'tensor', 0, 0, tiled=True)]
    pallas_call x8, Pallas kernels: 34.5 us -> 23 us  [project(): pl.pallas_call(matmul_kernel, grid_spec=pltpu.PrefetchScalarGridSpec(num_...]
    pallas_call x4, Pallas kernels: 20.4 us -> 9.9 us  [relay(): pl.pallas_call(relay_kernel, grid=(count // step,), in_specs=[pl.BlockSpe...]
    ppermute x20, waiting for transfers between devices: 41.6 us -> 51.6 us  [exchange(): return lax.ppermute(value, AXES, pairs)]
    all_to_all x1 -> x0, starting transfers between devices: 7.56 us -> none  [shards(): lax.all_to_all(jnp.broadcast_to(stats[None], (NY * NX, 3, rows)), 'tensor...]
    all_to_all x1 -> x0, waiting for transfers between devices: 6.98 us -> none  [shards(): lax.all_to_all(jnp.broadcast_to(stats[None], (NY * NX, 3, rows)), 'tensor...]
    reduce_sum x6 -> x0, other arithmetic: 4.22 us -> none  [the longest x3 2.7 us: shards(): sq = jnp.stack([jnp.sum(h * h, axis=1) for h in values])]
    pallas_call x1 -> x4, Pallas kernels: 2.34 us -> 3.9 us  [call(): pl.pallas_call(kernel, in_specs=[spec(v) for v in args], out_specs=[pl.Bl...]
  transfers between devices with their start and end apart: 21 -> 20, of which waited for: 13 -> 17; matrix products, arithmetic and copies ran while one was open for 2% -> 2% of each run, Pallas kernels for 32% -> 22%
where the time goes in v2:
time: 139 us; the launch traced here: 138 us
  waiting for transfers between devices  51.6 us (37%)
  Pallas kernels  36.8 us (26%)
  starting transfers between devices  30.1 us (22%)
  blocking collectives  14 us (10%)
  other arithmetic  2.9 us (2%)
  between operations  1.74 us (1%)
    ppermute x20, waiting for transfers between devices, exchange(): return lax.ppermute(value, AXES, pairs)  51.6 us
    ppermute x20, starting transfers between devices, exchange(): return lax.ppermute(value, AXES, pairs)  30.1 us
    pallas_call x8, Pallas kernels, project(): pl.pallas_call(matmul_kernel, grid_spec=pltpu.PrefetchScalarGridSpec(num_...  23 us
    all_to_all x1, blocking collectives, shards(): stats = lax.all_to_all(stats, 'tensor', 0, 0, tiled=True)  14 us
    pallas_call x4, Pallas kernels, relay(): pl.pallas_call(relay_kernel, grid=(count // step,), in_specs=[pl.BlockSpe...  9.9 us
    pallas_call x4, Pallas kernels, call(): pl.pallas_call(kernel, in_specs=[spec(v) for v in args], out_specs=[pl.Bl...  3.9 us
  transfers between devices with their start and end apart: 20, of which 17 were waited for; matrix products, arithmetic and copies ran while one was open for 2% of the time, Pallas kernels for 22%

profile of v2, /device:TPU:0, one launch (start us, length us, event | category | flops | bytes accessed | tf_op | source)
XLA Modules:
  0.0 138.3 jit_solution(17582529769995847679)
XLA Ops:
  0.6 1.0 shard_map.131
  1.6 1.7 %collective-permute-start = (f32[64,128]{1,0:T(8,128)S(1)}, f32[64,128]{1,0:T(8,128)S(1)}, u32[]{:S(2)}, u32[]{:S(2)}) collective-permute-start(f32[64,128]{1,0:T(8,128)S(1)} %shard_map.131), channel_id=1, source_target_pairs={{0,1},{1,0},{2,3},{3,2},{4,5},{5,4},{6,7},{7,6},{8,9},{9,8},{10,11... | collective-permute-start | bytes 98312 | tf_op jit(solution)/shard_map/ppermute | solution.py:39
  3.3 0.7 constant_dynamic-slice_fusion
  3.9 1.6 %collective-permute-done = f32[64,128]{1,0:T(8,128)S(1)} collective-permute-done((f32[64,128]{1,0:T(8,128)S(1)}, f32[64,128]{1,0:T(8,128)S(1)}, u32[]{:S(2)}, u32[]{:S(2)}) %collective-permute-start) | collective-permute-done | bytes 32800 | tf_op jit(solution)/shard_map/ppermute | solution.py:39
  5.6 2.9 %collective-permute-start.1 = (f32[64,128]{1,0:T(8,128)S(1)}, f32[64,128]{1,0:T(8,128)S(1)}, u32[]{:S(2)}, u32[]{:S(2)}) collective-permute-start(f32[64,128]{1,0:T(8,128)S(1)} %add.61), channel_id=1, source_target_pairs={{0,3},{1,2},{2,1},{3,0},{4,7},{5,6},{6,5},{7,4},{8,11},{9,10},{10,... | collective-permute-start | bytes 98312 | tf_op jit(solution)/shard_map/ppermute | solution.py:39
  8.6 3.6 %shard_map.132.wb0 = bf16[16,256,512]{2,1,0:T(8,128)(2,1)S(1)} custom-call(bf16[512,16,512]{2,1,0:T(8,128)(2,1)} %head.1), custom_call_target="tpu_custom_call" | custom-call | flops 10000000000 | bytes 16777216 | tf_op jit(solution)/shard_map/pallas_call | solution.py:63
  12.2 1.7 %collective-permute-start.2 = (f32[64,128]{1,0:T(8,128)S(1)}, f32[64,128]{1,0:T(8,128)S(1)}, u32[]{:S(2)}, u32[]{:S(2)}) collective-permute-start(f32[64,128]{1,0:T(8,128)S(1)} %add.62), channel_id=1, source_target_pairs={{0,4},{1,5},{2,6},{3,7},{4,0},{5,1},{6,2},{7,3},{8,12},{9,13},{10,... | collective-permute-start | bytes 98312 | tf_op jit(solution)/shard_map/ppermute | solution.py:39
  14.5 1.6 %collective-permute-done.2 = f32[64,128]{1,0:T(8,128)S(1)} collective-permute-done((f32[64,128]{1,0:T(8,128)S(1)}, f32[64,128]{1,0:T(8,128)S(1)}, u32[]{:S(2)}, u32[]{:S(2)}) %collective-permute-start.2) | collective-permute-done | bytes 32800 | tf_op jit(solution)/shard_map/ppermute | solution.py:39
  16.2 3.1 %collective-permute-start.3 = (f32[64,128]{1,0:T(8,128)S(1)}, f32[64,128]{1,0:T(8,128)S(1)}, u32[]{:S(2)}, u32[]{:S(2)}) collective-permute-start(f32[64,128]{1,0:T(8,128)S(1)} %add.63.refs_6_), channel_id=1, source_target_pairs={{0,12},{1,13},{2,14},{3,15},{4,8},{5,9},{6,10},{7,11},{8,4},{9,5},... | collective-permute-start | bytes 98312 | tf_op jit(solution)/shard_map/ppermute | solution.py:39
  19.3 3.6 %shard_map.133.wb1 = bf16[16,256,512]{2,1,0:T(8,128)(2,1)S(1)} custom-call(bf16[512,16,512]{2,1,0:T(8,128)(2,1)} %head.1), custom_call_target="tpu_custom_call" | custom-call | flops 10000000000 | bytes 16777216 | tf_op jit(solution)/shard_map/pallas_call | solution.py:63
  23.0 0.1 shard_map.134
  23.1 2.0 %collective-permute-start.4 = (bf16[64,1024]{1,0:T(8,128)(2,1)S(1)}, bf16[64,1024]{1,0:T(8,128)(2,1)S(1)}, u32[]{:S(2)}, u32[]{:S(2)}) collective-permute-start(bf16[64,1024]{1,0:T(8,128)(2,1)S(1)} %shard_map.134), channel_id=1, source_target_pairs={{0,32},{1,33},{2,34},{3,35},{4,36},{5,37},{6,38},{7,39},{8,40},{9,... | collective-permute-start | bytes 393224 | tf_op jit(solution)/shard_map/ppermute | solution.py:39
  25.1 1.4 shard_map.135.we
  26.5 3.1 %collective-permute-done.4 = bf16[64,1024]{1,0:T(8,128)(2,1)S(1)} collective-permute-done((bf16[64,1024]{1,0:T(8,128)(2,1)S(1)}, bf16[64,1024]{1,0:T(8,128)(2,1)S(1)}, u32[]{:S(2)}, u32[]{:S(2)}) %collective-permute-start.4) | collective-permute-done | bytes 131104 | tf_op jit(solution)/shard_map/ppermute | solution.py:39
  29.6 4.1 %collective-permute-start.5 = (bf16[2,64,1024]{2,1,0:T(8,128)(2,1)S(1)}, bf16[2,64,1024]{2,1,0:T(8,128)(2,1)S(1)}, u32[]{:S(2)}, u32[]{:S(2)}) collective-permute-start(bf16[2,64,1024]{2,1,0:T(8,128)(2,1)S(1)} %pad_maximum_fusion.3), channel_id=1, source_target_pairs={{0,96},{1,97},{2,98},{3,99},{4,100},{5,101},{6,102},{7,103},{8,104... | collective-permute-start | bytes 786440 | tf_op jit(solution)/shard_map/ppermute | solution.py:39
  33.7 1.4 shard_map.136.wa
  35.1 2.9 %collective-permute-done.5 = bf16[2,64,1024]{2,1,0:T(8,128)(2,1)S(1)} collective-permute-done((bf16[2,64,1024]{2,1,0:T(8,128)(2,1)S(1)}, bf16[2,64,1024]{2,1,0:T(8,128)(2,1)S(1)}, u32[]{:S(2)}, u32[]{:S(2)}) %collective-permute-start.5) | collective-permute-done | bytes 262176 | tf_op jit(solution)/shard_map/ppermute | solution.py:39
  38.3 1.8 %collective-permute-done.6 = bf16[256,1024]{1,0:T(8,128)(2,1)S(1)} collective-permute-done((bf16[256,1024]{1,0:T(8,128)(2,1)S(1)}, bf16[256,1024]{1,0:T(8,128)(2,1)S(1)}, u32[]{:S(2)}, u32[]{:S(2)}) %collective-permute-start.6) | collective-permute-done | bytes 524320 | tf_op jit(solution)/shard_map/ppermute | solution.py:39
  40.1 2.9 %shard_map.137 = bf16[4,512,256]{2,1,0:T(8,128)(2,1)S(1)} custom-call(s32[32]{0:T(128)S(1)} %slice_bitcast_fusion.5.table, f32[1]{0:T(128)S(6)} %copy.19.alpha, bf16[512,1024]{1,0:T(8,128)(2,1)S(1)} %constant_dynamic-update-slice_fusion.xb0.xb1.xe.xa, bf16[512,1024]{1,0:T(8,128)(2,1)S(1)} %constant_dynamic-update-slice_fusion.xb0.xb1.xe.xa, ...), custom_call_target="tpu_custom_call" | custom-call | flops 1 | bytes 1 | tf_op jit(solution)/shard_map/pallas_call | solution.py:93
  43.1 2.9 %shard_map.138 = bf16[4,512,256]{2,1,0:T(8,128)(2,1)S(1)} custom-call(s32[32]{0:T(128)S(1)} %slice_bitcast_fusion.5.table, f32[1]{0:T(128)S(6)} %copy.19.alpha, bf16[512,1024]{1,0:T(8,128)(2,1)S(1)} %constant_dynamic-update-slice_fusion.xb0.xb1.xe.xa, bf16[512,1024]{1,0:T(8,128)(2,1)S(1)} %constant_dynamic-update-slice_fusion.xb0.xb1.xe.xa, ...), custom_call_target="tpu_custom_call" | custom-call | flops 1 | bytes 1 | tf_op jit(solution)/shard_map/pallas_call | solution.py:93
  46.0 0.3 collective-permute-start.13
  46.3 2.9 %shard_map.139 = bf16[4,512,256]{2,1,0:T(8,128)(2,1)S(1)} custom-call(s32[32]{0:T(128)S(1)} %slice_bitcast_fusion.5.table, f32[1]{0:T(128)S(6)} %copy.19.alpha, bf16[512,1024]{1,0:T(8,128)(2,1)S(1)} %constant_dynamic-update-slice_fusion.xb0.xb1.xe.xa, bf16[512,1024]{1,0:T(8,128)(2,1)S(1)} %constant_dynamic-update-slice_fusion.xb0.xb1.xe.xa, ...), custom_call_target="tpu_custom_call" | custom-call | flops 1 | bytes 1 | tf_op jit(solution)/shard_map/pallas_call | solution.py:93
  49.2 2.9 %shard_map.140 = bf16[4,512,256]{2,1,0:T(8,128)(2,1)S(1)} custom-call(s32[32]{0:T(128)S(1)} %slice_bitcast_fusion.5.table, f32[1]{0:T(128)S(6)} %copy.19.alpha, bf16[512,1024]{1,0:T(8,128)(2,1)S(1)} %constant_dynamic-update-slice_fusion.xb0.xb1.xe.xa, bf16[512,1024]{1,0:T(8,128)(2,1)S(1)} %constant_dynamic-update-slice_fusion.xb0.xb1.xe.xa, ...), custom_call_target="tpu_custom_call" | custom-call | flops 1 | bytes 1 | tf_op jit(solution)/shard_map/pallas_call | solution.py:93
  52.1 2.1 %collective-permute-start.7 = (bf16[4,512,256]{2,1,0:T(8,128)(2,1)S(1)}, bf16[4,512,256]{2,1,0:T(8,128)(2,1)S(1)}, u32[]{:S(2)}, u32[]{:S(2)}) collective-permute-start(bf16[4,512,256]{2,1,0:T(8,128)(2,1)S(1)} %shard_map.139), channel_id=1, source_target_pairs={{0,1},{1,0},{2,3},{3,2},{4,5},{5,4},{6,7},{7,6},{8,9},{9,8},{10,11... | collective-permute-start | bytes 3145736 | tf_op jit(solution)/shard_map/ppermute | solution.py:39
  54.2 2.9 %shard_map.141 = f32[4,512,256]{2,1,0:T(8,128)S(1)} custom-call(s32[32]{0:T(128)S(1)} %slice_bitcast_fusion.5.table, f32[1]{0:T(128)S(6)} %copy.19.alpha, bf16[512,1024]{1,0:T(8,128)(2,1)S(1)} %constant_dynamic-update-slice_fusion.xb0.xb1.xe.xa, bf16[512,1024]{1,0:T(8,128)(2,1)S(1)} %constant_dynamic-update-slice_fusion.xb0.xb1.xe.xa, ...), custom_call_target="tpu_custom_call" | custom-call | flops 1 | bytes 1 | tf_op jit(solution)/shard_map/pallas_call | solution.py:93
  57.1 0.8 collective-permute-done.8
  57.9 0.4 multiply_convert_fusion.1
  58.3 1.5 %collective-permute-start.9 = (f16[4,512,256]{2,1,0:T(8,128)(2,1)S(1)}, f16[4,512,256]{2,1,0:T(8,128)(2,1)S(1)}, u32[]{:S(2)}, u32[]{:S(2)}) collective-permute-start(f16[4,512,256]{2,1,0:T(8,128)(2,1)S(1)} %multiply_convert_fusion.1), channel_id=1, source_target_pairs={{0,3},{1,2},{2,1},{3,0},{4,7},{5,6},{6,5},{7,4},{8,11},{9,10},{10,... | collective-permute-start | bytes 3145736 | tf_op jit(solution)/shard_map/ppermute | solution.py:39
  59.7 0.9 collective-permute-start.12
  60.7 2.9 %shard_map.142 = f32[4,512,256]{2,1,0:T(8,128)S(1)} custom-call(s32[32]{0:T(128)S(1)} %slice_bitcast_fusion.5.table, f32[1]{0:T(128)S(6)} %copy.19.alpha, bf16[512,1024]{1,0:T(8,128)(2,1)S(1)} %constant_dynamic-update-slice_fusion.xb0.xb1.xe.xa, bf16[512,1024]{1,0:T(8,128)(2,1)S(1)} %constant_dynamic-update-slice_fusion.xb0.xb1.xe.xa, ...), custom_call_target="tpu_custom_call" | custom-call | flops 1 | bytes 1 | tf_op jit(solution)/shard_map/pallas_call | solution.py:93
  63.6 0.4 multiply_convert_fusion
  64.0 0.4 collective-permute-start.14
  64.4 2.9 %shard_map.143 = f32[4,512,256]{2,1,0:T(8,128)S(1)} custom-call(s32[32]{0:T(128)S(1)} %slice_bitcast_fusion.5.table, f32[1]{0:T(128)S(6)} %copy.19.alpha, bf16[512,1024]{1,0:T(8,128)(2,1)S(1)} %constant_dynamic-update-slice_fusion.xb0.xb1.xe.xa, bf16[512,1024]{1,0:T(8,128)(2,1)S(1)} %constant_dynamic-update-slice_fusion.xb0.xb1.xe.xa, ...), custom_call_target="tpu_custom_call" | custom-call | flops 1 | bytes 1 | tf_op jit(solution)/shard_map/pallas_call | solution.py:93
  67.3 2.9 %shard_map.144 = f32[4,512,256]{2,1,0:T(8,128)S(1)} custom-call(s32[32]{0:T(128)S(1)} %slice_bitcast_fusion.5.table, f32[1]{0:T(128)S(6)} %copy.19.alpha, bf16[512,1024]{1,0:T(8,128)(2,1)S(1)} %constant_dynamic-update-slice_fusion.xb0.xb1.xe.xa, bf16[512,1024]{1,0:T(8,128)(2,1)S(1)} %constant_dynamic-update-slice_fusion.xb0.xb1.xe.xa, ...), custom_call_target="tpu_custom_call" | custom-call | flops 1 | bytes 1 | tf_op jit(solution)/shard_map/pallas_call | solution.py:93
  70.2 6.2 %collective-permute-done.7 = bf16[4,512,256]{2,1,0:T(8,128)(2,1)S(1)} collective-permute-done((bf16[4,512,256]{2,1,0:T(8,128)(2,1)S(1)}, bf16[4,512,256]{2,1,0:T(8,128)(2,1)S(1)}, u32[]{:S(2)}, u32[]{:S(2)}) %collective-permute-start.7) | collective-permute-done | bytes 1048608 | tf_op jit(solution)/shard_map/ppermute | solution.py:39
  76.4 4.4 %collective-permute-done.9 = f16[4,512,256]{2,1,0:T(8,128)(2,1)S(1)} collective-permute-done((f16[4,512,256]{2,1,0:T(8,128)(2,1)S(1)}, f16[4,512,256]{2,1,0:T(8,128)(2,1)S(1)}, u32[]{:S(2)}, u32[]{:S(2)}) %collective-permute-start.9) | collective-permute-done | bytes 1048608 | tf_op jit(solution)/shard_map/ppermute | solution.py:39
  80.7 0.4 multiply_add_fusion.1
  81.2 0.1 fusion.1
  81.3 0.3 collective-permute-start.10
  81.6 0.4 collective-permute-done.12
  82.0 4.2 %collective-permute-done.14 = f16[4,512,256]{2,1,0:T(8,128)(2,1)S(1)} collective-permute-done((f16[4,512,256]{2,1,0:T(8,128)(2,1)S(1)}, f16[4,512,256]{2,1,0:T(8,128)(2,1)S(1)}, u32[]{:S(2)}, u32[]{:S(2)}) %collective-permute-start.14) | collective-permute-done | bytes 1048608 | tf_op jit(solution)/shard_map/ppermute | solution.py:39
  86.2 0.3 multiply_add_fusion
  86.5 0.1 fusion
  86.7 3.4 %collective-permute-start.15 = (f16[2,512,256]{2,1,0:T(8,128)(2,1)S(1)}, f16[2,512,256]{2,1,0:T(8,128)(2,1)S(1)}, u32[]{:S(2)}, u32[]{:S(2)}) collective-permute-start(f16[2,512,256]{2,1,0:T(8,128)(2,1)S(1)} %fusion), channel_id=1, source_target_pairs={{0,1},{1,0},{2,3},{3,2},{4,5},{5,4},{6,7},{7,6},{8,9},{9,8},{10,11... | collective-permute-start | bytes 1572872 | tf_op jit(solution)/shard_map/ppermute | solution.py:39
  90.0 1.3 collective-permute-done.10
  91.4 0.1 fusion.16
  91.5 0.9 collective-permute-start.11
  92.4 4.8 %collective-permute-done.15 = f16[2,512,256]{2,1,0:T(8,128)(2,1)S(1)} collective-permute-done((f16[2,512,256]{2,1,0:T(8,128)(2,1)S(1)}, f16[2,512,256]{2,1,0:T(8,128)(2,1)S(1)}, u32[]{:S(2)}, u32[]{:S(2)}) %collective-permute-start.15) | collective-permute-done | bytes 524320 | tf_op jit(solution)/shard_map/ppermute | solution.py:39
  97.2 0.1 fusion.17
  97.3 1.0 collective-permute-start.16
  98.3 0.8 collective-permute-done.11
  99.2 0.2 fusion.13
  99.3 5.6 %collective-permute-done.16 = f16[512,256]{1,0:T(8,128)(2,1)S(1)} collective-permute-done((f16[512,256]{1,0:T(8,128)(2,1)S(1)}, f16[512,256]{1,0:T(8,128)(2,1)S(1)}, u32[]{:S(2)}, u32[]{:S(2)}) %collective-permute-start.16) | collective-permute-done | bytes 262176 | tf_op jit(solution)/shard_map/ppermute | solution.py:39
  105.0 0.2 fusion.7
  105.1 0.1 fusion.15
  105.4 1.5 %collective-permute-done.17 = f16[4,64,512]{2,1,0:T(8,128)(2,1)S(1)} collective-permute-done((f16[4,64,512]{2,1,0:T(8,128)(2,1)S(1)}, f16[4,64,512]{2,1,0:T(8,128)(2,1)S(1)}, u32[]{:S(2)}, u32[]{:S(2)}) %collective-permute-start.17) | collective-permute-done | bytes 262176 | tf_op jit(solution)/shard_map/ppermute | solution.py:39
  107.1 0.1 copy.14.wanted
  107.2 6.2 %collective-permute-done.18 = f16[2,2,64,512]{3,2,1,0:T(8,128)(2,1)S(1)} collective-permute-done((f16[2,2,64,512]{3,2,1,0:T(8,128)(2,1)S(1)}, f16[2,2,64,512]{3,2,1,0:T(8,128)(2,1)S(1)}, u32[]{:S(2)}, u32[]{:S(2)}) %collective-permute-start.18) | collective-permute-done | bytes 262176 | tf_op jit(solution)/shard_map/ppermute | solution.py:39
  113.5 3.3 %collective-permute-start.19 = (f16[2,2,64,512]{3,2,1,0:T(8,128)(2,1)S(1)}, f16[2,2,64,512]{3,2,1,0:T(8,128)(2,1)S(1)}, u32[]{:S(2)}, u32[]{:S(2)}) collective-permute-start(f16[2,2,64,512]{3,2,1,0:T(8,128)(2,1)S(1)} %fusion.18), channel_id=1, source_target_pairs={{0,96},{1,97},{2,98},{3,99},{4,100},{5,101},{6,102},{7,103},{8,104... | collective-permute-start | bytes 786440 | tf_op jit(solution)/shard_map/ppermute | solution.py:39
  116.9 4.2 %collective-permute-done.19 = f16[2,2,64,512]{3,2,1,0:T(8,128)(2,1)S(1)} collective-permute-done((f16[2,2,64,512]{3,2,1,0:T(8,128)(2,1)S(1)}, f16[2,2,64,512]{3,2,1,0:T(8,128)(2,1)S(1)}, u32[]{:S(2)}, u32[]{:S(2)}) %collective-permute-start.19) | collective-permute-done | bytes 262176 | tf_op jit(solution)/shard_map/ppermute | solution.py:39
  121.2 0.2 convert_multiply_fusion.home
  121.4 1.0 shard_map.145
  122.5 14.0 %all_to_all.5.stats = f32[16,8,128]{2,1,0:T(8,128)S(1)} all-to-all(f32[16,8,128]{2,1,0:T(8,128)S(1)} %shard_map.145), channel_id=1, replica_groups=mesh['rows'=8,'tensor'=16] {'tensor'}, dimensions={0} | all-to-all | bytes 131072 | tf_op jit(solution)/shard_map/all_to_all | solution.py:277
  136.5 1.8 %shard_map.146 = (f32[64,4096]{1,0:T(8,128)}, f32[1,64]{1,0:T(1,128)}) custom-call(s32[8]{0:T(128)S(1)} %slice_bitcast_fusion.6.source, f32[8,64,512]{2,1,0:T(8,128)S(1)} %convert_multiply_fusion.home, f32[16,8,128]{2,1,0:T(8,128)S(1)} %all_to_all.5.stats), custom_call_target="tpu_custom_call" | custom-call | tf_op jit(solution)/shard_map/pallas_call | solution.py:188
  (47 shorter events, 0.9 us)
Async XLA Ops:
  1.6 4.0 %collective-permute-start = (f32[64,128]{1,0:T(8,128)S(1)}, f32[64,128]{1,0:T(8,128)S(1)}, u32[]{:S(2)}, u32[]{:S(2)}) collective-permute-start(f32[64,128]{1,0:T(8,128)S(1)} %shard_map.131), channel_id=1, source_target_pairs={{0,1},{1,0},{2,3},{3,2},{4,5},{5,4},{6,7},{7,6},{8,9},{9,8},{10,11... | collective-permute-start | bytes 98312 | tf_op jit(solution)/shard_map/ppermute | solution.py:39
  5.6 8.9 %copy-start.6 = (bf16[256]{0:T(256)(128)(2,1)S(1)}, bf16[256]{0:T(256)(128)(2,1)}, u32[]{:S(2)}) copy-start(bf16[256]{0:T(256)(128)(2,1)} %param.16) | copy-start | bytes 1540
  5.6 8.9 %copy-start.7 = (bf16[256]{0:T(256)(128)(2,1)S(1)}, bf16[256]{0:T(256)(128)(2,1)}, u32[]{:S(2)}) copy-start(bf16[256]{0:T(256)(128)(2,1)} %param.17) | copy-start | bytes 1540
  5.6 8.9 %copy-start.5 = (bf16[512]{0:T(512)(128)(2,1)S(1)}, bf16[512]{0:T(512)(128)(2,1)}, u32[]{:S(2)}) copy-start(bf16[512]{0:T(512)(128)(2,1)} %param.15) | copy-start | bytes 3076
  5.6 6.5 %collective-permute-start.1 = (f32[64,128]{1,0:T(8,128)S(1)}, f32[64,128]{1,0:T(8,128)S(1)}, u32[]{:S(2)}, u32[]{:S(2)}) collective-permute-start(f32[64,128]{1,0:T(8,128)S(1)} %add.61), channel_id=1, source_target_pairs={{0,3},{1,2},{2,1},{3,0},{4,7},{5,6},{6,5},{7,4},{8,11},{9,10},{10,... | collective-permute-start | bytes 98312 | tf_op jit(solution)/shard_map/ppermute | solution.py:39
  12.2 4.0 %collective-permute-start.2 = (f32[64,128]{1,0:T(8,128)S(1)}, f32[64,128]{1,0:T(8,128)S(1)}, u32[]{:S(2)}, u32[]{:S(2)}) collective-permute-start(f32[64,128]{1,0:T(8,128)S(1)} %add.62), channel_id=1, source_target_pairs={{0,4},{1,5},{2,6},{3,7},{4,0},{5,1},{6,2},{7,3},{8,12},{9,13},{10,... | collective-permute-start | bytes 98312 | tf_op jit(solution)/shard_map/ppermute | solution.py:39
  16.2 6.8 %copy-start = (bf16[64,512]{1,0:T(8,128)(2,1)S(1)}, bf16[64,512]{1,0:T(8,128)(2,1)}, u32[]{:S(2)}) copy-start(bf16[64,512]{1,0:T(8,128)(2,1)} %refs_0_.3) | copy-start | bytes 196612
  16.2 6.8 %copy-start.1 = (bf16[64,256]{1,0:T(8,128)(2,1)S(1)}, bf16[64,256]{1,0:T(8,128)(2,1)}, u32[]{:S(2)}) copy-start(bf16[64,256]{1,0:T(8,128)(2,1)} %refs_1_.3) | copy-start | bytes 98308
  16.2 6.8 %copy-start.2 = (bf16[64,256]{1,0:T(8,128)(2,1)S(1)}, bf16[64,256]{1,0:T(8,128)(2,1)}, u32[]{:S(2)}) copy-start(bf16[64,256]{1,0:T(8,128)(2,1)} %refs_2_.3) | copy-start | bytes 98308
  16.2 8.9 %copy-start.3 = (bf16[256,16,512]{2,1,0:T(8,128)(2,1)S(1)}, bf16[256,16,512]{2,1,0:T(8,128)(2,1)}, u32[]{:S(2)}) copy-start(bf16[256,16,512]{2,1,0:T(8,128)(2,1)} %head.2) | copy-start | bytes 12582916
  16.2 6.7 %collective-permute-start.3 = (f32[64,128]{1,0:T(8,128)S(1)}, f32[64,128]{1,0:T(8,128)S(1)}, u32[]{:S(2)}, u32[]{:S(2)}) collective-permute-start(f32[64,128]{1,0:T(8,128)S(1)} %add.63.refs_6_), channel_id=1, source_target_pairs={{0,12},{1,13},{2,14},{3,15},{4,8},{5,9},{6,10},{7,11},{8,4},{9,5},... | collective-permute-start | bytes 98312 | tf_op jit(solution)/shard_map/ppermute | solution.py:39
  23.1 10.6 %copy-start.4 = (bf16[256,16,512]{2,1,0:T(8,128)(2,1)S(1)}, bf16[256,16,512]{2,1,0:T(8,128)(2,1)}, u32[]{:S(2)}) copy-start(bf16[256,16,512]{2,1,0:T(8,128)(2,1)} %head.3) | copy-start | bytes 12582916
  23.1 6.4 %collective-permute-start.4 = (bf16[64,1024]{1,0:T(8,128)(2,1)S(1)}, bf16[64,1024]{1,0:T(8,128)(2,1)S(1)}, u32[]{:S(2)}, u32[]{:S(2)}) collective-permute-start(bf16[64,1024]{1,0:T(8,128)(2,1)S(1)} %shard_map.134), channel_id=1, source_target_pairs={{0,32},{1,33},{2,34},{3,35},{4,36},{5,37},{6,38},{7,39},{8,40},{9,... | collective-permute-start | bytes 393224 | tf_op jit(solution)/shard_map/ppermute | solution.py:39
  29.6 8.5 %collective-permute-start.5 = (bf16[2,64,1024]{2,1,0:T(8,128)(2,1)S(1)}, bf16[2,64,1024]{2,1,0:T(8,128)(2,1)S(1)}, u32[]{:S(2)}, u32[]{:S(2)}) collective-permute-start(bf16[2,64,1024]{2,1,0:T(8,128)(2,1)S(1)} %pad_maximum_fusion.3), channel_id=1, source_target_pairs={{0,96},{1,97},{2,98},{3,99},{4,100},{5,101},{6,102},{7,103},{8,104... | collective-permute-start | bytes 786440 | tf_op jit(solution)/shard_map/ppermute | solution.py:39
  38.1 2.0 %collective-permute-start.6 = (bf16[256,1024]{1,0:T(8,128)(2,1)S(1)}, bf16[256,1024]{1,0:T(8,128)(2,1)S(1)}, u32[]{:S(2)}, u32[]{:S(2)}) collective-permute-start(bf16[256,1024]{1,0:T(8,128)(2,1)S(1)} %pad_maximum_fusion), channel_id=1, source_target_pairs={{0,16},{1,17},{2,18},{3,19},{4,20},{5,21},{6,22},{7,23},{8,24},{9,... | collective-permute-start | bytes 1572872 | tf_op jit(solution)/shard_map/ppermute | solution.py:39
  43.0 14.9 %collective-permute-start.8 = (bf16[4,512,256]{2,1,0:T(8,128)(2,1)S(1)}, bf16[4,512,256]{2,1,0:T(8,128)(2,1)S(1)}, u32[]{:S(2)}, u32[]{:S(2)}) collective-permute-start(bf16[4,512,256]{2,1,0:T(8,128)(2,1)S(1)} %shard_map.137), channel_id=1, source_target_pairs={{0,1},{1,0},{2,3},{3,2},{4,5},{5,4},{6,7},{7,6},{8,9},{9,8},{10,11... | collective-permute-start | bytes 3145736 | tf_op jit(solution)/shard_map/ppermute | solution.py:39
  46.0 17.6 %collective-permute-start.13 = (bf16[4,512,256]{2,1,0:T(8,128)(2,1)S(1)}, bf16[4,512,256]{2,1,0:T(8,128)(2,1)S(1)}, u32[]{:S(2)}, u32[]{:S(2)}) collective-permute-start(bf16[4,512,256]{2,1,0:T(8,128)(2,1)S(1)} %shard_map.138), channel_id=1, source_target_pairs={{0,4},{1,5},{2,6},{3,7},{4,0},{5,1},{6,2},{7,3},{8,12},{9,13},{10,... | collective-permute-start | bytes 3145736 | tf_op jit(solution)/shard_map/ppermute | solution.py:39
  52.1 24.3 %collective-permute-start.7 = (bf16[4,512,256]{2,1,0:T(8,128)(2,1)S(1)}, bf16[4,512,256]{2,1,0:T(8,128)(2,1)S(1)}, u32[]{:S(2)}, u32[]{:S(2)}) collective-permute-start(bf16[4,512,256]{2,1,0:T(8,128)(2,1)S(1)} %shard_map.139), channel_id=1, source_target_pairs={{0,1},{1,0},{2,3},{3,2},{4,5},{5,4},{6,7},{7,6},{8,9},{9,8},{10,11... | collective-permute-start | bytes 3145736 | tf_op jit(solution)/shard_map/ppermute | solution.py:39
  58.3 22.5 %collective-permute-start.9 = (f16[4,512,256]{2,1,0:T(8,128)(2,1)S(1)}, f16[4,512,256]{2,1,0:T(8,128)(2,1)S(1)}, u32[]{:S(2)}, u32[]{:S(2)}) collective-permute-start(f16[4,512,256]{2,1,0:T(8,128)(2,1)S(1)} %multiply_convert_fusion.1), channel_id=1, source_target_pairs={{0,3},{1,2},{2,1},{3,0},{4,7},{5,6},{6,5},{7,4},{8,11},{9,10},{10,... | collective-permute-start | bytes 3145736 | tf_op jit(solution)/shard_map/ppermute | solution.py:39
  59.7 22.3 %collective-permute-start.12 = (bf16[4,512,256]{2,1,0:T(8,128)(2,1)S(1)}, bf16[4,512,256]{2,1,0:T(8,128)(2,1)S(1)}, u32[]{:S(2)}, u32[]{:S(2)}) collective-permute-start(bf16[4,512,256]{2,1,0:T(8,128)(2,1)S(1)} %shard_map.140), channel_id=1, source_target_pairs={{0,4},{1,5},{2,6},{3,7},{4,0},{5,1},{6,2},{7,3},{8,12},{9,13},{10,... | collective-permute-start | bytes 3145736 | tf_op jit(solution)/shard_map/ppermute | solution.py:39
  64.0 22.2 %collective-permute-start.14 = (f16[4,512,256]{2,1,0:T(8,128)(2,1)S(1)}, f16[4,512,256]{2,1,0:T(8,128)(2,1)S(1)}, u32[]{:S(2)}, u32[]{:S(2)}) collective-permute-start(f16[4,512,256]{2,1,0:T(8,128)(2,1)S(1)} %multiply_convert_fusion), channel_id=1, source_target_pairs={{0,12},{1,13},{2,14},{3,15},{4,8},{5,9},{6,10},{7,11},{8,4},{9,5},... | collective-permute-start | bytes 3145736 | tf_op jit(solution)/shard_map/ppermute | solution.py:39
  81.3 10.1 %collective-permute-start.10 = (f16[2,512,256]{2,1,0:T(8,128)(2,1)S(1)}, f16[2,512,256]{2,1,0:T(8,128)(2,1)S(1)}, u32[]{:S(2)}, u32[]{:S(2)}) collective-permute-start(f16[2,512,256]{2,1,0:T(8,128)(2,1)S(1)} %fusion.1), channel_id=1, source_target_pairs={{0,4},{1,5},{2,6},{3,7},{4,0},{5,1},{6,2},{7,3},{8,12},{9,13},{10,... | collective-permute-start | bytes 1572872 | tf_op jit(solution)/shard_map/ppermute | solution.py:39
  86.7 10.5 %collective-permute-start.15 = (f16[2,512,256]{2,1,0:T(8,128)(2,1)S(1)}, f16[2,512,256]{2,1,0:T(8,128)(2,1)S(1)}, u32[]{:S(2)}, u32[]{:S(2)}) collective-permute-start(f16[2,512,256]{2,1,0:T(8,128)(2,1)S(1)} %fusion), channel_id=1, source_target_pairs={{0,1},{1,0},{2,3},{3,2},{4,5},{5,4},{6,7},{7,6},{8,9},{9,8},{10,11... | collective-permute-start | bytes 1572872 | tf_op jit(solution)/shard_map/ppermute | solution.py:39
  91.5 7.7 %collective-permute-start.11 = (f16[512,256]{1,0:T(8,128)(2,1)S(1)}, f16[512,256]{1,0:T(8,128)(2,1)S(1)}, u32[]{:S(2)}, u32[]{:S(2)}) collective-permute-start(f16[512,256]{1,0:T(8,128)(2,1)S(1)} %fusion.16), channel_id=1, source_target_pairs={{0,12},{1,13},{2,14},{3,15},{4,8},{5,9},{6,10},{7,11},{8,4},{9,5},... | collective-permute-start | bytes 786440 | tf_op jit(solution)/shard_map/ppermute | solution.py:39
  97.3 9.7 %copy-start.8 = (s32[64]{0:T(128)S(1)}, s32[64]{0:T(128)}, u32[]{:S(2)}) copy-start(s32[64]{0:T(128)} %param.22) | copy-start | bytes 772
  97.3 7.7 %collective-permute-start.16 = (f16[512,256]{1,0:T(8,128)(2,1)S(1)}, f16[512,256]{1,0:T(8,128)(2,1)S(1)}, u32[]{:S(2)}, u32[]{:S(2)}) collective-permute-start(f16[512,256]{1,0:T(8,128)(2,1)S(1)} %fusion.17), channel_id=1, source_target_pairs={{0,3},{1,2},{2,1},{3,0},{4,7},{5,6},{6,5},{7,4},{8,11},{9,10},{10,... | collective-permute-start | bytes 786440 | tf_op jit(solution)/shard_map/ppermute | solution.py:39
  105.3 1.6 %collective-permute-start.17 = (f16[4,64,512]{2,1,0:T(8,128)(2,1)S(1)}, f16[4,64,512]{2,1,0:T(8,128)(2,1)S(1)}, u32[]{:S(2)}, u32[]{:S(2)}) collective-permute-start(f16[4,64,512]{2,1,0:T(8,128)(2,1)S(1)} %bitcast.56), channel_id=1, source_target_pairs={{0,16},{1,17},{2,18},{3,19},{4,20},{5,21},{6,22},{7,23},{8,24},{9,... | collective-permute-start | bytes 786440 | tf_op jit(solution)/shard_map/ppermute | solution.py:39
  106.9 6.5 %collective-permute-start.18 = (f16[2,2,64,512]{3,2,1,0:T(8,128)(2,1)S(1)}, f16[2,2,64,512]{3,2,1,0:T(8,128)(2,1)S(1)}, u32[]{:S(2)}, u32[]{:S(2)}) collective-permute-start(f16[2,2,64,512]{3,2,1,0:T(8,128)(2,1)S(1)} %fusion.14), channel_id=1, source_target_pairs={{0,32},{1,33},{2,34},{3,35},{4,36},{5,37},{6,38},{7,39},{8,40},{9,... | collective-permute-start | bytes 786440 | tf_op jit(solution)/shard_map/ppermute | solution.py:39
  113.5 7.7 %collective-permute-start.19 = (f16[2,2,64,512]{3,2,1,0:T(8,128)(2,1)S(1)}, f16[2,2,64,512]{3,2,1,0:T(8,128)(2,1)S(1)}, u32[]{:S(2)}, u32[]{:S(2)}) collective-permute-start(f16[2,2,64,512]{3,2,1,0:T(8,128)(2,1)S(1)} %fusion.18), channel_id=1, source_target_pairs={{0,96},{1,97},{2,98},{3,99},{4,100},{5,101},{6,102},{7,103},{8,104... | collective-permute-start | bytes 786440 | tf_op jit(solution)/shard_map/ppermute | solution.py:39

commit v3 on v2

--- a/solution.py
+++ b/solution.py
@@ -49,7 +49,8 @@
                 for x in range(NX):
                     row = [(y ^ j) * NX + (x ^ i) for i in first for j in second]
                     row += [(y ^ i) * NX + (x ^ j) for i in first for j in second]
-                    row += [(z ^ i) * NC + k for i in (0, u, v, 2) for k in (c, 1 - c)]
+                    row += [(z ^ i) * NC + c for i in (0, u, v, 2)]
+                    row += [(z ^ i) * NC + 1 - c for i in (0, v, u, 2)]
                     out[device(z, c, y, x), : len(row)] = row
     return out
 
@@ -71,15 +72,19 @@
     )(head)
 
 
-def matmul_kernel(table, alpha, xb0, xb1, xe, xa, wb0, wb1, we, wa, out):
+def matmul_kernel(table, alpha, xb0, xb1, xe, xa, wb0, wb1, we, wa, *rest):
+    out = rest[-1]
     base0, base1, expert, anti = [
         jnp.dot(x[...], w[0], preferred_element_type=F32)
         for x, w in ((xb0, wb0), (xb1, wb1), (xe, we), (xa, wa))
     ]
-    out[0] = (base0 + base1 + alpha[0] * (expert - anti)).astype(out.dtype)
-
-
-def project(table, alpha, acts, heads, first, half, dtype):
+    total = base0 + base1 + alpha[0] * (expert - anti)
+    for arrived in rest[:-1]:
+        total += arrived[0].astype(F32)
+    out[0] = total.astype(out.dtype)
+
+
+def project(table, alpha, acts, heads, first, half, dtype, *arrived):
     tokens = acts.shape[0]
     half_c = heads[0].shape[2] // 2
     quarter = heads[0].shape[1]
@@ -90,6 +95,7 @@
     def weights():
         return pl.BlockSpec((1, quarter, half_c), lambda i, tab: (tab[first + i], 0, half))
 
+    block = pl.BlockSpec((1, tokens, half_c), lambda i, tab: (i, 0, 0))
     return pl.pallas_call(
         matmul_kernel,
         grid_spec=pltpu.PrefetchScalarGridSpec(
@@ -97,13 +103,14 @@
             grid=(4,),
             in_specs=[pl.BlockSpec(memory_space=pltpu.SMEM)]
             + [features(i) for i in range(4)]
-            + [weights() for _ in heads],
-            out_specs=pl.BlockSpec((1, tokens, half_c), lambda i, tab: (i, 0, 0)),
+            + [weights() for _ in heads]
+            + [block for _ in arrived],
+            out_specs=block,
         ),
         out_shape=jax.ShapeDtypeStruct((4, tokens, half_c), dtype),
         compiler_params=pltpu.CompilerParams(vmem_limit_bytes=12 << 20),
         cost_estimate=pl.CostEstimate(flops=1, bytes_accessed=1, transcendentals=0),
-    )(table, alpha, *[acts] * 4, *heads)
+    )(table, alpha, *[acts] * 4, *heads, *arrived)
 
 
 def wide(value):
@@ -128,6 +135,12 @@
     for i, column in enumerate(columns):
         out = jnp.where(lane == i, column, out)
     return out
+
+
+def to_all(out, columns):
+    rows = columns[0].shape[0]
+    square = jnp.concatenate([lanes(columns, rows), jnp.zeros((128 - rows, 128), F32)])
+    out[...] = jnp.broadcast_to(square.T[None, :8], out.shape)
 
 
 def square_kernel(*refs):
@@ -147,7 +160,14 @@
         at += h.shape[1]
 
 
-def stats_kernel(source, home, wanted, out):
+def join_kernel(source, mine, other, out):
+    rows = mine.shape[0] // NZ
+    for j in range(NZ * NC):
+        ref, first = (mine, j * rows) if j < NZ else (other, (j - NZ) * rows)
+        out[pl.ds(pl.multiple_of(source[j] * rows, rows), rows)] = ref[first : first + rows]
+
+
+def stats_kernel(home, wanted, out):
     pieces, rows, width = home.shape
     top = jnp.max(home[...], axis=(0,))
     top = jnp.max(top, axis=1, keepdims=True)
@@ -157,14 +177,13 @@
     for i in range(pieces):
         value = home[i]
         total += jnp.exp(value - top)
-        pick += jnp.where(lane == wanted[...] - source[i] * width, value, 0.0)
+        pick += jnp.where(lane == wanted[...] - i * width, value, 0.0)
     total = jnp.sum(total, axis=1, keepdims=True)
     pick = jnp.sum(pick, axis=1, keepdims=True)
-    square = jnp.concatenate([lanes([top, total, pick], rows), jnp.zeros((128 - rows, 128), F32)])
-    out[...] = jnp.broadcast_to(square.T[None, :8], out.shape)
-
-
-def final_kernel(source, home, stats, out, picked):
+    to_all(out, [top, total, pick])
+
+
+def final_kernel(home, stats, out, picked):
     pieces, rows, width = home.shape
     tops, totals, picks = [stats[:, i, :rows] for i in range(3)]
     top = jnp.max(tops, axis=0, keepdims=True)
@@ -175,8 +194,7 @@
     )
     column = square.T[:rows, :1]
     for i in range(pieces):
-        at = pl.multiple_of(source[i] * width, width)
-        out[:, pl.ds(at, width)] = home[i] - column
+        out[:, i * width : (i + 1) * width] = home[i] - column
 
 
 def call(kernel, shapes, *args):
@@ -215,41 +233,42 @@
     table, source = mine[:32], mine[32:40]
 
     quarter = expert_head.shape[0]
-    base = in_hbm(base_head)
-    raw = [(base, 0), (base, quarter), (expert_head, 0), (anti_head, 0)]
     heads = []
 
-    def swap(value, axis, stage, beside):
-        if not beside:
-            return exchange(value, axis, stage)
-        head, start = raw[len(heads)]
-        value, head = together(value, head)
-        got, head = together(exchange(value, axis, stage), relay(head, start, quarter))
-        heads.append(head)
+    def swap(value, axis, stage, *beside):
+        ready = together(value, *[head for head, _ in beside])
+        done = [relay(h, start, quarter) for h, (_, start) in zip(ready[1:], beside)]
+        got, *done = together(exchange(ready[0], axis, stage), *done)
+        heads.extend(done)
         return got
 
     hidden = (base_hidden, expert_hidden, anti_hidden)
     gains = [g[None] for g in (base_gain, expert_gain, anti_gain)]
-    sq = call(square_kernel, [((rows, 128), F32)], *[in_hbm(h) for h in hidden])
-    sq += swap(sq, "x", 0, False)
-    sq += swap(sq, "x", 1, True)
-    sq += swap(sq, "y", 0, False)
-    got = swap(sq, "y", 1, True)
     width = sum(h.shape[1] for h in hidden)
+    flat = [in_hbm(h) for h in hidden]
+    sq = call(square_kernel, [((rows, 128), F32)], *flat)
+    sq += exchange(sq, "x", 0)
+    sq += exchange(sq, "x", 1)
+    sq += exchange(sq, "y", 0)
+    got = exchange(sq, "y", 1)
     normed = call(
-        functools.partial(norm_kernel, (D, DE, DE)), [((rows, width), BF)], *hidden, *gains, sq, got
+        functools.partial(norm_kernel, (D, DE, DE)), [((rows, width), BF)], *flat, *gains, sq, got
     )
-    pair = swap(normed, "z", 0, True)
-    far = swap(jnp.stack([normed, pair]), "z", 1, True)
-    mine = jnp.concatenate([pair, far[1], normed, far[0]])
-    acts = jnp.concatenate([mine, exchange(mine, "core", 0)])
+    pair = swap(normed, "z", 0, (expert_head, 0), (anti_head, 0))
+    far = swap(jnp.stack([normed, pair]), "z", 1, (base_head, 0), (base_head, quarter))
+    mine = jnp.concatenate([normed, pair, far[0], far[1]])
+    other = exchange(mine, "core", 0)
+    heads = heads[2:] + heads[:2]
+    acts = call(join_kernel, [((NZ * NC * rows, width), BF)], source, mine, other)
 
     axes = (("x", "y"), ("y", "x"))
     kept = [[], []]
     moved = [[], []]
     for i in range(4):
         for half in range(2):
-            part = project(table, strength, acts, heads, 16 * half + 4 * i, half, BF if i < 2 else F32)
+            kind = BF if i < 2 else F32
+            arrived = moved[half][1:] if i == 3 else []
+            part = project(table, strength, acts, heads, 16 * half + 4 * i, half, kind, *arrived)
             table, part = together(table, part)
             if i < 2:
                 moved[half].append(exchange(part, axes[half][0], 0))
@@ -258,25 +277,21 @@
     second_step = [
         exchange(narrow(kept[h][0] + wide(moved[h][0])), axes[h][0], 1) for h in range(2)
     ]
-    sums = [kept[h][1] + wide(moved[h][1]) + wide(second_step[h]) for h in range(2)]
+    sums = [kept[h][1] + wide(second_step[h]) for h in range(2)]
     moved = [exchange(narrow(sums[h][:2]), axes[h][1], 0) for h in range(2)]
     second_step = [
         exchange(narrow(sums[h][3] + wide(moved[h][1])), axes[h][1], 1) for h in range(2)
     ]
     logits = jnp.concatenate(
         [narrow(sums[h][2] + wide(moved[h][0]) + wide(second_step[h])) for h in range(2)], axis=1
-    ).reshape(NC, NZ, rows, c_width)
-
-    other = exchange(logits[1], "core", 0)
-    both = jnp.stack([logits[0], other], axis=1)
-    near = exchange(both[:2], "z", 0)
-    last = exchange(jnp.stack([both[3], near[1]]), "z", 1)
-    home = jnp.concatenate([both[2], near[0], last[0], last[1]]).astype(F32) * UP
+    ).reshape(NZ * NC, rows, c_width)
+
+    home = wide(lax.all_to_all(logits, "rows", 0, 0, tiled=True))
     wanted = (token_ids - t * (8 * c_width))[:, None]
-    stats = call(stats_kernel, [((NY * NX, 8, 128), F32)], source, home, wanted)
+    stats = call(stats_kernel, [((NY * NX, 8, 128), F32)], home, wanted)
     stats = lax.all_to_all(stats, "tensor", 0, 0, tiled=True)
     log_probs, picked = call(
-        final_kernel, [((rows, 8 * c_width), F32), ((1, rows), F32)], source, home, stats
+        final_kernel, [((rows, 8 * c_width), F32), ((1, rows), F32)], home, stats
     )
     return log_probs, picked[0]
 

time: 139 us -> 132 us (0.950)
  waiting for transfers between devices: 51.6 us -> 45.7 us
  local copies, waits for them, and re-layouts: 1.11 us -> 5.89 us
  Pallas kernels: 36.8 us -> 32.8 us
  blocking collectives: 14 us -> 10.9 us
  starting transfers between devices: 30.1 us -> 31.6 us
    ppermute x20 -> x17, waiting for transfers between devices: 51.6 us -> 35.4 us  [exchange(): return lax.ppermute(value, AXES, pairs)]
    all_to_all x0 -> x1, waiting for transfers between devices: none -> 10.2 us  [shards(): home = wide(lax.all_to_all(logits, 'rows', 0, 0, tiled=True))]
    pallas_call x4, Pallas kernels: 9.9 us -> 5.55 us  [relay(): pl.pallas_call(relay_kernel, grid=(count // step,), in_specs=[pl.BlockSpe...]
    all_to_all x0 -> x1, starting transfers between devices: none -> 4.3 us  [shards(): home = wide(lax.all_to_all(logits, 'rows', 0, 0, tiled=True))]
    all_to_all x1, blocking collectives: 14 us -> 10.9 us  [shards(): stats = lax.all_to_all(stats, 'tensor', 0, 0, tiled=True)]
    unnamed x22 -> x10, local copies, waits for them, and re-layouts: 0.1 us -> 3 us
    ppermute x20 -> x17, starting transfers between devices: 30.1 us -> 27.3 us  [exchange(): return lax.ppermute(value, AXES, pairs)]
    broadcast_in_dim x3, local copies, waits for them, and re-layouts: 0.01 us -> 2 us  [shards(): gains = [g[None] for g in (base_gain, expert_gain, anti_gain)]]
  transfers between devices with their start and end apart: 20 -> 18, of which waited for: 17 -> 12; matrix products, arithmetic and copies ran while one was open for 2% -> 4% of each run, Pallas kernels for 22% -> 20%
where the time goes in v3:
time: 132 us
  waiting for transfers between devices  45.7 us (35%)
  Pallas kernels  32.8 us (25%)
  starting transfers between devices  31.6 us (24%)
  blocking collectives  10.9 us (8%)
  local copies, waits for them, and re-layouts  5.89 us (4%)
  other arithmetic  3.27 us (2%)
  between operations  1.57 us (1%)
    ppermute x17, waiting for transfers between devices, exchange(): return lax.ppermute(value, AXES, pairs)  35.4 us
    ppermute x17, starting transfers between devices, exchange(): return lax.ppermute(value, AXES, pairs)  27.3 us
    pallas_call x8, Pallas kernels, project(): pl.pallas_call(matmul_kernel, grid_spec=pltpu.PrefetchScalarGridSpec(num_...  23 us
    all_to_all x1, blocking collectives, shards(): stats = lax.all_to_all(stats, 'tensor', 0, 0, tiled=True)  10.9 us
    all_to_all x1, waiting for transfers between devices, shards(): home = wide(lax.all_to_all(logits, 'rows', 0, 0, tiled=True))  10.2 us
    pallas_call x4, Pallas kernels, relay(): pl.pallas_call(relay_kernel, grid=(count // step,), in_specs=[pl.BlockSpe...  5.55 us
    all_to_all x1, starting transfers between devices, shards(): home = wide(lax.all_to_all(logits, 'rows', 0, 0, tiled=True))  4.3 us
    pallas_call x5, Pallas kernels, call(): pl.pallas_call(kernel, in_specs=[spec(v) for v in args], out_specs=[pl.Bl...  4.26 us
  transfers between devices with their start and end apart: 18, of which 12 were waited for; matrix products, arithmetic and copies ran while one was open for 4% of the time, Pallas kernels for 20%

profile of v3, /device:TPU:0, one launch (start us, length us, event | category | flops | bytes accessed | tf_op | source)
XLA Modules:
  0.0 131.7 jit_solution(13718761495465912141)
XLA Ops:
  0.6 1.0 shard_map.131
  1.6 1.7 %collective-permute-start = (f32[64,128]{1,0:T(8,128)S(1)}, f32[64,128]{1,0:T(8,128)S(1)}, u32[]{:S(2)}, u32[]{:S(2)}) collective-permute-start(f32[64,128]{1,0:T(8,128)S(1)} %shard_map.131), channel_id=1, source_target_pairs={{0,1},{1,0},{2,3},{3,2},{4,5},{5,4},{6,7},{7,6},{8,9},{9,8},{10,11... | collective-permute-start | bytes 98312 | tf_op jit(solution)/shard_map/ppermute | solution.py:39
  3.3 2.3 %collective-permute-done = f32[64,128]{1,0:T(8,128)S(1)} collective-permute-done((f32[64,128]{1,0:T(8,128)S(1)}, f32[64,128]{1,0:T(8,128)S(1)}, u32[]{:S(2)}, u32[]{:S(2)}) %collective-permute-start) | collective-permute-done | bytes 32800 | tf_op jit(solution)/shard_map/ppermute | solution.py:39
  5.6 2.8 %collective-permute-start.1 = (f32[64,128]{1,0:T(8,128)S(1)}, f32[64,128]{1,0:T(8,128)S(1)}, u32[]{:S(2)}, u32[]{:S(2)}) collective-permute-start(f32[64,128]{1,0:T(8,128)S(1)} %add.55), channel_id=1, source_target_pairs={{0,3},{1,2},{2,1},{3,0},{4,7},{5,6},{6,5},{7,4},{8,11},{9,10},{10,... | collective-permute-start | bytes 98312 | tf_op jit(solution)/shard_map/ppermute | solution.py:39
  8.4 2.3 %collective-permute-done.1 = f32[64,128]{1,0:T(8,128)S(1)} collective-permute-done((f32[64,128]{1,0:T(8,128)S(1)}, f32[64,128]{1,0:T(8,128)S(1)}, u32[]{:S(2)}, u32[]{:S(2)}) %collective-permute-start.1) | collective-permute-done | bytes 32800 | tf_op jit(solution)/shard_map/ppermute | solution.py:39
  10.7 1.7 %collective-permute-start.2 = (f32[64,128]{1,0:T(8,128)S(1)}, f32[64,128]{1,0:T(8,128)S(1)}, u32[]{:S(2)}, u32[]{:S(2)}) collective-permute-start(f32[64,128]{1,0:T(8,128)S(1)} %add.56), channel_id=1, source_target_pairs={{0,4},{1,5},{2,6},{3,7},{4,0},{5,1},{6,2},{7,3},{8,12},{9,13},{10,... | collective-permute-start | bytes 98312 | tf_op jit(solution)/shard_map/ppermute | solution.py:39
  12.4 2.3 %collective-permute-done.2 = f32[64,128]{1,0:T(8,128)S(1)} collective-permute-done((f32[64,128]{1,0:T(8,128)S(1)}, f32[64,128]{1,0:T(8,128)S(1)}, u32[]{:S(2)}, u32[]{:S(2)}) %collective-permute-start.2) | collective-permute-done | bytes 32800 | tf_op jit(solution)/shard_map/ppermute | solution.py:39
  14.7 3.1 %collective-permute-start.3 = (f32[64,128]{1,0:T(8,128)S(1)}, f32[64,128]{1,0:T(8,128)S(1)}, u32[]{:S(2)}, u32[]{:S(2)}) collective-permute-start(f32[64,128]{1,0:T(8,128)S(1)} %add.57.refs_6_), channel_id=1, source_target_pairs={{0,12},{1,13},{2,14},{3,15},{4,8},{5,9},{6,10},{7,11},{8,4},{9,5},... | collective-permute-start | bytes 98312 | tf_op jit(solution)/shard_map/ppermute | solution.py:39
  18.4 0.7 broadcast_in_dim.13.refs_4_
  19.1 0.7 broadcast_in_dim.14.refs_5_
  19.7 0.7 broadcast_in_dim.12.refs_3_
  20.4 1.0 shard_map.132
  21.4 2.0 %collective-permute-start.4 = (bf16[64,1024]{1,0:T(8,128)(2,1)S(1)}, bf16[64,1024]{1,0:T(8,128)(2,1)S(1)}, u32[]{:S(2)}, u32[]{:S(2)}) collective-permute-start(bf16[64,1024]{1,0:T(8,128)(2,1)S(1)} %shard_map.132), channel_id=1, source_target_pairs={{0,32},{1,33},{2,34},{3,35},{4,36},{5,37},{6,38},{7,39},{8,40},{9,... | collective-permute-start | bytes 393224 | tf_op jit(solution)/shard_map/ppermute | solution.py:39
  23.4 2.2 %copy-done = bf16[256,16,512]{2,1,0:T(8,128)(2,1)S(1)} copy-done((bf16[256,16,512]{2,1,0:T(8,128)(2,1)S(1)}, bf16[256,16,512]{2,1,0:T(8,128)(2,1)}, u32[]{:S(2)}) %copy-start) | copy-done | bytes 4194328
  25.6 1.4 %shard_map.133.we = bf16[16,256,512]{2,1,0:T(8,128)(2,1)S(1)} custom-call(bf16[256,16,512]{2,1,0:T(8,128)(2,1)S(1)} %copy-done), custom_call_target="tpu_custom_call" | custom-call | flops 10000000000 | bytes 16777216 | tf_op jit(solution)/shard_map/pallas_call | solution.py:64
  27.0 0.8 copy-done.1
  27.8 1.4 %shard_map.134.wa = bf16[16,256,512]{2,1,0:T(8,128)(2,1)S(1)} custom-call(bf16[256,16,512]{2,1,0:T(8,128)(2,1)S(1)} %copy-done.1), custom_call_target="tpu_custom_call" | custom-call | flops 10000000000 | bytes 16777216 | tf_op jit(solution)/shard_map/pallas_call | solution.py:64
  29.2 2.8 %collective-permute-start.5 = (bf16[2,64,1024]{2,1,0:T(8,128)(2,1)S(1)}, bf16[2,64,1024]{2,1,0:T(8,128)(2,1)S(1)}, u32[]{:S(2)}, u32[]{:S(2)}) collective-permute-start(bf16[2,64,1024]{2,1,0:T(8,128)(2,1)S(1)} %pad_maximum_fusion.2), channel_id=1, source_target_pairs={{0,96},{1,97},{2,98},{3,99},{4,100},{5,101},{6,102},{7,103},{8,104... | collective-permute-start | bytes 786440 | tf_op jit(solution)/shard_map/ppermute | solution.py:39
  32.0 1.4 %shard_map.135.wb0 = bf16[16,256,512]{2,1,0:T(8,128)(2,1)S(1)} custom-call(bf16[512,16,512]{2,1,0:T(8,128)(2,1)S(1)} %bitcast.36), custom_call_target="tpu_custom_call" | custom-call | flops 10000000000 | bytes 16777216 | tf_op jit(solution)/shard_map/pallas_call | solution.py:64
  33.4 1.4 %shard_map.136.wb1 = bf16[16,256,512]{2,1,0:T(8,128)(2,1)S(1)} custom-call(bf16[512,16,512]{2,1,0:T(8,128)(2,1)S(1)} %bitcast.36), custom_call_target="tpu_custom_call" | custom-call | flops 10000000000 | bytes 16777216 | tf_op jit(solution)/shard_map/pallas_call | solution.py:64
  34.8 2.1 %collective-permute-done.5 = bf16[2,64,1024]{2,1,0:T(8,128)(2,1)S(1)} collective-permute-done((bf16[2,64,1024]{2,1,0:T(8,128)(2,1)S(1)}, bf16[2,64,1024]{2,1,0:T(8,128)(2,1)S(1)}, u32[]{:S(2)}, u32[]{:S(2)}) %collective-permute-start.5) | collective-permute-done | bytes 262176 | tf_op jit(solution)/shard_map/ppermute | solution.py:39
  37.0 0.7 constant_dynamic-slice_fusion
  37.8 1.1 collective-permute-done.6.other
  38.9 0.6 shard_map.137.xb0.xb1.xe.xa
  39.5 2.9 %shard_map.138 = bf16[4,512,256]{2,1,0:T(8,128)(2,1)S(1)} custom-call(s32[32]{0:T(128)S(1)} %slice_bitcast_fusion.3.table, f32[1]{0:T(128)S(6)} %copy.15.alpha, bf16[512,1024]{1,0:T(8,128)(2,1)S(1)} %shard_map.137.xb0.xb1.xe.xa, bf16[512,1024]{1,0:T(8,128)(2,1)S(1)} %shard_map.137.xb0.xb1.xe.xa, bf16[512,1024]{1,0:T(8,128)(2,1)S(1)} %shard_map.137.xb0.xb1.xe.xa, ...), custom_call_target="tpu_custom_call" | custom-call | flops 1 | bytes 1 | tf_op jit(solution)/shard_map/pallas_call | solution.py:99
  42.4 0.4 collective-permute-start.8
  42.8 2.9 %shard_map.139 = bf16[4,512,256]{2,1,0:T(8,128)(2,1)S(1)} custom-call(s32[32]{0:T(128)S(1)} %slice_bitcast_fusion.3.table, f32[1]{0:T(128)S(6)} %copy.15.alpha, bf16[512,1024]{1,0:T(8,128)(2,1)S(1)} %shard_map.137.xb0.xb1.xe.xa, bf16[512,1024]{1,0:T(8,128)(2,1)S(1)} %shard_map.137.xb0.xb1.xe.xa, bf16[512,1024]{1,0:T(8,128)(2,1)S(1)} %shard_map.137.xb0.xb1.xe.xa, ...), custom_call_target="tpu_custom_call" | custom-call | flops 1 | bytes 1 | tf_op jit(solution)/shard_map/pallas_call | solution.py:99
  45.6 0.5 collective-permute-start.13
  46.1 2.9 %shard_map.140 = bf16[4,512,256]{2,1,0:T(8,128)(2,1)S(1)} custom-call(s32[32]{0:T(128)S(1)} %slice_bitcast_fusion.3.table, f32[1]{0:T(128)S(6)} %copy.15.alpha, bf16[512,1024]{1,0:T(8,128)(2,1)S(1)} %shard_map.137.xb0.xb1.xe.xa, bf16[512,1024]{1,0:T(8,128)(2,1)S(1)} %shard_map.137.xb0.xb1.xe.xa, bf16[512,1024]{1,0:T(8,128)(2,1)S(1)} %shard_map.137.xb0.xb1.xe.xa, ...), custom_call_target="tpu_custom_call" | custom-call | flops 1 | bytes 1 | tf_op jit(solution)/shard_map/pallas_call | solution.py:99
  49.0 2.9 %shard_map.141 = bf16[4,512,256]{2,1,0:T(8,128)(2,1)S(1)} custom-call(s32[32]{0:T(128)S(1)} %slice_bitcast_fusion.3.table, f32[1]{0:T(128)S(6)} %copy.15.alpha, bf16[512,1024]{1,0:T(8,128)(2,1)S(1)} %shard_map.137.xb0.xb1.xe.xa, bf16[512,1024]{1,0:T(8,128)(2,1)S(1)} %shard_map.137.xb0.xb1.xe.xa, bf16[512,1024]{1,0:T(8,128)(2,1)S(1)} %shard_map.137.xb0.xb1.xe.xa, ...), custom_call_target="tpu_custom_call" | custom-call | flops 1 | bytes 1 | tf_op jit(solution)/shard_map/pallas_call | solution.py:99
  51.9 1.7 %collective-permute-start.12 = (bf16[4,512,256]{2,1,0:T(8,128)(2,1)S(1)}, bf16[4,512,256]{2,1,0:T(8,128)(2,1)S(1)}, u32[]{:S(2)}, u32[]{:S(2)}) collective-permute-start(bf16[4,512,256]{2,1,0:T(8,128)(2,1)S(1)} %shard_map.141), channel_id=1, source_target_pairs={{0,4},{1,5},{2,6},{3,7},{4,0},{5,1},{6,2},{7,3},{8,12},{9,13},{10,... | collective-permute-start | bytes 3145736 | tf_op jit(solution)/shard_map/ppermute | solution.py:39
  53.6 1.8 %collective-permute-start.7 = (bf16[4,512,256]{2,1,0:T(8,128)(2,1)S(1)}, bf16[4,512,256]{2,1,0:T(8,128)(2,1)S(1)}, u32[]{:S(2)}, u32[]{:S(2)}) collective-permute-start(bf16[4,512,256]{2,1,0:T(8,128)(2,1)S(1)} %shard_map.140), channel_id=1, source_target_pairs={{0,1},{1,0},{2,3},{3,2},{4,5},{5,4},{6,7},{7,6},{8,9},{9,8},{10,11... | collective-permute-start | bytes 3145736 | tf_op jit(solution)/shard_map/ppermute | solution.py:39
  55.3 2.9 %shard_map.142 = f32[4,512,256]{2,1,0:T(8,128)S(1)} custom-call(s32[32]{0:T(128)S(1)} %slice_bitcast_fusion.3.table, f32[1]{0:T(128)S(6)} %copy.15.alpha, bf16[512,1024]{1,0:T(8,128)(2,1)S(1)} %shard_map.137.xb0.xb1.xe.xa, bf16[512,1024]{1,0:T(8,128)(2,1)S(1)} %shard_map.137.xb0.xb1.xe.xa, bf16[512,1024]{1,0:T(8,128)(2,1)S(1)} %shard_map.137.xb0.xb1.xe.xa, ...), custom_call_target="tpu_custom_call" | custom-call | flops 1 | bytes 1 | tf_op jit(solution)/shard_map/pallas_call | solution.py:99
  58.2 0.4 multiply_convert_fusion.1
  58.6 2.8 %collective-permute-start.9 = (f16[4,512,256]{2,1,0:T(8,128)(2,1)S(1)}, f16[4,512,256]{2,1,0:T(8,128)(2,1)S(1)}, u32[]{:S(2)}, u32[]{:S(2)}) collective-permute-start(f16[4,512,256]{2,1,0:T(8,128)(2,1)S(1)} %multiply_convert_fusion.1), channel_id=1, source_target_pairs={{0,3},{1,2},{2,1},{3,0},{4,7},{5,6},{6,5},{7,4},{8,11},{9,10},{10,... | collective-permute-start | bytes 3145736 | tf_op jit(solution)/shard_map/ppermute | solution.py:39
  61.4 2.9 %shard_map.143 = f32[4,512,256]{2,1,0:T(8,128)S(1)} custom-call(s32[32]{0:T(128)S(1)} %slice_bitcast_fusion.3.table, f32[1]{0:T(128)S(6)} %copy.15.alpha, bf16[512,1024]{1,0:T(8,128)(2,1)S(1)} %shard_map.137.xb0.xb1.xe.xa, bf16[512,1024]{1,0:T(8,128)(2,1)S(1)} %shard_map.137.xb0.xb1.xe.xa, bf16[512,1024]{1,0:T(8,128)(2,1)S(1)} %shard_map.137.xb0.xb1.xe.xa, ...), custom_call_target="tpu_custom_call" | custom-call | flops 1 | bytes 1 | tf_op jit(solution)/shard_map/pallas_call | solution.py:99
  64.3 0.4 multiply_convert_fusion
  64.7 2.5 %collective-permute-start.14 = (f16[4,512,256]{2,1,0:T(8,128)(2,1)S(1)}, f16[4,512,256]{2,1,0:T(8,128)(2,1)S(1)}, u32[]{:S(2)}, u32[]{:S(2)}) collective-permute-start(f16[4,512,256]{2,1,0:T(8,128)(2,1)S(1)} %multiply_convert_fusion), channel_id=1, source_target_pairs={{0,12},{1,13},{2,14},{3,15},{4,8},{5,9},{6,10},{7,11},{8,4},{9,5},... | collective-permute-start | bytes 3145736 | tf_op jit(solution)/shard_map/ppermute | solution.py:39
  67.2 7.5 %collective-permute-done.7.rest_0_ = bf16[4,512,256]{2,1,0:T(8,128)(2,1)S(1)} collective-permute-done((bf16[4,512,256]{2,1,0:T(8,128)(2,1)S(1)}, bf16[4,512,256]{2,1,0:T(8,128)(2,1)S(1)}, u32[]{:S(2)}, u32[]{:S(2)}) %collective-permute-start.7) | collective-permute-done | bytes 1048608 | tf_op jit(solution)/shard_map/ppermute | solution.py:39
  74.7 2.9 %shard_map.144 = f32[4,512,256]{2,1,0:T(8,128)S(1)} custom-call(s32[32]{0:T(128)S(1)} %slice_bitcast_fusion.3.table, f32[1]{0:T(128)S(6)} %copy.15.alpha, bf16[512,1024]{1,0:T(8,128)(2,1)S(1)} %shard_map.137.xb0.xb1.xe.xa, bf16[512,1024]{1,0:T(8,128)(2,1)S(1)} %shard_map.137.xb0.xb1.xe.xa, bf16[512,1024]{1,0:T(8,128)(2,1)S(1)} %shard_map.137.xb0.xb1.xe.xa, ...), custom_call_target="tpu_custom_call" | custom-call | flops 1 | bytes 1 | tf_op jit(solution)/shard_map/pallas_call | solution.py:99
  77.7 2.9 %shard_map.145 = f32[4,512,256]{2,1,0:T(8,128)S(1)} custom-call(s32[32]{0:T(128)S(1)} %slice_bitcast_fusion.3.table, f32[1]{0:T(128)S(6)} %copy.15.alpha, bf16[512,1024]{1,0:T(8,128)(2,1)S(1)} %shard_map.137.xb0.xb1.xe.xa, bf16[512,1024]{1,0:T(8,128)(2,1)S(1)} %shard_map.137.xb0.xb1.xe.xa, bf16[512,1024]{1,0:T(8,128)(2,1)S(1)} %shard_map.137.xb0.xb1.xe.xa, ...), custom_call_target="tpu_custom_call" | custom-call | flops 1 | bytes 1 | tf_op jit(solution)/shard_map/pallas_call | solution.py:99
  80.6 2.3 %collective-permute-done.9 = f16[4,512,256]{2,1,0:T(8,128)(2,1)S(1)} collective-permute-done((f16[4,512,256]{2,1,0:T(8,128)(2,1)S(1)}, f16[4,512,256]{2,1,0:T(8,128)(2,1)S(1)}, u32[]{:S(2)}, u32[]{:S(2)}) %collective-permute-start.9) | collective-permute-done | bytes 1048608 | tf_op jit(solution)/shard_map/ppermute | solution.py:39
  82.8 0.3 multiply_add_fusion.1
  83.2 0.1 fusion.1
  83.3 0.3 collective-permute-start.10
  83.6 2.0 %collective-permute-done.14 = f16[4,512,256]{2,1,0:T(8,128)(2,1)S(1)} collective-permute-done((f16[4,512,256]{2,1,0:T(8,128)(2,1)S(1)}, f16[4,512,256]{2,1,0:T(8,128)(2,1)S(1)}, u32[]{:S(2)}, u32[]{:S(2)}) %collective-permute-start.14) | collective-permute-done | bytes 1048608 | tf_op jit(solution)/shard_map/ppermute | solution.py:39
  85.6 0.3 multiply_add_fusion
  85.9 0.1 fusion
  86.1 6.6 %collective-permute-done.10 = f16[2,512,256]{2,1,0:T(8,128)(2,1)S(1)} collective-permute-done((f16[2,512,256]{2,1,0:T(8,128)(2,1)S(1)}, f16[2,512,256]{2,1,0:T(8,128)(2,1)S(1)}, u32[]{:S(2)}, u32[]{:S(2)}) %collective-permute-start.10) | collective-permute-done | bytes 524320 | tf_op jit(solution)/shard_map/ppermute | solution.py:39
  92.7 0.1 fusion.14
  92.8 2.5 %collective-permute-start.11 = (f16[512,256]{1,0:T(8,128)(2,1)S(1)}, f16[512,256]{1,0:T(8,128)(2,1)S(1)}, u32[]{:S(2)}, u32[]{:S(2)}) collective-permute-start(f16[512,256]{1,0:T(8,128)(2,1)S(1)} %fusion.14), channel_id=1, source_target_pairs={{0,12},{1,13},{2,14},{3,15},{4,8},{5,9},{6,10},{7,11},{8,4},{9,5},... | collective-permute-start | bytes 786440 | tf_op jit(solution)/shard_map/ppermute | solution.py:39
  95.4 0.1 fusion.15
  95.5 0.6 collective-permute-start.16
  96.1 4.4 %collective-permute-done.11 = f16[512,256]{1,0:T(8,128)(2,1)S(1)} collective-permute-done((f16[512,256]{1,0:T(8,128)(2,1)S(1)}, f16[512,256]{1,0:T(8,128)(2,1)S(1)}, u32[]{:S(2)}, u32[]{:S(2)}) %collective-permute-start.11) | collective-permute-done | bytes 262176 | tf_op jit(solution)/shard_map/ppermute | solution.py:39
  100.5 0.2 fusion.13
  100.6 2.5 %collective-permute-done.16 = f16[512,256]{1,0:T(8,128)(2,1)S(1)} collective-permute-done((f16[512,256]{1,0:T(8,128)(2,1)S(1)}, f16[512,256]{1,0:T(8,128)(2,1)S(1)}, u32[]{:S(2)}, u32[]{:S(2)}) %collective-permute-start.16) | collective-permute-done | bytes 262176 | tf_op jit(solution)/shard_map/ppermute | solution.py:39
  103.2 0.2 fusion.7
  103.4 0.9 pad_maximum_fusion.1
  104.3 4.3 %all-to-all-start = ((f16[8,64,512]{2,1,0:T(8,128)(2,1)}), f16[8,64,512]{2,1,0:T(8,128)(2,1)S(1)}, u32[]{:S(2)}, u32[]{:S(2)}) async-start(f16[8,64,512]{2,1,0:T(8,128)(2,1)} %bitcast.10), calls=%async_computation | async-start | bytes 1048576 | tf_op jit(solution)/shard_map/all_to_all | solution.py:289
  108.7 10.2 %all-to-all-done = f16[8,64,512]{2,1,0:T(8,128)(2,1)S(1)} async-done(((f16[8,64,512]{2,1,0:T(8,128)(2,1)}), f16[8,64,512]{2,1,0:T(8,128)(2,1)S(1)}, u32[]{:S(2)}, u32[]{:S(2)}) %all-to-all-start) | async-done | bytes 524320 | tf_op jit(solution)/shard_map/all_to_all | solution.py:289
  118.9 0.1 convert_multiply_fusion.home
  119.1 0.5 shard_map.146
  119.6 10.9 %all_to_all.10.stats = f32[16,8,128]{2,1,0:T(8,128)S(1)} all-to-all(f32[16,8,128]{2,1,0:T(8,128)S(1)} %shard_map.146), channel_id=1, replica_groups=mesh['rows'=8,'tensor'=16] {'tensor'}, dimensions={0} | all-to-all | bytes 131072 | tf_op jit(solution)/shard_map/all_to_all | solution.py:292
  130.5 1.2 shard_map.147
  (27 shorter events, 0.5 us)
Async XLA Ops:
  1.6 4.0 %collective-permute-start = (f32[64,128]{1,0:T(8,128)S(1)}, f32[64,128]{1,0:T(8,128)S(1)}, u32[]{:S(2)}, u32[]{:S(2)}) collective-permute-start(f32[64,128]{1,0:T(8,128)S(1)} %shard_map.131), channel_id=1, source_target_pairs={{0,1},{1,0},{2,3},{3,2},{4,5},{5,4},{6,7},{7,6},{8,9},{9,8},{10,11... | collective-permute-start | bytes 98312 | tf_op jit(solution)/shard_map/ppermute | solution.py:39
  5.6 5.1 %collective-permute-start.1 = (f32[64,128]{1,0:T(8,128)S(1)}, f32[64,128]{1,0:T(8,128)S(1)}, u32[]{:S(2)}, u32[]{:S(2)}) collective-permute-start(f32[64,128]{1,0:T(8,128)S(1)} %add.55), channel_id=1, source_target_pairs={{0,3},{1,2},{2,1},{3,0},{4,7},{5,6},{6,5},{7,4},{8,11},{9,10},{10,... | collective-permute-start | bytes 98312 | tf_op jit(solution)/shard_map/ppermute | solution.py:39
  10.7 3.9 %collective-permute-start.2 = (f32[64,128]{1,0:T(8,128)S(1)}, f32[64,128]{1,0:T(8,128)S(1)}, u32[]{:S(2)}, u32[]{:S(2)}) collective-permute-start(f32[64,128]{1,0:T(8,128)S(1)} %add.56), channel_id=1, source_target_pairs={{0,4},{1,5},{2,6},{3,7},{4,0},{5,1},{6,2},{7,3},{8,12},{9,13},{10,... | collective-permute-start | bytes 98312 | tf_op jit(solution)/shard_map/ppermute | solution.py:39
  14.7 5.8 %collective-permute-start.3 = (f32[64,128]{1,0:T(8,128)S(1)}, f32[64,128]{1,0:T(8,128)S(1)}, u32[]{:S(2)}, u32[]{:S(2)}) collective-permute-start(f32[64,128]{1,0:T(8,128)S(1)} %add.57.refs_6_), channel_id=1, source_target_pairs={{0,12},{1,13},{2,14},{3,15},{4,8},{5,9},{6,10},{7,11},{8,4},{9,5},... | collective-permute-start | bytes 98312 | tf_op jit(solution)/shard_map/ppermute | solution.py:39
  21.4 7.8 %collective-permute-start.4 = (bf16[64,1024]{1,0:T(8,128)(2,1)S(1)}, bf16[64,1024]{1,0:T(8,128)(2,1)S(1)}, u32[]{:S(2)}, u32[]{:S(2)}) collective-permute-start(bf16[64,1024]{1,0:T(8,128)(2,1)S(1)} %shard_map.132), channel_id=1, source_target_pairs={{0,32},{1,33},{2,34},{3,35},{4,36},{5,37},{6,38},{7,39},{8,40},{9,... | collective-permute-start | bytes 393224 | tf_op jit(solution)/shard_map/ppermute | solution.py:39
  23.4 2.2 %copy-start = (bf16[256,16,512]{2,1,0:T(8,128)(2,1)S(1)}, bf16[256,16,512]{2,1,0:T(8,128)(2,1)}, u32[]{:S(2)}) copy-start(bf16[256,16,512]{2,1,0:T(8,128)(2,1)} %head) | copy-start | bytes 12582916
  25.6 2.2 %copy-start.1 = (bf16[256,16,512]{2,1,0:T(8,128)(2,1)S(1)}, bf16[256,16,512]{2,1,0:T(8,128)(2,1)}, u32[]{:S(2)}) copy-start(bf16[256,16,512]{2,1,0:T(8,128)(2,1)} %head.1) | copy-start | bytes 12582916
  25.6 6.4 %slice-start = ((s8[8388608]{0:T(1024)(128)(4,1)}), s8[4194304]{0:T(1024)(128)(4,1)S(1)}, s32[]{:S(2)}) async-start(s8[8388608]{0:T(1024)(128)(4,1)} %bitcast.35), calls=%async_computation.2 | async-start | bytes 8388608
  27.8 4.2 %slice-start.1 = ((s8[8388608]{0:T(1024)(128)(4,1)}), s8[4194304]{0:T(1024)(128)(4,1)S(1)}, s32[]{:S(2)}) async-start(s8[8388608]{0:T(1024)(128)(4,1)} %bitcast.35), calls=%async_computation.3 | async-start | bytes 8388608
  29.2 7.7 %collective-permute-start.5 = (bf16[2,64,1024]{2,1,0:T(8,128)(2,1)S(1)}, bf16[2,64,1024]{2,1,0:T(8,128)(2,1)S(1)}, u32[]{:S(2)}, u32[]{:S(2)}) collective-permute-start(bf16[2,64,1024]{2,1,0:T(8,128)(2,1)S(1)} %pad_maximum_fusion.2), channel_id=1, source_target_pairs={{0,96},{1,97},{2,98},{3,99},{4,100},{5,101},{6,102},{7,103},{8,104... | collective-permute-start | bytes 786440 | tf_op jit(solution)/shard_map/ppermute | solution.py:39
  36.9 2.0 %collective-permute-start.6 = (bf16[256,1024]{1,0:T(8,128)(2,1)S(1)}, bf16[256,1024]{1,0:T(8,128)(2,1)S(1)}, u32[]{:S(2)}, u32[]{:S(2)}) collective-permute-start(bf16[256,1024]{1,0:T(8,128)(2,1)S(1)} %pad_maximum_fusion.mine), channel_id=1, source_target_pairs={{0,16},{1,17},{2,18},{3,19},{4,20},{5,21},{6,22},{7,23},{8,24},{9,... | collective-permute-start | bytes 1572872 | tf_op jit(solution)/shard_map/ppermute | solution.py:39
  42.4 15.8 %collective-permute-start.8 = (bf16[4,512,256]{2,1,0:T(8,128)(2,1)S(1)}, bf16[4,512,256]{2,1,0:T(8,128)(2,1)S(1)}, u32[]{:S(2)}, u32[]{:S(2)}) collective-permute-start(bf16[4,512,256]{2,1,0:T(8,128)(2,1)S(1)} %shard_map.138), channel_id=1, source_target_pairs={{0,1},{1,0},{2,3},{3,2},{4,5},{5,4},{6,7},{7,6},{8,9},{9,8},{10,11... | collective-permute-start | bytes 3145736 | tf_op jit(solution)/shard_map/ppermute | solution.py:39
  45.6 18.7 %collective-permute-start.13 = (bf16[4,512,256]{2,1,0:T(8,128)(2,1)S(1)}, bf16[4,512,256]{2,1,0:T(8,128)(2,1)S(1)}, u32[]{:S(2)}, u32[]{:S(2)}) collective-permute-start(bf16[4,512,256]{2,1,0:T(8,128)(2,1)S(1)} %shard_map.139), channel_id=1, source_target_pairs={{0,4},{1,5},{2,6},{3,7},{4,0},{5,1},{6,2},{7,3},{8,12},{9,13},{10,... | collective-permute-start | bytes 3145736 | tf_op jit(solution)/shard_map/ppermute | solution.py:39
  51.9 25.8 %collective-permute-start.12 = (bf16[4,512,256]{2,1,0:T(8,128)(2,1)S(1)}, bf16[4,512,256]{2,1,0:T(8,128)(2,1)S(1)}, u32[]{:S(2)}, u32[]{:S(2)}) collective-permute-start(bf16[4,512,256]{2,1,0:T(8,128)(2,1)S(1)} %shard_map.141), channel_id=1, source_target_pairs={{0,4},{1,5},{2,6},{3,7},{4,0},{5,1},{6,2},{7,3},{8,12},{9,13},{10,... | collective-permute-start | bytes 3145736 | tf_op jit(solution)/shard_map/ppermute | solution.py:39
  53.6 21.1 %collective-permute-start.7 = (bf16[4,512,256]{2,1,0:T(8,128)(2,1)S(1)}, bf16[4,512,256]{2,1,0:T(8,128)(2,1)S(1)}, u32[]{:S(2)}, u32[]{:S(2)}) collective-permute-start(bf16[4,512,256]{2,1,0:T(8,128)(2,1)S(1)} %shard_map.140), channel_id=1, source_target_pairs={{0,1},{1,0},{2,3},{3,2},{4,5},{5,4},{6,7},{7,6},{8,9},{9,8},{10,11... | collective-permute-start | bytes 3145736 | tf_op jit(solution)/shard_map/ppermute | solution.py:39
  58.6 24.3 %collective-permute-start.9 = (f16[4,512,256]{2,1,0:T(8,128)(2,1)S(1)}, f16[4,512,256]{2,1,0:T(8,128)(2,1)S(1)}, u32[]{:S(2)}, u32[]{:S(2)}) collective-permute-start(f16[4,512,256]{2,1,0:T(8,128)(2,1)S(1)} %multiply_convert_fusion.1), channel_id=1, source_target_pairs={{0,3},{1,2},{2,1},{3,0},{4,7},{5,6},{6,5},{7,4},{8,11},{9,10},{10,... | collective-permute-start | bytes 3145736 | tf_op jit(solution)/shard_map/ppermute | solution.py:39
  64.7 20.9 %collective-permute-start.14 = (f16[4,512,256]{2,1,0:T(8,128)(2,1)S(1)}, f16[4,512,256]{2,1,0:T(8,128)(2,1)S(1)}, u32[]{:S(2)}, u32[]{:S(2)}) collective-permute-start(f16[4,512,256]{2,1,0:T(8,128)(2,1)S(1)} %multiply_convert_fusion), channel_id=1, source_target_pairs={{0,12},{1,13},{2,14},{3,15},{4,8},{5,9},{6,10},{7,11},{8,4},{9,5},... | collective-permute-start | bytes 3145736 | tf_op jit(solution)/shard_map/ppermute | solution.py:39
  83.3 9.4 %collective-permute-start.10 = (f16[2,512,256]{2,1,0:T(8,128)(2,1)S(1)}, f16[2,512,256]{2,1,0:T(8,128)(2,1)S(1)}, u32[]{:S(2)}, u32[]{:S(2)}) collective-permute-start(f16[2,512,256]{2,1,0:T(8,128)(2,1)S(1)} %fusion.1), channel_id=1, source_target_pairs={{0,4},{1,5},{2,6},{3,7},{4,0},{5,1},{6,2},{7,3},{8,12},{9,13},{10,... | collective-permute-start | bytes 1572872 | tf_op jit(solution)/shard_map/ppermute | solution.py:39
  86.0 9.4 %collective-permute-start.15 = (f16[2,512,256]{2,1,0:T(8,128)(2,1)S(1)}, f16[2,512,256]{2,1,0:T(8,128)(2,1)S(1)}, u32[]{:S(2)}, u32[]{:S(2)}) collective-permute-start(f16[2,512,256]{2,1,0:T(8,128)(2,1)S(1)} %fusion), channel_id=1, source_target_pairs={{0,1},{1,0},{2,3},{3,2},{4,5},{5,4},{6,7},{7,6},{8,9},{9,8},{10,11... | collective-permute-start | bytes 1572872 | tf_op jit(solution)/shard_map/ppermute | solution.py:39
  92.8 7.7 %collective-permute-start.11 = (f16[512,256]{1,0:T(8,128)(2,1)S(1)}, f16[512,256]{1,0:T(8,128)(2,1)S(1)}, u32[]{:S(2)}, u32[]{:S(2)}) collective-permute-start(f16[512,256]{1,0:T(8,128)(2,1)S(1)} %fusion.14), channel_id=1, source_target_pairs={{0,12},{1,13},{2,14},{3,15},{4,8},{5,9},{6,10},{7,11},{8,4},{9,5},... | collective-permute-start | bytes 786440 | tf_op jit(solution)/shard_map/ppermute | solution.py:39
  95.5 13.1 %copy-start.2 = (s32[64]{0:T(128)S(1)}, s32[64]{0:T(128)}, u32[]{:S(2)}) copy-start(s32[64]{0:T(128)} %param.22) | copy-start | bytes 772
  95.5 7.7 %collective-permute-start.16 = (f16[512,256]{1,0:T(8,128)(2,1)S(1)}, f16[512,256]{1,0:T(8,128)(2,1)S(1)}, u32[]{:S(2)}, u32[]{:S(2)}) collective-permute-start(f16[512,256]{1,0:T(8,128)(2,1)S(1)} %fusion.15), channel_id=1, source_target_pairs={{0,3},{1,2},{2,1},{3,0},{4,7},{5,6},{6,5},{7,4},{8,11},{9,10},{10,... | collective-permute-start | bytes 786440 | tf_op jit(solution)/shard_map/ppermute | solution.py:39
  104.3 14.6 %all-to-all-start = ((f16[8,64,512]{2,1,0:T(8,128)(2,1)}), f16[8,64,512]{2,1,0:T(8,128)(2,1)S(1)}, u32[]{:S(2)}, u32[]{:S(2)}) async-start(f16[8,64,512]{2,1,0:T(8,128)(2,1)} %bitcast.10), calls=%async_computation | async-start | bytes 1048576 | tf_op jit(solution)/shard_map/all_to_all | solution.py:289

commit v4 on v3

--- a/solution.py
+++ b/solution.py
@@ -72,45 +72,37 @@
     )(head)
 
 
-def matmul_kernel(table, alpha, xb0, xb1, xe, xa, wb0, wb1, we, wa, *rest):
+def matmul_kernel(first, half, table, alpha, acts, wb0, wb1, we, wa, *rest):
     out = rest[-1]
-    base0, base1, expert, anti = [
-        jnp.dot(x[...], w[0], preferred_element_type=F32)
-        for x, w in ((xb0, wb0), (xb1, wb1), (xe, we), (xa, wa))
-    ]
-    total = base0 + base1 + alpha[0] * (expert - anti)
-    for arrived in rest[:-1]:
-        total += arrived[0].astype(F32)
-    out[0] = total.astype(out.dtype)
+    quarter, cols = wb0.shape[1], out.shape[2]
+    for i in range(out.shape[0]):
+        block = table[first + i]
+        base0, base1, expert, anti = [
+            jnp.dot(
+                acts[:, j * quarter : (j + 1) * quarter],
+                w[block, :, half * cols : (half + 1) * cols],
+                preferred_element_type=F32,
+            )
+            for j, w in enumerate((wb0, wb1, we, wa))
+        ]
+        total = base0 + base1 + alpha[0] * (expert - anti)
+        for arrived in rest[:-1]:
+            total += arrived[i].astype(F32)
+        out[i] = total.astype(out.dtype)
 
 
 def project(table, alpha, acts, heads, first, half, dtype, *arrived):
-    tokens = acts.shape[0]
-    half_c = heads[0].shape[2] // 2
-    quarter = heads[0].shape[1]
-
-    def features(i):
-        return pl.BlockSpec((tokens, quarter), lambda _, tab: (0, i))
-
-    def weights():
-        return pl.BlockSpec((1, quarter, half_c), lambda i, tab: (tab[first + i], 0, half))
-
-    block = pl.BlockSpec((1, tokens, half_c), lambda i, tab: (i, 0, 0))
+    smem = pl.BlockSpec(memory_space=pltpu.SMEM)
+    vmem = pl.BlockSpec(memory_space=pltpu.VMEM)
+    args = (table, alpha, acts, *heads, *arrived)
     return pl.pallas_call(
-        matmul_kernel,
-        grid_spec=pltpu.PrefetchScalarGridSpec(
-            num_scalar_prefetch=1,
-            grid=(4,),
-            in_specs=[pl.BlockSpec(memory_space=pltpu.SMEM)]
-            + [features(i) for i in range(4)]
-            + [weights() for _ in heads]
-            + [block for _ in arrived],
-            out_specs=block,
-        ),
-        out_shape=jax.ShapeDtypeStruct((4, tokens, half_c), dtype),
+        functools.partial(matmul_kernel, first, half),
+        in_specs=[smem] * 2 + [vmem] * (len(args) - 2),
+        out_specs=vmem,
+        out_shape=jax.ShapeDtypeStruct((4, acts.shape[0], heads[0].shape[2] // 2), dtype),
         compiler_params=pltpu.CompilerParams(vmem_limit_bytes=12 << 20),
         cost_estimate=pl.CostEstimate(flops=1, bytes_accessed=1, transcendentals=0),
-    )(table, alpha, *[acts] * 4, *heads, *arrived)
+    )(*args)
 
 
 def wide(value):
@@ -145,17 +137,17 @@
 
 def square_kernel(*refs):
     values = [h[...].astype(F32) for h in refs[:-1]]
-    sums = [jnp.sum(h * h, axis=1, keepdims=True) for h in values]
-    refs[-1][...] = lanes(sums, refs[-1].shape[0])
+    to_all(refs[-1], [jnp.sum(h * h, axis=1, keepdims=True) for h in values])
 
 
 def norm_kernel(widths, *refs):
-    hidden, gains, sq, got, out = refs[:3], refs[3:6], refs[6], refs[7], refs[8]
-    total = sq[...] + got[...]
+    hidden, gains, sums, out = refs[:3], refs[3:6], refs[6], refs[7]
+    total = jnp.sum(sums[...], axis=0)
+    total = jnp.concatenate([total, jnp.zeros((120, 128), F32)]).T[: out.shape[0]]
     at = 0
     for i, h in enumerate(hidden):
         scale = lax.rsqrt(total[:, i : i + 1] / widths[i] + 1e-05)
-        value = h[...].astype(F32) * scale * gains[i][...].astype(F32)
+        value = h[...].astype(F32) * scale * gains[i][...].astype(F32)[None]
         out[:, at : at + h.shape[1]] = value.astype(out.dtype)
         at += h.shape[1]
 
@@ -243,16 +235,13 @@
         return got
 
     hidden = (base_hidden, expert_hidden, anti_hidden)
-    gains = [g[None] for g in (base_gain, expert_gain, anti_gain)]
+    gains = [in_hbm(g) for g in (base_gain, expert_gain, anti_gain)]
     width = sum(h.shape[1] for h in hidden)
     flat = [in_hbm(h) for h in hidden]
-    sq = call(square_kernel, [((rows, 128), F32)], *flat)
-    sq += exchange(sq, "x", 0)
-    sq += exchange(sq, "x", 1)
-    sq += exchange(sq, "y", 0)
-    got = exchange(sq, "y", 1)
+    sums = call(square_kernel, [((NY * NX, 8, 128), F32)], *flat)
+    sums = lax.all_to_all(sums, "tensor", 0, 0, tiled=True)
     normed = call(
-        functools.partial(norm_kernel, (D, DE, DE)), [((rows, width), BF)], *flat, *gains, sq, got
+        functools.partial(norm_kernel, (D, DE, DE)), [((rows, width), BF)], *flat, *gains, sums
     )
     pair = swap(normed, "z", 0, (expert_head, 0), (anti_head, 0))
     far = swap(jnp.stack([normed, pair]), "z", 1, (base_head, 0), (base_head, quarter))

time: 132 us -> 125 us (0.947)
  Pallas kernels: 32.8 us -> 25.4 us
  waiting for transfers between devices: 45.7 us -> 52.4 us
  starting transfers between devices: 31.6 us -> 26.9 us
  local copies, waits for them, and re-layouts: 5.89 us -> 3.89 us
    ppermute x17 -> x13, starting transfers between devices: 27.3 us -> 16 us  [exchange(): return lax.ppermute(value, AXES, pairs)]
    pallas_call x8, Pallas kernels: 23 us -> 14.8 us  [project(): pl.pallas_call(functools.partial(matmul_kernel, first, half), in_specs=[s...]
    all_to_all x0 -> x1, starting transfers between devices: none -> 7.12 us  [shards(): sums = lax.all_to_all(sums, 'tensor', 0, 0, tiled=True)]
    all_to_all x0 -> x1, waiting for transfers between devices: none -> 7.01 us  [shards(): sums = lax.all_to_all(sums, 'tensor', 0, 0, tiled=True)]
    broadcast_in_dim x3 -> x0, local copies, waits for them, and re-layouts: 2 us -> none  [shards(): gains = [g[None] for g in (base_gain, expert_gain, anti_gain)]]
    ppermute x17 -> x13, waiting for transfers between devices: 35.4 us -> 35.1 us  [exchange(): return lax.ppermute(value, AXES, pairs)]
  transfers between devices with their start and end apart: 18 -> 15, of which waited for: 12 -> 12; matrix products, arithmetic and copies ran while one was open for 4% -> 2% of each run, Pallas kernels for 20% -> 15%
where the time goes in v4:
time: 125 us
  waiting for transfers between devices  52.4 us (42%)
  starting transfers between devices  26.9 us (22%)
  Pallas kernels  25.4 us (20%)
  blocking collectives  11.5 us (9%)
  local copies, waits for them, and re-layouts  3.89 us (3%)
  other arithmetic  3.25 us (3%)
  between operations  1.53 us (1%)
    ppermute x13, waiting for transfers between devices, exchange(): return lax.ppermute(value, AXES, pairs)  35.1 us
    ppermute x13, starting transfers between devices, exchange(): return lax.ppermute(value, AXES, pairs)  16 us
    pallas_call x8, Pallas kernels, project(): pl.pallas_call(functools.partial(matmul_kernel, first, half), in_specs=[s...  14.8 us
    all_to_all x1, blocking collectives, shards(): stats = lax.all_to_all(stats, 'tensor', 0, 0, tiled=True)  11.5 us
    all_to_all x1, waiting for transfers between devices, shards(): home = wide(lax.all_to_all(logits, 'rows', 0, 0, tiled=True))  10.2 us
    all_to_all x1, starting transfers between devices, shards(): sums = lax.all_to_all(sums, 'tensor', 0, 0, tiled=True)  7.12 us
    all_to_all x1, waiting for transfers between devices, shards(): sums = lax.all_to_all(sums, 'tensor', 0, 0, tiled=True)  7.01 us
    pallas_call x4, Pallas kernels, relay(): pl.pallas_call(relay_kernel, grid=(count // step,), in_specs=[pl.BlockSpe...  5.55 us
  transfers between devices with their start and end apart: 15, of which 12 were waited for; matrix products, arithmetic and copies ran while one was open for 2% of the time, Pallas kernels for 15%

profile of v4, /device:TPU:0, one launch (start us, length us, event | category | flops | bytes accessed | tf_op | source)
XLA Modules:
  0.0 124.8 jit_solution(16307875653594431811)
XLA Ops:
  0.6 1.7 %shard_map.131 = f32[16,8,128]{2,1,0:T(8,128)} custom-call(bf16[64,512]{1,0:T(8,128)(2,1)} %refs_0_.3, bf16[64,256]{1,0:T(8,128)(2,1)} %refs_1_.3, bf16[64,256]{1,0:T(8,128)(2,1)} %refs_2_.3), custom_call_target="tpu_custom_call" | custom-call | tf_op jit(solution)/shard_map/pallas_call | solution.py:198
  2.3 7.1 %all-to-all-start = ((f32[16,8,128]{2,1,0:T(8,128)}), f32[16,8,128]{2,1,0:T(8,128)S(1)}, u32[]{:S(2)}, u32[]{:S(2)}) async-start(f32[16,8,128]{2,1,0:T(8,128)} %shard_map.131), calls=%async_computation | async-start | bytes 131072 | tf_op jit(solution)/shard_map/all_to_all | solution.py:242
  10.1 7.0 %all-to-all-done.refs_6_ = f32[16,8,128]{2,1,0:T(8,128)S(1)} async-done(((f32[16,8,128]{2,1,0:T(8,128)}), f32[16,8,128]{2,1,0:T(8,128)S(1)}, u32[]{:S(2)}, u32[]{:S(2)}) %all-to-all-start) | async-done | bytes 65568 | tf_op jit(solution)/shard_map/all_to_all | solution.py:242
  17.1 1.1 shard_map.132
  18.2 2.0 %collective-permute-start = (bf16[64,1024]{1,0:T(8,128)(2,1)S(1)}, bf16[64,1024]{1,0:T(8,128)(2,1)S(1)}, u32[]{:S(2)}, u32[]{:S(2)}) collective-permute-start(bf16[64,1024]{1,0:T(8,128)(2,1)S(1)} %shard_map.132), channel_id=1, source_target_pairs={{0,32},{1,33},{2,34},{3,35},{4,36},{5,37},{6,38},{7,39},{8,40},{9,... | collective-permute-start | bytes 393224 | tf_op jit(solution)/shard_map/ppermute | solution.py:39
  20.2 2.2 %copy-done = bf16[256,16,512]{2,1,0:T(8,128)(2,1)S(1)} copy-done((bf16[256,16,512]{2,1,0:T(8,128)(2,1)S(1)}, bf16[256,16,512]{2,1,0:T(8,128)(2,1)}, u32[]{:S(2)}) %copy-start) | copy-done | bytes 4194328
  22.4 1.4 %shard_map.133.we = bf16[16,256,512]{2,1,0:T(8,128)(2,1)S(1)} custom-call(bf16[256,16,512]{2,1,0:T(8,128)(2,1)S(1)} %copy-done), custom_call_target="tpu_custom_call" | custom-call | flops 10000000000 | bytes 16777216 | tf_op jit(solution)/shard_map/pallas_call | solution.py:64
  23.8 0.8 copy-done.1
  24.6 1.4 %shard_map.134.wa = bf16[16,256,512]{2,1,0:T(8,128)(2,1)S(1)} custom-call(bf16[256,16,512]{2,1,0:T(8,128)(2,1)S(1)} %copy-done.1), custom_call_target="tpu_custom_call" | custom-call | flops 10000000000 | bytes 16777216 | tf_op jit(solution)/shard_map/pallas_call | solution.py:64
  25.9 0.0 collective-permute-done
  26.0 2.6 %collective-permute-start.1 = (bf16[2,64,1024]{2,1,0:T(8,128)(2,1)S(1)}, bf16[2,64,1024]{2,1,0:T(8,128)(2,1)S(1)}, u32[]{:S(2)}, u32[]{:S(2)}) collective-permute-start(bf16[2,64,1024]{2,1,0:T(8,128)(2,1)S(1)} %pad_maximum_fusion.2), channel_id=1, source_target_pairs={{0,96},{1,97},{2,98},{3,99},{4,100},{5,101},{6,102},{7,103},{8,104... | collective-permute-start | bytes 786440 | tf_op jit(solution)/shard_map/ppermute | solution.py:39
  28.6 1.4 %shard_map.135.wb0 = bf16[16,256,512]{2,1,0:T(8,128)(2,1)S(1)} custom-call(bf16[512,16,512]{2,1,0:T(8,128)(2,1)S(1)} %bitcast.36), custom_call_target="tpu_custom_call" | custom-call | flops 10000000000 | bytes 16777216 | tf_op jit(solution)/shard_map/pallas_call | solution.py:64
  30.0 1.4 %shard_map.136.wb1 = bf16[16,256,512]{2,1,0:T(8,128)(2,1)S(1)} custom-call(bf16[512,16,512]{2,1,0:T(8,128)(2,1)S(1)} %bitcast.36), custom_call_target="tpu_custom_call" | custom-call | flops 10000000000 | bytes 16777216 | tf_op jit(solution)/shard_map/pallas_call | solution.py:64
  31.4 2.2 %collective-permute-done.1 = bf16[2,64,1024]{2,1,0:T(8,128)(2,1)S(1)} collective-permute-done((bf16[2,64,1024]{2,1,0:T(8,128)(2,1)S(1)}, bf16[2,64,1024]{2,1,0:T(8,128)(2,1)S(1)}, u32[]{:S(2)}, u32[]{:S(2)}) %collective-permute-start.1) | collective-permute-done | bytes 262176 | tf_op jit(solution)/shard_map/ppermute | solution.py:39
  33.7 0.1 collective-permute-start.2
  33.8 0.7 constant_dynamic-slice_fusion
  34.5 0.1 slice_bitcast_fusion.2.source
  34.6 1.1 collective-permute-done.2.other
  35.7 0.6 shard_map.137.acts
  36.3 1.8 %shard_map.138 = bf16[4,512,256]{2,1,0:T(8,128)(2,1)S(1)} custom-call(s32[32]{0:T(128)S(1)} %slice_bitcast_fusion.3.table, f32[1]{0:T(128)S(6)} %copy.15.alpha, bf16[512,1024]{1,0:T(8,128)(2,1)S(1)} %shard_map.137.acts, bf16[16,256,512]{2,1,0:T(8,128)(2,1)S(1)} %shard_map.135.wb0, bf16[16,256,512]{2,1,0:T(8,128)(2,1)S(1)} %shard_map.136.wb1, ...), custom_call_target="tpu_custom_call" | custom-call | flops 1 | bytes 1 | tf_op jit(solution)/shard_map/pallas_call | solution.py:98
  38.2 0.6 collective-permute-start.4
  38.8 1.8 %shard_map.139 = bf16[4,512,256]{2,1,0:T(8,128)(2,1)S(1)} custom-call(s32[32]{0:T(128)S(1)} %slice_bitcast_fusion.3.table, f32[1]{0:T(128)S(6)} %copy.15.alpha, bf16[512,1024]{1,0:T(8,128)(2,1)S(1)} %shard_map.137.acts, bf16[16,256,512]{2,1,0:T(8,128)(2,1)S(1)} %shard_map.135.wb0, bf16[16,256,512]{2,1,0:T(8,128)(2,1)S(1)} %shard_map.136.wb1, ...), custom_call_target="tpu_custom_call" | custom-call | flops 1 | bytes 1 | tf_op jit(solution)/shard_map/pallas_call | solution.py:98
  40.7 0.6 collective-permute-start.9
  41.3 1.8 %shard_map.140 = bf16[4,512,256]{2,1,0:T(8,128)(2,1)S(1)} custom-call(s32[32]{0:T(128)S(1)} %slice_bitcast_fusion.3.table, f32[1]{0:T(128)S(6)} %copy.15.alpha, bf16[512,1024]{1,0:T(8,128)(2,1)S(1)} %shard_map.137.acts, bf16[16,256,512]{2,1,0:T(8,128)(2,1)S(1)} %shard_map.135.wb0, bf16[16,256,512]{2,1,0:T(8,128)(2,1)S(1)} %shard_map.136.wb1, ...), custom_call_target="tpu_custom_call" | custom-call | flops 1 | bytes 1 | tf_op jit(solution)/shard_map/pallas_call | solution.py:98
  43.1 1.8 %shard_map.141 = bf16[4,512,256]{2,1,0:T(8,128)(2,1)S(1)} custom-call(s32[32]{0:T(128)S(1)} %slice_bitcast_fusion.3.table, f32[1]{0:T(128)S(6)} %copy.15.alpha, bf16[512,1024]{1,0:T(8,128)(2,1)S(1)} %shard_map.137.acts, bf16[16,256,512]{2,1,0:T(8,128)(2,1)S(1)} %shard_map.135.wb0, bf16[16,256,512]{2,1,0:T(8,128)(2,1)S(1)} %shard_map.136.wb1, ...), custom_call_target="tpu_custom_call" | custom-call | flops 1 | bytes 1 | tf_op jit(solution)/shard_map/pallas_call | solution.py:98
  45.0 1.6 %collective-permute-start.8 = (bf16[4,512,256]{2,1,0:T(8,128)(2,1)S(1)}, bf16[4,512,256]{2,1,0:T(8,128)(2,1)S(1)}, u32[]{:S(2)}, u32[]{:S(2)}) collective-permute-start(bf16[4,512,256]{2,1,0:T(8,128)(2,1)S(1)} %shard_map.141), channel_id=1, source_target_pairs={{0,4},{1,5},{2,6},{3,7},{4,0},{5,1},{6,2},{7,3},{8,12},{9,13},{10,... | collective-permute-start | bytes 3145736 | tf_op jit(solution)/shard_map/ppermute | solution.py:39
  46.5 1.5 %collective-permute-start.3 = (bf16[4,512,256]{2,1,0:T(8,128)(2,1)S(1)}, bf16[4,512,256]{2,1,0:T(8,128)(2,1)S(1)}, u32[]{:S(2)}, u32[]{:S(2)}) collective-permute-start(bf16[4,512,256]{2,1,0:T(8,128)(2,1)S(1)} %shard_map.140), channel_id=1, source_target_pairs={{0,1},{1,0},{2,3},{3,2},{4,5},{5,4},{6,7},{7,6},{8,9},{9,8},{10,11... | collective-permute-start | bytes 3145736 | tf_op jit(solution)/shard_map/ppermute | solution.py:39
  48.0 1.8 %shard_map.142 = f32[4,512,256]{2,1,0:T(8,128)S(1)} custom-call(s32[32]{0:T(128)S(1)} %slice_bitcast_fusion.3.table, f32[1]{0:T(128)S(6)} %copy.15.alpha, bf16[512,1024]{1,0:T(8,128)(2,1)S(1)} %shard_map.137.acts, bf16[16,256,512]{2,1,0:T(8,128)(2,1)S(1)} %shard_map.135.wb0, bf16[16,256,512]{2,1,0:T(8,128)(2,1)S(1)} %shard_map.136.wb1, ...), custom_call_target="tpu_custom_call" | custom-call | flops 1 | bytes 1 | tf_op jit(solution)/shard_map/pallas_call | solution.py:98
  49.8 3.2 %collective-permute-done.4 = bf16[4,512,256]{2,1,0:T(8,128)(2,1)S(1)} collective-permute-done((bf16[4,512,256]{2,1,0:T(8,128)(2,1)S(1)}, bf16[4,512,256]{2,1,0:T(8,128)(2,1)S(1)}, u32[]{:S(2)}, u32[]{:S(2)}) %collective-permute-start.4) | collective-permute-done | bytes 1048608 | tf_op jit(solution)/shard_map/ppermute | solution.py:39
  53.1 0.4 multiply_convert_fusion.1
  53.4 1.4 %collective-permute-start.5 = (f16[4,512,256]{2,1,0:T(8,128)(2,1)S(1)}, f16[4,512,256]{2,1,0:T(8,128)(2,1)S(1)}, u32[]{:S(2)}, u32[]{:S(2)}) collective-permute-start(f16[4,512,256]{2,1,0:T(8,128)(2,1)S(1)} %multiply_convert_fusion.1), channel_id=1, source_target_pairs={{0,3},{1,2},{2,1},{3,0},{4,7},{5,6},{6,5},{7,4},{8,11},{9,10},{10,... | collective-permute-start | bytes 3145736 | tf_op jit(solution)/shard_map/ppermute | solution.py:39
  54.8 1.8 %shard_map.143 = f32[4,512,256]{2,1,0:T(8,128)S(1)} custom-call(s32[32]{0:T(128)S(1)} %slice_bitcast_fusion.3.table, f32[1]{0:T(128)S(6)} %copy.15.alpha, bf16[512,1024]{1,0:T(8,128)(2,1)S(1)} %shard_map.137.acts, bf16[16,256,512]{2,1,0:T(8,128)(2,1)S(1)} %shard_map.135.wb0, bf16[16,256,512]{2,1,0:T(8,128)(2,1)S(1)} %shard_map.136.wb1, ...), custom_call_target="tpu_custom_call" | custom-call | flops 1 | bytes 1 | tf_op jit(solution)/shard_map/pallas_call | solution.py:98
  56.7 0.4 multiply_convert_fusion
  57.1 1.2 collective-permute-start.10
  58.3 13.7 %collective-permute-done.3.rest_0_ = bf16[4,512,256]{2,1,0:T(8,128)(2,1)S(1)} collective-permute-done((bf16[4,512,256]{2,1,0:T(8,128)(2,1)S(1)}, bf16[4,512,256]{2,1,0:T(8,128)(2,1)S(1)}, u32[]{:S(2)}, u32[]{:S(2)}) %collective-permute-start.3) | collective-permute-done | bytes 1048608 | tf_op jit(solution)/shard_map/ppermute | solution.py:39
  72.0 1.9 %shard_map.144 = f32[4,512,256]{2,1,0:T(8,128)S(1)} custom-call(s32[32]{0:T(128)S(1)} %slice_bitcast_fusion.3.table, f32[1]{0:T(128)S(6)} %copy.15.alpha, bf16[512,1024]{1,0:T(8,128)(2,1)S(1)} %shard_map.137.acts, bf16[16,256,512]{2,1,0:T(8,128)(2,1)S(1)} %shard_map.135.wb0, bf16[16,256,512]{2,1,0:T(8,128)(2,1)S(1)} %shard_map.136.wb1, ...), custom_call_target="tpu_custom_call" | custom-call | flops 1 | bytes 1 | tf_op jit(solution)/shard_map/pallas_call | solution.py:98
  73.9 0.5 collective-permute-done.8.rest_0_
  74.4 1.9 %shard_map.145 = f32[4,512,256]{2,1,0:T(8,128)S(1)} custom-call(s32[32]{0:T(128)S(1)} %slice_bitcast_fusion.3.table, f32[1]{0:T(128)S(6)} %copy.15.alpha, bf16[512,1024]{1,0:T(8,128)(2,1)S(1)} %shard_map.137.acts, bf16[16,256,512]{2,1,0:T(8,128)(2,1)S(1)} %shard_map.135.wb0, bf16[16,256,512]{2,1,0:T(8,128)(2,1)S(1)} %shard_map.136.wb1, ...), custom_call_target="tpu_custom_call" | custom-call | flops 1 | bytes 1 | tf_op jit(solution)/shard_map/pallas_call | solution.py:98
  76.3 0.3 multiply_add_fusion.1
  76.6 0.1 fusion.1
  76.7 0.8 collective-permute-start.6
  77.5 1.2 collective-permute-done.10
  78.7 0.3 multiply_add_fusion
  79.0 0.1 fusion
  79.2 0.2 collective-permute-start.11
  79.4 6.6 %collective-permute-done.6 = f16[2,512,256]{2,1,0:T(8,128)(2,1)S(1)} collective-permute-done((f16[2,512,256]{2,1,0:T(8,128)(2,1)S(1)}, f16[2,512,256]{2,1,0:T(8,128)(2,1)S(1)}, u32[]{:S(2)}, u32[]{:S(2)}) %collective-permute-start.6) | collective-permute-done | bytes 524320 | tf_op jit(solution)/shard_map/ppermute | solution.py:39
  86.0 0.1 fusion.14
  86.1 1.1 collective-permute-start.7
  87.2 1.2 collective-permute-done.11
  88.4 0.1 fusion.15
  88.5 0.0 copy-start.2
  88.5 2.1 %collective-permute-start.12 = (f16[512,256]{1,0:T(8,128)(2,1)S(1)}, f16[512,256]{1,0:T(8,128)(2,1)S(1)}, u32[]{:S(2)}, u32[]{:S(2)}) collective-permute-start(f16[512,256]{1,0:T(8,128)(2,1)S(1)} %fusion.15), channel_id=1, source_target_pairs={{0,3},{1,2},{2,1},{3,0},{4,7},{5,6},{6,5},{7,4},{8,11},{9,10},{10,... | collective-permute-start | bytes 786440 | tf_op jit(solution)/shard_map/ppermute | solution.py:39
  90.7 3.0 %collective-permute-done.7 = f16[512,256]{1,0:T(8,128)(2,1)S(1)} collective-permute-done((f16[512,256]{1,0:T(8,128)(2,1)S(1)}, f16[512,256]{1,0:T(8,128)(2,1)S(1)}, u32[]{:S(2)}, u32[]{:S(2)}) %collective-permute-start.7) | collective-permute-done | bytes 262176 | tf_op jit(solution)/shard_map/ppermute | solution.py:39
  93.7 0.2 fusion.13
  93.9 2.3 %collective-permute-done.12 = f16[512,256]{1,0:T(8,128)(2,1)S(1)} collective-permute-done((f16[512,256]{1,0:T(8,128)(2,1)S(1)}, f16[512,256]{1,0:T(8,128)(2,1)S(1)}, u32[]{:S(2)}, u32[]{:S(2)}) %collective-permute-start.12) | collective-permute-done | bytes 262176 | tf_op jit(solution)/shard_map/ppermute | solution.py:39
  96.2 0.2 fusion.7
  96.4 0.9 pad_maximum_fusion.1
  97.3 3.8 %all-to-all-start.1 = ((f16[8,64,512]{2,1,0:T(8,128)(2,1)}), f16[8,64,512]{2,1,0:T(8,128)(2,1)S(1)}, u32[]{:S(2)}, u32[]{:S(2)}) async-start(f16[8,64,512]{2,1,0:T(8,128)(2,1)} %bitcast.10), calls=%async_computation.1 | async-start | bytes 1048576 | tf_op jit(solution)/shard_map/all_to_all | solution.py:278
  101.1 0.1 copy.14.wanted
  101.2 10.2 %all-to-all-done.1 = f16[8,64,512]{2,1,0:T(8,128)(2,1)S(1)} async-done(((f16[8,64,512]{2,1,0:T(8,128)(2,1)}), f16[8,64,512]{2,1,0:T(8,128)(2,1)S(1)}, u32[]{:S(2)}, u32[]{:S(2)}) %all-to-all-start.1) | async-done | bytes 524320 | tf_op jit(solution)/shard_map/all_to_all | solution.py:278
  111.5 0.1 convert_multiply_fusion.home
  111.6 0.5 shard_map.146
  112.1 11.5 %all_to_all.15.stats = f32[16,8,128]{2,1,0:T(8,128)S(1)} all-to-all(f32[16,8,128]{2,1,0:T(8,128)S(1)} %shard_map.146), channel_id=1, replica_groups=mesh['rows'=8,'tensor'=16] {'tensor'}, dimensions={0} | all-to-all | bytes 131072 | tf_op jit(solution)/shard_map/all_to_all | solution.py:281
  123.6 1.2 shard_map.147
  (15 shorter events, 0.1 us)
Async XLA Ops:
  2.3 14.8 %all-to-all-start = ((f32[16,8,128]{2,1,0:T(8,128)}), f32[16,8,128]{2,1,0:T(8,128)S(1)}, u32[]{:S(2)}, u32[]{:S(2)}) async-start(f32[16,8,128]{2,1,0:T(8,128)} %shard_map.131), calls=%async_computation | async-start | bytes 131072 | tf_op jit(solution)/shard_map/all_to_all | solution.py:242
  18.2 7.8 %collective-permute-start = (bf16[64,1024]{1,0:T(8,128)(2,1)S(1)}, bf16[64,1024]{1,0:T(8,128)(2,1)S(1)}, u32[]{:S(2)}, u32[]{:S(2)}) collective-permute-start(bf16[64,1024]{1,0:T(8,128)(2,1)S(1)} %shard_map.132), channel_id=1, source_target_pairs={{0,32},{1,33},{2,34},{3,35},{4,36},{5,37},{6,38},{7,39},{8,40},{9,... | collective-permute-start | bytes 393224 | tf_op jit(solution)/shard_map/ppermute | solution.py:39
  20.2 2.2 %copy-start = (bf16[256,16,512]{2,1,0:T(8,128)(2,1)S(1)}, bf16[256,16,512]{2,1,0:T(8,128)(2,1)}, u32[]{:S(2)}) copy-start(bf16[256,16,512]{2,1,0:T(8,128)(2,1)} %head) | copy-start | bytes 12582916
  22.4 2.2 %copy-start.1 = (bf16[256,16,512]{2,1,0:T(8,128)(2,1)S(1)}, bf16[256,16,512]{2,1,0:T(8,128)(2,1)}, u32[]{:S(2)}) copy-start(bf16[256,16,512]{2,1,0:T(8,128)(2,1)} %head.1) | copy-start | bytes 12582916
  22.4 6.2 %slice-start = ((s8[8388608]{0:T(1024)(128)(4,1)}), s8[4194304]{0:T(1024)(128)(4,1)S(1)}, s32[]{:S(2)}) async-start(s8[8388608]{0:T(1024)(128)(4,1)} %bitcast.35), calls=%async_computation.3 | async-start | bytes 8388608
  24.5 4.0 %slice-start.1 = ((s8[8388608]{0:T(1024)(128)(4,1)}), s8[4194304]{0:T(1024)(128)(4,1)S(1)}, s32[]{:S(2)}) async-start(s8[8388608]{0:T(1024)(128)(4,1)} %bitcast.35), calls=%async_computation.4 | async-start | bytes 8388608
  26.0 7.7 %collective-permute-start.1 = (bf16[2,64,1024]{2,1,0:T(8,128)(2,1)S(1)}, bf16[2,64,1024]{2,1,0:T(8,128)(2,1)S(1)}, u32[]{:S(2)}, u32[]{:S(2)}) collective-permute-start(bf16[2,64,1024]{2,1,0:T(8,128)(2,1)S(1)} %pad_maximum_fusion.2), channel_id=1, source_target_pairs={{0,96},{1,97},{2,98},{3,99},{4,100},{5,101},{6,102},{7,103},{8,104... | collective-permute-start | bytes 786440 | tf_op jit(solution)/shard_map/ppermute | solution.py:39
  33.7 2.0 %collective-permute-start.2 = (bf16[256,1024]{1,0:T(8,128)(2,1)S(1)}, bf16[256,1024]{1,0:T(8,128)(2,1)S(1)}, u32[]{:S(2)}, u32[]{:S(2)}) collective-permute-start(bf16[256,1024]{1,0:T(8,128)(2,1)S(1)} %pad_maximum_fusion.mine), channel_id=1, source_target_pairs={{0,16},{1,17},{2,18},{3,19},{4,20},{5,21},{6,22},{7,23},{8,24},{9,... | collective-permute-start | bytes 1572872 | tf_op jit(solution)/shard_map/ppermute | solution.py:39
  38.2 14.9 %collective-permute-start.4 = (bf16[4,512,256]{2,1,0:T(8,128)(2,1)S(1)}, bf16[4,512,256]{2,1,0:T(8,128)(2,1)S(1)}, u32[]{:S(2)}, u32[]{:S(2)}) collective-permute-start(bf16[4,512,256]{2,1,0:T(8,128)(2,1)S(1)} %shard_map.138), channel_id=1, source_target_pairs={{0,1},{1,0},{2,3},{3,2},{4,5},{5,4},{6,7},{7,6},{8,9},{9,8},{10,11... | collective-permute-start | bytes 3145736 | tf_op jit(solution)/shard_map/ppermute | solution.py:39
  40.7 16.0 %collective-permute-start.9 = (bf16[4,512,256]{2,1,0:T(8,128)(2,1)S(1)}, bf16[4,512,256]{2,1,0:T(8,128)(2,1)S(1)}, u32[]{:S(2)}, u32[]{:S(2)}) collective-permute-start(bf16[4,512,256]{2,1,0:T(8,128)(2,1)S(1)} %shard_map.139), channel_id=1, source_target_pairs={{0,4},{1,5},{2,6},{3,7},{4,0},{5,1},{6,2},{7,3},{8,12},{9,13},{10,... | collective-permute-start | bytes 3145736 | tf_op jit(solution)/shard_map/ppermute | solution.py:39
  45.0 29.4 %collective-permute-start.8 = (bf16[4,512,256]{2,1,0:T(8,128)(2,1)S(1)}, bf16[4,512,256]{2,1,0:T(8,128)(2,1)S(1)}, u32[]{:S(2)}, u32[]{:S(2)}) collective-permute-start(bf16[4,512,256]{2,1,0:T(8,128)(2,1)S(1)} %shard_map.141), channel_id=1, source_target_pairs={{0,4},{1,5},{2,6},{3,7},{4,0},{5,1},{6,2},{7,3},{8,12},{9,13},{10,... | collective-permute-start | bytes 3145736 | tf_op jit(solution)/shard_map/ppermute | solution.py:39
  46.5 25.5 %collective-permute-start.3 = (bf16[4,512,256]{2,1,0:T(8,128)(2,1)S(1)}, bf16[4,512,256]{2,1,0:T(8,128)(2,1)S(1)}, u32[]{:S(2)}, u32[]{:S(2)}) collective-permute-start(bf16[4,512,256]{2,1,0:T(8,128)(2,1)S(1)} %shard_map.140), channel_id=1, source_target_pairs={{0,1},{1,0},{2,3},{3,2},{4,5},{5,4},{6,7},{7,6},{8,9},{9,8},{10,11... | collective-permute-start | bytes 3145736 | tf_op jit(solution)/shard_map/ppermute | solution.py:39
  53.4 22.8 %collective-permute-start.5 = (f16[4,512,256]{2,1,0:T(8,128)(2,1)S(1)}, f16[4,512,256]{2,1,0:T(8,128)(2,1)S(1)}, u32[]{:S(2)}, u32[]{:S(2)}) collective-permute-start(f16[4,512,256]{2,1,0:T(8,128)(2,1)S(1)} %multiply_convert_fusion.1), channel_id=1, source_target_pairs={{0,3},{1,2},{2,1},{3,0},{4,7},{5,6},{6,5},{7,4},{8,11},{9,10},{10,... | collective-permute-start | bytes 3145736 | tf_op jit(solution)/shard_map/ppermute | solution.py:39
  57.1 21.7 %collective-permute-start.10 = (f16[4,512,256]{2,1,0:T(8,128)(2,1)S(1)}, f16[4,512,256]{2,1,0:T(8,128)(2,1)S(1)}, u32[]{:S(2)}, u32[]{:S(2)}) collective-permute-start(f16[4,512,256]{2,1,0:T(8,128)(2,1)S(1)} %multiply_convert_fusion), channel_id=1, source_target_pairs={{0,12},{1,13},{2,14},{3,15},{4,8},{5,9},{6,10},{7,11},{8,4},{9,5},... | collective-permute-start | bytes 3145736 | tf_op jit(solution)/shard_map/ppermute | solution.py:39
  76.7 9.3 %collective-permute-start.6 = (f16[2,512,256]{2,1,0:T(8,128)(2,1)S(1)}, f16[2,512,256]{2,1,0:T(8,128)(2,1)S(1)}, u32[]{:S(2)}, u32[]{:S(2)}) collective-permute-start(f16[2,512,256]{2,1,0:T(8,128)(2,1)S(1)} %fusion.1), channel_id=1, source_target_pairs={{0,4},{1,5},{2,6},{3,7},{4,0},{5,1},{6,2},{7,3},{8,12},{9,13},{10,... | collective-permute-start | bytes 1572872 | tf_op jit(solution)/shard_map/ppermute | solution.py:39
  79.2 9.3 %collective-permute-start.11 = (f16[2,512,256]{2,1,0:T(8,128)(2,1)S(1)}, f16[2,512,256]{2,1,0:T(8,128)(2,1)S(1)}, u32[]{:S(2)}, u32[]{:S(2)}) collective-permute-start(f16[2,512,256]{2,1,0:T(8,128)(2,1)S(1)} %fusion), channel_id=1, source_target_pairs={{0,1},{1,0},{2,3},{3,2},{4,5},{5,4},{6,7},{7,6},{8,9},{9,8},{10,11... | collective-permute-start | bytes 1572872 | tf_op jit(solution)/shard_map/ppermute | solution.py:39
  86.1 7.7 %collective-permute-start.7 = (f16[512,256]{1,0:T(8,128)(2,1)S(1)}, f16[512,256]{1,0:T(8,128)(2,1)S(1)}, u32[]{:S(2)}, u32[]{:S(2)}) collective-permute-start(f16[512,256]{1,0:T(8,128)(2,1)S(1)} %fusion.14), channel_id=1, source_target_pairs={{0,12},{1,13},{2,14},{3,15},{4,8},{5,9},{6,10},{7,11},{8,4},{9,5},... | collective-permute-start | bytes 786440 | tf_op jit(solution)/shard_map/ppermute | solution.py:39
  88.5 12.6 %copy-start.2 = (s32[64]{0:T(128)S(1)}, s32[64]{0:T(128)}, u32[]{:S(2)}) copy-start(s32[64]{0:T(128)} %param.22) | copy-start | bytes 772
  88.5 7.7 %collective-permute-start.12 = (f16[512,256]{1,0:T(8,128)(2,1)S(1)}, f16[512,256]{1,0:T(8,128)(2,1)S(1)}, u32[]{:S(2)}, u32[]{:S(2)}) collective-permute-start(f16[512,256]{1,0:T(8,128)(2,1)S(1)} %fusion.15), channel_id=1, source_target_pairs={{0,3},{1,2},{2,1},{3,0},{4,7},{5,6},{6,5},{7,4},{8,11},{9,10},{10,... | collective-permute-start | bytes 786440 | tf_op jit(solution)/shard_map/ppermute | solution.py:39
  97.3 14.2 %all-to-all-start.1 = ((f16[8,64,512]{2,1,0:T(8,128)(2,1)}), f16[8,64,512]{2,1,0:T(8,128)(2,1)S(1)}, u32[]{:S(2)}, u32[]{:S(2)}) async-start(f16[8,64,512]{2,1,0:T(8,128)(2,1)} %bitcast.10), calls=%async_computation.1 | async-start | bytes 1048576 | tf_op jit(solution)/shard_map/all_to_all | solution.py:278

commit v5 on v4

--- a/solution.py
+++ b/solution.py
@@ -16,17 +16,18 @@
 F16 = jnp.float16
 F32 = jnp.float32
 DOWN, UP = 0.0625, 16.0
+ALONG_Z = (1, 3, 2)
 
 
 def device(z, c, y, x):
     return (z * NC + c) * (NY * NX) + y * NX + x
 
 
-def exchange(value, axis, stage):
+def exchange(value, axis, stage=0, by=None):
     pairs = []
     for z in range(NZ):
         for c in range(NC):
-            u = 1 if (stage + c) % 2 == 0 else 3
+            u = by or (1 if (stage + c) % 2 == 0 else 3)
             for y in range(NY):
                 for x in range(NX):
                     to = {
@@ -49,8 +50,7 @@
                 for x in range(NX):
                     row = [(y ^ j) * NX + (x ^ i) for i in first for j in second]
                     row += [(y ^ i) * NX + (x ^ j) for i in first for j in second]
-                    row += [(z ^ i) * NC + c for i in (0, u, v, 2)]
-                    row += [(z ^ i) * NC + 1 - c for i in (0, v, u, 2)]
+                    row += [(z ^ i) * NC + k for i in (0,) + ALONG_Z for k in (c, 1 - c)]
                     out[device(z, c, y, x), : len(row)] = row
     return out
 
@@ -152,14 +152,14 @@
         at += h.shape[1]
 
 
-def join_kernel(source, mine, other, out):
-    rows = mine.shape[0] // NZ
-    for j in range(NZ * NC):
-        ref, first = (mine, j * rows) if j < NZ else (other, (j - NZ) * rows)
-        out[pl.ds(pl.multiple_of(source[j] * rows, rows), rows)] = ref[first : first + rows]
-
-
-def stats_kernel(home, wanted, out):
+def join_kernel(*refs):
+    at = 0
+    for ref in refs[:-1]:
+        refs[-1][at : at + ref.shape[0]] = ref[...]
+        at += ref.shape[0]
+
+
+def stats_kernel(source, home, wanted, out):
     pieces, rows, width = home.shape
     top = jnp.max(home[...], axis=(0,))
     top = jnp.max(top, axis=1, keepdims=True)
@@ -169,13 +169,13 @@
     for i in range(pieces):
         value = home[i]
         total += jnp.exp(value - top)
-        pick += jnp.where(lane == wanted[...] - i * width, value, 0.0)
+        pick += jnp.where(lane == wanted[...] - source[i] * width, value, 0.0)
     total = jnp.sum(total, axis=1, keepdims=True)
     pick = jnp.sum(pick, axis=1, keepdims=True)
     to_all(out, [top, total, pick])
 
 
-def final_kernel(home, stats, out, picked):
+def final_kernel(source, home, stats, out, picked):
     pieces, rows, width = home.shape
     tops, totals, picks = [stats[:, i, :rows] for i in range(3)]
     top = jnp.max(tops, axis=0, keepdims=True)
@@ -186,7 +186,8 @@
     )
     column = square.T[:rows, :1]
     for i in range(pieces):
-        out[:, i * width : (i + 1) * width] = home[i] - column
+        at = pl.multiple_of(source[i] * width, width)
+        out[:, pl.ds(at, width)] = home[i] - column
 
 
 def call(kernel, shapes, *args):
@@ -227,12 +228,13 @@
     quarter = expert_head.shape[0]
     heads = []
 
-    def swap(value, axis, stage, *beside):
+    def swap(value, moves, *beside):
         ready = together(value, *[head for head, _ in beside])
+        got = [exchange(ready[0], *move) for move in moves]
         done = [relay(h, start, quarter) for h, (_, start) in zip(ready[1:], beside)]
-        got, *done = together(exchange(ready[0], axis, stage), *done)
-        heads.extend(done)
-        return got
+        results = together(*got, *done)
+        heads.extend(results[len(moves) :])
+        return results[: len(moves)]
 
     hidden = (base_hidden, expert_hidden, anti_hidden)
     gains = [in_hbm(g) for g in (base_gain, expert_gain, anti_gain)]
@@ -243,12 +245,12 @@
     normed = call(
         functools.partial(norm_kernel, (D, DE, DE)), [((rows, width), BF)], *flat, *gains, sums
     )
-    pair = swap(normed, "z", 0, (expert_head, 0), (anti_head, 0))
-    far = swap(jnp.stack([normed, pair]), "z", 1, (base_head, 0), (base_head, quarter))
-    mine = jnp.concatenate([normed, pair, far[0], far[1]])
-    other = exchange(mine, "core", 0)
-    heads = heads[2:] + heads[:2]
-    acts = call(join_kernel, [((NZ * NC * rows, width), BF)], source, mine, other)
+    along_z = [("z", 0, k) for k in ALONG_Z]
+    got = swap(normed, along_z, (expert_head, 0), (base_head, 0), (base_head, quarter))
+    mine = jnp.concatenate([normed, *got])
+    (other,) = swap(mine, [("core",)], (anti_head, 0))
+    heads = heads[1:3] + [heads[0], heads[3]]
+    acts = call(join_kernel, [((NZ * NC * rows, width), BF)], mine, other)
 
     axes = (("x", "y"), ("y", "x"))
     kept = [[], []]
@@ -273,14 +275,18 @@
     ]
     logits = jnp.concatenate(
         [narrow(sums[h][2] + wide(moved[h][0]) + wide(second_step[h])) for h in range(2)], axis=1
-    ).reshape(NZ * NC, rows, c_width)
-
-    home = wide(lax.all_to_all(logits, "rows", 0, 0, tiled=True))
+    ).reshape(NC, NZ, rows, c_width)
+
+    other = exchange(logits[1], "core")
+    both = [jnp.stack([logits[0, i], other[i]]) for i in range(NZ)]
+    home = [both[0]] + [exchange(m, *move) for m, move in zip(both[1:], along_z)]
+    home = wide(jnp.concatenate(home))
+
     wanted = (token_ids - t * (8 * c_width))[:, None]
-    stats = call(stats_kernel, [((NY * NX, 8, 128), F32)], home, wanted)
+    stats = call(stats_kernel, [((NY * NX, 8, 128), F32)], source, home, wanted)
     stats = lax.all_to_all(stats, "tensor", 0, 0, tiled=True)
     log_probs, picked = call(
-        final_kernel, [((rows, 8 * c_width), F32), ((1, rows), F32)], home, stats
+        final_kernel, [((rows, 8 * c_width), F32), ((1, rows), F32)], source, home, stats
     )
     return log_probs, picked[0]
 

time: 125 us -> 124 us (level)
  waiting for transfers between devices: 52.4 us -> 44 us
  other arithmetic: 3.25 us -> 6.61 us
  starting transfers between devices: 26.9 us -> 28.2 us
  local copies, waits for them, and re-layouts: 3.89 us -> 5.19 us
    all_to_all x1 -> x0, waiting for transfers between devices: 10.2 us -> none  [shards(): home = wide(lax.all_to_all(logits, 'rows', 0, 0, tiled=True))]
    ppermute x13 -> x18, starting transfers between devices: 16 us -> 21 us  [exchange(): return lax.ppermute(value, AXES, pairs)]
    all_to_all x1 -> x0, starting transfers between devices: 3.8 us -> none  [shards(): home = wide(lax.all_to_all(logits, 'rows', 0, 0, tiled=True))]
    ppermute x13 -> x18, waiting for transfers between devices: 35.1 us -> 37.7 us  [exchange(): return lax.ppermute(value, AXES, pairs)]
    convert_element_type x6, other arithmetic: 1.28 us -> 3.38 us  [narrow(): return (value * DOWN).astype(F16)]
    mul x2, other arithmetic: 0.21 us -> 2.27 us  [narrow(): return (value * DOWN).astype(F16)]
    unnamed x10 -> x15, local copies, waits for them, and re-layouts: 3 us -> 4.21 us
  transfers between devices with their start and end apart: 15 -> 19, of which waited for: 12 -> 12; matrix products, arithmetic and copies ran while one was open for 2% -> 5% of each run, Pallas kernels for 15% -> 15%
where the time goes in v5:
time: 124 us; the launch traced here: 123 us
  waiting for transfers between devices  44 us (35%)
  starting transfers between devices  28.2 us (23%)
  Pallas kernels  26.1 us (21%)
  blocking collectives  11.5 us (9%)
  other arithmetic  6.61 us (5%)
  local copies, waits for them, and re-layouts  5.19 us (4%)
  between operations  1.68 us (1%)
    ppermute x18, waiting for transfers between devices, exchange(): return lax.ppermute(value, AXES, pairs)  37.7 us
    ppermute x18, starting transfers between devices, exchange(): return lax.ppermute(value, AXES, pairs)  21 us
    pallas_call x8, Pallas kernels, project(): pl.pallas_call(functools.partial(matmul_kernel, first, half), in_specs=[s...  14.7 us
    all_to_all x1, blocking collectives, shards(): stats = lax.all_to_all(stats, 'tensor', 0, 0, tiled=True)  11.5 us
    all_to_all x1, starting transfers between devices, shards(): sums = lax.all_to_all(sums, 'tensor', 0, 0, tiled=True)  7.12 us
    all_to_all x1, waiting for transfers between devices, shards(): sums = lax.all_to_all(sums, 'tensor', 0, 0, tiled=True)  6.3 us
    pallas_call x5, Pallas kernels, call(): pl.pallas_call(kernel, in_specs=[spec(v) for v in args], out_specs=[pl.Bl...  5.78 us
    pallas_call x4, Pallas kernels, relay(): pl.pallas_call(relay_kernel, grid=(count // step,), in_specs=[pl.BlockSpe...  5.57 us
  transfers between devices with their start and end apart: 19, of which 12 were waited for; matrix products, arithmetic and copies ran while one was open for 5% of the time, Pallas kernels for 15%

profile of v5, /device:TPU:0, one launch (start us, length us, event | category | flops | bytes accessed | tf_op | source)
XLA Modules:
  0.0 123.2 jit_solution(16036454401184728036)
XLA Ops:
  0.6 1.7 %shard_map.131 = f32[16,8,128]{2,1,0:T(8,128)} custom-call(bf16[64,512]{1,0:T(8,128)(2,1)} %refs_0_.3, bf16[64,256]{1,0:T(8,128)(2,1)} %refs_1_.3, bf16[64,256]{1,0:T(8,128)(2,1)} %refs_2_.3), custom_call_target="tpu_custom_call" | custom-call | tf_op jit(solution)/shard_map/pallas_call | solution.py:199
  2.3 7.1 %all-to-all-start = ((f32[16,8,128]{2,1,0:T(8,128)}), f32[16,8,128]{2,1,0:T(8,128)S(1)}, u32[]{:S(2)}, u32[]{:S(2)}) async-start(f32[16,8,128]{2,1,0:T(8,128)} %shard_map.131), calls=%async_computation | async-start | bytes 131072 | tf_op jit(solution)/shard_map/all_to_all | solution.py:244
  9.4 0.7 constant_dynamic-slice_fusion
  10.8 6.3 %all-to-all-done.refs_6_ = f32[16,8,128]{2,1,0:T(8,128)S(1)} async-done(((f32[16,8,128]{2,1,0:T(8,128)}), f32[16,8,128]{2,1,0:T(8,128)S(1)}, u32[]{:S(2)}, u32[]{:S(2)}) %all-to-all-start) | async-done | bytes 65568 | tf_op jit(solution)/shard_map/all_to_all | solution.py:244
  17.1 1.2 %shard_map.132 = bf16[64,1024]{1,0:T(8,128)(2,1)S(1)} custom-call(bf16[64,512]{1,0:T(8,128)(2,1)} %refs_0_.3, bf16[64,256]{1,0:T(8,128)(2,1)} %refs_1_.3, bf16[64,256]{1,0:T(8,128)(2,1)} %refs_2_.3, bf16[512]{0:T(512)(128)(2,1)} %refs_3_.1, bf16[256]{0:T(256)(128)(2,1)} %refs_4_.1, bf16[256]{0:T(256)(128)(2,1)} %refs_5_.1, ...), custom_call_target="tpu_custom_call" | custom-call | tf_op jit(solution)/shard_map/pallas_call | solution.py:199
  18.3 4.0 %collective-permute-start.2 = (bf16[64,1024]{1,0:T(8,128)(2,1)S(1)}, bf16[64,1024]{1,0:T(8,128)(2,1)S(1)}, u32[]{:S(2)}, u32[]{:S(2)}) collective-permute-start(bf16[64,1024]{1,0:T(8,128)(2,1)S(1)} %shard_map.132), channel_id=1, source_target_pairs={{0,64},{1,65},{2,66},{3,67},{4,68},{5,69},{6,70},{7,71},{8,72},{9,... | collective-permute-start | bytes 393224 | tf_op jit(solution)/shard_map/ppermute | solution.py:40
  22.3 0.7 collective-permute-start.1
  23.0 0.3 collective-permute-start
  23.3 2.2 %copy-done = bf16[256,16,512]{2,1,0:T(8,128)(2,1)S(1)} copy-done((bf16[256,16,512]{2,1,0:T(8,128)(2,1)S(1)}, bf16[256,16,512]{2,1,0:T(8,128)(2,1)}, u32[]{:S(2)}) %copy-start) | copy-done | bytes 4194328
  25.5 1.4 %shard_map.133.we = bf16[16,256,512]{2,1,0:T(8,128)(2,1)S(1)} custom-call(bf16[256,16,512]{2,1,0:T(8,128)(2,1)S(1)} %copy-done), custom_call_target="tpu_custom_call" | custom-call | flops 10000000000 | bytes 16777216 | tf_op jit(solution)/shard_map/pallas_call | solution.py:64
  26.9 1.4 %shard_map.134.wb0 = bf16[16,256,512]{2,1,0:T(8,128)(2,1)S(1)} custom-call(bf16[512,16,512]{2,1,0:T(8,128)(2,1)S(1)} %bitcast.40), custom_call_target="tpu_custom_call" | custom-call | flops 10000000000 | bytes 16777216 | tf_op jit(solution)/shard_map/pallas_call | solution.py:64
  28.3 1.4 %shard_map.135.wb1 = bf16[16,256,512]{2,1,0:T(8,128)(2,1)S(1)} custom-call(bf16[512,16,512]{2,1,0:T(8,128)(2,1)S(1)} %bitcast.40), custom_call_target="tpu_custom_call" | custom-call | flops 10000000000 | bytes 16777216 | tf_op jit(solution)/shard_map/pallas_call | solution.py:64
  29.8 0.1 collective-permute-start.3
  29.9 0.6 copy-done.1
  30.5 1.4 %shard_map.136.wa = bf16[16,256,512]{2,1,0:T(8,128)(2,1)S(1)} custom-call(bf16[256,16,512]{2,1,0:T(8,128)(2,1)S(1)} %copy-done.1), custom_call_target="tpu_custom_call" | custom-call | flops 10000000000 | bytes 16777216 | tf_op jit(solution)/shard_map/pallas_call | solution.py:64
  32.0 1.8 %shard_map.138 = bf16[4,512,256]{2,1,0:T(8,128)(2,1)S(1)} custom-call(s32[32]{0:T(128)S(1)} %slice_bitcast_fusion.4.table, f32[1]{0:T(128)S(6)} %copy.19.alpha, bf16[512,1024]{1,0:T(8,128)(2,1)S(1)} %shard_map.137.acts, bf16[16,256,512]{2,1,0:T(8,128)(2,1)S(1)} %shard_map.134.wb0, bf16[16,256,512]{2,1,0:T(8,128)(2,1)S(1)} %shard_map.135.wb1, ...), custom_call_target="tpu_custom_call" | custom-call | flops 1 | bytes 1 | tf_op jit(solution)/shard_map/pallas_call | solution.py:98
  33.9 0.6 collective-permute-start.5
  34.5 1.8 %shard_map.139 = bf16[4,512,256]{2,1,0:T(8,128)(2,1)S(1)} custom-call(s32[32]{0:T(128)S(1)} %slice_bitcast_fusion.4.table, f32[1]{0:T(128)S(6)} %copy.19.alpha, bf16[512,1024]{1,0:T(8,128)(2,1)S(1)} %shard_map.137.acts, bf16[16,256,512]{2,1,0:T(8,128)(2,1)S(1)} %shard_map.134.wb0, bf16[16,256,512]{2,1,0:T(8,128)(2,1)S(1)} %shard_map.135.wb1, ...), custom_call_target="tpu_custom_call" | custom-call | flops 1 | bytes 1 | tf_op jit(solution)/shard_map/pallas_call | solution.py:98
  36.3 0.6 collective-permute-start.10
  37.0 1.8 %shard_map.140 = bf16[4,512,256]{2,1,0:T(8,128)(2,1)S(1)} custom-call(s32[32]{0:T(128)S(1)} %slice_bitcast_fusion.4.table, f32[1]{0:T(128)S(6)} %copy.19.alpha, bf16[512,1024]{1,0:T(8,128)(2,1)S(1)} %shard_map.137.acts, bf16[16,256,512]{2,1,0:T(8,128)(2,1)S(1)} %shard_map.134.wb0, bf16[16,256,512]{2,1,0:T(8,128)(2,1)S(1)} %shard_map.135.wb1, ...), custom_call_target="tpu_custom_call" | custom-call | flops 1 | bytes 1 | tf_op jit(solution)/shard_map/pallas_call | solution.py:98
  38.8 1.8 %shard_map.141 = bf16[4,512,256]{2,1,0:T(8,128)(2,1)S(1)} custom-call(s32[32]{0:T(128)S(1)} %slice_bitcast_fusion.4.table, f32[1]{0:T(128)S(6)} %copy.19.alpha, bf16[512,1024]{1,0:T(8,128)(2,1)S(1)} %shard_map.137.acts, bf16[16,256,512]{2,1,0:T(8,128)(2,1)S(1)} %shard_map.134.wb0, bf16[16,256,512]{2,1,0:T(8,128)(2,1)S(1)} %shard_map.135.wb1, ...), custom_call_target="tpu_custom_call" | custom-call | flops 1 | bytes 1 | tf_op jit(solution)/shard_map/pallas_call | solution.py:98
  40.7 1.6 %collective-permute-start.9 = (bf16[4,512,256]{2,1,0:T(8,128)(2,1)S(1)}, bf16[4,512,256]{2,1,0:T(8,128)(2,1)S(1)}, u32[]{:S(2)}, u32[]{:S(2)}) collective-permute-start(bf16[4,512,256]{2,1,0:T(8,128)(2,1)S(1)} %shard_map.141), channel_id=1, source_target_pairs={{0,4},{1,5},{2,6},{3,7},{4,0},{5,1},{6,2},{7,3},{8,12},{9,13},{10,... | collective-permute-start | bytes 3145736 | tf_op jit(solution)/shard_map/ppermute | solution.py:40
  42.2 1.5 %collective-permute-start.4 = (bf16[4,512,256]{2,1,0:T(8,128)(2,1)S(1)}, bf16[4,512,256]{2,1,0:T(8,128)(2,1)S(1)}, u32[]{:S(2)}, u32[]{:S(2)}) collective-permute-start(bf16[4,512,256]{2,1,0:T(8,128)(2,1)S(1)} %shard_map.140), channel_id=1, source_target_pairs={{0,1},{1,0},{2,3},{3,2},{4,5},{5,4},{6,7},{7,6},{8,9},{9,8},{10,11... | collective-permute-start | bytes 3145736 | tf_op jit(solution)/shard_map/ppermute | solution.py:40
  43.7 1.8 %shard_map.142 = f32[4,512,256]{2,1,0:T(8,128)S(1)} custom-call(s32[32]{0:T(128)S(1)} %slice_bitcast_fusion.4.table, f32[1]{0:T(128)S(6)} %copy.19.alpha, bf16[512,1024]{1,0:T(8,128)(2,1)S(1)} %shard_map.137.acts, bf16[16,256,512]{2,1,0:T(8,128)(2,1)S(1)} %shard_map.134.wb0, bf16[16,256,512]{2,1,0:T(8,128)(2,1)S(1)} %shard_map.135.wb1, ...), custom_call_target="tpu_custom_call" | custom-call | flops 1 | bytes 1 | tf_op jit(solution)/shard_map/pallas_call | solution.py:98
  45.5 3.2 %collective-permute-done.5 = bf16[4,512,256]{2,1,0:T(8,128)(2,1)S(1)} collective-permute-done((bf16[4,512,256]{2,1,0:T(8,128)(2,1)S(1)}, bf16[4,512,256]{2,1,0:T(8,128)(2,1)S(1)}, u32[]{:S(2)}, u32[]{:S(2)}) %collective-permute-start.5) | collective-permute-done | bytes 1048608 | tf_op jit(solution)/shard_map/ppermute | solution.py:40
  48.7 0.4 multiply_convert_fusion.1
  49.1 1.4 %collective-permute-start.6 = (f16[4,512,256]{2,1,0:T(8,128)(2,1)S(1)}, f16[4,512,256]{2,1,0:T(8,128)(2,1)S(1)}, u32[]{:S(2)}, u32[]{:S(2)}) collective-permute-start(f16[4,512,256]{2,1,0:T(8,128)(2,1)S(1)} %multiply_convert_fusion.1), channel_id=1, source_target_pairs={{0,3},{1,2},{2,1},{3,0},{4,7},{5,6},{6,5},{7,4},{8,11},{9,10},{10,... | collective-permute-start | bytes 3145736 | tf_op jit(solution)/shard_map/ppermute | solution.py:40
  50.5 1.8 %shard_map.143 = f32[4,512,256]{2,1,0:T(8,128)S(1)} custom-call(s32[32]{0:T(128)S(1)} %slice_bitcast_fusion.4.table, f32[1]{0:T(128)S(6)} %copy.19.alpha, bf16[512,1024]{1,0:T(8,128)(2,1)S(1)} %shard_map.137.acts, bf16[16,256,512]{2,1,0:T(8,128)(2,1)S(1)} %shard_map.134.wb0, bf16[16,256,512]{2,1,0:T(8,128)(2,1)S(1)} %shard_map.135.wb1, ...), custom_call_target="tpu_custom_call" | custom-call | flops 1 | bytes 1 | tf_op jit(solution)/shard_map/pallas_call | solution.py:98
  52.4 0.4 multiply_convert_fusion
  52.7 1.2 %collective-permute-start.11 = (f16[4,512,256]{2,1,0:T(8,128)(2,1)S(1)}, f16[4,512,256]{2,1,0:T(8,128)(2,1)S(1)}, u32[]{:S(2)}, u32[]{:S(2)}) collective-permute-start(f16[4,512,256]{2,1,0:T(8,128)(2,1)S(1)} %multiply_convert_fusion), channel_id=1, source_target_pairs={{0,12},{1,13},{2,14},{3,15},{4,8},{5,9},{6,10},{7,11},{8,4},{9,5},... | collective-permute-start | bytes 3145736 | tf_op jit(solution)/shard_map/ppermute | solution.py:40
  54.0 13.8 %collective-permute-done.4.rest_0_ = bf16[4,512,256]{2,1,0:T(8,128)(2,1)S(1)} collective-permute-done((bf16[4,512,256]{2,1,0:T(8,128)(2,1)S(1)}, bf16[4,512,256]{2,1,0:T(8,128)(2,1)S(1)}, u32[]{:S(2)}, u32[]{:S(2)}) %collective-permute-start.4) | collective-permute-done | bytes 1048608 | tf_op jit(solution)/shard_map/ppermute | solution.py:40
  67.8 1.8 %shard_map.144 = f32[4,512,256]{2,1,0:T(8,128)S(1)} custom-call(s32[32]{0:T(128)S(1)} %slice_bitcast_fusion.4.table, f32[1]{0:T(128)S(6)} %copy.19.alpha, bf16[512,1024]{1,0:T(8,128)(2,1)S(1)} %shard_map.137.acts, bf16[16,256,512]{2,1,0:T(8,128)(2,1)S(1)} %shard_map.134.wb0, bf16[16,256,512]{2,1,0:T(8,128)(2,1)S(1)} %shard_map.135.wb1, ...), custom_call_target="tpu_custom_call" | custom-call | flops 1 | bytes 1 | tf_op jit(solution)/shard_map/pallas_call | solution.py:98
  69.7 0.5 collective-permute-done.9.rest_0_
  70.2 1.8 %shard_map.145 = f32[4,512,256]{2,1,0:T(8,128)S(1)} custom-call(s32[32]{0:T(128)S(1)} %slice_bitcast_fusion.4.table, f32[1]{0:T(128)S(6)} %copy.19.alpha, bf16[512,1024]{1,0:T(8,128)(2,1)S(1)} %shard_map.137.acts, bf16[16,256,512]{2,1,0:T(8,128)(2,1)S(1)} %shard_map.134.wb0, bf16[16,256,512]{2,1,0:T(8,128)(2,1)S(1)} %shard_map.135.wb1, ...), custom_call_target="tpu_custom_call" | custom-call | flops 1 | bytes 1 | tf_op jit(solution)/shard_map/pallas_call | solution.py:98
  72.0 0.2 multiply_add_fusion.1
  72.3 0.1 fusion.1
  72.4 0.8 collective-permute-start.7
  73.2 1.1 collective-permute-done.11
  74.3 0.2 multiply_add_fusion
  74.6 1.3 %copy-done.2 = f32[4,512,256]{2,1,0:T(8,128)} copy-done((f32[4,512,256]{2,1,0:T(8,128)}, f32[4,512,256]{2,1,0:T(8,128)S(1)}, u32[]{:S(2)}) %copy-start.2) | copy-done | bytes 2097176
  75.9 0.1 fusion
  76.0 0.3 collective-permute-start.12
  76.4 5.4 %collective-permute-done.7 = f16[2,512,256]{2,1,0:T(8,128)(2,1)} collective-permute-done((f16[2,512,256]{2,1,0:T(8,128)(2,1)S(1)}, f16[2,512,256]{2,1,0:T(8,128)(2,1)}, u32[]{:S(2)}, u32[]{:S(2)}) %collective-permute-start.7) | collective-permute-done | bytes 524320 | tf_op jit(solution)/shard_map/ppermute | solution.py:40
  81.8 1.1 fusion.14
  82.8 1.2 collective-permute-start.8
  84.0 1.4 %collective-permute-done.12 = f16[2,512,256]{2,1,0:T(8,128)(2,1)} collective-permute-done((f16[2,512,256]{2,1,0:T(8,128)(2,1)S(1)}, f16[2,512,256]{2,1,0:T(8,128)(2,1)}, u32[]{:S(2)}, u32[]{:S(2)}) %collective-permute-start.12) | collective-permute-done | bytes 524320 | tf_op jit(solution)/shard_map/ppermute | solution.py:40
  85.4 1.2 fusion.15
  86.6 2.1 %collective-permute-start.13 = (f16[512,256]{1,0:T(8,128)(2,1)S(1)}, f16[512,256]{1,0:T(8,128)(2,1)S(1)}, u32[]{:S(2)}, u32[]{:S(2)}) collective-permute-start(f16[512,256]{1,0:T(8,128)(2,1)S(1)} %fusion.15), channel_id=1, source_target_pairs={{0,3},{1,2},{2,1},{3,0},{4,7},{5,6},{6,5},{7,4},{8,11},{9,10},{10,... | collective-permute-start | bytes 786440 | tf_op jit(solution)/shard_map/ppermute | solution.py:40
  88.8 0.1 copy.14.wanted
  88.9 1.6 %collective-permute-done.8 = f16[512,256]{1,0:T(8,128)(2,1)S(1)} collective-permute-done((f16[512,256]{1,0:T(8,128)(2,1)S(1)}, f16[512,256]{1,0:T(8,128)(2,1)S(1)}, u32[]{:S(2)}, u32[]{:S(2)}) %collective-permute-start.8) | collective-permute-done | bytes 262176 | tf_op jit(solution)/shard_map/ppermute | solution.py:40
  90.5 1.1 fusion.13
  91.6 2.7 %collective-permute-done.13 = f16[512,256]{1,0:T(8,128)(2,1)S(1)} collective-permute-done((f16[512,256]{1,0:T(8,128)(2,1)S(1)}, f16[512,256]{1,0:T(8,128)(2,1)S(1)}, u32[]{:S(2)}, u32[]{:S(2)}) %collective-permute-start.13) | collective-permute-done | bytes 262176 | tf_op jit(solution)/shard_map/ppermute | solution.py:40
  94.3 1.3 %fusion.7 = f16[512,256]{1,0:T(8,128)(2,1)S(1)} fusion(f32[4,512,256]{2,1,0:T(8,128)} %copy-done.2, f16[512,256]{1,0:T(8,128)(2,1)S(1)} %collective-permute-done.13, f16[2,512,256]{2,1,0:T(8,128)(2,1)} %collective-permute-done.12), kind=kLoop, calls=%fused_computation.19 | loop fusion | flops 1048576 | bytes 1310720 | tf_op jit(solution)/shard_map/convert_element_type | solution.py:113
  95.6 0.1 pad_maximum_fusion
  95.9 1.5 %collective-permute-done.14 = f16[4,64,512]{2,1,0:T(8,128)(2,1)S(1)} collective-permute-done((f16[4,64,512]{2,1,0:T(8,128)(2,1)S(1)}, f16[4,64,512]{2,1,0:T(8,128)(2,1)S(1)}, u32[]{:S(2)}, u32[]{:S(2)}) %collective-permute-start.14) | collective-permute-done | bytes 262176 | tf_op jit(solution)/shard_map/ppermute | solution.py:40
  97.5 1.8 %collective-permute-start.15 = (f16[2,64,512]{2,1,0:T(8,128)(2,1)S(1)}, f16[2,64,512]{2,1,0:T(8,128)(2,1)S(1)}, u32[]{:S(2)}, u32[]{:S(2)}) collective-permute-start(f16[2,64,512]{2,1,0:T(8,128)(2,1)S(1)} %pad_maximum_fusion.2), channel_id=1, source_target_pairs={{0,32},{1,33},{2,34},{3,35},{4,36},{5,37},{6,38},{7,39},{8,40},{9,... | collective-permute-start | bytes 393224 | tf_op jit(solution)/shard_map/ppermute | solution.py:40
  99.3 2.6 %collective-permute-start.16 = (f16[2,64,512]{2,1,0:T(8,128)(2,1)S(1)}, f16[2,64,512]{2,1,0:T(8,128)(2,1)S(1)}, u32[]{:S(2)}, u32[]{:S(2)}) collective-permute-start(f16[2,64,512]{2,1,0:T(8,128)(2,1)S(1)} %pad_maximum_fusion.3), channel_id=1, source_target_pairs={{0,96},{1,97},{2,98},{3,99},{4,100},{5,101},{6,102},{7,103},{8,104... | collective-permute-start | bytes 393224 | tf_op jit(solution)/shard_map/ppermute | solution.py:40
  101.9 0.1 collective-permute-start.17
  102.0 1.0 collective-permute-done.15
  103.1 5.5 %collective-permute-done.16 = f16[2,64,512]{2,1,0:T(8,128)(2,1)S(1)} collective-permute-done((f16[2,64,512]{2,1,0:T(8,128)(2,1)S(1)}, f16[2,64,512]{2,1,0:T(8,128)(2,1)S(1)}, u32[]{:S(2)}, u32[]{:S(2)}) %collective-permute-start.16) | collective-permute-done | bytes 131104 | tf_op jit(solution)/shard_map/ppermute | solution.py:40
  108.7 0.1 convert_multiply_fusion.home
  108.9 1.0 shard_map.146
  109.9 11.5 %all_to_all.10.stats = f32[16,8,128]{2,1,0:T(8,128)S(1)} all-to-all(f32[16,8,128]{2,1,0:T(8,128)S(1)} %shard_map.146), channel_id=1, replica_groups=mesh['rows'=8,'tensor'=16] {'tensor'}, dimensions={0} | all-to-all | bytes 131072 | tf_op jit(solution)/shard_map/all_to_all | solution.py:287
  121.4 1.8 %shard_map.147 = (f32[64,4096]{1,0:T(8,128)}, f32[1,64]{1,0:T(1,128)}) custom-call(s32[8]{0:T(128)S(1)} %slice_bitcast_fusion.5.source, f32[8,64,512]{2,1,0:T(8,128)S(1)} %convert_multiply_fusion.home, f32[16,8,128]{2,1,0:T(8,128)S(1)} %all_to_all.10.stats), custom_call_target="tpu_custom_call" | custom-call | tf_op jit(solution)/shard_map/pallas_call | solution.py:199
  (33 shorter events, 0.7 us)
Async XLA Ops:
  2.3 14.8 %all-to-all-start = ((f32[16,8,128]{2,1,0:T(8,128)}), f32[16,8,128]{2,1,0:T(8,128)S(1)}, u32[]{:S(2)}, u32[]{:S(2)}) async-start(f32[16,8,128]{2,1,0:T(8,128)} %shard_map.131), calls=%async_computation | async-start | bytes 131072 | tf_op jit(solution)/shard_map/all_to_all | solution.py:244
  17.1 9.8 %slice-start = ((s8[8388608]{0:T(1024)(128)(4,1)}), s8[4194304]{0:T(1024)(128)(4,1)S(1)}, s32[]{:S(2)}) async-start(s8[8388608]{0:T(1024)(128)(4,1)} %bitcast.39), calls=%async_computation.2 | async-start | bytes 8388608
  18.3 8.6 %slice-start.1 = ((s8[8388608]{0:T(1024)(128)(4,1)}), s8[4194304]{0:T(1024)(128)(4,1)S(1)}, s32[]{:S(2)}) async-start(s8[8388608]{0:T(1024)(128)(4,1)} %bitcast.39), calls=%async_computation.3 | async-start | bytes 8388608
  18.3 11.4 %collective-permute-start.2 = (bf16[64,1024]{1,0:T(8,128)(2,1)S(1)}, bf16[64,1024]{1,0:T(8,128)(2,1)S(1)}, u32[]{:S(2)}, u32[]{:S(2)}) collective-permute-start(bf16[64,1024]{1,0:T(8,128)(2,1)S(1)} %shard_map.132), channel_id=1, source_target_pairs={{0,64},{1,65},{2,66},{3,67},{4,68},{5,69},{6,70},{7,71},{8,72},{9,... | collective-permute-start | bytes 393224 | tf_op jit(solution)/shard_map/ppermute | solution.py:40
  22.3 7.5 %collective-permute-start.1 = (bf16[64,1024]{1,0:T(8,128)(2,1)S(1)}, bf16[64,1024]{1,0:T(8,128)(2,1)S(1)}, u32[]{:S(2)}, u32[]{:S(2)}) collective-permute-start(bf16[64,1024]{1,0:T(8,128)(2,1)S(1)} %shard_map.132), channel_id=1, source_target_pairs={{0,96},{1,97},{2,98},{3,99},{4,100},{5,101},{6,102},{7,103},{8,104... | collective-permute-start | bytes 393224 | tf_op jit(solution)/shard_map/ppermute | solution.py:40
  23.0 6.8 %collective-permute-start = (bf16[64,1024]{1,0:T(8,128)(2,1)S(1)}, bf16[64,1024]{1,0:T(8,128)(2,1)S(1)}, u32[]{:S(2)}, u32[]{:S(2)}) collective-permute-start(bf16[64,1024]{1,0:T(8,128)(2,1)S(1)} %shard_map.132), channel_id=1, source_target_pairs={{0,32},{1,33},{2,34},{3,35},{4,36},{5,37},{6,38},{7,39},{8,40},{9,... | collective-permute-start | bytes 393224 | tf_op jit(solution)/shard_map/ppermute | solution.py:40
  23.3 2.2 %copy-start = (bf16[256,16,512]{2,1,0:T(8,128)(2,1)S(1)}, bf16[256,16,512]{2,1,0:T(8,128)(2,1)}, u32[]{:S(2)}) copy-start(bf16[256,16,512]{2,1,0:T(8,128)(2,1)} %head) | copy-start | bytes 12582916
  28.3 2.2 %copy-start.1 = (bf16[256,16,512]{2,1,0:T(8,128)(2,1)S(1)}, bf16[256,16,512]{2,1,0:T(8,128)(2,1)}, u32[]{:S(2)}) copy-start(bf16[256,16,512]{2,1,0:T(8,128)(2,1)} %head.3) | copy-start | bytes 12582916
  29.8 2.1 %collective-permute-start.3 = (bf16[256,1024]{1,0:T(8,128)(2,1)S(1)}, bf16[256,1024]{1,0:T(8,128)(2,1)S(1)}, u32[]{:S(2)}, u32[]{:S(2)}) collective-permute-start(bf16[256,1024]{1,0:T(8,128)(2,1)S(1)} %pad_maximum_fusion.1.refs_0_), channel_id=1, source_target_pairs={{0,16},{1,17},{2,18},{3,19},{4,20},{5,21},{6,22},{7,23},{8,24},{9,... | collective-permute-start | bytes 1572872 | tf_op jit(solution)/shard_map/ppermute | solution.py:40
  33.9 14.9 %collective-permute-start.5 = (bf16[4,512,256]{2,1,0:T(8,128)(2,1)S(1)}, bf16[4,512,256]{2,1,0:T(8,128)(2,1)S(1)}, u32[]{:S(2)}, u32[]{:S(2)}) collective-permute-start(bf16[4,512,256]{2,1,0:T(8,128)(2,1)S(1)} %shard_map.138), channel_id=1, source_target_pairs={{0,1},{1,0},{2,3},{3,2},{4,5},{5,4},{6,7},{7,6},{8,9},{9,8},{10,11... | collective-permute-start | bytes 3145736 | tf_op jit(solution)/shard_map/ppermute | solution.py:40
  36.3 16.0 %collective-permute-start.10 = (bf16[4,512,256]{2,1,0:T(8,128)(2,1)S(1)}, bf16[4,512,256]{2,1,0:T(8,128)(2,1)S(1)}, u32[]{:S(2)}, u32[]{:S(2)}) collective-permute-start(bf16[4,512,256]{2,1,0:T(8,128)(2,1)S(1)} %shard_map.139), channel_id=1, source_target_pairs={{0,4},{1,5},{2,6},{3,7},{4,0},{5,1},{6,2},{7,3},{8,12},{9,13},{10,... | collective-permute-start | bytes 3145736 | tf_op jit(solution)/shard_map/ppermute | solution.py:40
  40.7 29.5 %collective-permute-start.9 = (bf16[4,512,256]{2,1,0:T(8,128)(2,1)S(1)}, bf16[4,512,256]{2,1,0:T(8,128)(2,1)S(1)}, u32[]{:S(2)}, u32[]{:S(2)}) collective-permute-start(bf16[4,512,256]{2,1,0:T(8,128)(2,1)S(1)} %shard_map.141), channel_id=1, source_target_pairs={{0,4},{1,5},{2,6},{3,7},{4,0},{5,1},{6,2},{7,3},{8,12},{9,13},{10,... | collective-permute-start | bytes 3145736 | tf_op jit(solution)/shard_map/ppermute | solution.py:40
  42.2 25.6 %collective-permute-start.4 = (bf16[4,512,256]{2,1,0:T(8,128)(2,1)S(1)}, bf16[4,512,256]{2,1,0:T(8,128)(2,1)S(1)}, u32[]{:S(2)}, u32[]{:S(2)}) collective-permute-start(bf16[4,512,256]{2,1,0:T(8,128)(2,1)S(1)} %shard_map.140), channel_id=1, source_target_pairs={{0,1},{1,0},{2,3},{3,2},{4,5},{5,4},{6,7},{7,6},{8,9},{9,8},{10,11... | collective-permute-start | bytes 3145736 | tf_op jit(solution)/shard_map/ppermute | solution.py:40
  49.1 22.9 %collective-permute-start.6 = (f16[4,512,256]{2,1,0:T(8,128)(2,1)S(1)}, f16[4,512,256]{2,1,0:T(8,128)(2,1)S(1)}, u32[]{:S(2)}, u32[]{:S(2)}) collective-permute-start(f16[4,512,256]{2,1,0:T(8,128)(2,1)S(1)} %multiply_convert_fusion.1), channel_id=1, source_target_pairs={{0,3},{1,2},{2,1},{3,0},{4,7},{5,6},{6,5},{7,4},{8,11},{9,10},{10,... | collective-permute-start | bytes 3145736 | tf_op jit(solution)/shard_map/ppermute | solution.py:40
  52.7 21.5 %collective-permute-start.11 = (f16[4,512,256]{2,1,0:T(8,128)(2,1)S(1)}, f16[4,512,256]{2,1,0:T(8,128)(2,1)S(1)}, u32[]{:S(2)}, u32[]{:S(2)}) collective-permute-start(f16[4,512,256]{2,1,0:T(8,128)(2,1)S(1)} %multiply_convert_fusion), channel_id=1, source_target_pairs={{0,12},{1,13},{2,14},{3,15},{4,8},{5,9},{6,10},{7,11},{8,4},{9,5},... | collective-permute-start | bytes 3145736 | tf_op jit(solution)/shard_map/ppermute | solution.py:40
  72.4 9.4 %collective-permute-start.7 = (f16[2,512,256]{2,1,0:T(8,128)(2,1)S(1)}, f16[2,512,256]{2,1,0:T(8,128)(2,1)}, u32[]{:S(2)}, u32[]{:S(2)}) collective-permute-start(f16[2,512,256]{2,1,0:T(8,128)(2,1)S(1)} %fusion.1), channel_id=1, source_target_pairs={{0,4},{1,5},{2,6},{3,7},{4,0},{5,1},{6,2},{7,3},{8,12},{9,13},{10,... | collective-permute-start | bytes 1572872 | tf_op jit(solution)/shard_map/ppermute | solution.py:40
  74.6 1.4 %copy-start.2 = (f32[4,512,256]{2,1,0:T(8,128)}, f32[4,512,256]{2,1,0:T(8,128)S(1)}, u32[]{:S(2)}) copy-start(f32[4,512,256]{2,1,0:T(8,128)S(1)} %multiply_add_fusion) | copy-start | bytes 6291460
  75.9 12.8 %copy-start.3 = (s32[64]{0:T(128)S(1)}, s32[64]{0:T(128)}, u32[]{:S(2)}) copy-start(s32[64]{0:T(128)} %param.22) | copy-start | bytes 772
  76.0 9.4 %collective-permute-start.12 = (f16[2,512,256]{2,1,0:T(8,128)(2,1)S(1)}, f16[2,512,256]{2,1,0:T(8,128)(2,1)}, u32[]{:S(2)}, u32[]{:S(2)}) collective-permute-start(f16[2,512,256]{2,1,0:T(8,128)(2,1)S(1)} %fusion), channel_id=1, source_target_pairs={{0,1},{1,0},{2,3},{3,2},{4,5},{5,4},{6,7},{7,6},{8,9},{9,8},{10,11... | collective-permute-start | bytes 1572872 | tf_op jit(solution)/shard_map/ppermute | solution.py:40
  82.8 7.7 %collective-permute-start.8 = (f16[512,256]{1,0:T(8,128)(2,1)S(1)}, f16[512,256]{1,0:T(8,128)(2,1)S(1)}, u32[]{:S(2)}, u32[]{:S(2)}) collective-permute-start(f16[512,256]{1,0:T(8,128)(2,1)S(1)} %fusion.14), channel_id=1, source_target_pairs={{0,12},{1,13},{2,14},{3,15},{4,8},{5,9},{6,10},{7,11},{8,4},{9,5},... | collective-permute-start | bytes 786440 | tf_op jit(solution)/shard_map/ppermute | solution.py:40
  86.6 7.7 %collective-permute-start.13 = (f16[512,256]{1,0:T(8,128)(2,1)S(1)}, f16[512,256]{1,0:T(8,128)(2,1)S(1)}, u32[]{:S(2)}, u32[]{:S(2)}) collective-permute-start(f16[512,256]{1,0:T(8,128)(2,1)S(1)} %fusion.15), channel_id=1, source_target_pairs={{0,3},{1,2},{2,1},{3,0},{4,7},{5,6},{6,5},{7,4},{8,11},{9,10},{10,... | collective-permute-start | bytes 786440 | tf_op jit(solution)/shard_map/ppermute | solution.py:40
  95.8 1.6 %collective-permute-start.14 = (f16[4,64,512]{2,1,0:T(8,128)(2,1)S(1)}, f16[4,64,512]{2,1,0:T(8,128)(2,1)S(1)}, u32[]{:S(2)}, u32[]{:S(2)}) collective-permute-start(f16[4,64,512]{2,1,0:T(8,128)(2,1)S(1)} %bitcast.43), channel_id=1, source_target_pairs={{0,16},{1,17},{2,18},{3,19},{4,20},{5,21},{6,22},{7,23},{8,24},{9,... | collective-permute-start | bytes 786440 | tf_op jit(solution)/shard_map/ppermute | solution.py:40
  97.5 5.6 %collective-permute-start.15 = (f16[2,64,512]{2,1,0:T(8,128)(2,1)S(1)}, f16[2,64,512]{2,1,0:T(8,128)(2,1)S(1)}, u32[]{:S(2)}, u32[]{:S(2)}) collective-permute-start(f16[2,64,512]{2,1,0:T(8,128)(2,1)S(1)} %pad_maximum_fusion.2), channel_id=1, source_target_pairs={{0,32},{1,33},{2,34},{3,35},{4,36},{5,37},{6,38},{7,39},{8,40},{9,... | collective-permute-start | bytes 393224 | tf_op jit(solution)/shard_map/ppermute | solution.py:40
  99.3 9.4 %collective-permute-start.16 = (f16[2,64,512]{2,1,0:T(8,128)(2,1)S(1)}, f16[2,64,512]{2,1,0:T(8,128)(2,1)S(1)}, u32[]{:S(2)}, u32[]{:S(2)}) collective-permute-start(f16[2,64,512]{2,1,0:T(8,128)(2,1)S(1)} %pad_maximum_fusion.3), channel_id=1, source_target_pairs={{0,96},{1,97},{2,98},{3,99},{4,100},{5,101},{6,102},{7,103},{8,104... | collective-permute-start | bytes 393224 | tf_op jit(solution)/shard_map/ppermute | solution.py:40
  101.9 6.7 %collective-permute-start.17 = (f16[2,64,512]{2,1,0:T(8,128)(2,1)S(1)}, f16[2,64,512]{2,1,0:T(8,128)(2,1)S(1)}, u32[]{:S(2)}, u32[]{:S(2)}) collective-permute-start(f16[2,64,512]{2,1,0:T(8,128)(2,1)S(1)} %pad_maximum_fusion.4), channel_id=1, source_target_pairs={{0,64},{1,65},{2,66},{3,67},{4,68},{5,69},{6,70},{7,71},{8,72},{9,... | collective-permute-start | bytes 393224 | tf_op jit(solution)/shard_map/ppermute | solution.py:40

commit v6 on v5

--- a/solution.py
+++ b/solution.py
@@ -10,6 +10,7 @@
 
 D = 8192
 DE = 4096
+VOCAB = 65536
 NZ, NC, NY, NX = 4, 2, 4, 4
 AXES = ("rows", "tensor")
 BF = jnp.bfloat16
@@ -51,6 +52,7 @@
                     row = [(y ^ j) * NX + (x ^ i) for i in first for j in second]
                     row += [(y ^ i) * NX + (x ^ j) for i in first for j in second]
                     row += [(z ^ i) * NC + k for i in (0,) + ALONG_Z for k in (c, 1 - c)]
+                    row += [(y * NX + x) * (VOCAB // (NY * NX))]
                     out[device(z, c, y, x), : len(row)] = row
     return out
 
@@ -72,8 +74,7 @@
     )(head)
 
 
-def matmul_kernel(first, half, table, alpha, acts, wb0, wb1, we, wa, *rest):
-    out = rest[-1]
+def matmul_kernel(first, half, table, alpha, acts, wb0, wb1, we, wa, out):
     quarter, cols = wb0.shape[1], out.shape[2]
     for i in range(out.shape[0]):
         block = table[first + i]
@@ -86,15 +87,13 @@
             for j, w in enumerate((wb0, wb1, we, wa))
         ]
         total = base0 + base1 + alpha[0] * (expert - anti)
-        for arrived in rest[:-1]:
-            total += arrived[i].astype(F32)
         out[i] = total.astype(out.dtype)
 
 
-def project(table, alpha, acts, heads, first, half, dtype, *arrived):
+def project(table, alpha, acts, heads, first, half, dtype):
     smem = pl.BlockSpec(memory_space=pltpu.SMEM)
     vmem = pl.BlockSpec(memory_space=pltpu.VMEM)
-    args = (table, alpha, acts, *heads, *arrived)
+    args = (table, alpha, acts, *heads)
     return pl.pallas_call(
         functools.partial(matmul_kernel, first, half),
         in_specs=[smem] * 2 + [vmem] * (len(args) - 2),
@@ -159,8 +158,12 @@
         at += ref.shape[0]
 
 
-def stats_kernel(source, home, wanted, out):
+def stats_kernel(source, home, ids, out):
     pieces, rows, width = home.shape
+    row = ids[...][None].astype(F32)
+    row = jnp.concatenate([row, jnp.zeros((1, 128 - rows), F32)], axis=1)
+    column = jnp.broadcast_to(row, (128, 128)).T[:rows, :1]
+    wanted = column.astype(jnp.int32) - source[pieces]
     top = jnp.max(home[...], axis=(0,))
     top = jnp.max(top, axis=1, keepdims=True)
     total = jnp.zeros((rows, width), F32)
@@ -169,7 +172,7 @@
     for i in range(pieces):
         value = home[i]
         total += jnp.exp(value - top)
-        pick += jnp.where(lane == wanted[...] - source[i] * width, value, 0.0)
+        pick += jnp.where(lane == wanted - source[i] * width, value, 0.0)
     total = jnp.sum(total, axis=1, keepdims=True)
     pick = jnp.sum(pick, axis=1, keepdims=True)
     to_all(out, [top, total, pick])
@@ -192,7 +195,7 @@
 
 def call(kernel, shapes, *args):
     def spec(v):
-        small = v.ndim == 1 and v.dtype == jnp.int32
+        small = v.dtype == jnp.int32 and v.size < 32
         return pl.BlockSpec(memory_space=pltpu.SMEM) if small else pl.BlockSpec()
 
     outs = [jax.ShapeDtypeStruct(s, d) for s, d in shapes]
@@ -223,7 +226,7 @@
     t = lax.axis_index("tensor")
     rows, c_width = token_ids.shape[0], base_head.shape[2]
     mine = lax.dynamic_slice(jnp.asarray(tables()), (r * (NY * NX) + t, 0), (1, 48))[0]
-    table, source = mine[:32], mine[32:40]
+    table, source = mine[:32], mine[32:41]
 
     quarter = expert_head.shape[0]
     heads = []
@@ -258,8 +261,7 @@
     for i in range(4):
         for half in range(2):
             kind = BF if i < 2 else F32
-            arrived = moved[half][1:] if i == 3 else []
-            part = project(table, strength, acts, heads, 16 * half + 4 * i, half, kind, *arrived)
+            part = project(table, strength, acts, heads, 16 * half + 4 * i, half, kind)
             table, part = together(table, part)
             if i < 2:
                 moved[half].append(exchange(part, axes[half][0], 0))
@@ -268,7 +270,8 @@
     second_step = [
         exchange(narrow(kept[h][0] + wide(moved[h][0])), axes[h][0], 1) for h in range(2)
     ]
-    sums = [kept[h][1] + wide(second_step[h]) for h in range(2)]
+    sums = together(*[kept[h][1] + wide(moved[h][1]) for h in range(2)])
+    sums = [sums[h] + wide(second_step[h]) for h in range(2)]
     moved = [exchange(narrow(sums[h][:2]), axes[h][1], 0) for h in range(2)]
     second_step = [
         exchange(narrow(sums[h][3] + wide(moved[h][1])), axes[h][1], 1) for h in range(2)
@@ -282,8 +285,7 @@
     home = [both[0]] + [exchange(m, *move) for m, move in zip(both[1:], along_z)]
     home = wide(jnp.concatenate(home))
 
-    wanted = (token_ids - t * (8 * c_width))[:, None]
-    stats = call(stats_kernel, [((NY * NX, 8, 128), F32)], source, home, wanted)
+    stats = call(stats_kernel, [((NY * NX, 8, 128), F32)], source, home, in_hbm(token_ids))
     stats = lax.all_to_all(stats, "tensor", 0, 0, tiled=True)
     log_probs, picked = call(
         final_kernel, [((rows, 8 * c_width), F32), ((1, rows), F32)], source, home, stats

time: 124 us -> 120 us (0.968)
  other arithmetic: 6.61 us -> 3.05 us
  local copies, waits for them, and re-layouts: 5.19 us -> 3.75 us
  waiting for transfers between devices: 44 us -> 45.4 us
    convert_element_type x6, other arithmetic: 3.38 us -> 1.31 us  [narrow(): return (value * DOWN).astype(F16)]
    mul x2, other arithmetic: 2.27 us -> 0.2 us  [narrow(): return (value * DOWN).astype(F16)]
    ppermute x18, waiting for transfers between devices: 37.7 us -> 39.1 us  [exchange(): return lax.ppermute(value, AXES, pairs)]
    unnamed x15 -> x11, local copies, waits for them, and re-layouts: 4.21 us -> 2.86 us
  transfers between devices with their start and end apart: 19 -> 19, of which waited for: 12 -> 12; matrix products, arithmetic and copies ran while one was open for 5% -> 3% of each run, Pallas kernels for 15% -> 16%
where the time goes in v6:
time: 120 us
  waiting for transfers between devices  45.4 us (38%)
  starting transfers between devices  27.9 us (23%)
  Pallas kernels  26.5 us (22%)
  blocking collectives  11.5 us (10%)
  local copies, waits for them, and re-layouts  3.75 us (3%)
  other arithmetic  3.05 us (3%)
  between operations  1.66 us (1%)
    ppermute x18, waiting for transfers between devices, exchange(): return lax.ppermute(value, AXES, pairs)  39.1 us
    ppermute x18, starting transfers between devices, exchange(): return lax.ppermute(value, AXES, pairs)  20.8 us
    pallas_call x8, Pallas kernels, project(): pl.pallas_call(functools.partial(matmul_kernel, first, half), in_specs=[s...  15 us
    all_to_all x1, blocking collectives, shards(): stats = lax.all_to_all(stats, 'tensor', 0, 0, tiled=True)  11.5 us
    all_to_all x1, starting transfers between devices, shards(): sums = lax.all_to_all(sums, 'tensor', 0, 0, tiled=True)  7.12 us
    all_to_all x1, waiting for transfers between devices, shards(): sums = lax.all_to_all(sums, 'tensor', 0, 0, tiled=True)  6.3 us
    pallas_call x5, Pallas kernels, call(): pl.pallas_call(kernel, in_specs=[spec(v) for v in args], out_specs=[pl.Bl...  5.93 us
    pallas_call x4, Pallas kernels, relay(): pl.pallas_call(relay_kernel, grid=(count // step,), in_specs=[pl.BlockSpe...  5.57 us
  transfers between devices with their start and end apart: 19, of which 12 were waited for; matrix products, arithmetic and copies ran while one was open for 3% of the time, Pallas kernels for 16%

profile of v6, /device:TPU:0, one launch (start us, length us, event | category | flops | bytes accessed | tf_op | source)
XLA Modules:
  0.0 119.7 jit_solution(16070567884509648220)
XLA Ops:
  0.6 1.7 %shard_map.131 = f32[16,8,128]{2,1,0:T(8,128)} custom-call(bf16[64,512]{1,0:T(8,128)(2,1)} %refs_0_.3, bf16[64,256]{1,0:T(8,128)(2,1)} %refs_1_.3, bf16[64,256]{1,0:T(8,128)(2,1)} %refs_2_.3), custom_call_target="tpu_custom_call" | custom-call | tf_op jit(solution)/shard_map/pallas_call | solution.py:202
  2.3 7.1 %all-to-all-start = ((f32[16,8,128]{2,1,0:T(8,128)}), f32[16,8,128]{2,1,0:T(8,128)S(1)}, u32[]{:S(2)}, u32[]{:S(2)}) async-start(f32[16,8,128]{2,1,0:T(8,128)} %shard_map.131), calls=%async_computation | async-start | bytes 131072 | tf_op jit(solution)/shard_map/all_to_all | solution.py:247
  9.4 0.7 constant_dynamic-slice_fusion
  10.8 6.3 %all-to-all-done.refs_6_ = f32[16,8,128]{2,1,0:T(8,128)S(1)} async-done(((f32[16,8,128]{2,1,0:T(8,128)}), f32[16,8,128]{2,1,0:T(8,128)S(1)}, u32[]{:S(2)}, u32[]{:S(2)}) %all-to-all-start) | async-done | bytes 65568 | tf_op jit(solution)/shard_map/all_to_all | solution.py:247
  17.1 1.2 %shard_map.132 = bf16[64,1024]{1,0:T(8,128)(2,1)S(1)} custom-call(bf16[64,512]{1,0:T(8,128)(2,1)} %refs_0_.3, bf16[64,256]{1,0:T(8,128)(2,1)} %refs_1_.3, bf16[64,256]{1,0:T(8,128)(2,1)} %refs_2_.3, bf16[512]{0:T(512)(128)(2,1)} %refs_3_.1, bf16[256]{0:T(256)(128)(2,1)} %refs_4_.1, bf16[256]{0:T(256)(128)(2,1)} %refs_5_.1, ...), custom_call_target="tpu_custom_call" | custom-call | tf_op jit(solution)/shard_map/pallas_call | solution.py:202
  18.3 4.0 %collective-permute-start.2 = (bf16[64,1024]{1,0:T(8,128)(2,1)S(1)}, bf16[64,1024]{1,0:T(8,128)(2,1)S(1)}, u32[]{:S(2)}, u32[]{:S(2)}) collective-permute-start(bf16[64,1024]{1,0:T(8,128)(2,1)S(1)} %shard_map.132), channel_id=1, source_target_pairs={{0,64},{1,65},{2,66},{3,67},{4,68},{5,69},{6,70},{7,71},{8,72},{9,... | collective-permute-start | bytes 393224 | tf_op jit(solution)/shard_map/ppermute | solution.py:41
  22.3 0.7 collective-permute-start.1
  23.0 0.3 collective-permute-start
  23.3 2.2 %copy-done = bf16[256,16,512]{2,1,0:T(8,128)(2,1)S(1)} copy-done((bf16[256,16,512]{2,1,0:T(8,128)(2,1)S(1)}, bf16[256,16,512]{2,1,0:T(8,128)(2,1)}, u32[]{:S(2)}) %copy-start) | copy-done | bytes 4194328
  25.5 1.4 %shard_map.133.we = bf16[16,256,512]{2,1,0:T(8,128)(2,1)S(1)} custom-call(bf16[256,16,512]{2,1,0:T(8,128)(2,1)S(1)} %copy-done), custom_call_target="tpu_custom_call" | custom-call | flops 10000000000 | bytes 16777216 | tf_op jit(solution)/shard_map/pallas_call | solution.py:66
  26.9 1.4 %shard_map.134.wb0 = bf16[16,256,512]{2,1,0:T(8,128)(2,1)S(1)} custom-call(bf16[512,16,512]{2,1,0:T(8,128)(2,1)S(1)} %bitcast.38), custom_call_target="tpu_custom_call" | custom-call | flops 10000000000 | bytes 16777216 | tf_op jit(solution)/shard_map/pallas_call | solution.py:66
  28.3 1.4 %shard_map.135.wb1 = bf16[16,256,512]{2,1,0:T(8,128)(2,1)S(1)} custom-call(bf16[512,16,512]{2,1,0:T(8,128)(2,1)S(1)} %bitcast.38), custom_call_target="tpu_custom_call" | custom-call | flops 10000000000 | bytes 16777216 | tf_op jit(solution)/shard_map/pallas_call | solution.py:66
  29.8 0.1 collective-permute-start.3
  29.9 0.6 copy-done.1
  30.5 1.4 %shard_map.136.wa = bf16[16,256,512]{2,1,0:T(8,128)(2,1)S(1)} custom-call(bf16[256,16,512]{2,1,0:T(8,128)(2,1)S(1)} %copy-done.1), custom_call_target="tpu_custom_call" | custom-call | flops 10000000000 | bytes 16777216 | tf_op jit(solution)/shard_map/pallas_call | solution.py:66
  32.0 1.9 %shard_map.138 = bf16[4,512,256]{2,1,0:T(8,128)(2,1)S(1)} custom-call(s32[32]{0:T(128)S(1)} %slice_bitcast_fusion.4.table, f32[1]{0:T(128)S(6)} %copy.18.alpha, bf16[512,1024]{1,0:T(8,128)(2,1)S(1)} %shard_map.137.acts, bf16[16,256,512]{2,1,0:T(8,128)(2,1)S(1)} %shard_map.134.wb0, bf16[16,256,512]{2,1,0:T(8,128)(2,1)S(1)} %shard_map.135.wb1, ...), custom_call_target="tpu_custom_call" | custom-call | flops 1 | bytes 1 | tf_op jit(solution)/shard_map/pallas_call | solution.py:97
  33.9 0.6 collective-permute-start.6
  34.5 1.9 %shard_map.139 = bf16[4,512,256]{2,1,0:T(8,128)(2,1)S(1)} custom-call(s32[32]{0:T(128)S(1)} %slice_bitcast_fusion.4.table, f32[1]{0:T(128)S(6)} %copy.18.alpha, bf16[512,1024]{1,0:T(8,128)(2,1)S(1)} %shard_map.137.acts, bf16[16,256,512]{2,1,0:T(8,128)(2,1)S(1)} %shard_map.134.wb0, bf16[16,256,512]{2,1,0:T(8,128)(2,1)S(1)} %shard_map.135.wb1, ...), custom_call_target="tpu_custom_call" | custom-call | flops 1 | bytes 1 | tf_op jit(solution)/shard_map/pallas_call | solution.py:97
  36.4 0.6 collective-permute-start.10
  37.0 1.9 %shard_map.140 = bf16[4,512,256]{2,1,0:T(8,128)(2,1)S(1)} custom-call(s32[32]{0:T(128)S(1)} %slice_bitcast_fusion.4.table, f32[1]{0:T(128)S(6)} %copy.18.alpha, bf16[512,1024]{1,0:T(8,128)(2,1)S(1)} %shard_map.137.acts, bf16[16,256,512]{2,1,0:T(8,128)(2,1)S(1)} %shard_map.134.wb0, bf16[16,256,512]{2,1,0:T(8,128)(2,1)S(1)} %shard_map.135.wb1, ...), custom_call_target="tpu_custom_call" | custom-call | flops 1 | bytes 1 | tf_op jit(solution)/shard_map/pallas_call | solution.py:97
  38.9 1.5 %collective-permute-start.4 = (bf16[4,512,256]{2,1,0:T(8,128)(2,1)S(1)}, bf16[4,512,256]{2,1,0:T(8,128)(2,1)S(1)}, u32[]{:S(2)}, u32[]{:S(2)}) collective-permute-start(bf16[4,512,256]{2,1,0:T(8,128)(2,1)S(1)} %shard_map.140), channel_id=1, source_target_pairs={{0,1},{1,0},{2,3},{3,2},{4,5},{5,4},{6,7},{7,6},{8,9},{9,8},{10,11... | collective-permute-start | bytes 3145736 | tf_op jit(solution)/shard_map/ppermute | solution.py:41
  40.4 1.9 %shard_map.141 = bf16[4,512,256]{2,1,0:T(8,128)(2,1)S(1)} custom-call(s32[32]{0:T(128)S(1)} %slice_bitcast_fusion.4.table, f32[1]{0:T(128)S(6)} %copy.18.alpha, bf16[512,1024]{1,0:T(8,128)(2,1)S(1)} %shard_map.137.acts, bf16[16,256,512]{2,1,0:T(8,128)(2,1)S(1)} %shard_map.134.wb0, bf16[16,256,512]{2,1,0:T(8,128)(2,1)S(1)} %shard_map.135.wb1, ...), custom_call_target="tpu_custom_call" | custom-call | flops 1 | bytes 1 | tf_op jit(solution)/shard_map/pallas_call | solution.py:97
  42.3 1.6 %collective-permute-start.5 = (bf16[4,512,256]{2,1,0:T(8,128)(2,1)S(1)}, bf16[4,512,256]{2,1,0:T(8,128)(2,1)S(1)}, u32[]{:S(2)}, u32[]{:S(2)}) collective-permute-start(bf16[4,512,256]{2,1,0:T(8,128)(2,1)S(1)} %shard_map.141), channel_id=1, source_target_pairs={{0,4},{1,5},{2,6},{3,7},{4,0},{5,1},{6,2},{7,3},{8,12},{9,13},{10,... | collective-permute-start | bytes 3145736 | tf_op jit(solution)/shard_map/ppermute | solution.py:41
  43.9 1.9 %shard_map.142 = f32[4,512,256]{2,1,0:T(8,128)S(1)} custom-call(s32[32]{0:T(128)S(1)} %slice_bitcast_fusion.4.table, f32[1]{0:T(128)S(6)} %copy.18.alpha, bf16[512,1024]{1,0:T(8,128)(2,1)S(1)} %shard_map.137.acts, bf16[16,256,512]{2,1,0:T(8,128)(2,1)S(1)} %shard_map.134.wb0, bf16[16,256,512]{2,1,0:T(8,128)(2,1)S(1)} %shard_map.135.wb1, ...), custom_call_target="tpu_custom_call" | custom-call | flops 1 | bytes 1 | tf_op jit(solution)/shard_map/pallas_call | solution.py:97
  45.8 3.0 %collective-permute-done.6 = bf16[4,512,256]{2,1,0:T(8,128)(2,1)S(1)} collective-permute-done((bf16[4,512,256]{2,1,0:T(8,128)(2,1)S(1)}, bf16[4,512,256]{2,1,0:T(8,128)(2,1)S(1)}, u32[]{:S(2)}, u32[]{:S(2)}) %collective-permute-start.6) | collective-permute-done | bytes 1048608 | tf_op jit(solution)/shard_map/ppermute | solution.py:41
  48.8 0.4 multiply_convert_fusion.1
  49.1 1.4 %collective-permute-start.7 = (f16[4,512,256]{2,1,0:T(8,128)(2,1)S(1)}, f16[4,512,256]{2,1,0:T(8,128)(2,1)S(1)}, u32[]{:S(2)}, u32[]{:S(2)}) collective-permute-start(f16[4,512,256]{2,1,0:T(8,128)(2,1)S(1)} %multiply_convert_fusion.1), channel_id=1, source_target_pairs={{0,3},{1,2},{2,1},{3,0},{4,7},{5,6},{6,5},{7,4},{8,11},{9,10},{10,... | collective-permute-start | bytes 3145736 | tf_op jit(solution)/shard_map/ppermute | solution.py:41
  50.6 1.9 %shard_map.143 = f32[4,512,256]{2,1,0:T(8,128)S(1)} custom-call(s32[32]{0:T(128)S(1)} %slice_bitcast_fusion.4.table, f32[1]{0:T(128)S(6)} %copy.18.alpha, bf16[512,1024]{1,0:T(8,128)(2,1)S(1)} %shard_map.137.acts, bf16[16,256,512]{2,1,0:T(8,128)(2,1)S(1)} %shard_map.134.wb0, bf16[16,256,512]{2,1,0:T(8,128)(2,1)S(1)} %shard_map.135.wb1, ...), custom_call_target="tpu_custom_call" | custom-call | flops 1 | bytes 1 | tf_op jit(solution)/shard_map/pallas_call | solution.py:97
  52.4 1.9 %shard_map.144 = f32[4,512,256]{2,1,0:T(8,128)S(1)} custom-call(s32[32]{0:T(128)S(1)} %slice_bitcast_fusion.4.table, f32[1]{0:T(128)S(6)} %copy.18.alpha, bf16[512,1024]{1,0:T(8,128)(2,1)S(1)} %shard_map.137.acts, bf16[16,256,512]{2,1,0:T(8,128)(2,1)S(1)} %shard_map.134.wb0, bf16[16,256,512]{2,1,0:T(8,128)(2,1)S(1)} %shard_map.135.wb1, ...), custom_call_target="tpu_custom_call" | custom-call | flops 1 | bytes 1 | tf_op jit(solution)/shard_map/pallas_call | solution.py:97
  54.3 1.9 %shard_map.145 = f32[4,512,256]{2,1,0:T(8,128)S(1)} custom-call(s32[32]{0:T(128)S(1)} %slice_bitcast_fusion.4.table, f32[1]{0:T(128)S(6)} %copy.18.alpha, bf16[512,1024]{1,0:T(8,128)(2,1)S(1)} %shard_map.137.acts, bf16[16,256,512]{2,1,0:T(8,128)(2,1)S(1)} %shard_map.134.wb0, bf16[16,256,512]{2,1,0:T(8,128)(2,1)S(1)} %shard_map.135.wb1, ...), custom_call_target="tpu_custom_call" | custom-call | flops 1 | bytes 1 | tf_op jit(solution)/shard_map/pallas_call | solution.py:97
  56.2 0.4 multiply_convert_fusion
  56.6 1.2 %collective-permute-start.11 = (f16[4,512,256]{2,1,0:T(8,128)(2,1)S(1)}, f16[4,512,256]{2,1,0:T(8,128)(2,1)S(1)}, u32[]{:S(2)}, u32[]{:S(2)}) collective-permute-start(f16[4,512,256]{2,1,0:T(8,128)(2,1)S(1)} %multiply_convert_fusion), channel_id=1, source_target_pairs={{0,12},{1,13},{2,14},{3,15},{4,8},{5,9},{6,10},{7,11},{8,4},{9,5},... | collective-permute-start | bytes 3145736 | tf_op jit(solution)/shard_map/ppermute | solution.py:41
  57.8 10.0 %collective-permute-done.4 = bf16[4,512,256]{2,1,0:T(8,128)(2,1)S(1)} collective-permute-done((bf16[4,512,256]{2,1,0:T(8,128)(2,1)S(1)}, bf16[4,512,256]{2,1,0:T(8,128)(2,1)S(1)}, u32[]{:S(2)}, u32[]{:S(2)}) %collective-permute-start.4) | collective-permute-done | bytes 1048608 | tf_op jit(solution)/shard_map/ppermute | solution.py:41
  67.9 0.2 convert_add_fusion.1
  68.1 0.2 convert_add_fusion
  68.3 3.2 %collective-permute-done.7 = f16[4,512,256]{2,1,0:T(8,128)(2,1)S(1)} collective-permute-done((f16[4,512,256]{2,1,0:T(8,128)(2,1)S(1)}, f16[4,512,256]{2,1,0:T(8,128)(2,1)S(1)}, u32[]{:S(2)}, u32[]{:S(2)}) %collective-permute-start.7) | collective-permute-done | bytes 1048608 | tf_op jit(solution)/shard_map/ppermute | solution.py:41
  71.5 0.3 multiply_add_fusion.1
  71.8 0.1 fusion.1
  72.0 0.6 collective-permute-start.8
  72.6 1.8 %collective-permute-done.11 = f16[4,512,256]{2,1,0:T(8,128)(2,1)S(1)} collective-permute-done((f16[4,512,256]{2,1,0:T(8,128)(2,1)S(1)}, f16[4,512,256]{2,1,0:T(8,128)(2,1)S(1)}, u32[]{:S(2)}, u32[]{:S(2)}) %collective-permute-start.11) | collective-permute-done | bytes 1048608 | tf_op jit(solution)/shard_map/ppermute | solution.py:41
  74.4 0.3 multiply_add_fusion
  74.7 0.1 fusion
  74.8 0.2 collective-permute-start.12
  75.0 6.2 %collective-permute-done.8 = f16[2,512,256]{2,1,0:T(8,128)(2,1)S(1)} collective-permute-done((f16[2,512,256]{2,1,0:T(8,128)(2,1)S(1)}, f16[2,512,256]{2,1,0:T(8,128)(2,1)S(1)}, u32[]{:S(2)}, u32[]{:S(2)}) %collective-permute-start.8) | collective-permute-done | bytes 524320 | tf_op jit(solution)/shard_map/ppermute | solution.py:41
  81.2 0.1 fusion.14
  81.3 1.2 %collective-permute-start.9 = (f16[512,256]{1,0:T(8,128)(2,1)S(1)}, f16[512,256]{1,0:T(8,128)(2,1)S(1)}, u32[]{:S(2)}, u32[]{:S(2)}) collective-permute-start(f16[512,256]{1,0:T(8,128)(2,1)S(1)} %fusion.14), channel_id=1, source_target_pairs={{0,12},{1,13},{2,14},{3,15},{4,8},{5,9},{6,10},{7,11},{8,4},{9,5},... | collective-permute-start | bytes 786440 | tf_op jit(solution)/shard_map/ppermute | solution.py:41
  82.5 1.5 %collective-permute-done.12 = f16[2,512,256]{2,1,0:T(8,128)(2,1)S(1)} collective-permute-done((f16[2,512,256]{2,1,0:T(8,128)(2,1)S(1)}, f16[2,512,256]{2,1,0:T(8,128)(2,1)S(1)}, u32[]{:S(2)}, u32[]{:S(2)}) %collective-permute-start.12) | collective-permute-done | bytes 524320 | tf_op jit(solution)/shard_map/ppermute | solution.py:41
  84.1 0.1 fusion.15
  84.2 2.1 %collective-permute-start.13 = (f16[512,256]{1,0:T(8,128)(2,1)S(1)}, f16[512,256]{1,0:T(8,128)(2,1)S(1)}, u32[]{:S(2)}, u32[]{:S(2)}) collective-permute-start(f16[512,256]{1,0:T(8,128)(2,1)S(1)} %fusion.15), channel_id=1, source_target_pairs={{0,3},{1,2},{2,1},{3,0},{4,7},{5,6},{6,5},{7,4},{8,11},{9,10},{10,... | collective-permute-start | bytes 786440 | tf_op jit(solution)/shard_map/ppermute | solution.py:41
  86.4 2.6 %collective-permute-done.9 = f16[512,256]{1,0:T(8,128)(2,1)S(1)} collective-permute-done((f16[512,256]{1,0:T(8,128)(2,1)S(1)}, f16[512,256]{1,0:T(8,128)(2,1)S(1)}, u32[]{:S(2)}, u32[]{:S(2)}) %collective-permute-start.9) | collective-permute-done | bytes 262176 | tf_op jit(solution)/shard_map/ppermute | solution.py:41
  89.0 0.2 fusion.13
  89.1 2.7 %collective-permute-done.13 = f16[512,256]{1,0:T(8,128)(2,1)S(1)} collective-permute-done((f16[512,256]{1,0:T(8,128)(2,1)S(1)}, f16[512,256]{1,0:T(8,128)(2,1)S(1)}, u32[]{:S(2)}, u32[]{:S(2)}) %collective-permute-start.13) | collective-permute-done | bytes 262176 | tf_op jit(solution)/shard_map/ppermute | solution.py:41
  91.8 0.2 fusion.7
  92.0 0.1 pad_maximum_fusion
  92.3 1.5 %collective-permute-done.14 = f16[4,64,512]{2,1,0:T(8,128)(2,1)S(1)} collective-permute-done((f16[4,64,512]{2,1,0:T(8,128)(2,1)S(1)}, f16[4,64,512]{2,1,0:T(8,128)(2,1)S(1)}, u32[]{:S(2)}, u32[]{:S(2)}) %collective-permute-start.14) | collective-permute-done | bytes 262176 | tf_op jit(solution)/shard_map/ppermute | solution.py:41
  93.9 1.8 %collective-permute-start.15 = (f16[2,64,512]{2,1,0:T(8,128)(2,1)S(1)}, f16[2,64,512]{2,1,0:T(8,128)(2,1)S(1)}, u32[]{:S(2)}, u32[]{:S(2)}) collective-permute-start(f16[2,64,512]{2,1,0:T(8,128)(2,1)S(1)} %pad_maximum_fusion.2), channel_id=1, source_target_pairs={{0,32},{1,33},{2,34},{3,35},{4,36},{5,37},{6,38},{7,39},{8,40},{9,... | collective-permute-start | bytes 393224 | tf_op jit(solution)/shard_map/ppermute | solution.py:41
  95.7 2.6 %collective-permute-start.16 = (f16[2,64,512]{2,1,0:T(8,128)(2,1)S(1)}, f16[2,64,512]{2,1,0:T(8,128)(2,1)S(1)}, u32[]{:S(2)}, u32[]{:S(2)}) collective-permute-start(f16[2,64,512]{2,1,0:T(8,128)(2,1)S(1)} %pad_maximum_fusion.3), channel_id=1, source_target_pairs={{0,96},{1,97},{2,98},{3,99},{4,100},{5,101},{6,102},{7,103},{8,104... | collective-permute-start | bytes 393224 | tf_op jit(solution)/shard_map/ppermute | solution.py:41
  98.4 0.1 collective-permute-start.17
  98.5 1.0 collective-permute-done.15
  99.5 5.5 %collective-permute-done.16 = f16[2,64,512]{2,1,0:T(8,128)(2,1)S(1)} collective-permute-done((f16[2,64,512]{2,1,0:T(8,128)(2,1)S(1)}, f16[2,64,512]{2,1,0:T(8,128)(2,1)S(1)}, u32[]{:S(2)}, u32[]{:S(2)}) %collective-permute-start.16) | collective-permute-done | bytes 131104 | tf_op jit(solution)/shard_map/ppermute | solution.py:41
  105.2 0.1 convert_multiply_fusion.home
  105.3 1.2 shard_map.146
  106.5 11.5 %all_to_all.10.stats = f32[16,8,128]{2,1,0:T(8,128)S(1)} all-to-all(f32[16,8,128]{2,1,0:T(8,128)S(1)} %shard_map.146), channel_id=1, replica_groups=mesh['rows'=8,'tensor'=16] {'tensor'}, dimensions={0} | all-to-all | bytes 131072 | tf_op jit(solution)/shard_map/all_to_all | solution.py:289
  118.0 1.8 %shard_map.147 = (f32[64,4096]{1,0:T(8,128)}, f32[1,64]{1,0:T(1,128)}) custom-call(s32[9]{0:T(128)S(1)} %slice_bitcast_fusion.5.source, f32[8,64,512]{2,1,0:T(8,128)S(1)} %convert_multiply_fusion.home, f32[16,8,128]{2,1,0:T(8,128)S(1)} %all_to_all.10.stats), custom_call_target="tpu_custom_call" | custom-call | tf_op jit(solution)/shard_map/pallas_call | solution.py:202
  (29 shorter events, 0.6 us)
Async XLA Ops:
  2.3 14.8 %all-to-all-start = ((f32[16,8,128]{2,1,0:T(8,128)}), f32[16,8,128]{2,1,0:T(8,128)S(1)}, u32[]{:S(2)}, u32[]{:S(2)}) async-start(f32[16,8,128]{2,1,0:T(8,128)} %shard_map.131), calls=%async_computation | async-start | bytes 131072 | tf_op jit(solution)/shard_map/all_to_all | solution.py:247
  17.1 9.8 %slice-start = ((s8[8388608]{0:T(1024)(128)(4,1)}), s8[4194304]{0:T(1024)(128)(4,1)S(1)}, s32[]{:S(2)}) async-start(s8[8388608]{0:T(1024)(128)(4,1)} %bitcast.37), calls=%async_computation.2 | async-start | bytes 8388608
  18.3 8.6 %slice-start.1 = ((s8[8388608]{0:T(1024)(128)(4,1)}), s8[4194304]{0:T(1024)(128)(4,1)S(1)}, s32[]{:S(2)}) async-start(s8[8388608]{0:T(1024)(128)(4,1)} %bitcast.37), calls=%async_computation.3 | async-start | bytes 8388608
  18.3 11.4 %collective-permute-start.2 = (bf16[64,1024]{1,0:T(8,128)(2,1)S(1)}, bf16[64,1024]{1,0:T(8,128)(2,1)S(1)}, u32[]{:S(2)}, u32[]{:S(2)}) collective-permute-start(bf16[64,1024]{1,0:T(8,128)(2,1)S(1)} %shard_map.132), channel_id=1, source_target_pairs={{0,64},{1,65},{2,66},{3,67},{4,68},{5,69},{6,70},{7,71},{8,72},{9,... | collective-permute-start | bytes 393224 | tf_op jit(solution)/shard_map/ppermute | solution.py:41
  22.3 7.5 %collective-permute-start.1 = (bf16[64,1024]{1,0:T(8,128)(2,1)S(1)}, bf16[64,1024]{1,0:T(8,128)(2,1)S(1)}, u32[]{:S(2)}, u32[]{:S(2)}) collective-permute-start(bf16[64,1024]{1,0:T(8,128)(2,1)S(1)} %shard_map.132), channel_id=1, source_target_pairs={{0,96},{1,97},{2,98},{3,99},{4,100},{5,101},{6,102},{7,103},{8,104... | collective-permute-start | bytes 393224 | tf_op jit(solution)/shard_map/ppermute | solution.py:41
  23.0 6.8 %collective-permute-start = (bf16[64,1024]{1,0:T(8,128)(2,1)S(1)}, bf16[64,1024]{1,0:T(8,128)(2,1)S(1)}, u32[]{:S(2)}, u32[]{:S(2)}) collective-permute-start(bf16[64,1024]{1,0:T(8,128)(2,1)S(1)} %shard_map.132), channel_id=1, source_target_pairs={{0,32},{1,33},{2,34},{3,35},{4,36},{5,37},{6,38},{7,39},{8,40},{9,... | collective-permute-start | bytes 393224 | tf_op jit(solution)/shard_map/ppermute | solution.py:41
  23.3 2.2 %copy-start = (bf16[256,16,512]{2,1,0:T(8,128)(2,1)S(1)}, bf16[256,16,512]{2,1,0:T(8,128)(2,1)}, u32[]{:S(2)}) copy-start(bf16[256,16,512]{2,1,0:T(8,128)(2,1)} %head) | copy-start | bytes 12582916
  28.3 2.2 %copy-start.1 = (bf16[256,16,512]{2,1,0:T(8,128)(2,1)S(1)}, bf16[256,16,512]{2,1,0:T(8,128)(2,1)}, u32[]{:S(2)}) copy-start(bf16[256,16,512]{2,1,0:T(8,128)(2,1)} %head.3) | copy-start | bytes 12582916
  29.8 2.1 %collective-permute-start.3 = (bf16[256,1024]{1,0:T(8,128)(2,1)S(1)}, bf16[256,1024]{1,0:T(8,128)(2,1)S(1)}, u32[]{:S(2)}, u32[]{:S(2)}) collective-permute-start(bf16[256,1024]{1,0:T(8,128)(2,1)S(1)} %pad_maximum_fusion.1.refs_0_), channel_id=1, source_target_pairs={{0,16},{1,17},{2,18},{3,19},{4,20},{5,21},{6,22},{7,23},{8,24},{9,... | collective-permute-start | bytes 1572872 | tf_op jit(solution)/shard_map/ppermute | solution.py:41
  33.9 14.9 %collective-permute-start.6 = (bf16[4,512,256]{2,1,0:T(8,128)(2,1)S(1)}, bf16[4,512,256]{2,1,0:T(8,128)(2,1)S(1)}, u32[]{:S(2)}, u32[]{:S(2)}) collective-permute-start(bf16[4,512,256]{2,1,0:T(8,128)(2,1)S(1)} %shard_map.138), channel_id=1, source_target_pairs={{0,1},{1,0},{2,3},{3,2},{4,5},{5,4},{6,7},{7,6},{8,9},{9,8},{10,11... | collective-permute-start | bytes 3145736 | tf_op jit(solution)/shard_map/ppermute | solution.py:41
  36.4 19.8 %collective-permute-start.10 = (bf16[4,512,256]{2,1,0:T(8,128)(2,1)S(1)}, bf16[4,512,256]{2,1,0:T(8,128)(2,1)S(1)}, u32[]{:S(2)}, u32[]{:S(2)}) collective-permute-start(bf16[4,512,256]{2,1,0:T(8,128)(2,1)S(1)} %shard_map.139), channel_id=1, source_target_pairs={{0,4},{1,5},{2,6},{3,7},{4,0},{5,1},{6,2},{7,3},{8,12},{9,13},{10,... | collective-permute-start | bytes 3145736 | tf_op jit(solution)/shard_map/ppermute | solution.py:41
  38.9 29.0 %collective-permute-start.4 = (bf16[4,512,256]{2,1,0:T(8,128)(2,1)S(1)}, bf16[4,512,256]{2,1,0:T(8,128)(2,1)S(1)}, u32[]{:S(2)}, u32[]{:S(2)}) collective-permute-start(bf16[4,512,256]{2,1,0:T(8,128)(2,1)S(1)} %shard_map.140), channel_id=1, source_target_pairs={{0,1},{1,0},{2,3},{3,2},{4,5},{5,4},{6,7},{7,6},{8,9},{9,8},{10,11... | collective-permute-start | bytes 3145736 | tf_op jit(solution)/shard_map/ppermute | solution.py:41
  42.3 25.8 %collective-permute-start.5 = (bf16[4,512,256]{2,1,0:T(8,128)(2,1)S(1)}, bf16[4,512,256]{2,1,0:T(8,128)(2,1)S(1)}, u32[]{:S(2)}, u32[]{:S(2)}) collective-permute-start(bf16[4,512,256]{2,1,0:T(8,128)(2,1)S(1)} %shard_map.141), channel_id=1, source_target_pairs={{0,4},{1,5},{2,6},{3,7},{4,0},{5,1},{6,2},{7,3},{8,12},{9,13},{10,... | collective-permute-start | bytes 3145736 | tf_op jit(solution)/shard_map/ppermute | solution.py:41
  49.1 22.4 %collective-permute-start.7 = (f16[4,512,256]{2,1,0:T(8,128)(2,1)S(1)}, f16[4,512,256]{2,1,0:T(8,128)(2,1)S(1)}, u32[]{:S(2)}, u32[]{:S(2)}) collective-permute-start(f16[4,512,256]{2,1,0:T(8,128)(2,1)S(1)} %multiply_convert_fusion.1), channel_id=1, source_target_pairs={{0,3},{1,2},{2,1},{3,0},{4,7},{5,6},{6,5},{7,4},{8,11},{9,10},{10,... | collective-permute-start | bytes 3145736 | tf_op jit(solution)/shard_map/ppermute | solution.py:41
  56.6 17.8 %collective-permute-start.11 = (f16[4,512,256]{2,1,0:T(8,128)(2,1)S(1)}, f16[4,512,256]{2,1,0:T(8,128)(2,1)S(1)}, u32[]{:S(2)}, u32[]{:S(2)}) collective-permute-start(f16[4,512,256]{2,1,0:T(8,128)(2,1)S(1)} %multiply_convert_fusion), channel_id=1, source_target_pairs={{0,12},{1,13},{2,14},{3,15},{4,8},{5,9},{6,10},{7,11},{8,4},{9,5},... | collective-permute-start | bytes 3145736 | tf_op jit(solution)/shard_map/ppermute | solution.py:41
  72.0 9.3 %collective-permute-start.8 = (f16[2,512,256]{2,1,0:T(8,128)(2,1)S(1)}, f16[2,512,256]{2,1,0:T(8,128)(2,1)S(1)}, u32[]{:S(2)}, u32[]{:S(2)}) collective-permute-start(f16[2,512,256]{2,1,0:T(8,128)(2,1)S(1)} %fusion.1), channel_id=1, source_target_pairs={{0,4},{1,5},{2,6},{3,7},{4,0},{5,1},{6,2},{7,3},{8,12},{9,13},{10,... | collective-permute-start | bytes 1572872 | tf_op jit(solution)/shard_map/ppermute | solution.py:41
  74.8 9.3 %collective-permute-start.12 = (f16[2,512,256]{2,1,0:T(8,128)(2,1)S(1)}, f16[2,512,256]{2,1,0:T(8,128)(2,1)S(1)}, u32[]{:S(2)}, u32[]{:S(2)}) collective-permute-start(f16[2,512,256]{2,1,0:T(8,128)(2,1)S(1)} %fusion), channel_id=1, source_target_pairs={{0,1},{1,0},{2,3},{3,2},{4,5},{5,4},{6,7},{7,6},{8,9},{9,8},{10,11... | collective-permute-start | bytes 1572872 | tf_op jit(solution)/shard_map/ppermute | solution.py:41
  81.3 7.7 %collective-permute-start.9 = (f16[512,256]{1,0:T(8,128)(2,1)S(1)}, f16[512,256]{1,0:T(8,128)(2,1)S(1)}, u32[]{:S(2)}, u32[]{:S(2)}) collective-permute-start(f16[512,256]{1,0:T(8,128)(2,1)S(1)} %fusion.14), channel_id=1, source_target_pairs={{0,12},{1,13},{2,14},{3,15},{4,8},{5,9},{6,10},{7,11},{8,4},{9,5},... | collective-permute-start | bytes 786440 | tf_op jit(solution)/shard_map/ppermute | solution.py:41
  84.2 7.7 %collective-permute-start.13 = (f16[512,256]{1,0:T(8,128)(2,1)S(1)}, f16[512,256]{1,0:T(8,128)(2,1)S(1)}, u32[]{:S(2)}, u32[]{:S(2)}) collective-permute-start(f16[512,256]{1,0:T(8,128)(2,1)S(1)} %fusion.15), channel_id=1, source_target_pairs={{0,3},{1,2},{2,1},{3,0},{4,7},{5,6},{6,5},{7,4},{8,11},{9,10},{10,... | collective-permute-start | bytes 786440 | tf_op jit(solution)/shard_map/ppermute | solution.py:41
  92.2 1.6 %collective-permute-start.14 = (f16[4,64,512]{2,1,0:T(8,128)(2,1)S(1)}, f16[4,64,512]{2,1,0:T(8,128)(2,1)S(1)}, u32[]{:S(2)}, u32[]{:S(2)}) collective-permute-start(f16[4,64,512]{2,1,0:T(8,128)(2,1)S(1)} %bitcast.41), channel_id=1, source_target_pairs={{0,16},{1,17},{2,18},{3,19},{4,20},{5,21},{6,22},{7,23},{8,24},{9,... | collective-permute-start | bytes 786440 | tf_op jit(solution)/shard_map/ppermute | solution.py:41
  93.9 5.6 %collective-permute-start.15 = (f16[2,64,512]{2,1,0:T(8,128)(2,1)S(1)}, f16[2,64,512]{2,1,0:T(8,128)(2,1)S(1)}, u32[]{:S(2)}, u32[]{:S(2)}) collective-permute-start(f16[2,64,512]{2,1,0:T(8,128)(2,1)S(1)} %pad_maximum_fusion.2), channel_id=1, source_target_pairs={{0,32},{1,33},{2,34},{3,35},{4,36},{5,37},{6,38},{7,39},{8,40},{9,... | collective-permute-start | bytes 393224 | tf_op jit(solution)/shard_map/ppermute | solution.py:41
  95.7 9.4 %collective-permute-start.16 = (f16[2,64,512]{2,1,0:T(8,128)(2,1)S(1)}, f16[2,64,512]{2,1,0:T(8,128)(2,1)S(1)}, u32[]{:S(2)}, u32[]{:S(2)}) collective-permute-start(f16[2,64,512]{2,1,0:T(8,128)(2,1)S(1)} %pad_maximum_fusion.3), channel_id=1, source_target_pairs={{0,96},{1,97},{2,98},{3,99},{4,100},{5,101},{6,102},{7,103},{8,104... | collective-permute-start | bytes 393224 | tf_op jit(solution)/shard_map/ppermute | solution.py:41
  98.4 6.7 %collective-permute-start.17 = (f16[2,64,512]{2,1,0:T(8,128)(2,1)S(1)}, f16[2,64,512]{2,1,0:T(8,128)(2,1)S(1)}, u32[]{:S(2)}, u32[]{:S(2)}) collective-permute-start(f16[2,64,512]{2,1,0:T(8,128)(2,1)S(1)} %pad_maximum_fusion.4), channel_id=1, source_target_pairs={{0,64},{1,65},{2,66},{3,67},{4,68},{5,69},{6,70},{7,71},{8,72},{9,... | collective-permute-start | bytes 393224 | tf_op jit(solution)/shard_map/ppermute | solution.py:41

commit v7 on v6

--- a/solution.py
+++ b/solution.py
@@ -18,6 +18,7 @@
 F32 = jnp.float32
 DOWN, UP = 0.0625, 16.0
 ALONG_Z = (1, 3, 2)
+HOME_Z = (2, 1, 3)
 
 
 def device(z, c, y, x):
@@ -51,7 +52,7 @@
                 for x in range(NX):
                     row = [(y ^ j) * NX + (x ^ i) for i in first for j in second]
                     row += [(y ^ i) * NX + (x ^ j) for i in first for j in second]
-                    row += [(z ^ i) * NC + k for i in (0,) + ALONG_Z for k in (c, 1 - c)]
+                    row += [(z ^ i) * NC + k for i in (0,) + HOME_Z for k in (c, 1 - c)]
                     row += [(y * NX + x) * (VOCAB // (NY * NX))]
                     out[device(z, c, y, x), : len(row)] = row
     return out
@@ -272,17 +273,21 @@
     ]
     sums = together(*[kept[h][1] + wide(moved[h][1]) for h in range(2)])
     sums = [sums[h] + wide(second_step[h]) for h in range(2)]
-    moved = [exchange(narrow(sums[h][:2]), axes[h][1], 0) for h in range(2)]
+    moved = [
+        [exchange(narrow(sums[h][i]), axes[h][1], 0) for i in (1, 0)] for h in range(2)
+    ]
     second_step = [
-        exchange(narrow(sums[h][3] + wide(moved[h][1])), axes[h][1], 1) for h in range(2)
+        exchange(narrow(sums[h][3] + wide(moved[h][0])), axes[h][1], 1) for h in range(2)
     ]
     logits = jnp.concatenate(
-        [narrow(sums[h][2] + wide(moved[h][0]) + wide(second_step[h])) for h in range(2)], axis=1
+        [narrow(sums[h][2] + wide(moved[h][1]) + wide(second_step[h])) for h in range(2)], axis=1
     ).reshape(NC, NZ, rows, c_width)
 
     other = exchange(logits[1], "core")
-    both = [jnp.stack([logits[0, i], other[i]]) for i in range(NZ)]
-    home = [both[0]] + [exchange(m, *move) for m, move in zip(both[1:], along_z)]
+    home = [jnp.stack([logits[0, 0], other[0]])]
+    for k in HOME_Z:
+        i = 1 + ALONG_Z.index(k)
+        home.append(exchange(jnp.stack([logits[0, i], other[i]]), "z", by=k))
     home = wide(jnp.concatenate(home))
 
     stats = call(stats_kernel, [((NY * NX, 8, 128), F32)], source, home, in_hbm(token_ids))

time: 120 us -> 117 us (0.975)
  waiting for transfers between devices: 45.4 us -> 40 us
  starting transfers between devices: 27.9 us -> 30 us
    ppermute x18 -> x20, waiting for transfers between devices: 39.1 us -> 33.7 us  [exchange(): return lax.ppermute(value, AXES, pairs)]
    ppermute x18 -> x20, starting transfers between devices: 20.8 us -> 22.9 us  [exchange(): return lax.ppermute(value, AXES, pairs)]
  transfers between devices with their start and end apart: 19 -> 21, of which waited for: 12 -> 13; matrix products, arithmetic and copies ran while one was open for 3% -> 3% of each run, Pallas kernels for 16% -> 16%
where the time goes in v7:
time: 117 us; the launch traced here: 116 us
  waiting for transfers between devices  40 us (34%)
  starting transfers between devices  30 us (26%)
  Pallas kernels  26.5 us (23%)
  blocking collectives  11.5 us (10%)
  local copies, waits for them, and re-layouts  3.74 us (3%)
  other arithmetic  3.09 us (3%)
  between operations  1.67 us (1%)
    ppermute x20, waiting for transfers between devices, exchange(): return lax.ppermute(value, AXES, pairs)  33.7 us
    ppermute x20, starting transfers between devices, exchange(): return lax.ppermute(value, AXES, pairs)  22.9 us
    pallas_call x8, Pallas kernels, project(): pl.pallas_call(functools.partial(matmul_kernel, first, half), in_specs=[s...  15 us
    all_to_all x1, blocking collectives, shards(): stats = lax.all_to_all(stats, 'tensor', 0, 0, tiled=True)  11.5 us
    all_to_all x1, starting transfers between devices, shards(): sums = lax.all_to_all(sums, 'tensor', 0, 0, tiled=True)  7.12 us
    all_to_all x1, waiting for transfers between devices, shards(): sums = lax.all_to_all(sums, 'tensor', 0, 0, tiled=True)  6.3 us
    pallas_call x5, Pallas kernels, call(): pl.pallas_call(kernel, in_specs=[spec(v) for v in args], out_specs=[pl.Bl...  5.93 us
    pallas_call x4, Pallas kernels, relay(): pl.pallas_call(relay_kernel, grid=(count // step,), in_specs=[pl.BlockSpe...  5.57 us
  transfers between devices with their start and end apart: 21, of which 13 were waited for; matrix products, arithmetic and copies ran while one was open for 3% of the time, Pallas kernels for 16%

profile of v7, /device:TPU:0, one launch (start us, length us, event | category | flops | bytes accessed | tf_op | source)
XLA Modules:
  0.0 116.4 jit_solution(11978943427078894444)
XLA Ops:
  0.6 1.7 %shard_map.131 = f32[16,8,128]{2,1,0:T(8,128)} custom-call(bf16[64,512]{1,0:T(8,128)(2,1)} %refs_0_.3, bf16[64,256]{1,0:T(8,128)(2,1)} %refs_1_.3, bf16[64,256]{1,0:T(8,128)(2,1)} %refs_2_.3), custom_call_target="tpu_custom_call" | custom-call | tf_op jit(solution)/shard_map/pallas_call | solution.py:203
  2.3 7.1 %all-to-all-start = ((f32[16,8,128]{2,1,0:T(8,128)}), f32[16,8,128]{2,1,0:T(8,128)S(1)}, u32[]{:S(2)}, u32[]{:S(2)}) async-start(f32[16,8,128]{2,1,0:T(8,128)} %shard_map.131), calls=%async_computation | async-start | bytes 131072 | tf_op jit(solution)/shard_map/all_to_all | solution.py:248
  9.4 0.7 constant_dynamic-slice_fusion
  10.8 6.3 %all-to-all-done.refs_6_ = f32[16,8,128]{2,1,0:T(8,128)S(1)} async-done(((f32[16,8,128]{2,1,0:T(8,128)}), f32[16,8,128]{2,1,0:T(8,128)S(1)}, u32[]{:S(2)}, u32[]{:S(2)}) %all-to-all-start) | async-done | bytes 65568 | tf_op jit(solution)/shard_map/all_to_all | solution.py:248
  17.1 1.2 %shard_map.132 = bf16[64,1024]{1,0:T(8,128)(2,1)S(1)} custom-call(bf16[64,512]{1,0:T(8,128)(2,1)} %refs_0_.3, bf16[64,256]{1,0:T(8,128)(2,1)} %refs_1_.3, bf16[64,256]{1,0:T(8,128)(2,1)} %refs_2_.3, bf16[512]{0:T(512)(128)(2,1)} %refs_3_.1, bf16[256]{0:T(256)(128)(2,1)} %refs_4_.1, bf16[256]{0:T(256)(128)(2,1)} %refs_5_.1, ...), custom_call_target="tpu_custom_call" | custom-call | tf_op jit(solution)/shard_map/pallas_call | solution.py:203
  18.3 4.0 %collective-permute-start.2 = (bf16[64,1024]{1,0:T(8,128)(2,1)S(1)}, bf16[64,1024]{1,0:T(8,128)(2,1)S(1)}, u32[]{:S(2)}, u32[]{:S(2)}) collective-permute-start(bf16[64,1024]{1,0:T(8,128)(2,1)S(1)} %shard_map.132), channel_id=1, source_target_pairs={{0,64},{1,65},{2,66},{3,67},{4,68},{5,69},{6,70},{7,71},{8,72},{9,... | collective-permute-start | bytes 393224 | tf_op jit(solution)/shard_map/ppermute | solution.py:42
  22.3 0.7 collective-permute-start.1
  23.0 0.3 collective-permute-start
  23.3 2.2 %copy-done = bf16[256,16,512]{2,1,0:T(8,128)(2,1)S(1)} copy-done((bf16[256,16,512]{2,1,0:T(8,128)(2,1)S(1)}, bf16[256,16,512]{2,1,0:T(8,128)(2,1)}, u32[]{:S(2)}) %copy-start) | copy-done | bytes 4194328
  25.5 1.4 %shard_map.133.we = bf16[16,256,512]{2,1,0:T(8,128)(2,1)S(1)} custom-call(bf16[256,16,512]{2,1,0:T(8,128)(2,1)S(1)} %copy-done), custom_call_target="tpu_custom_call" | custom-call | flops 10000000000 | bytes 16777216 | tf_op jit(solution)/shard_map/pallas_call | solution.py:67
  26.9 1.4 %shard_map.134.wb0 = bf16[16,256,512]{2,1,0:T(8,128)(2,1)S(1)} custom-call(bf16[512,16,512]{2,1,0:T(8,128)(2,1)S(1)} %bitcast.62), custom_call_target="tpu_custom_call" | custom-call | flops 10000000000 | bytes 16777216 | tf_op jit(solution)/shard_map/pallas_call | solution.py:67
  28.3 1.4 %shard_map.135.wb1 = bf16[16,256,512]{2,1,0:T(8,128)(2,1)S(1)} custom-call(bf16[512,16,512]{2,1,0:T(8,128)(2,1)S(1)} %bitcast.62), custom_call_target="tpu_custom_call" | custom-call | flops 10000000000 | bytes 16777216 | tf_op jit(solution)/shard_map/pallas_call | solution.py:67
  29.9 0.6 copy-done.1
  30.5 1.4 %shard_map.136.wa = bf16[16,256,512]{2,1,0:T(8,128)(2,1)S(1)} custom-call(bf16[256,16,512]{2,1,0:T(8,128)(2,1)S(1)} %copy-done.1), custom_call_target="tpu_custom_call" | custom-call | flops 10000000000 | bytes 16777216 | tf_op jit(solution)/shard_map/pallas_call | solution.py:67
  32.0 1.9 %shard_map.138 = bf16[4,512,256]{2,1,0:T(8,128)(2,1)S(1)} custom-call(s32[32]{0:T(128)S(1)} %slice_bitcast_fusion.8.table, f32[1]{0:T(128)S(6)} %copy.18.alpha, bf16[512,1024]{1,0:T(8,128)(2,1)S(1)} %shard_map.137.acts, bf16[16,256,512]{2,1,0:T(8,128)(2,1)S(1)} %shard_map.134.wb0, bf16[16,256,512]{2,1,0:T(8,128)(2,1)S(1)} %shard_map.135.wb1, ...), custom_call_target="tpu_custom_call" | custom-call | flops 1 | bytes 1 | tf_op jit(solution)/shard_map/pallas_call | solution.py:98
  33.9 0.6 collective-permute-start.6
  34.5 1.9 %shard_map.139 = bf16[4,512,256]{2,1,0:T(8,128)(2,1)S(1)} custom-call(s32[32]{0:T(128)S(1)} %slice_bitcast_fusion.8.table, f32[1]{0:T(128)S(6)} %copy.18.alpha, bf16[512,1024]{1,0:T(8,128)(2,1)S(1)} %shard_map.137.acts, bf16[16,256,512]{2,1,0:T(8,128)(2,1)S(1)} %shard_map.134.wb0, bf16[16,256,512]{2,1,0:T(8,128)(2,1)S(1)} %shard_map.135.wb1, ...), custom_call_target="tpu_custom_call" | custom-call | flops 1 | bytes 1 | tf_op jit(solution)/shard_map/pallas_call | solution.py:98
  36.4 0.6 collective-permute-start.11
  37.0 1.9 %shard_map.140 = bf16[4,512,256]{2,1,0:T(8,128)(2,1)S(1)} custom-call(s32[32]{0:T(128)S(1)} %slice_bitcast_fusion.8.table, f32[1]{0:T(128)S(6)} %copy.18.alpha, bf16[512,1024]{1,0:T(8,128)(2,1)S(1)} %shard_map.137.acts, bf16[16,256,512]{2,1,0:T(8,128)(2,1)S(1)} %shard_map.134.wb0, bf16[16,256,512]{2,1,0:T(8,128)(2,1)S(1)} %shard_map.135.wb1, ...), custom_call_target="tpu_custom_call" | custom-call | flops 1 | bytes 1 | tf_op jit(solution)/shard_map/pallas_call | solution.py:98
  38.9 1.5 %collective-permute-start.4 = (bf16[4,512,256]{2,1,0:T(8,128)(2,1)S(1)}, bf16[4,512,256]{2,1,0:T(8,128)(2,1)S(1)}, u32[]{:S(2)}, u32[]{:S(2)}) collective-permute-start(bf16[4,512,256]{2,1,0:T(8,128)(2,1)S(1)} %shard_map.140), channel_id=1, source_target_pairs={{0,1},{1,0},{2,3},{3,2},{4,5},{5,4},{6,7},{7,6},{8,9},{9,8},{10,11... | collective-permute-start | bytes 3145736 | tf_op jit(solution)/shard_map/ppermute | solution.py:42
  40.4 1.9 %shard_map.141 = bf16[4,512,256]{2,1,0:T(8,128)(2,1)S(1)} custom-call(s32[32]{0:T(128)S(1)} %slice_bitcast_fusion.8.table, f32[1]{0:T(128)S(6)} %copy.18.alpha, bf16[512,1024]{1,0:T(8,128)(2,1)S(1)} %shard_map.137.acts, bf16[16,256,512]{2,1,0:T(8,128)(2,1)S(1)} %shard_map.134.wb0, bf16[16,256,512]{2,1,0:T(8,128)(2,1)S(1)} %shard_map.135.wb1, ...), custom_call_target="tpu_custom_call" | custom-call | flops 1 | bytes 1 | tf_op jit(solution)/shard_map/pallas_call | solution.py:98
  42.3 1.6 %collective-permute-start.5 = (bf16[4,512,256]{2,1,0:T(8,128)(2,1)S(1)}, bf16[4,512,256]{2,1,0:T(8,128)(2,1)S(1)}, u32[]{:S(2)}, u32[]{:S(2)}) collective-permute-start(bf16[4,512,256]{2,1,0:T(8,128)(2,1)S(1)} %shard_map.141), channel_id=1, source_target_pairs={{0,4},{1,5},{2,6},{3,7},{4,0},{5,1},{6,2},{7,3},{8,12},{9,13},{10,... | collective-permute-start | bytes 3145736 | tf_op jit(solution)/shard_map/ppermute | solution.py:42
  43.9 1.9 %shard_map.142 = f32[4,512,256]{2,1,0:T(8,128)S(1)} custom-call(s32[32]{0:T(128)S(1)} %slice_bitcast_fusion.8.table, f32[1]{0:T(128)S(6)} %copy.18.alpha, bf16[512,1024]{1,0:T(8,128)(2,1)S(1)} %shard_map.137.acts, bf16[16,256,512]{2,1,0:T(8,128)(2,1)S(1)} %shard_map.134.wb0, bf16[16,256,512]{2,1,0:T(8,128)(2,1)S(1)} %shard_map.135.wb1, ...), custom_call_target="tpu_custom_call" | custom-call | flops 1 | bytes 1 | tf_op jit(solution)/shard_map/pallas_call | solution.py:98
  45.8 3.0 %collective-permute-done.6 = bf16[4,512,256]{2,1,0:T(8,128)(2,1)S(1)} collective-permute-done((bf16[4,512,256]{2,1,0:T(8,128)(2,1)S(1)}, bf16[4,512,256]{2,1,0:T(8,128)(2,1)S(1)}, u32[]{:S(2)}, u32[]{:S(2)}) %collective-permute-start.6) | collective-permute-done | bytes 1048608 | tf_op jit(solution)/shard_map/ppermute | solution.py:42
  48.8 0.4 multiply_convert_fusion.1
  49.1 1.4 %collective-permute-start.7 = (f16[4,512,256]{2,1,0:T(8,128)(2,1)S(1)}, f16[4,512,256]{2,1,0:T(8,128)(2,1)S(1)}, u32[]{:S(2)}, u32[]{:S(2)}) collective-permute-start(f16[4,512,256]{2,1,0:T(8,128)(2,1)S(1)} %multiply_convert_fusion.1), channel_id=1, source_target_pairs={{0,3},{1,2},{2,1},{3,0},{4,7},{5,6},{6,5},{7,4},{8,11},{9,10},{10,... | collective-permute-start | bytes 3145736 | tf_op jit(solution)/shard_map/ppermute | solution.py:42
  50.6 1.9 %shard_map.143 = f32[4,512,256]{2,1,0:T(8,128)S(1)} custom-call(s32[32]{0:T(128)S(1)} %slice_bitcast_fusion.8.table, f32[1]{0:T(128)S(6)} %copy.18.alpha, bf16[512,1024]{1,0:T(8,128)(2,1)S(1)} %shard_map.137.acts, bf16[16,256,512]{2,1,0:T(8,128)(2,1)S(1)} %shard_map.134.wb0, bf16[16,256,512]{2,1,0:T(8,128)(2,1)S(1)} %shard_map.135.wb1, ...), custom_call_target="tpu_custom_call" | custom-call | flops 1 | bytes 1 | tf_op jit(solution)/shard_map/pallas_call | solution.py:98
  52.4 1.9 %shard_map.144 = f32[4,512,256]{2,1,0:T(8,128)S(1)} custom-call(s32[32]{0:T(128)S(1)} %slice_bitcast_fusion.8.table, f32[1]{0:T(128)S(6)} %copy.18.alpha, bf16[512,1024]{1,0:T(8,128)(2,1)S(1)} %shard_map.137.acts, bf16[16,256,512]{2,1,0:T(8,128)(2,1)S(1)} %shard_map.134.wb0, bf16[16,256,512]{2,1,0:T(8,128)(2,1)S(1)} %shard_map.135.wb1, ...), custom_call_target="tpu_custom_call" | custom-call | flops 1 | bytes 1 | tf_op jit(solution)/shard_map/pallas_call | solution.py:98
  54.3 1.9 %shard_map.145 = f32[4,512,256]{2,1,0:T(8,128)S(1)} custom-call(s32[32]{0:T(128)S(1)} %slice_bitcast_fusion.8.table, f32[1]{0:T(128)S(6)} %copy.18.alpha, bf16[512,1024]{1,0:T(8,128)(2,1)S(1)} %shard_map.137.acts, bf16[16,256,512]{2,1,0:T(8,128)(2,1)S(1)} %shard_map.134.wb0, bf16[16,256,512]{2,1,0:T(8,128)(2,1)S(1)} %shard_map.135.wb1, ...), custom_call_target="tpu_custom_call" | custom-call | flops 1 | bytes 1 | tf_op jit(solution)/shard_map/pallas_call | solution.py:98
  56.2 0.4 multiply_convert_fusion
  56.6 1.2 %collective-permute-start.12 = (f16[4,512,256]{2,1,0:T(8,128)(2,1)S(1)}, f16[4,512,256]{2,1,0:T(8,128)(2,1)S(1)}, u32[]{:S(2)}, u32[]{:S(2)}) collective-permute-start(f16[4,512,256]{2,1,0:T(8,128)(2,1)S(1)} %multiply_convert_fusion), channel_id=1, source_target_pairs={{0,12},{1,13},{2,14},{3,15},{4,8},{5,9},{6,10},{7,11},{8,4},{9,5},... | collective-permute-start | bytes 3145736 | tf_op jit(solution)/shard_map/ppermute | solution.py:42
  57.8 10.0 %collective-permute-done.4 = bf16[4,512,256]{2,1,0:T(8,128)(2,1)S(1)} collective-permute-done((bf16[4,512,256]{2,1,0:T(8,128)(2,1)S(1)}, bf16[4,512,256]{2,1,0:T(8,128)(2,1)S(1)}, u32[]{:S(2)}, u32[]{:S(2)}) %collective-permute-start.4) | collective-permute-done | bytes 1048608 | tf_op jit(solution)/shard_map/ppermute | solution.py:42
  67.9 0.2 convert_add_fusion.1
  68.1 0.2 convert_add_fusion
  68.3 3.2 %collective-permute-done.7 = f16[4,512,256]{2,1,0:T(8,128)(2,1)S(1)} collective-permute-done((f16[4,512,256]{2,1,0:T(8,128)(2,1)S(1)}, f16[4,512,256]{2,1,0:T(8,128)(2,1)S(1)}, u32[]{:S(2)}, u32[]{:S(2)}) %collective-permute-start.7) | collective-permute-done | bytes 1048608 | tf_op jit(solution)/shard_map/ppermute | solution.py:42
  71.5 0.3 multiply_add_fusion.1
  71.8 0.1 fusion.18
  71.9 0.6 collective-permute-start.9
  72.6 1.8 %collective-permute-done.12 = f16[4,512,256]{2,1,0:T(8,128)(2,1)S(1)} collective-permute-done((f16[4,512,256]{2,1,0:T(8,128)(2,1)S(1)}, f16[4,512,256]{2,1,0:T(8,128)(2,1)S(1)}, u32[]{:S(2)}, u32[]{:S(2)}) %collective-permute-start.12) | collective-permute-done | bytes 1048608 | tf_op jit(solution)/shard_map/ppermute | solution.py:42
  74.4 0.3 multiply_add_fusion
  74.7 0.1 fusion.20
  74.8 0.2 collective-permute-start.14
  75.0 1.9 %collective-permute-start.13 = (f16[512,256]{1,0:T(8,128)(2,1)S(1)}, f16[512,256]{1,0:T(8,128)(2,1)S(1)}, u32[]{:S(2)}, u32[]{:S(2)}) collective-permute-start(f16[512,256]{1,0:T(8,128)(2,1)S(1)} %get-tuple-element.70), channel_id=1, source_target_pairs={{0,1},{1,0},{2,3},{3,2},{4,5},{5,4},{6,7},{7,6},{8,9},{9,8},{10,11... | collective-permute-start | bytes 786440 | tf_op jit(solution)/shard_map/ppermute | solution.py:42
  76.9 1.5 %collective-permute-done.9 = f16[512,256]{1,0:T(8,128)(2,1)S(1)} collective-permute-done((f16[512,256]{1,0:T(8,128)(2,1)S(1)}, f16[512,256]{1,0:T(8,128)(2,1)S(1)}, u32[]{:S(2)}, u32[]{:S(2)}) %collective-permute-start.9) | collective-permute-done | bytes 262176 | tf_op jit(solution)/shard_map/ppermute | solution.py:42
  78.4 0.1 fusion.12
  78.5 1.2 %collective-permute-start.10 = (f16[512,256]{1,0:T(8,128)(2,1)S(1)}, f16[512,256]{1,0:T(8,128)(2,1)S(1)}, u32[]{:S(2)}, u32[]{:S(2)}) collective-permute-start(f16[512,256]{1,0:T(8,128)(2,1)S(1)} %fusion.12), channel_id=1, source_target_pairs={{0,12},{1,13},{2,14},{3,15},{4,8},{5,9},{6,10},{7,11},{8,4},{9,5},... | collective-permute-start | bytes 786440 | tf_op jit(solution)/shard_map/ppermute | solution.py:42
  79.7 1.5 %collective-permute-done.14 = f16[512,256]{1,0:T(8,128)(2,1)S(1)} collective-permute-done((f16[512,256]{1,0:T(8,128)(2,1)S(1)}, f16[512,256]{1,0:T(8,128)(2,1)S(1)}, u32[]{:S(2)}, u32[]{:S(2)}) %collective-permute-start.14) | collective-permute-done | bytes 262176 | tf_op jit(solution)/shard_map/ppermute | solution.py:42
  81.2 0.1 fusion.3
  81.4 2.1 %collective-permute-start.15 = (f16[512,256]{1,0:T(8,128)(2,1)S(1)}, f16[512,256]{1,0:T(8,128)(2,1)S(1)}, u32[]{:S(2)}, u32[]{:S(2)}) collective-permute-start(f16[512,256]{1,0:T(8,128)(2,1)S(1)} %fusion.3), channel_id=1, source_target_pairs={{0,3},{1,2},{2,1},{3,0},{4,7},{5,6},{6,5},{7,4},{8,11},{9,10},{10,... | collective-permute-start | bytes 786440 | tf_op jit(solution)/shard_map/ppermute | solution.py:42
  83.6 2.6 %collective-permute-done.10 = f16[512,256]{1,0:T(8,128)(2,1)S(1)} collective-permute-done((f16[512,256]{1,0:T(8,128)(2,1)S(1)}, f16[512,256]{1,0:T(8,128)(2,1)S(1)}, u32[]{:S(2)}, u32[]{:S(2)}) %collective-permute-start.10) | collective-permute-done | bytes 262176 | tf_op jit(solution)/shard_map/ppermute | solution.py:42
  86.2 0.2 fusion.17
  86.3 2.7 %collective-permute-done.15 = f16[512,256]{1,0:T(8,128)(2,1)S(1)} collective-permute-done((f16[512,256]{1,0:T(8,128)(2,1)S(1)}, f16[512,256]{1,0:T(8,128)(2,1)S(1)}, u32[]{:S(2)}, u32[]{:S(2)}) %collective-permute-start.15) | collective-permute-done | bytes 262176 | tf_op jit(solution)/shard_map/ppermute | solution.py:42
  89.0 0.2 fusion.8
  89.3 0.1 pad_maximum_fusion
  89.6 1.5 %collective-permute-done.16 = f16[4,64,512]{2,1,0:T(8,128)(2,1)S(1)} collective-permute-done((f16[4,64,512]{2,1,0:T(8,128)(2,1)S(1)}, f16[4,64,512]{2,1,0:T(8,128)(2,1)S(1)}, u32[]{:S(2)}, u32[]{:S(2)}) %collective-permute-start.16) | collective-permute-done | bytes 262176 | tf_op jit(solution)/shard_map/ppermute | solution.py:42
  91.1 3.8 %collective-permute-start.17 = (f16[2,64,512]{2,1,0:T(8,128)(2,1)S(1)}, f16[2,64,512]{2,1,0:T(8,128)(2,1)S(1)}, u32[]{:S(2)}, u32[]{:S(2)}) collective-permute-start(f16[2,64,512]{2,1,0:T(8,128)(2,1)S(1)} %pad_maximum_fusion.2), channel_id=1, source_target_pairs={{0,64},{1,65},{2,66},{3,67},{4,68},{5,69},{6,70},{7,71},{8,72},{9,... | collective-permute-start | bytes 393224 | tf_op jit(solution)/shard_map/ppermute | solution.py:42
  95.0 0.8 collective-permute-start.19
  95.8 3.3 %collective-permute-done.17 = f16[2,64,512]{2,1,0:T(8,128)(2,1)S(1)} collective-permute-done((f16[2,64,512]{2,1,0:T(8,128)(2,1)S(1)}, f16[2,64,512]{2,1,0:T(8,128)(2,1)S(1)}, u32[]{:S(2)}, u32[]{:S(2)}) %collective-permute-start.17) | collective-permute-done | bytes 131104 | tf_op jit(solution)/shard_map/ppermute | solution.py:42
  99.2 1.8 %collective-permute-done.18 = f16[2,64,512]{2,1,0:T(8,128)(2,1)S(1)} collective-permute-done((f16[2,64,512]{2,1,0:T(8,128)(2,1)S(1)}, f16[2,64,512]{2,1,0:T(8,128)(2,1)S(1)}, u32[]{:S(2)}, u32[]{:S(2)}) %collective-permute-start.18) | collective-permute-done | bytes 131104 | tf_op jit(solution)/shard_map/ppermute | solution.py:42
  101.0 0.8 collective-permute-done.19
  101.8 0.1 convert_multiply_fusion.home
  102.0 1.2 %shard_map.146 = f32[16,8,128]{2,1,0:T(8,128)S(1)} custom-call(s32[9]{0:T(128)S(1)} %slice_bitcast_fusion.9.source, f32[8,64,512]{2,1,0:T(8,128)S(1)} %convert_multiply_fusion.home, s32[64]{0:T(128)} %ids.1), custom_call_target="tpu_custom_call" | custom-call | tf_op jit(solution)/shard_map/pallas_call | solution.py:203
  103.1 11.5 %all_to_all.10.stats = f32[16,8,128]{2,1,0:T(8,128)S(1)} all-to-all(f32[16,8,128]{2,1,0:T(8,128)S(1)} %shard_map.146), channel_id=1, replica_groups=mesh['rows'=8,'tensor'=16] {'tensor'}, dimensions={0} | all-to-all | bytes 131072 | tf_op jit(solution)/shard_map/all_to_all | solution.py:294
  114.6 1.8 %shard_map.147 = (f32[64,4096]{1,0:T(8,128)}, f32[1,64]{1,0:T(1,128)}) custom-call(s32[9]{0:T(128)S(1)} %slice_bitcast_fusion.9.source, f32[8,64,512]{2,1,0:T(8,128)S(1)} %convert_multiply_fusion.home, f32[16,8,128]{2,1,0:T(8,128)S(1)} %all_to_all.10.stats), custom_call_target="tpu_custom_call" | custom-call | tf_op jit(solution)/shard_map/pallas_call | solution.py:203
  (33 shorter events, 0.8 us)
Async XLA Ops:
  2.3 14.8 %all-to-all-start = ((f32[16,8,128]{2,1,0:T(8,128)}), f32[16,8,128]{2,1,0:T(8,128)S(1)}, u32[]{:S(2)}, u32[]{:S(2)}) async-start(f32[16,8,128]{2,1,0:T(8,128)} %shard_map.131), calls=%async_computation | async-start | bytes 131072 | tf_op jit(solution)/shard_map/all_to_all | solution.py:248
  17.1 9.8 %slice-start = ((s8[8388608]{0:T(1024)(128)(4,1)}), s8[4194304]{0:T(1024)(128)(4,1)S(1)}, s32[]{:S(2)}) async-start(s8[8388608]{0:T(1024)(128)(4,1)} %bitcast.61), calls=%async_computation.2 | async-start | bytes 8388608
  18.3 8.6 %slice-start.1 = ((s8[8388608]{0:T(1024)(128)(4,1)}), s8[4194304]{0:T(1024)(128)(4,1)S(1)}, s32[]{:S(2)}) async-start(s8[8388608]{0:T(1024)(128)(4,1)} %bitcast.61), calls=%async_computation.3 | async-start | bytes 8388608
  18.3 11.4 %collective-permute-start.2 = (bf16[64,1024]{1,0:T(8,128)(2,1)S(1)}, bf16[64,1024]{1,0:T(8,128)(2,1)S(1)}, u32[]{:S(2)}, u32[]{:S(2)}) collective-permute-start(bf16[64,1024]{1,0:T(8,128)(2,1)S(1)} %shard_map.132), channel_id=1, source_target_pairs={{0,64},{1,65},{2,66},{3,67},{4,68},{5,69},{6,70},{7,71},{8,72},{9,... | collective-permute-start | bytes 393224 | tf_op jit(solution)/shard_map/ppermute | solution.py:42
  22.3 7.5 %collective-permute-start.1 = (bf16[64,1024]{1,0:T(8,128)(2,1)S(1)}, bf16[64,1024]{1,0:T(8,128)(2,1)S(1)}, u32[]{:S(2)}, u32[]{:S(2)}) collective-permute-start(bf16[64,1024]{1,0:T(8,128)(2,1)S(1)} %shard_map.132), channel_id=1, source_target_pairs={{0,96},{1,97},{2,98},{3,99},{4,100},{5,101},{6,102},{7,103},{8,104... | collective-permute-start | bytes 393224 | tf_op jit(solution)/shard_map/ppermute | solution.py:42
  23.0 6.8 %collective-permute-start = (bf16[64,1024]{1,0:T(8,128)(2,1)S(1)}, bf16[64,1024]{1,0:T(8,128)(2,1)S(1)}, u32[]{:S(2)}, u32[]{:S(2)}) collective-permute-start(bf16[64,1024]{1,0:T(8,128)(2,1)S(1)} %shard_map.132), channel_id=1, source_target_pairs={{0,32},{1,33},{2,34},{3,35},{4,36},{5,37},{6,38},{7,39},{8,40},{9,... | collective-permute-start | bytes 393224 | tf_op jit(solution)/shard_map/ppermute | solution.py:42
  23.3 2.2 %copy-start = (bf16[256,16,512]{2,1,0:T(8,128)(2,1)S(1)}, bf16[256,16,512]{2,1,0:T(8,128)(2,1)}, u32[]{:S(2)}) copy-start(bf16[256,16,512]{2,1,0:T(8,128)(2,1)} %head) | copy-start | bytes 12582916
  28.3 2.2 %copy-start.1 = (bf16[256,16,512]{2,1,0:T(8,128)(2,1)S(1)}, bf16[256,16,512]{2,1,0:T(8,128)(2,1)}, u32[]{:S(2)}) copy-start(bf16[256,16,512]{2,1,0:T(8,128)(2,1)} %head.3) | copy-start | bytes 12582916
  29.8 2.1 %collective-permute-start.3 = (bf16[256,1024]{1,0:T(8,128)(2,1)S(1)}, bf16[256,1024]{1,0:T(8,128)(2,1)S(1)}, u32[]{:S(2)}, u32[]{:S(2)}) collective-permute-start(bf16[256,1024]{1,0:T(8,128)(2,1)S(1)} %pad_maximum_fusion.1.refs_0_), channel_id=1, source_target_pairs={{0,16},{1,17},{2,18},{3,19},{4,20},{5,21},{6,22},{7,23},{8,24},{9,... | collective-permute-start | bytes 1572872 | tf_op jit(solution)/shard_map/ppermute | solution.py:42
  33.9 14.9 %collective-permute-start.6 = (bf16[4,512,256]{2,1,0:T(8,128)(2,1)S(1)}, bf16[4,512,256]{2,1,0:T(8,128)(2,1)S(1)}, u32[]{:S(2)}, u32[]{:S(2)}) collective-permute-start(bf16[4,512,256]{2,1,0:T(8,128)(2,1)S(1)} %shard_map.138), channel_id=1, source_target_pairs={{0,1},{1,0},{2,3},{3,2},{4,5},{5,4},{6,7},{7,6},{8,9},{9,8},{10,11... | collective-permute-start | bytes 3145736 | tf_op jit(solution)/shard_map/ppermute | solution.py:42
  36.4 19.8 %collective-permute-start.11 = (bf16[4,512,256]{2,1,0:T(8,128)(2,1)S(1)}, bf16[4,512,256]{2,1,0:T(8,128)(2,1)S(1)}, u32[]{:S(2)}, u32[]{:S(2)}) collective-permute-start(bf16[4,512,256]{2,1,0:T(8,128)(2,1)S(1)} %shard_map.139), channel_id=1, source_target_pairs={{0,4},{1,5},{2,6},{3,7},{4,0},{5,1},{6,2},{7,3},{8,12},{9,13},{10,... | collective-permute-start | bytes 3145736 | tf_op jit(solution)/shard_map/ppermute | solution.py:42
  38.9 29.0 %collective-permute-start.4 = (bf16[4,512,256]{2,1,0:T(8,128)(2,1)S(1)}, bf16[4,512,256]{2,1,0:T(8,128)(2,1)S(1)}, u32[]{:S(2)}, u32[]{:S(2)}) collective-permute-start(bf16[4,512,256]{2,1,0:T(8,128)(2,1)S(1)} %shard_map.140), channel_id=1, source_target_pairs={{0,1},{1,0},{2,3},{3,2},{4,5},{5,4},{6,7},{7,6},{8,9},{9,8},{10,11... | collective-permute-start | bytes 3145736 | tf_op jit(solution)/shard_map/ppermute | solution.py:42
  42.3 25.8 %collective-permute-start.5 = (bf16[4,512,256]{2,1,0:T(8,128)(2,1)S(1)}, bf16[4,512,256]{2,1,0:T(8,128)(2,1)S(1)}, u32[]{:S(2)}, u32[]{:S(2)}) collective-permute-start(bf16[4,512,256]{2,1,0:T(8,128)(2,1)S(1)} %shard_map.141), channel_id=1, source_target_pairs={{0,4},{1,5},{2,6},{3,7},{4,0},{5,1},{6,2},{7,3},{8,12},{9,13},{10,... | collective-permute-start | bytes 3145736 | tf_op jit(solution)/shard_map/ppermute | solution.py:42
  49.1 22.4 %collective-permute-start.7 = (f16[4,512,256]{2,1,0:T(8,128)(2,1)S(1)}, f16[4,512,256]{2,1,0:T(8,128)(2,1)S(1)}, u32[]{:S(2)}, u32[]{:S(2)}) collective-permute-start(f16[4,512,256]{2,1,0:T(8,128)(2,1)S(1)} %multiply_convert_fusion.1), channel_id=1, source_target_pairs={{0,3},{1,2},{2,1},{3,0},{4,7},{5,6},{6,5},{7,4},{8,11},{9,10},{10,... | collective-permute-start | bytes 3145736 | tf_op jit(solution)/shard_map/ppermute | solution.py:42
  56.6 17.8 %collective-permute-start.12 = (f16[4,512,256]{2,1,0:T(8,128)(2,1)S(1)}, f16[4,512,256]{2,1,0:T(8,128)(2,1)S(1)}, u32[]{:S(2)}, u32[]{:S(2)}) collective-permute-start(f16[4,512,256]{2,1,0:T(8,128)(2,1)S(1)} %multiply_convert_fusion), channel_id=1, source_target_pairs={{0,12},{1,13},{2,14},{3,15},{4,8},{5,9},{6,10},{7,11},{8,4},{9,5},... | collective-permute-start | bytes 3145736 | tf_op jit(solution)/shard_map/ppermute | solution.py:42
  71.9 6.5 %collective-permute-start.9 = (f16[512,256]{1,0:T(8,128)(2,1)S(1)}, f16[512,256]{1,0:T(8,128)(2,1)S(1)}, u32[]{:S(2)}, u32[]{:S(2)}) collective-permute-start(f16[512,256]{1,0:T(8,128)(2,1)S(1)} %get-tuple-element.69), channel_id=1, source_target_pairs={{0,4},{1,5},{2,6},{3,7},{4,0},{5,1},{6,2},{7,3},{8,12},{9,13},{10,... | collective-permute-start | bytes 786440 | tf_op jit(solution)/shard_map/ppermute | solution.py:42
  74.8 6.5 %collective-permute-start.14 = (f16[512,256]{1,0:T(8,128)(2,1)S(1)}, f16[512,256]{1,0:T(8,128)(2,1)S(1)}, u32[]{:S(2)}, u32[]{:S(2)}) collective-permute-start(f16[512,256]{1,0:T(8,128)(2,1)S(1)} %get-tuple-element.71), channel_id=1, source_target_pairs={{0,1},{1,0},{2,3},{3,2},{4,5},{5,4},{6,7},{7,6},{8,9},{9,8},{10,11... | collective-permute-start | bytes 786440 | tf_op jit(solution)/shard_map/ppermute | solution.py:42
  75.0 8.6 %collective-permute-start.8 = (f16[512,256]{1,0:T(8,128)(2,1)S(1)}, f16[512,256]{1,0:T(8,128)(2,1)S(1)}, u32[]{:S(2)}, u32[]{:S(2)}) collective-permute-start(f16[512,256]{1,0:T(8,128)(2,1)S(1)} %get-tuple-element.68), channel_id=1, source_target_pairs={{0,4},{1,5},{2,6},{3,7},{4,0},{5,1},{6,2},{7,3},{8,12},{9,13},{10,... | collective-permute-start | bytes 786440 | tf_op jit(solution)/shard_map/ppermute | solution.py:42
  75.0 11.4 %collective-permute-start.13 = (f16[512,256]{1,0:T(8,128)(2,1)S(1)}, f16[512,256]{1,0:T(8,128)(2,1)S(1)}, u32[]{:S(2)}, u32[]{:S(2)}) collective-permute-start(f16[512,256]{1,0:T(8,128)(2,1)S(1)} %get-tuple-element.70), channel_id=1, source_target_pairs={{0,1},{1,0},{2,3},{3,2},{4,5},{5,4},{6,7},{7,6},{8,9},{9,8},{10,11... | collective-permute-start | bytes 786440 | tf_op jit(solution)/shard_map/ppermute | solution.py:42
  78.5 7.7 %collective-permute-start.10 = (f16[512,256]{1,0:T(8,128)(2,1)S(1)}, f16[512,256]{1,0:T(8,128)(2,1)S(1)}, u32[]{:S(2)}, u32[]{:S(2)}) collective-permute-start(f16[512,256]{1,0:T(8,128)(2,1)S(1)} %fusion.12), channel_id=1, source_target_pairs={{0,12},{1,13},{2,14},{3,15},{4,8},{5,9},{6,10},{7,11},{8,4},{9,5},... | collective-permute-start | bytes 786440 | tf_op jit(solution)/shard_map/ppermute | solution.py:42
  81.4 7.7 %collective-permute-start.15 = (f16[512,256]{1,0:T(8,128)(2,1)S(1)}, f16[512,256]{1,0:T(8,128)(2,1)S(1)}, u32[]{:S(2)}, u32[]{:S(2)}) collective-permute-start(f16[512,256]{1,0:T(8,128)(2,1)S(1)} %fusion.3), channel_id=1, source_target_pairs={{0,3},{1,2},{2,1},{3,0},{4,7},{5,6},{6,5},{7,4},{8,11},{9,10},{10,... | collective-permute-start | bytes 786440 | tf_op jit(solution)/shard_map/ppermute | solution.py:42
  89.4 1.6 %collective-permute-start.16 = (f16[4,64,512]{2,1,0:T(8,128)(2,1)S(1)}, f16[4,64,512]{2,1,0:T(8,128)(2,1)S(1)}, u32[]{:S(2)}, u32[]{:S(2)}) collective-permute-start(f16[4,64,512]{2,1,0:T(8,128)(2,1)S(1)} %bitcast.65), channel_id=1, source_target_pairs={{0,16},{1,17},{2,18},{3,19},{4,20},{5,21},{6,22},{7,23},{8,24},{9,... | collective-permute-start | bytes 786440 | tf_op jit(solution)/shard_map/ppermute | solution.py:42
  91.1 8.0 %collective-permute-start.17 = (f16[2,64,512]{2,1,0:T(8,128)(2,1)S(1)}, f16[2,64,512]{2,1,0:T(8,128)(2,1)S(1)}, u32[]{:S(2)}, u32[]{:S(2)}) collective-permute-start(f16[2,64,512]{2,1,0:T(8,128)(2,1)S(1)} %pad_maximum_fusion.2), channel_id=1, source_target_pairs={{0,64},{1,65},{2,66},{3,67},{4,68},{5,69},{6,70},{7,71},{8,72},{9,... | collective-permute-start | bytes 393224 | tf_op jit(solution)/shard_map/ppermute | solution.py:42
  94.9 6.1 %collective-permute-start.18 = (f16[2,64,512]{2,1,0:T(8,128)(2,1)S(1)}, f16[2,64,512]{2,1,0:T(8,128)(2,1)S(1)}, u32[]{:S(2)}, u32[]{:S(2)}) collective-permute-start(f16[2,64,512]{2,1,0:T(8,128)(2,1)S(1)} %pad_maximum_fusion.3), channel_id=1, source_target_pairs={{0,32},{1,33},{2,34},{3,35},{4,36},{5,37},{6,38},{7,39},{8,40},{9,... | collective-permute-start | bytes 393224 | tf_op jit(solution)/shard_map/ppermute | solution.py:42
  95.0 6.7 %collective-permute-start.19 = (f16[2,64,512]{2,1,0:T(8,128)(2,1)S(1)}, f16[2,64,512]{2,1,0:T(8,128)(2,1)S(1)}, u32[]{:S(2)}, u32[]{:S(2)}) collective-permute-start(f16[2,64,512]{2,1,0:T(8,128)(2,1)S(1)} %pad_maximum_fusion.4), channel_id=1, source_target_pairs={{0,96},{1,97},{2,98},{3,99},{4,100},{5,101},{6,102},{7,103},{8,104... | collective-permute-start | bytes 393224 | tf_op jit(solution)/shard_map/ppermute | solution.py:42

commit v8 on v7

--- a/solution.py
+++ b/solution.py
@@ -17,6 +17,7 @@
 F16 = jnp.float16
 F32 = jnp.float32
 DOWN, UP = 0.0625, 16.0
+LONG = pl.CostEstimate(flops=10**10, bytes_accessed=2**24, transcendentals=0)
 ALONG_Z = (1, 3, 2)
 HOME_Z = (2, 1, 3)
 
@@ -71,7 +72,7 @@
         out_specs=pl.BlockSpec((n_a, step, c), lambda i: (0, i, 0)),
         out_shape=jax.ShapeDtypeStruct((n_a, count, c), head.dtype),
         compiler_params=pltpu.CompilerParams(vmem_limit_bytes=12 << 20),
-        cost_estimate=pl.CostEstimate(flops=10**10, bytes_accessed=2**24, transcendentals=0),
+        cost_estimate=LONG,
     )(head)
 
 
@@ -194,7 +195,7 @@
         out[:, pl.ds(at, width)] = home[i] - column
 
 
-def call(kernel, shapes, *args):
+def call(kernel, shapes, *args, cost=None):
     def spec(v):
         small = v.dtype == jnp.int32 and v.size < 32
         return pl.BlockSpec(memory_space=pltpu.SMEM) if small else pl.BlockSpec()
@@ -206,6 +207,7 @@
         out_specs=[pl.BlockSpec() for _ in outs],
         out_shape=outs,
         compiler_params=pltpu.CompilerParams(vmem_limit_bytes=16 << 20),
+        cost_estimate=cost,
     )(*args)
     return result if len(outs) > 1 else result[0]
 
@@ -247,18 +249,23 @@
     sums = call(square_kernel, [((NY * NX, 8, 128), F32)], *flat)
     sums = lax.all_to_all(sums, "tensor", 0, 0, tiled=True)
     normed = call(
-        functools.partial(norm_kernel, (D, DE, DE)), [((rows, width), BF)], *flat, *gains, sums
+        functools.partial(norm_kernel, (D, DE, DE)),
+        [((rows, width), BF)],
+        *flat,
+        *gains,
+        sums,
+        cost=LONG,
     )
     along_z = [("z", 0, k) for k in ALONG_Z]
-    got = swap(normed, along_z, (expert_head, 0), (base_head, 0), (base_head, quarter))
+    got = swap(normed, along_z, (base_head, 0), (base_head, quarter), (expert_head, 0))
     mine = jnp.concatenate([normed, *got])
     (other,) = swap(mine, [("core",)], (anti_head, 0))
-    heads = heads[1:3] + [heads[0], heads[3]]
     acts = call(join_kernel, [((NZ * NC * rows, width), BF)], mine, other)
 
     axes = (("x", "y"), ("y", "x"))
     kept = [[], []]
     moved = [[], []]
+    second_step = []
     for i in range(4):
         for half in range(2):
             kind = BF if i < 2 else F32
@@ -268,10 +275,12 @@
                 moved[half].append(exchange(part, axes[half][0], 0))
             else:
                 kept[half].append(part)
-    second_step = [
-        exchange(narrow(kept[h][0] + wide(moved[h][0])), axes[h][0], 1) for h in range(2)
-    ]
-    sums = together(*[kept[h][1] + wide(moved[h][1]) for h in range(2)])
+        if i == 2:
+            totals = [narrow(kept[h][0] + wide(moved[h][0])) for h in range(2)]
+            second_step = [exchange(totals[h], axes[h][0], 1) for h in range(2)]
+            table, _ = together(table, totals[1])
+    own = together(kept[0][1], kept[1][1])
+    sums = together(*[own[h] + wide(moved[h][1]) for h in range(2)])
     sums = [sums[h] + wide(second_step[h]) for h in range(2)]
     moved = [
         [exchange(narrow(sums[h][i]), axes[h][1], 0) for i in (1, 0)] for h in range(2)

time: 117 us -> 115 us (0.983)
  local copies, waits for them, and re-layouts: 3.74 us -> 2.2 us
    unnamed x11 -> x9, local copies, waits for them, and re-layouts: 2.86 us -> 1.32 us
  transfers between devices with their start and end apart: 21 -> 21, of which waited for: 13 -> 15; matrix products, arithmetic and copies ran while one was open for 3% -> 3% of each run, Pallas kernels for 16% -> 16%
where the time goes in v8:
time: 115 us
  waiting for transfers between devices  40.2 us (35%)
  starting transfers between devices  29.9 us (26%)
  Pallas kernels  26.5 us (23%)
  blocking collectives  11.5 us (10%)
  other arithmetic  3.08 us (3%)
  local copies, waits for them, and re-layouts  2.2 us (2%)
  between operations  1.61 us (1%)
    ppermute x20, waiting for transfers between devices, exchange(): return lax.ppermute(value, AXES, pairs)  33.9 us
    ppermute x20, starting transfers between devices, exchange(): return lax.ppermute(value, AXES, pairs)  22.7 us
    pallas_call x8, Pallas kernels, project(): pl.pallas_call(functools.partial(matmul_kernel, first, half), in_specs=[s...  15 us
    all_to_all x1, blocking collectives, shards(): stats = lax.all_to_all(stats, 'tensor', 0, 0, tiled=True)  11.5 us
    all_to_all x1, starting transfers between devices, shards(): sums = lax.all_to_all(sums, 'tensor', 0, 0, tiled=True)  7.12 us
    all_to_all x1, waiting for transfers between devices, shards(): sums = lax.all_to_all(sums, 'tensor', 0, 0, tiled=True)  6.3 us
    pallas_call x5, Pallas kernels, call(): pl.pallas_call(kernel, in_specs=[spec(v) for v in args], out_specs=[pl.Bl...  5.93 us
    pallas_call x4, Pallas kernels, relay(): pl.pallas_call(relay_kernel, grid=(count // step,), in_specs=[pl.BlockSpe...  5.55 us
  transfers between devices with their start and end apart: 21, of which 15 were waited for; matrix products, arithmetic and copies ran while one was open for 3% of the time, Pallas kernels for 16%

profile of v8, /device:TPU:0, one launch (start us, length us, event | category | flops | bytes accessed | tf_op | source)
XLA Modules:
  0.0 114.9 jit_solution(9642524122138267216)
XLA Ops:
  0.6 1.7 %shard_map.131 = f32[16,8,128]{2,1,0:T(8,128)} custom-call(bf16[64,512]{1,0:T(8,128)(2,1)} %refs_0_.3, bf16[64,256]{1,0:T(8,128)(2,1)} %refs_1_.3, bf16[64,256]{1,0:T(8,128)(2,1)} %refs_2_.3), custom_call_target="tpu_custom_call" | custom-call | tf_op jit(solution)/shard_map/pallas_call | solution.py:204
  2.3 7.1 %all-to-all-start = ((f32[16,8,128]{2,1,0:T(8,128)}), f32[16,8,128]{2,1,0:T(8,128)S(1)}, u32[]{:S(2)}, u32[]{:S(2)}) async-start(f32[16,8,128]{2,1,0:T(8,128)} %shard_map.131), calls=%async_computation | async-start | bytes 131072 | tf_op jit(solution)/shard_map/all_to_all | solution.py:250
  9.4 0.7 constant_dynamic-slice_fusion
  10.8 6.3 %all-to-all-done.refs_6_ = f32[16,8,128]{2,1,0:T(8,128)S(1)} async-done(((f32[16,8,128]{2,1,0:T(8,128)}), f32[16,8,128]{2,1,0:T(8,128)S(1)}, u32[]{:S(2)}, u32[]{:S(2)}) %all-to-all-start) | async-done | bytes 65568 | tf_op jit(solution)/shard_map/all_to_all | solution.py:250
  17.1 1.2 %shard_map.132 = bf16[64,1024]{1,0:T(8,128)(2,1)S(1)} custom-call(bf16[64,512]{1,0:T(8,128)(2,1)} %refs_0_.3, bf16[64,256]{1,0:T(8,128)(2,1)} %refs_1_.3, bf16[64,256]{1,0:T(8,128)(2,1)} %refs_2_.3, bf16[512]{0:T(512)(128)(2,1)} %refs_3_.1, bf16[256]{0:T(256)(128)(2,1)} %refs_4_.1, bf16[256]{0:T(256)(128)(2,1)} %refs_5_.1, ...), custom_call_target="tpu_custom_call" | custom-call | flops 10000000000 | bytes 16777216 | tf_op jit(solution)/shard_map/pallas_call | solution.py:204
  18.3 4.0 %collective-permute-start.2 = (bf16[64,1024]{1,0:T(8,128)(2,1)S(1)}, bf16[64,1024]{1,0:T(8,128)(2,1)S(1)}, u32[]{:S(2)}, u32[]{:S(2)}) collective-permute-start(bf16[64,1024]{1,0:T(8,128)(2,1)S(1)} %shard_map.132), channel_id=1, source_target_pairs={{0,64},{1,65},{2,66},{3,67},{4,68},{5,69},{6,70},{7,71},{8,72},{9,... | collective-permute-start | bytes 393224 | tf_op jit(solution)/shard_map/ppermute | solution.py:43
  22.3 0.7 collective-permute-start.1
  23.0 0.3 collective-permute-start
  23.3 1.4 %shard_map.133.wb0 = bf16[16,256,512]{2,1,0:T(8,128)(2,1)S(1)} custom-call(bf16[512,16,512]{2,1,0:T(8,128)(2,1)S(1)} %copy-done), custom_call_target="tpu_custom_call" | custom-call | flops 10000000000 | bytes 16777216 | tf_op jit(solution)/shard_map/pallas_call | solution.py:68
  24.7 1.4 %shard_map.134.wb1 = bf16[16,256,512]{2,1,0:T(8,128)(2,1)S(1)} custom-call(bf16[512,16,512]{2,1,0:T(8,128)(2,1)S(1)} %copy-done), custom_call_target="tpu_custom_call" | custom-call | flops 10000000000 | bytes 16777216 | tf_op jit(solution)/shard_map/pallas_call | solution.py:68
  26.1 0.8 copy-done.1
  26.9 1.4 %shard_map.135.we = bf16[16,256,512]{2,1,0:T(8,128)(2,1)S(1)} custom-call(bf16[256,16,512]{2,1,0:T(8,128)(2,1)S(1)} %copy-done.1), custom_call_target="tpu_custom_call" | custom-call | flops 10000000000 | bytes 16777216 | tf_op jit(solution)/shard_map/pallas_call | solution.py:68
  28.3 0.2 collective-permute-done.1
  28.6 0.5 copy-done.2
  29.1 1.4 %shard_map.136.wa = bf16[16,256,512]{2,1,0:T(8,128)(2,1)S(1)} custom-call(bf16[256,16,512]{2,1,0:T(8,128)(2,1)S(1)} %copy-done.2), custom_call_target="tpu_custom_call" | custom-call | flops 10000000000 | bytes 16777216 | tf_op jit(solution)/shard_map/pallas_call | solution.py:68
  30.6 1.9 %shard_map.138 = bf16[4,512,256]{2,1,0:T(8,128)(2,1)S(1)} custom-call(s32[32]{0:T(128)S(1)} %slice_bitcast_fusion.8.table, f32[1]{0:T(128)S(6)} %copy.18.alpha, bf16[512,1024]{1,0:T(8,128)(2,1)S(1)} %shard_map.137.acts, bf16[16,256,512]{2,1,0:T(8,128)(2,1)S(1)} %shard_map.133.wb0, bf16[16,256,512]{2,1,0:T(8,128)(2,1)S(1)} %shard_map.134.wb1, ...), custom_call_target="tpu_custom_call" | custom-call | flops 1 | bytes 1 | tf_op jit(solution)/shard_map/pallas_call | solution.py:99
  32.5 0.6 collective-permute-start.7
  33.1 1.9 %shard_map.139 = bf16[4,512,256]{2,1,0:T(8,128)(2,1)S(1)} custom-call(s32[32]{0:T(128)S(1)} %slice_bitcast_fusion.8.table, f32[1]{0:T(128)S(6)} %copy.18.alpha, bf16[512,1024]{1,0:T(8,128)(2,1)S(1)} %shard_map.137.acts, bf16[16,256,512]{2,1,0:T(8,128)(2,1)S(1)} %shard_map.133.wb0, bf16[16,256,512]{2,1,0:T(8,128)(2,1)S(1)} %shard_map.134.wb1, ...), custom_call_target="tpu_custom_call" | custom-call | flops 1 | bytes 1 | tf_op jit(solution)/shard_map/pallas_call | solution.py:99
  35.0 0.6 collective-permute-start.4
  35.6 1.9 %shard_map.140 = bf16[4,512,256]{2,1,0:T(8,128)(2,1)S(1)} custom-call(s32[32]{0:T(128)S(1)} %slice_bitcast_fusion.8.table, f32[1]{0:T(128)S(6)} %copy.18.alpha, bf16[512,1024]{1,0:T(8,128)(2,1)S(1)} %shard_map.137.acts, bf16[16,256,512]{2,1,0:T(8,128)(2,1)S(1)} %shard_map.133.wb0, bf16[16,256,512]{2,1,0:T(8,128)(2,1)S(1)} %shard_map.134.wb1, ...), custom_call_target="tpu_custom_call" | custom-call | flops 1 | bytes 1 | tf_op jit(solution)/shard_map/pallas_call | solution.py:99
  37.5 1.5 %collective-permute-start.5 = (bf16[4,512,256]{2,1,0:T(8,128)(2,1)S(1)}, bf16[4,512,256]{2,1,0:T(8,128)(2,1)S(1)}, u32[]{:S(2)}, u32[]{:S(2)}) collective-permute-start(bf16[4,512,256]{2,1,0:T(8,128)(2,1)S(1)} %shard_map.140), channel_id=1, source_target_pairs={{0,1},{1,0},{2,3},{3,2},{4,5},{5,4},{6,7},{7,6},{8,9},{9,8},{10,11... | collective-permute-start | bytes 3145736 | tf_op jit(solution)/shard_map/ppermute | solution.py:43
  39.0 1.9 %shard_map.141 = bf16[4,512,256]{2,1,0:T(8,128)(2,1)S(1)} custom-call(s32[32]{0:T(128)S(1)} %slice_bitcast_fusion.8.table, f32[1]{0:T(128)S(6)} %copy.18.alpha, bf16[512,1024]{1,0:T(8,128)(2,1)S(1)} %shard_map.137.acts, bf16[16,256,512]{2,1,0:T(8,128)(2,1)S(1)} %shard_map.133.wb0, bf16[16,256,512]{2,1,0:T(8,128)(2,1)S(1)} %shard_map.134.wb1, ...), custom_call_target="tpu_custom_call" | custom-call | flops 1 | bytes 1 | tf_op jit(solution)/shard_map/pallas_call | solution.py:99
  40.9 1.6 %collective-permute-start.6 = (bf16[4,512,256]{2,1,0:T(8,128)(2,1)S(1)}, bf16[4,512,256]{2,1,0:T(8,128)(2,1)S(1)}, u32[]{:S(2)}, u32[]{:S(2)}) collective-permute-start(bf16[4,512,256]{2,1,0:T(8,128)(2,1)S(1)} %shard_map.141), channel_id=1, source_target_pairs={{0,4},{1,5},{2,6},{3,7},{4,0},{5,1},{6,2},{7,3},{8,12},{9,13},{10,... | collective-permute-start | bytes 3145736 | tf_op jit(solution)/shard_map/ppermute | solution.py:43
  42.5 1.9 %shard_map.142 = f32[4,512,256]{2,1,0:T(8,128)S(1)} custom-call(s32[32]{0:T(128)S(1)} %slice_bitcast_fusion.8.table, f32[1]{0:T(128)S(6)} %copy.18.alpha, bf16[512,1024]{1,0:T(8,128)(2,1)S(1)} %shard_map.137.acts, bf16[16,256,512]{2,1,0:T(8,128)(2,1)S(1)} %shard_map.133.wb0, bf16[16,256,512]{2,1,0:T(8,128)(2,1)S(1)} %shard_map.134.wb1, ...), custom_call_target="tpu_custom_call" | custom-call | flops 1 | bytes 1 | tf_op jit(solution)/shard_map/pallas_call | solution.py:99
  44.4 3.0 %collective-permute-done.7 = bf16[4,512,256]{2,1,0:T(8,128)(2,1)S(1)} collective-permute-done((bf16[4,512,256]{2,1,0:T(8,128)(2,1)S(1)}, bf16[4,512,256]{2,1,0:T(8,128)(2,1)S(1)}, u32[]{:S(2)}, u32[]{:S(2)}) %collective-permute-start.7) | collective-permute-done | bytes 1048608 | tf_op jit(solution)/shard_map/ppermute | solution.py:43
  47.3 0.4 multiply_convert_fusion
  47.7 1.4 %collective-permute-start.8 = (f16[4,512,256]{2,1,0:T(8,128)(2,1)S(1)}, f16[4,512,256]{2,1,0:T(8,128)(2,1)S(1)}, u32[]{:S(2)}, u32[]{:S(2)}) collective-permute-start(f16[4,512,256]{2,1,0:T(8,128)(2,1)S(1)} %multiply_convert_fusion), channel_id=1, source_target_pairs={{0,3},{1,2},{2,1},{3,0},{4,7},{5,6},{6,5},{7,4},{8,11},{9,10},{10,... | collective-permute-start | bytes 3145736 | tf_op jit(solution)/shard_map/ppermute | solution.py:43
  49.1 1.9 %shard_map.143 = f32[4,512,256]{2,1,0:T(8,128)S(1)} custom-call(s32[32]{0:T(128)S(1)} %slice_bitcast_fusion.8.table, f32[1]{0:T(128)S(6)} %copy.18.alpha, bf16[512,1024]{1,0:T(8,128)(2,1)S(1)} %shard_map.137.acts, bf16[16,256,512]{2,1,0:T(8,128)(2,1)S(1)} %shard_map.133.wb0, bf16[16,256,512]{2,1,0:T(8,128)(2,1)S(1)} %shard_map.134.wb1, ...), custom_call_target="tpu_custom_call" | custom-call | flops 1 | bytes 1 | tf_op jit(solution)/shard_map/pallas_call | solution.py:99
  51.0 0.4 multiply_convert_fusion.1
  51.4 1.3 %collective-permute-start.12 = (f16[4,512,256]{2,1,0:T(8,128)(2,1)S(1)}, f16[4,512,256]{2,1,0:T(8,128)(2,1)S(1)}, u32[]{:S(2)}, u32[]{:S(2)}) collective-permute-start(f16[4,512,256]{2,1,0:T(8,128)(2,1)S(1)} %multiply_convert_fusion.1), channel_id=1, source_target_pairs={{0,12},{1,13},{2,14},{3,15},{4,8},{5,9},{6,10},{7,11},{8,4},{9,5},... | collective-permute-start | bytes 3145736 | tf_op jit(solution)/shard_map/ppermute | solution.py:43
  52.6 1.9 %shard_map.144 = f32[4,512,256]{2,1,0:T(8,128)S(1)} custom-call(s32[32]{0:T(128)S(1)} %slice_bitcast_fusion.8.table, f32[1]{0:T(128)S(6)} %copy.18.alpha, bf16[512,1024]{1,0:T(8,128)(2,1)S(1)} %shard_map.137.acts, bf16[16,256,512]{2,1,0:T(8,128)(2,1)S(1)} %shard_map.133.wb0, bf16[16,256,512]{2,1,0:T(8,128)(2,1)S(1)} %shard_map.134.wb1, ...), custom_call_target="tpu_custom_call" | custom-call | flops 1 | bytes 1 | tf_op jit(solution)/shard_map/pallas_call | solution.py:99
  54.5 1.9 %shard_map.145 = f32[4,512,256]{2,1,0:T(8,128)S(1)} custom-call(s32[32]{0:T(128)S(1)} %slice_bitcast_fusion.8.table, f32[1]{0:T(128)S(6)} %copy.18.alpha, bf16[512,1024]{1,0:T(8,128)(2,1)S(1)} %shard_map.137.acts, bf16[16,256,512]{2,1,0:T(8,128)(2,1)S(1)} %shard_map.133.wb0, bf16[16,256,512]{2,1,0:T(8,128)(2,1)S(1)} %shard_map.134.wb1, ...), custom_call_target="tpu_custom_call" | custom-call | flops 1 | bytes 1 | tf_op jit(solution)/shard_map/pallas_call | solution.py:99
  56.4 9.9 %collective-permute-done.5 = bf16[4,512,256]{2,1,0:T(8,128)(2,1)S(1)} collective-permute-done((bf16[4,512,256]{2,1,0:T(8,128)(2,1)S(1)}, bf16[4,512,256]{2,1,0:T(8,128)(2,1)S(1)}, u32[]{:S(2)}, u32[]{:S(2)}) %collective-permute-start.5) | collective-permute-done | bytes 1048608 | tf_op jit(solution)/shard_map/ppermute | solution.py:43
  66.3 0.3 convert_add_fusion.1
  66.6 2.1 %collective-permute-done.6 = bf16[4,512,256]{2,1,0:T(8,128)(2,1)S(1)} collective-permute-done((bf16[4,512,256]{2,1,0:T(8,128)(2,1)S(1)}, bf16[4,512,256]{2,1,0:T(8,128)(2,1)S(1)}, u32[]{:S(2)}, u32[]{:S(2)}) %collective-permute-start.6) | collective-permute-done | bytes 1048608 | tf_op jit(solution)/shard_map/ppermute | solution.py:43
  68.7 0.2 convert_add_fusion
  68.9 1.3 %collective-permute-done.8 = f16[4,512,256]{2,1,0:T(8,128)(2,1)S(1)} collective-permute-done((f16[4,512,256]{2,1,0:T(8,128)(2,1)S(1)}, f16[4,512,256]{2,1,0:T(8,128)(2,1)S(1)}, u32[]{:S(2)}, u32[]{:S(2)}) %collective-permute-start.8) | collective-permute-done | bytes 1048608 | tf_op jit(solution)/shard_map/ppermute | solution.py:43
  70.2 0.3 multiply_add_fusion.1
  70.5 0.1 fusion.18
  70.6 0.6 collective-permute-start.10
  71.2 1.8 %collective-permute-done.12 = f16[4,512,256]{2,1,0:T(8,128)(2,1)S(1)} collective-permute-done((f16[4,512,256]{2,1,0:T(8,128)(2,1)S(1)}, f16[4,512,256]{2,1,0:T(8,128)(2,1)S(1)}, u32[]{:S(2)}, u32[]{:S(2)}) %collective-permute-start.12) | collective-permute-done | bytes 1048608 | tf_op jit(solution)/shard_map/ppermute | solution.py:43
  73.0 0.3 multiply_add_fusion
  73.3 0.1 fusion.20
  73.5 0.2 collective-permute-start.14
  73.7 1.9 %collective-permute-start.13 = (f16[512,256]{1,0:T(8,128)(2,1)S(1)}, f16[512,256]{1,0:T(8,128)(2,1)S(1)}, u32[]{:S(2)}, u32[]{:S(2)}) collective-permute-start(f16[512,256]{1,0:T(8,128)(2,1)S(1)} %get-tuple-element.76), channel_id=1, source_target_pairs={{0,1},{1,0},{2,3},{3,2},{4,5},{5,4},{6,7},{7,6},{8,9},{9,8},{10,11... | collective-permute-start | bytes 786440 | tf_op jit(solution)/shard_map/ppermute | solution.py:43
  75.6 1.5 %collective-permute-done.10 = f16[512,256]{1,0:T(8,128)(2,1)S(1)} collective-permute-done((f16[512,256]{1,0:T(8,128)(2,1)S(1)}, f16[512,256]{1,0:T(8,128)(2,1)S(1)}, u32[]{:S(2)}, u32[]{:S(2)}) %collective-permute-start.10) | collective-permute-done | bytes 262176 | tf_op jit(solution)/shard_map/ppermute | solution.py:43
  77.2 1.2 %collective-permute-start.11 = (f16[512,256]{1,0:T(8,128)(2,1)S(1)}, f16[512,256]{1,0:T(8,128)(2,1)S(1)}, u32[]{:S(2)}, u32[]{:S(2)}) collective-permute-start(f16[512,256]{1,0:T(8,128)(2,1)S(1)} %fusion.12), channel_id=1, source_target_pairs={{0,12},{1,13},{2,14},{3,15},{4,8},{5,9},{6,10},{7,11},{8,4},{9,5},... | collective-permute-start | bytes 786440 | tf_op jit(solution)/shard_map/ppermute | solution.py:43
  78.4 1.5 %collective-permute-done.14 = f16[512,256]{1,0:T(8,128)(2,1)S(1)} collective-permute-done((f16[512,256]{1,0:T(8,128)(2,1)S(1)}, f16[512,256]{1,0:T(8,128)(2,1)S(1)}, u32[]{:S(2)}, u32[]{:S(2)}) %collective-permute-start.14) | collective-permute-done | bytes 262176 | tf_op jit(solution)/shard_map/ppermute | solution.py:43
  80.0 2.1 %collective-permute-start.15 = (f16[512,256]{1,0:T(8,128)(2,1)S(1)}, f16[512,256]{1,0:T(8,128)(2,1)S(1)}, u32[]{:S(2)}, u32[]{:S(2)}) collective-permute-start(f16[512,256]{1,0:T(8,128)(2,1)S(1)} %fusion.3), channel_id=1, source_target_pairs={{0,3},{1,2},{2,1},{3,0},{4,7},{5,6},{6,5},{7,4},{8,11},{9,10},{10,... | collective-permute-start | bytes 786440 | tf_op jit(solution)/shard_map/ppermute | solution.py:43
  82.3 2.6 %collective-permute-done.11 = f16[512,256]{1,0:T(8,128)(2,1)S(1)} collective-permute-done((f16[512,256]{1,0:T(8,128)(2,1)S(1)}, f16[512,256]{1,0:T(8,128)(2,1)S(1)}, u32[]{:S(2)}, u32[]{:S(2)}) %collective-permute-start.11) | collective-permute-done | bytes 262176 | tf_op jit(solution)/shard_map/ppermute | solution.py:43
  84.8 0.2 fusion.17
  85.0 2.7 %collective-permute-done.15 = f16[512,256]{1,0:T(8,128)(2,1)S(1)} collective-permute-done((f16[512,256]{1,0:T(8,128)(2,1)S(1)}, f16[512,256]{1,0:T(8,128)(2,1)S(1)}, u32[]{:S(2)}, u32[]{:S(2)}) %collective-permute-start.15) | collective-permute-done | bytes 262176 | tf_op jit(solution)/shard_map/ppermute | solution.py:43
  87.7 0.2 fusion.8
  87.9 0.1 pad_maximum_fusion
  88.2 1.5 %collective-permute-done.16 = f16[4,64,512]{2,1,0:T(8,128)(2,1)S(1)} collective-permute-done((f16[4,64,512]{2,1,0:T(8,128)(2,1)S(1)}, f16[4,64,512]{2,1,0:T(8,128)(2,1)S(1)}, u32[]{:S(2)}, u32[]{:S(2)}) %collective-permute-start.16) | collective-permute-done | bytes 262176 | tf_op jit(solution)/shard_map/ppermute | solution.py:43
  89.8 3.6 %collective-permute-start.17 = (f16[2,64,512]{2,1,0:T(8,128)(2,1)S(1)}, f16[2,64,512]{2,1,0:T(8,128)(2,1)S(1)}, u32[]{:S(2)}, u32[]{:S(2)}) collective-permute-start(f16[2,64,512]{2,1,0:T(8,128)(2,1)S(1)} %pad_maximum_fusion.2), channel_id=1, source_target_pairs={{0,64},{1,65},{2,66},{3,67},{4,68},{5,69},{6,70},{7,71},{8,72},{9,... | collective-permute-start | bytes 393224 | tf_op jit(solution)/shard_map/ppermute | solution.py:43
  93.6 0.8 collective-permute-start.19
  94.4 3.3 %collective-permute-done.17 = f16[2,64,512]{2,1,0:T(8,128)(2,1)S(1)} collective-permute-done((f16[2,64,512]{2,1,0:T(8,128)(2,1)S(1)}, f16[2,64,512]{2,1,0:T(8,128)(2,1)S(1)}, u32[]{:S(2)}, u32[]{:S(2)}) %collective-permute-start.17) | collective-permute-done | bytes 131104 | tf_op jit(solution)/shard_map/ppermute | solution.py:43
  97.7 1.8 %collective-permute-done.18 = f16[2,64,512]{2,1,0:T(8,128)(2,1)S(1)} collective-permute-done((f16[2,64,512]{2,1,0:T(8,128)(2,1)S(1)}, f16[2,64,512]{2,1,0:T(8,128)(2,1)S(1)}, u32[]{:S(2)}, u32[]{:S(2)}) %collective-permute-start.18) | collective-permute-done | bytes 131104 | tf_op jit(solution)/shard_map/ppermute | solution.py:43
  99.5 0.8 collective-permute-done.19
  100.3 0.1 convert_multiply_fusion.home
  100.5 1.2 %shard_map.146 = f32[16,8,128]{2,1,0:T(8,128)S(1)} custom-call(s32[9]{0:T(128)S(1)} %slice_bitcast_fusion.9.source, f32[8,64,512]{2,1,0:T(8,128)S(1)} %convert_multiply_fusion.home, s32[64]{0:T(128)} %ids.1), custom_call_target="tpu_custom_call" | custom-call | tf_op jit(solution)/shard_map/pallas_call | solution.py:204
  101.7 11.5 %all_to_all.10.stats = f32[16,8,128]{2,1,0:T(8,128)S(1)} all-to-all(f32[16,8,128]{2,1,0:T(8,128)S(1)} %shard_map.146), channel_id=1, replica_groups=mesh['rows'=8,'tensor'=16] {'tensor'}, dimensions={0} | all-to-all | bytes 131072 | tf_op jit(solution)/shard_map/all_to_all | solution.py:303
  113.1 1.8 %shard_map.147 = (f32[64,4096]{1,0:T(8,128)}, f32[1,64]{1,0:T(1,128)}) custom-call(s32[9]{0:T(128)S(1)} %slice_bitcast_fusion.9.source, f32[8,64,512]{2,1,0:T(8,128)S(1)} %convert_multiply_fusion.home, f32[16,8,128]{2,1,0:T(8,128)S(1)} %all_to_all.10.stats), custom_call_target="tpu_custom_call" | custom-call | tf_op jit(solution)/shard_map/pallas_call | solution.py:204
  (30 shorter events, 1.1 us)
Async XLA Ops:
  2.3 14.8 %all-to-all-start = ((f32[16,8,128]{2,1,0:T(8,128)}), f32[16,8,128]{2,1,0:T(8,128)S(1)}, u32[]{:S(2)}, u32[]{:S(2)}) async-start(f32[16,8,128]{2,1,0:T(8,128)} %shard_map.131), calls=%async_computation | async-start | bytes 131072 | tf_op jit(solution)/shard_map/all_to_all | solution.py:250
  17.1 6.2 %copy-start = (bf16[512,16,512]{2,1,0:T(8,128)(2,1)S(1)}, bf16[512,16,512]{2,1,0:T(8,128)(2,1)}, u32[]{:S(2)}) copy-start(bf16[512,16,512]{2,1,0:T(8,128)(2,1)} %head.1) | copy-start | bytes 25165828
  18.3 10.0 %collective-permute-start.2 = (bf16[64,1024]{1,0:T(8,128)(2,1)S(1)}, bf16[64,1024]{1,0:T(8,128)(2,1)S(1)}, u32[]{:S(2)}, u32[]{:S(2)}) collective-permute-start(bf16[64,1024]{1,0:T(8,128)(2,1)S(1)} %shard_map.132), channel_id=1, source_target_pairs={{0,64},{1,65},{2,66},{3,67},{4,68},{5,69},{6,70},{7,71},{8,72},{9,... | collective-permute-start | bytes 393224 | tf_op jit(solution)/shard_map/ppermute | solution.py:43
  22.3 6.2 %collective-permute-start.1 = (bf16[64,1024]{1,0:T(8,128)(2,1)S(1)}, bf16[64,1024]{1,0:T(8,128)(2,1)S(1)}, u32[]{:S(2)}, u32[]{:S(2)}) collective-permute-start(bf16[64,1024]{1,0:T(8,128)(2,1)S(1)} %shard_map.132), channel_id=1, source_target_pairs={{0,96},{1,97},{2,98},{3,99},{4,100},{5,101},{6,102},{7,103},{8,104... | collective-permute-start | bytes 393224 | tf_op jit(solution)/shard_map/ppermute | solution.py:43
  23.0 5.5 %collective-permute-start = (bf16[64,1024]{1,0:T(8,128)(2,1)S(1)}, bf16[64,1024]{1,0:T(8,128)(2,1)S(1)}, u32[]{:S(2)}, u32[]{:S(2)}) collective-permute-start(bf16[64,1024]{1,0:T(8,128)(2,1)S(1)} %shard_map.132), channel_id=1, source_target_pairs={{0,32},{1,33},{2,34},{3,35},{4,36},{5,37},{6,38},{7,39},{8,40},{9,... | collective-permute-start | bytes 393224 | tf_op jit(solution)/shard_map/ppermute | solution.py:43
  24.7 2.2 %copy-start.1 = (bf16[256,16,512]{2,1,0:T(8,128)(2,1)S(1)}, bf16[256,16,512]{2,1,0:T(8,128)(2,1)}, u32[]{:S(2)}) copy-start(bf16[256,16,512]{2,1,0:T(8,128)(2,1)} %head.2) | copy-start | bytes 12582916
  26.9 2.2 %copy-start.2 = (bf16[256,16,512]{2,1,0:T(8,128)(2,1)S(1)}, bf16[256,16,512]{2,1,0:T(8,128)(2,1)}, u32[]{:S(2)}) copy-start(bf16[256,16,512]{2,1,0:T(8,128)(2,1)} %head.3) | copy-start | bytes 12582916
  28.5 2.0 %collective-permute-start.3 = (bf16[256,1024]{1,0:T(8,128)(2,1)S(1)}, bf16[256,1024]{1,0:T(8,128)(2,1)S(1)}, u32[]{:S(2)}, u32[]{:S(2)}) collective-permute-start(bf16[256,1024]{1,0:T(8,128)(2,1)S(1)} %pad_maximum_fusion.1.refs_0_), channel_id=1, source_target_pairs={{0,16},{1,17},{2,18},{3,19},{4,20},{5,21},{6,22},{7,23},{8,24},{9,... | collective-permute-start | bytes 1572872 | tf_op jit(solution)/shard_map/ppermute | solution.py:43
  32.5 14.9 %collective-permute-start.7 = (bf16[4,512,256]{2,1,0:T(8,128)(2,1)S(1)}, bf16[4,512,256]{2,1,0:T(8,128)(2,1)S(1)}, u32[]{:S(2)}, u32[]{:S(2)}) collective-permute-start(bf16[4,512,256]{2,1,0:T(8,128)(2,1)S(1)} %shard_map.138), channel_id=1, source_target_pairs={{0,1},{1,0},{2,3},{3,2},{4,5},{5,4},{6,7},{7,6},{8,9},{9,8},{10,11... | collective-permute-start | bytes 3145736 | tf_op jit(solution)/shard_map/ppermute | solution.py:43
  35.0 16.0 %collective-permute-start.4 = (bf16[4,512,256]{2,1,0:T(8,128)(2,1)S(1)}, bf16[4,512,256]{2,1,0:T(8,128)(2,1)S(1)}, u32[]{:S(2)}, u32[]{:S(2)}) collective-permute-start(bf16[4,512,256]{2,1,0:T(8,128)(2,1)S(1)} %shard_map.139), channel_id=1, source_target_pairs={{0,4},{1,5},{2,6},{3,7},{4,0},{5,1},{6,2},{7,3},{8,12},{9,13},{10,... | collective-permute-start | bytes 3145736 | tf_op jit(solution)/shard_map/ppermute | solution.py:43
  37.5 28.9 %collective-permute-start.5 = (bf16[4,512,256]{2,1,0:T(8,128)(2,1)S(1)}, bf16[4,512,256]{2,1,0:T(8,128)(2,1)S(1)}, u32[]{:S(2)}, u32[]{:S(2)}) collective-permute-start(bf16[4,512,256]{2,1,0:T(8,128)(2,1)S(1)} %shard_map.140), channel_id=1, source_target_pairs={{0,1},{1,0},{2,3},{3,2},{4,5},{5,4},{6,7},{7,6},{8,9},{9,8},{10,11... | collective-permute-start | bytes 3145736 | tf_op jit(solution)/shard_map/ppermute | solution.py:43
  40.9 27.8 %collective-permute-start.6 = (bf16[4,512,256]{2,1,0:T(8,128)(2,1)S(1)}, bf16[4,512,256]{2,1,0:T(8,128)(2,1)S(1)}, u32[]{:S(2)}, u32[]{:S(2)}) collective-permute-start(bf16[4,512,256]{2,1,0:T(8,128)(2,1)S(1)} %shard_map.141), channel_id=1, source_target_pairs={{0,4},{1,5},{2,6},{3,7},{4,0},{5,1},{6,2},{7,3},{8,12},{9,13},{10,... | collective-permute-start | bytes 3145736 | tf_op jit(solution)/shard_map/ppermute | solution.py:43
  47.7 22.5 %collective-permute-start.8 = (f16[4,512,256]{2,1,0:T(8,128)(2,1)S(1)}, f16[4,512,256]{2,1,0:T(8,128)(2,1)S(1)}, u32[]{:S(2)}, u32[]{:S(2)}) collective-permute-start(f16[4,512,256]{2,1,0:T(8,128)(2,1)S(1)} %multiply_convert_fusion), channel_id=1, source_target_pairs={{0,3},{1,2},{2,1},{3,0},{4,7},{5,6},{6,5},{7,4},{8,11},{9,10},{10,... | collective-permute-start | bytes 3145736 | tf_op jit(solution)/shard_map/ppermute | solution.py:43
  51.4 21.7 %collective-permute-start.12 = (f16[4,512,256]{2,1,0:T(8,128)(2,1)S(1)}, f16[4,512,256]{2,1,0:T(8,128)(2,1)S(1)}, u32[]{:S(2)}, u32[]{:S(2)}) collective-permute-start(f16[4,512,256]{2,1,0:T(8,128)(2,1)S(1)} %multiply_convert_fusion.1), channel_id=1, source_target_pairs={{0,12},{1,13},{2,14},{3,15},{4,8},{5,9},{6,10},{7,11},{8,4},{9,5},... | collective-permute-start | bytes 3145736 | tf_op jit(solution)/shard_map/ppermute | solution.py:43
  70.6 6.5 %collective-permute-start.10 = (f16[512,256]{1,0:T(8,128)(2,1)S(1)}, f16[512,256]{1,0:T(8,128)(2,1)S(1)}, u32[]{:S(2)}, u32[]{:S(2)}) collective-permute-start(f16[512,256]{1,0:T(8,128)(2,1)S(1)} %get-tuple-element.75), channel_id=1, source_target_pairs={{0,4},{1,5},{2,6},{3,7},{4,0},{5,1},{6,2},{7,3},{8,12},{9,13},{10,... | collective-permute-start | bytes 786440 | tf_op jit(solution)/shard_map/ppermute | solution.py:43
  73.5 6.5 %collective-permute-start.14 = (f16[512,256]{1,0:T(8,128)(2,1)S(1)}, f16[512,256]{1,0:T(8,128)(2,1)S(1)}, u32[]{:S(2)}, u32[]{:S(2)}) collective-permute-start(f16[512,256]{1,0:T(8,128)(2,1)S(1)} %get-tuple-element.77), channel_id=1, source_target_pairs={{0,1},{1,0},{2,3},{3,2},{4,5},{5,4},{6,7},{7,6},{8,9},{9,8},{10,11... | collective-permute-start | bytes 786440 | tf_op jit(solution)/shard_map/ppermute | solution.py:43
  73.6 8.6 %collective-permute-start.9 = (f16[512,256]{1,0:T(8,128)(2,1)S(1)}, f16[512,256]{1,0:T(8,128)(2,1)S(1)}, u32[]{:S(2)}, u32[]{:S(2)}) collective-permute-start(f16[512,256]{1,0:T(8,128)(2,1)S(1)} %get-tuple-element.74), channel_id=1, source_target_pairs={{0,4},{1,5},{2,6},{3,7},{4,0},{5,1},{6,2},{7,3},{8,12},{9,13},{10,... | collective-permute-start | bytes 786440 | tf_op jit(solution)/shard_map/ppermute | solution.py:43
  73.7 11.4 %collective-permute-start.13 = (f16[512,256]{1,0:T(8,128)(2,1)S(1)}, f16[512,256]{1,0:T(8,128)(2,1)S(1)}, u32[]{:S(2)}, u32[]{:S(2)}) collective-permute-start(f16[512,256]{1,0:T(8,128)(2,1)S(1)} %get-tuple-element.76), channel_id=1, source_target_pairs={{0,1},{1,0},{2,3},{3,2},{4,5},{5,4},{6,7},{7,6},{8,9},{9,8},{10,11... | collective-permute-start | bytes 786440 | tf_op jit(solution)/shard_map/ppermute | solution.py:43
  77.2 7.7 %collective-permute-start.11 = (f16[512,256]{1,0:T(8,128)(2,1)S(1)}, f16[512,256]{1,0:T(8,128)(2,1)S(1)}, u32[]{:S(2)}, u32[]{:S(2)}) collective-permute-start(f16[512,256]{1,0:T(8,128)(2,1)S(1)} %fusion.12), channel_id=1, source_target_pairs={{0,12},{1,13},{2,14},{3,15},{4,8},{5,9},{6,10},{7,11},{8,4},{9,5},... | collective-permute-start | bytes 786440 | tf_op jit(solution)/shard_map/ppermute | solution.py:43
  80.0 7.7 %collective-permute-start.15 = (f16[512,256]{1,0:T(8,128)(2,1)S(1)}, f16[512,256]{1,0:T(8,128)(2,1)S(1)}, u32[]{:S(2)}, u32[]{:S(2)}) collective-permute-start(f16[512,256]{1,0:T(8,128)(2,1)S(1)} %fusion.3), channel_id=1, source_target_pairs={{0,3},{1,2},{2,1},{3,0},{4,7},{5,6},{6,5},{7,4},{8,11},{9,10},{10,... | collective-permute-start | bytes 786440 | tf_op jit(solution)/shard_map/ppermute | solution.py:43
  88.1 1.6 %collective-permute-start.16 = (f16[4,64,512]{2,1,0:T(8,128)(2,1)S(1)}, f16[4,64,512]{2,1,0:T(8,128)(2,1)S(1)}, u32[]{:S(2)}, u32[]{:S(2)}) collective-permute-start(f16[4,64,512]{2,1,0:T(8,128)(2,1)S(1)} %bitcast.63), channel_id=1, source_target_pairs={{0,16},{1,17},{2,18},{3,19},{4,20},{5,21},{6,22},{7,23},{8,24},{9,... | collective-permute-start | bytes 786440 | tf_op jit(solution)/shard_map/ppermute | solution.py:43
  89.8 7.9 %collective-permute-start.17 = (f16[2,64,512]{2,1,0:T(8,128)(2,1)S(1)}, f16[2,64,512]{2,1,0:T(8,128)(2,1)S(1)}, u32[]{:S(2)}, u32[]{:S(2)}) collective-permute-start(f16[2,64,512]{2,1,0:T(8,128)(2,1)S(1)} %pad_maximum_fusion.2), channel_id=1, source_target_pairs={{0,64},{1,65},{2,66},{3,67},{4,68},{5,69},{6,70},{7,71},{8,72},{9,... | collective-permute-start | bytes 393224 | tf_op jit(solution)/shard_map/ppermute | solution.py:43
  93.4 6.1 %collective-permute-start.18 = (f16[2,64,512]{2,1,0:T(8,128)(2,1)S(1)}, f16[2,64,512]{2,1,0:T(8,128)(2,1)S(1)}, u32[]{:S(2)}, u32[]{:S(2)}) collective-permute-start(f16[2,64,512]{2,1,0:T(8,128)(2,1)S(1)} %pad_maximum_fusion.3), channel_id=1, source_target_pairs={{0,32},{1,33},{2,34},{3,35},{4,36},{5,37},{6,38},{7,39},{8,40},{9,... | collective-permute-start | bytes 393224 | tf_op jit(solution)/shard_map/ppermute | solution.py:43
  93.6 6.7 %collective-permute-start.19 = (f16[2,64,512]{2,1,0:T(8,128)(2,1)S(1)}, f16[2,64,512]{2,1,0:T(8,128)(2,1)S(1)}, u32[]{:S(2)}, u32[]{:S(2)}) collective-permute-start(f16[2,64,512]{2,1,0:T(8,128)(2,1)S(1)} %pad_maximum_fusion.4), channel_id=1, source_target_pairs={{0,96},{1,97},{2,98},{3,99},{4,100},{5,101},{6,102},{7,103},{8,104... | collective-permute-start | bytes 393224 | tf_op jit(solution)/shard_map/ppermute | solution.py:43

commit v9 on v8

--- a/solution.py
+++ b/solution.py
@@ -2,7 +2,6 @@
 
 import jax
 import jax.numpy as jnp
-import numpy as np
 from jax import lax
 from jax.experimental import pallas as pl
 from jax.experimental.pallas import tpu as pltpu
@@ -43,20 +42,14 @@
     return lax.ppermute(value, AXES, pairs)
 
 
-def tables():
-    out = np.zeros((NZ * NC * NY * NX, 48), np.int32)
-    for z in range(NZ):
-        for c in range(NC):
-            u, v = (1, 3) if c == 0 else (3, 1)
-            first, second = (2, u, v, 0), (u, 2, 0, v)
-            for y in range(NY):
-                for x in range(NX):
-                    row = [(y ^ j) * NX + (x ^ i) for i in first for j in second]
-                    row += [(y ^ i) * NX + (x ^ j) for i in first for j in second]
-                    row += [(z ^ i) * NC + k for i in (0,) + HOME_Z for k in (c, 1 - c)]
-                    row += [(y * NX + x) * (VOCAB // (NY * NX))]
-                    out[device(z, c, y, x), : len(row)] = row
-    return out
+def here():
+    r, t = lax.axis_index("rows"), lax.axis_index("tensor")
+    return r // NC, r % NC, t // NX, t % NX
+
+
+def sources():
+    z, c, _, _ = here()
+    return [(z ^ k) * NC + core for k in (0,) + HOME_Z for core in (c, 1 - c)]
 
 
 def relay_kernel(head, out):
@@ -72,14 +65,18 @@
         out_specs=pl.BlockSpec((n_a, step, c), lambda i: (0, i, 0)),
         out_shape=jax.ShapeDtypeStruct((n_a, count, c), head.dtype),
         compiler_params=pltpu.CompilerParams(vmem_limit_bytes=12 << 20),
-        cost_estimate=LONG,
+        cost_estimate=pl.CostEstimate(flops=0, bytes_accessed=2**23, transcendentals=0),
     )(head)
 
 
-def matmul_kernel(first, half, table, alpha, acts, wb0, wb1, we, wa, out):
+def matmul_kernel(step, half, alpha, acts, wb0, wb1, we, wa, out):
     quarter, cols = wb0.shape[1], out.shape[2]
+    _, c, y, x = here()
+    u, v = 1 + 2 * c, 3 - 2 * c
+    first, second = (2, u, v, 0)[step], (u, 2, 0, v)
     for i in range(out.shape[0]):
-        block = table[first + i]
+        along_y, along_x = (second[i], first) if half == 0 else (first, second[i])
+        block = (y ^ along_y) * NX + (x ^ along_x)
         base0, base1, expert, anti = [
             jnp.dot(
                 acts[:, j * quarter : (j + 1) * quarter],
@@ -92,18 +89,17 @@
         out[i] = total.astype(out.dtype)
 
 
-def project(table, alpha, acts, heads, first, half, dtype):
+def project(alpha, acts, heads, step, half, dtype):
     smem = pl.BlockSpec(memory_space=pltpu.SMEM)
     vmem = pl.BlockSpec(memory_space=pltpu.VMEM)
-    args = (table, alpha, acts, *heads)
     return pl.pallas_call(
-        functools.partial(matmul_kernel, first, half),
-        in_specs=[smem] * 2 + [vmem] * (len(args) - 2),
+        functools.partial(matmul_kernel, step, half),
+        in_specs=[smem] + [vmem] * (1 + len(heads)),
         out_specs=vmem,
         out_shape=jax.ShapeDtypeStruct((4, acts.shape[0], heads[0].shape[2] // 2), dtype),
         compiler_params=pltpu.CompilerParams(vmem_limit_bytes=12 << 20),
         cost_estimate=pl.CostEstimate(flops=1, bytes_accessed=1, transcendentals=0),
-    )(*args)
+    )(alpha, acts, *heads)
 
 
 def wide(value):
@@ -160,12 +156,13 @@
         at += ref.shape[0]
 
 
-def stats_kernel(source, home, ids, out):
+def stats_kernel(home, ids, out):
     pieces, rows, width = home.shape
+    source = sources()
     row = ids[...][None].astype(F32)
     row = jnp.concatenate([row, jnp.zeros((1, 128 - rows), F32)], axis=1)
     column = jnp.broadcast_to(row, (128, 128)).T[:rows, :1]
-    wanted = column.astype(jnp.int32) - source[pieces]
+    wanted = column.astype(jnp.int32) - lax.axis_index("tensor") * (VOCAB // (NY * NX))
     top = jnp.max(home[...], axis=(0,))
     top = jnp.max(top, axis=1, keepdims=True)
     total = jnp.zeros((rows, width), F32)
@@ -180,8 +177,9 @@
     to_all(out, [top, total, pick])
 
 
-def final_kernel(source, home, stats, out, picked):
+def final_kernel(home, stats, out, picked):
     pieces, rows, width = home.shape
+    source = sources()
     tops, totals, picks = [stats[:, i, :rows] for i in range(3)]
     top = jnp.max(tops, axis=0, keepdims=True)
     logz = top + jnp.log(jnp.sum(totals * jnp.exp(tops - top), axis=0, keepdims=True))
@@ -196,14 +194,10 @@
 
 
 def call(kernel, shapes, *args, cost=None):
-    def spec(v):
-        small = v.dtype == jnp.int32 and v.size < 32
-        return pl.BlockSpec(memory_space=pltpu.SMEM) if small else pl.BlockSpec()
-
     outs = [jax.ShapeDtypeStruct(s, d) for s, d in shapes]
     result = pl.pallas_call(
         kernel,
-        in_specs=[spec(v) for v in args],
+        in_specs=[pl.BlockSpec() for _ in args],
         out_specs=[pl.BlockSpec() for _ in outs],
         out_shape=outs,
         compiler_params=pltpu.CompilerParams(vmem_limit_bytes=16 << 20),
@@ -225,11 +219,7 @@
     strength,
     token_ids,
 ):
-    r = lax.axis_index("rows")
-    t = lax.axis_index("tensor")
     rows, c_width = token_ids.shape[0], base_head.shape[2]
-    mine = lax.dynamic_slice(jnp.asarray(tables()), (r * (NY * NX) + t, 0), (1, 48))[0]
-    table, source = mine[:32], mine[32:41]
 
     quarter = expert_head.shape[0]
     heads = []
@@ -256,6 +246,7 @@
         sums,
         cost=LONG,
     )
+    strength, normed = together(strength, normed)
     along_z = [("z", 0, k) for k in ALONG_Z]
     got = swap(normed, along_z, (base_head, 0), (base_head, quarter), (expert_head, 0))
     mine = jnp.concatenate([normed, *got])
@@ -269,8 +260,8 @@
     for i in range(4):
         for half in range(2):
             kind = BF if i < 2 else F32
-            part = project(table, strength, acts, heads, 16 * half + 4 * i, half, kind)
-            table, part = together(table, part)
+            part = project(strength, acts, heads, i, half, kind)
+            strength, part = together(strength, part)
             if i < 2:
                 moved[half].append(exchange(part, axes[half][0], 0))
             else:
@@ -278,7 +269,7 @@
         if i == 2:
             totals = [narrow(kept[h][0] + wide(moved[h][0])) for h in range(2)]
             second_step = [exchange(totals[h], axes[h][0], 1) for h in range(2)]
-            table, _ = together(table, totals[1])
+            strength, _ = together(strength, totals[1])
     own = together(kept[0][1], kept[1][1])
     sums = together(*[own[h] + wide(moved[h][1]) for h in range(2)])
     sums = [sums[h] + wide(second_step[h]) for h in range(2)]
@@ -299,10 +290,10 @@
         home.append(exchange(jnp.stack([logits[0, i], other[i]]), "z", by=k))
     home = wide(jnp.concatenate(home))
 
-    stats = call(stats_kernel, [((NY * NX, 8, 128), F32)], source, home, in_hbm(token_ids))
+    stats = call(stats_kernel, [((NY * NX, 8, 128), F32)], home, in_hbm(token_ids))
     stats = lax.all_to_all(stats, "tensor", 0, 0, tiled=True)
     log_probs, picked = call(
-        final_kernel, [((rows, 8 * c_width), F32), ((1, rows), F32)], source, home, stats
+        final_kernel, [((rows, 8 * c_width), F32), ((1, rows), F32)], home, stats
     )
     return log_probs, picked[0]
 

time: 115 us -> 114 us (level)
  blocking collectives: 11.5 us -> 26.3 us
  starting transfers between devices: 29.9 us -> 21.5 us
  Pallas kernels: 26.5 us -> 20.7 us
  local copies, waits for them, and re-layouts: 2.2 us -> 0.99 us
    all_to_all x0 -> x1, blocking collectives: none -> 14.8 us  [shards(): sums = lax.all_to_all(sums, 'tensor', 0, 0, tiled=True)]
    all_to_all x1 -> x0, starting transfers between devices: 7.12 us -> none  [shards(): sums = lax.all_to_all(sums, 'tensor', 0, 0, tiled=True)]
    all_to_all x1 -> x0, waiting for transfers between devices: 6.3 us -> none  [shards(): sums = lax.all_to_all(sums, 'tensor', 0, 0, tiled=True)]
    pallas_call x13, Pallas kernels: 20.9 us -> 15.2 us  [the longest x8 10.4 us: project(): pl.pallas_call(functools.partial(matmul_kernel, step, half), in_specs=[sm...]
    ppermute x20, waiting for transfers between devices: 33.9 us -> 39.2 us  [exchange(): return lax.ppermute(value, AXES, pairs)]
    ppermute x20, starting transfers between devices: 22.7 us -> 21.5 us  [exchange(): return lax.ppermute(value, AXES, pairs)]
  transfers between devices with their start and end apart: 21 -> 20, of which waited for: 15 -> 14; matrix products, arithmetic and copies ran while one was open for 3% -> 2% of each run, Pallas kernels for 16% -> 13%
where the time goes in v9:
time: 114 us
  waiting for transfers between devices  39.2 us (34%)
  blocking collectives  26.3 us (23%)
  starting transfers between devices  21.5 us (19%)
  Pallas kernels  20.7 us (18%)
  other arithmetic  3.23 us (3%)
  between operations  1.62 us (1%)
    ppermute x20, waiting for transfers between devices, exchange(): return lax.ppermute(value, AXES, pairs)  39.2 us
    ppermute x20, starting transfers between devices, exchange(): return lax.ppermute(value, AXES, pairs)  21.5 us
    all_to_all x1, blocking collectives, shards(): sums = lax.all_to_all(sums, 'tensor', 0, 0, tiled=True)  14.8 us
    all_to_all x1, blocking collectives, shards(): stats = lax.all_to_all(stats, 'tensor', 0, 0, tiled=True)  11.5 us
    pallas_call x8, Pallas kernels, project(): pl.pallas_call(functools.partial(matmul_kernel, step, half), in_specs=[sm...  10.4 us
    pallas_call x4, Pallas kernels, relay(): pl.pallas_call(relay_kernel, grid=(count // step,), in_specs=[pl.BlockSpe...  5.57 us
    pallas_call x5, Pallas kernels, call(): pl.pallas_call(kernel, in_specs=[pl.BlockSpec() for _ in args], out_specs...  4.74 us
  transfers between devices with their start and end apart: 20, of which 14 were waited for; matrix products, arithmetic and copies ran while one was open for 2% of the time, Pallas kernels for 13%

profile of v9, /device:TPU:0, one launch (start us, length us, event | category | flops | bytes accessed | tf_op | source)
XLA Modules:
  0.0 113.6 jit_solution(8343485557700272137)
XLA Ops:
  0.6 1.0 shard_map.122
  1.6 14.8 %all_to_all.10.refs_6_ = f32[16,8,128]{2,1,0:T(8,128)S(1)} all-to-all(f32[16,8,128]{2,1,0:T(8,128)S(1)} %shard_map.122), channel_id=1, replica_groups=mesh['rows'=8,'tensor'=16] {'tensor'}, dimensions={0} | all-to-all | bytes 131072 | tf_op jit(solution)/shard_map/all_to_all | solution.py:240
  16.5 1.2 %shard_map.123 = bf16[64,1024]{1,0:T(8,128)(2,1)S(1)} custom-call(bf16[64,512]{1,0:T(8,128)(2,1)} %refs_0_.3, bf16[64,256]{1,0:T(8,128)(2,1)} %refs_1_.3, bf16[64,256]{1,0:T(8,128)(2,1)} %refs_2_.3, bf16[512]{0:T(512)(128)(2,1)} %refs_3_.1, bf16[256]{0:T(256)(128)(2,1)} %refs_4_.1, bf16[256]{0:T(256)(128)(2,1)} %refs_5_.1, f32[16,8,128]{2,1,0:T(8,128)S(1)} %all_to_all.10.refs_6_), custom_call_target="tpu_custom_call" | custom-call | flops 10000000000 | bytes 16777216 | tf_op jit(solution)/shard_map/pallas_call | solution.py:198
  17.7 2.0 %collective-permute-start = (bf16[64,1024]{1,0:T(8,128)(2,1)S(1)}, bf16[64,1024]{1,0:T(8,128)(2,1)S(1)}, u32[]{:S(2)}, u32[]{:S(2)}) collective-permute-start(bf16[64,1024]{1,0:T(8,128)(2,1)S(1)} %shard_map.123), channel_id=1, source_target_pairs={{0,32},{1,33},{2,34},{3,35},{4,36},{5,37},{6,38},{7,39},{8,40},{9,... | collective-permute-start | bytes 393224 | tf_op jit(solution)/shard_map/ppermute | solution.py:42
  19.7 2.5 %collective-permute-start.1 = (bf16[64,1024]{1,0:T(8,128)(2,1)S(1)}, bf16[64,1024]{1,0:T(8,128)(2,1)S(1)}, u32[]{:S(2)}, u32[]{:S(2)}) collective-permute-start(bf16[64,1024]{1,0:T(8,128)(2,1)S(1)} %shard_map.123), channel_id=1, source_target_pairs={{0,96},{1,97},{2,98},{3,99},{4,100},{5,101},{6,102},{7,103},{8,104... | collective-permute-start | bytes 393224 | tf_op jit(solution)/shard_map/ppermute | solution.py:42
  22.3 1.1 collective-permute-start.2
  23.3 1.4 %shard_map.124.wb0 = bf16[16,256,512]{2,1,0:T(8,128)(2,1)S(1)} custom-call(bf16[512,16,512]{2,1,0:T(8,128)(2,1)S(1)} %bitcast.58), custom_call_target="tpu_custom_call" | custom-call | bytes 8388608 | tf_op jit(solution)/shard_map/pallas_call | solution.py:61
  24.7 1.4 %shard_map.125.wb1 = bf16[16,256,512]{2,1,0:T(8,128)(2,1)S(1)} custom-call(bf16[512,16,512]{2,1,0:T(8,128)(2,1)S(1)} %bitcast.58), custom_call_target="tpu_custom_call" | custom-call | bytes 8388608 | tf_op jit(solution)/shard_map/pallas_call | solution.py:61
  26.1 0.8 copy-done
  26.9 1.4 %shard_map.126.we = bf16[16,256,512]{2,1,0:T(8,128)(2,1)S(1)} custom-call(bf16[256,16,512]{2,1,0:T(8,128)(2,1)S(1)} %copy-done), custom_call_target="tpu_custom_call" | custom-call | bytes 8388608 | tf_op jit(solution)/shard_map/pallas_call | solution.py:61
  28.3 0.4 collective-permute-done.2
  29.5 1.4 %shard_map.127.wa = bf16[16,256,512]{2,1,0:T(8,128)(2,1)S(1)} custom-call(bf16[256,16,512]{2,1,0:T(8,128)(2,1)S(1)} %copy-done.1), custom_call_target="tpu_custom_call" | custom-call | bytes 8388608 | tf_op jit(solution)/shard_map/pallas_call | solution.py:61
  31.0 1.3 %shard_map.129 = bf16[4,512,256]{2,1,0:T(8,128)(2,1)S(1)} custom-call(f32[1]{0:T(128)S(6)} %copy.20.alpha, bf16[512,1024]{1,0:T(8,128)(2,1)S(1)} %shard_map.128.acts, bf16[16,256,512]{2,1,0:T(8,128)(2,1)S(1)} %shard_map.124.wb0, bf16[16,256,512]{2,1,0:T(8,128)(2,1)S(1)} %shard_map.125.wb1, bf16[16,256,512]{2,1,0:T(8,128)(2,1)S(1)} %shard_map.126.we, ...), custom_call_target="tpu_custom_call" | custom-call | flops 1 | bytes 1 | tf_op jit(solution)/shard_map/pallas_call | solution.py:95
  32.4 0.6 collective-permute-start.7
  33.0 1.3 %shard_map.130 = bf16[4,512,256]{2,1,0:T(8,128)(2,1)S(1)} custom-call(f32[1]{0:T(128)S(6)} %copy.20.alpha, bf16[512,1024]{1,0:T(8,128)(2,1)S(1)} %shard_map.128.acts, bf16[16,256,512]{2,1,0:T(8,128)(2,1)S(1)} %shard_map.124.wb0, bf16[16,256,512]{2,1,0:T(8,128)(2,1)S(1)} %shard_map.125.wb1, bf16[16,256,512]{2,1,0:T(8,128)(2,1)S(1)} %shard_map.126.we, ...), custom_call_target="tpu_custom_call" | custom-call | flops 1 | bytes 1 | tf_op jit(solution)/shard_map/pallas_call | solution.py:95
  34.3 0.6 collective-permute-start.4
  34.9 1.3 %shard_map.131 = bf16[4,512,256]{2,1,0:T(8,128)(2,1)S(1)} custom-call(f32[1]{0:T(128)S(6)} %copy.20.alpha, bf16[512,1024]{1,0:T(8,128)(2,1)S(1)} %shard_map.128.acts, bf16[16,256,512]{2,1,0:T(8,128)(2,1)S(1)} %shard_map.124.wb0, bf16[16,256,512]{2,1,0:T(8,128)(2,1)S(1)} %shard_map.125.wb1, bf16[16,256,512]{2,1,0:T(8,128)(2,1)S(1)} %shard_map.126.we, ...), custom_call_target="tpu_custom_call" | custom-call | flops 1 | bytes 1 | tf_op jit(solution)/shard_map/pallas_call | solution.py:95
  36.2 1.5 %collective-permute-start.5 = (bf16[4,512,256]{2,1,0:T(8,128)(2,1)S(1)}, bf16[4,512,256]{2,1,0:T(8,128)(2,1)S(1)}, u32[]{:S(2)}, u32[]{:S(2)}) collective-permute-start(bf16[4,512,256]{2,1,0:T(8,128)(2,1)S(1)} %shard_map.131), channel_id=1, source_target_pairs={{0,1},{1,0},{2,3},{3,2},{4,5},{5,4},{6,7},{7,6},{8,9},{9,8},{10,11... | collective-permute-start | bytes 3145736 | tf_op jit(solution)/shard_map/ppermute | solution.py:42
  37.8 1.3 %shard_map.132 = bf16[4,512,256]{2,1,0:T(8,128)(2,1)S(1)} custom-call(f32[1]{0:T(128)S(6)} %copy.20.alpha, bf16[512,1024]{1,0:T(8,128)(2,1)S(1)} %shard_map.128.acts, bf16[16,256,512]{2,1,0:T(8,128)(2,1)S(1)} %shard_map.124.wb0, bf16[16,256,512]{2,1,0:T(8,128)(2,1)S(1)} %shard_map.125.wb1, bf16[16,256,512]{2,1,0:T(8,128)(2,1)S(1)} %shard_map.126.we, ...), custom_call_target="tpu_custom_call" | custom-call | flops 1 | bytes 1 | tf_op jit(solution)/shard_map/pallas_call | solution.py:95
  39.1 1.6 %collective-permute-start.6 = (bf16[4,512,256]{2,1,0:T(8,128)(2,1)S(1)}, bf16[4,512,256]{2,1,0:T(8,128)(2,1)S(1)}, u32[]{:S(2)}, u32[]{:S(2)}) collective-permute-start(bf16[4,512,256]{2,1,0:T(8,128)(2,1)S(1)} %shard_map.132), channel_id=1, source_target_pairs={{0,4},{1,5},{2,6},{3,7},{4,0},{5,1},{6,2},{7,3},{8,12},{9,13},{10,... | collective-permute-start | bytes 3145736 | tf_op jit(solution)/shard_map/ppermute | solution.py:42
  40.7 1.3 %shard_map.133 = f32[4,512,256]{2,1,0:T(8,128)S(1)} custom-call(f32[1]{0:T(128)S(6)} %copy.20.alpha, bf16[512,1024]{1,0:T(8,128)(2,1)S(1)} %shard_map.128.acts, bf16[16,256,512]{2,1,0:T(8,128)(2,1)S(1)} %shard_map.124.wb0, bf16[16,256,512]{2,1,0:T(8,128)(2,1)S(1)} %shard_map.125.wb1, bf16[16,256,512]{2,1,0:T(8,128)(2,1)S(1)} %shard_map.126.we, ...), custom_call_target="tpu_custom_call" | custom-call | flops 1 | bytes 1 | tf_op jit(solution)/shard_map/pallas_call | solution.py:95
  42.0 5.3 %collective-permute-done.7 = bf16[4,512,256]{2,1,0:T(8,128)(2,1)S(1)} collective-permute-done((bf16[4,512,256]{2,1,0:T(8,128)(2,1)S(1)}, bf16[4,512,256]{2,1,0:T(8,128)(2,1)S(1)}, u32[]{:S(2)}, u32[]{:S(2)}) %collective-permute-start.7) | collective-permute-done | bytes 1048608 | tf_op jit(solution)/shard_map/ppermute | solution.py:42
  47.2 0.4 multiply_convert_fusion
  47.7 1.4 %collective-permute-start.8 = (f16[4,512,256]{2,1,0:T(8,128)(2,1)S(1)}, f16[4,512,256]{2,1,0:T(8,128)(2,1)S(1)}, u32[]{:S(2)}, u32[]{:S(2)}) collective-permute-start(f16[4,512,256]{2,1,0:T(8,128)(2,1)S(1)} %multiply_convert_fusion), channel_id=1, source_target_pairs={{0,3},{1,2},{2,1},{3,0},{4,7},{5,6},{6,5},{7,4},{8,11},{9,10},{10,... | collective-permute-start | bytes 3145736 | tf_op jit(solution)/shard_map/ppermute | solution.py:42
  49.1 1.3 %shard_map.134 = f32[4,512,256]{2,1,0:T(8,128)S(1)} custom-call(f32[1]{0:T(128)S(6)} %copy.20.alpha, bf16[512,1024]{1,0:T(8,128)(2,1)S(1)} %shard_map.128.acts, bf16[16,256,512]{2,1,0:T(8,128)(2,1)S(1)} %shard_map.124.wb0, bf16[16,256,512]{2,1,0:T(8,128)(2,1)S(1)} %shard_map.125.wb1, bf16[16,256,512]{2,1,0:T(8,128)(2,1)S(1)} %shard_map.126.we, ...), custom_call_target="tpu_custom_call" | custom-call | flops 1 | bytes 1 | tf_op jit(solution)/shard_map/pallas_call | solution.py:95
  50.4 1.3 %shard_map.135 = f32[4,512,256]{2,1,0:T(8,128)S(1)} custom-call(f32[1]{0:T(128)S(6)} %copy.20.alpha, bf16[512,1024]{1,0:T(8,128)(2,1)S(1)} %shard_map.128.acts, bf16[16,256,512]{2,1,0:T(8,128)(2,1)S(1)} %shard_map.124.wb0, bf16[16,256,512]{2,1,0:T(8,128)(2,1)S(1)} %shard_map.125.wb1, bf16[16,256,512]{2,1,0:T(8,128)(2,1)S(1)} %shard_map.126.we, ...), custom_call_target="tpu_custom_call" | custom-call | flops 1 | bytes 1 | tf_op jit(solution)/shard_map/pallas_call | solution.py:95
  51.7 1.3 %shard_map.136 = f32[4,512,256]{2,1,0:T(8,128)S(1)} custom-call(f32[1]{0:T(128)S(6)} %copy.20.alpha, bf16[512,1024]{1,0:T(8,128)(2,1)S(1)} %shard_map.128.acts, bf16[16,256,512]{2,1,0:T(8,128)(2,1)S(1)} %shard_map.124.wb0, bf16[16,256,512]{2,1,0:T(8,128)(2,1)S(1)} %shard_map.125.wb1, bf16[16,256,512]{2,1,0:T(8,128)(2,1)S(1)} %shard_map.126.we, ...), custom_call_target="tpu_custom_call" | custom-call | flops 1 | bytes 1 | tf_op jit(solution)/shard_map/pallas_call | solution.py:95
  53.0 0.4 multiply_convert_fusion.1
  53.5 1.2 %collective-permute-start.12 = (f16[4,512,256]{2,1,0:T(8,128)(2,1)S(1)}, f16[4,512,256]{2,1,0:T(8,128)(2,1)S(1)}, u32[]{:S(2)}, u32[]{:S(2)}) collective-permute-start(f16[4,512,256]{2,1,0:T(8,128)(2,1)S(1)} %multiply_convert_fusion.1), channel_id=1, source_target_pairs={{0,12},{1,13},{2,14},{3,15},{4,8},{5,9},{6,10},{7,11},{8,4},{9,5},... | collective-permute-start | bytes 3145736 | tf_op jit(solution)/shard_map/ppermute | solution.py:42
  54.7 11.1 %collective-permute-done.5 = bf16[4,512,256]{2,1,0:T(8,128)(2,1)S(1)} collective-permute-done((bf16[4,512,256]{2,1,0:T(8,128)(2,1)S(1)}, bf16[4,512,256]{2,1,0:T(8,128)(2,1)S(1)}, u32[]{:S(2)}, u32[]{:S(2)}) %collective-permute-start.5) | collective-permute-done | bytes 1048608 | tf_op jit(solution)/shard_map/ppermute | solution.py:42
  65.8 0.3 convert_add_fusion.1
  66.1 0.3 convert_add_fusion
  66.4 4.1 %collective-permute-done.8 = f16[4,512,256]{2,1,0:T(8,128)(2,1)S(1)} collective-permute-done((f16[4,512,256]{2,1,0:T(8,128)(2,1)S(1)}, f16[4,512,256]{2,1,0:T(8,128)(2,1)S(1)}, u32[]{:S(2)}, u32[]{:S(2)}) %collective-permute-start.8) | collective-permute-done | bytes 1048608 | tf_op jit(solution)/shard_map/ppermute | solution.py:42
  70.5 0.3 multiply_add_fusion.1
  70.8 0.1 fusion.18
  70.9 0.6 collective-permute-start.10
  71.5 1.2 %collective-permute-done.12 = f16[4,512,256]{2,1,0:T(8,128)(2,1)S(1)} collective-permute-done((f16[4,512,256]{2,1,0:T(8,128)(2,1)S(1)}, f16[4,512,256]{2,1,0:T(8,128)(2,1)S(1)}, u32[]{:S(2)}, u32[]{:S(2)}) %collective-permute-start.12) | collective-permute-done | bytes 1048608 | tf_op jit(solution)/shard_map/ppermute | solution.py:42
  72.7 0.3 multiply_add_fusion
  73.0 0.1 fusion.20
  73.1 0.2 collective-permute-start.14
  73.3 0.3 collective-permute-start.9
  73.6 3.8 %collective-permute-done.10 = f16[512,256]{1,0:T(8,128)(2,1)S(1)} collective-permute-done((f16[512,256]{1,0:T(8,128)(2,1)S(1)}, f16[512,256]{1,0:T(8,128)(2,1)S(1)}, u32[]{:S(2)}, u32[]{:S(2)}) %collective-permute-start.10) | collective-permute-done | bytes 262176 | tf_op jit(solution)/shard_map/ppermute | solution.py:42
  77.4 0.1 fusion.12
  77.5 1.2 %collective-permute-start.11 = (f16[512,256]{1,0:T(8,128)(2,1)S(1)}, f16[512,256]{1,0:T(8,128)(2,1)S(1)}, u32[]{:S(2)}, u32[]{:S(2)}) collective-permute-start(f16[512,256]{1,0:T(8,128)(2,1)S(1)} %fusion.12), channel_id=1, source_target_pairs={{0,12},{1,13},{2,14},{3,15},{4,8},{5,9},{6,10},{7,11},{8,4},{9,5},... | collective-permute-start | bytes 786440 | tf_op jit(solution)/shard_map/ppermute | solution.py:42
  78.7 0.9 collective-permute-done.14
  79.6 0.1 fusion.3
  79.7 2.1 %collective-permute-start.15 = (f16[512,256]{1,0:T(8,128)(2,1)S(1)}, f16[512,256]{1,0:T(8,128)(2,1)S(1)}, u32[]{:S(2)}, u32[]{:S(2)}) collective-permute-start(f16[512,256]{1,0:T(8,128)(2,1)S(1)} %fusion.3), channel_id=1, source_target_pairs={{0,3},{1,2},{2,1},{3,0},{4,7},{5,6},{6,5},{7,4},{8,11},{9,10},{10,... | collective-permute-start | bytes 786440 | tf_op jit(solution)/shard_map/ppermute | solution.py:42
  81.8 3.3 %collective-permute-done.11 = f16[512,256]{1,0:T(8,128)(2,1)S(1)} collective-permute-done((f16[512,256]{1,0:T(8,128)(2,1)S(1)}, f16[512,256]{1,0:T(8,128)(2,1)S(1)}, u32[]{:S(2)}, u32[]{:S(2)}) %collective-permute-start.11) | collective-permute-done | bytes 262176 | tf_op jit(solution)/shard_map/ppermute | solution.py:42
  85.1 0.2 fusion.17
  85.3 1.8 %collective-permute-done.13 = f16[512,256]{1,0:T(8,128)(2,1)S(1)} collective-permute-done((f16[512,256]{1,0:T(8,128)(2,1)S(1)}, f16[512,256]{1,0:T(8,128)(2,1)S(1)}, u32[]{:S(2)}, u32[]{:S(2)}) %collective-permute-start.13) | collective-permute-done | bytes 262176 | tf_op jit(solution)/shard_map/ppermute | solution.py:42
  87.1 0.3 collective-permute-done.15
  87.3 0.2 fusion.8
  87.6 0.1 pad_maximum_fusion
  87.9 1.5 %collective-permute-done.16 = f16[4,64,512]{2,1,0:T(8,128)(2,1)S(1)} collective-permute-done((f16[4,64,512]{2,1,0:T(8,128)(2,1)S(1)}, f16[4,64,512]{2,1,0:T(8,128)(2,1)S(1)}, u32[]{:S(2)}, u32[]{:S(2)}) %collective-permute-start.16) | collective-permute-done | bytes 262176 | tf_op jit(solution)/shard_map/ppermute | solution.py:42
  89.4 2.2 %collective-permute-start.17 = (f16[2,64,512]{2,1,0:T(8,128)(2,1)S(1)}, f16[2,64,512]{2,1,0:T(8,128)(2,1)S(1)}, u32[]{:S(2)}, u32[]{:S(2)}) collective-permute-start(f16[2,64,512]{2,1,0:T(8,128)(2,1)S(1)} %pad_maximum_fusion.1), channel_id=1, source_target_pairs={{0,64},{1,65},{2,66},{3,67},{4,68},{5,69},{6,70},{7,71},{8,72},{9,... | collective-permute-start | bytes 393224 | tf_op jit(solution)/shard_map/ppermute | solution.py:42
  91.6 1.1 collective-permute-start.18
  92.8 1.1 collective-permute-start.19
  93.8 3.5 %collective-permute-done.17 = f16[2,64,512]{2,1,0:T(8,128)(2,1)S(1)} collective-permute-done((f16[2,64,512]{2,1,0:T(8,128)(2,1)S(1)}, f16[2,64,512]{2,1,0:T(8,128)(2,1)S(1)}, u32[]{:S(2)}, u32[]{:S(2)}) %collective-permute-start.17) | collective-permute-done | bytes 131104 | tf_op jit(solution)/shard_map/ppermute | solution.py:42
  97.4 1.6 %collective-permute-done.18 = f16[2,64,512]{2,1,0:T(8,128)(2,1)S(1)} collective-permute-done((f16[2,64,512]{2,1,0:T(8,128)(2,1)S(1)}, f16[2,64,512]{2,1,0:T(8,128)(2,1)S(1)}, u32[]{:S(2)}, u32[]{:S(2)}) %collective-permute-start.18) | collective-permute-done | bytes 131104 | tf_op jit(solution)/shard_map/ppermute | solution.py:42
  99.0 0.6 collective-permute-done.19
  99.6 0.1 convert_multiply_fusion.home
  99.8 1.2 %shard_map.137 = f32[16,8,128]{2,1,0:T(8,128)S(1)} custom-call(f32[8,64,512]{2,1,0:T(8,128)S(1)} %convert_multiply_fusion.home, s32[64]{0:T(128)} %ids.1), custom_call_target="tpu_custom_call" | custom-call | tf_op jit(solution)/shard_map/pallas_call | solution.py:198
  100.9 11.5 %all_to_all.11.stats = f32[16,8,128]{2,1,0:T(8,128)S(1)} all-to-all(f32[16,8,128]{2,1,0:T(8,128)S(1)} %shard_map.137), channel_id=1, replica_groups=mesh['rows'=8,'tensor'=16] {'tensor'}, dimensions={0} | all-to-all | bytes 131072 | tf_op jit(solution)/shard_map/all_to_all | solution.py:294
  112.4 1.2 %shard_map.138 = (f32[64,4096]{1,0:T(8,128)}, f32[1,64]{1,0:T(1,128)}) custom-call(f32[8,64,512]{2,1,0:T(8,128)S(1)} %convert_multiply_fusion.home, f32[16,8,128]{2,1,0:T(8,128)S(1)} %all_to_all.11.stats), custom_call_target="tpu_custom_call" | custom-call | tf_op jit(solution)/shard_map/pallas_call | solution.py:198
  (32 shorter events, 0.7 us)
Async XLA Ops:
  1.6 21.7 %slice-start = ((s8[8388608]{0:T(1024)(128)(4,1)}), s8[4194304]{0:T(1024)(128)(4,1)S(1)}, s32[]{:S(2)}) async-start(s8[8388608]{0:T(1024)(128)(4,1)} %bitcast.57), calls=%async_computation.2 | async-start | bytes 8388608
  16.5 6.8 %slice-start.1 = ((s8[8388608]{0:T(1024)(128)(4,1)}), s8[4194304]{0:T(1024)(128)(4,1)S(1)}, s32[]{:S(2)}) async-start(s8[8388608]{0:T(1024)(128)(4,1)} %bitcast.57), calls=%async_computation.3 | async-start | bytes 8388608
  17.7 10.6 %collective-permute-start = (bf16[64,1024]{1,0:T(8,128)(2,1)S(1)}, bf16[64,1024]{1,0:T(8,128)(2,1)S(1)}, u32[]{:S(2)}, u32[]{:S(2)}) collective-permute-start(bf16[64,1024]{1,0:T(8,128)(2,1)S(1)} %shard_map.123), channel_id=1, source_target_pairs={{0,32},{1,33},{2,34},{3,35},{4,36},{5,37},{6,38},{7,39},{8,40},{9,... | collective-permute-start | bytes 393224 | tf_op jit(solution)/shard_map/ppermute | solution.py:42
  19.7 8.6 %collective-permute-start.1 = (bf16[64,1024]{1,0:T(8,128)(2,1)S(1)}, bf16[64,1024]{1,0:T(8,128)(2,1)S(1)}, u32[]{:S(2)}, u32[]{:S(2)}) collective-permute-start(bf16[64,1024]{1,0:T(8,128)(2,1)S(1)} %shard_map.123), channel_id=1, source_target_pairs={{0,96},{1,97},{2,98},{3,99},{4,100},{5,101},{6,102},{7,103},{8,104... | collective-permute-start | bytes 393224 | tf_op jit(solution)/shard_map/ppermute | solution.py:42
  22.3 6.5 %collective-permute-start.2 = (bf16[64,1024]{1,0:T(8,128)(2,1)S(1)}, bf16[64,1024]{1,0:T(8,128)(2,1)S(1)}, u32[]{:S(2)}, u32[]{:S(2)}) collective-permute-start(bf16[64,1024]{1,0:T(8,128)(2,1)S(1)} %shard_map.123), channel_id=1, source_target_pairs={{0,64},{1,65},{2,66},{3,67},{4,68},{5,69},{6,70},{7,71},{8,72},{9,... | collective-permute-start | bytes 393224 | tf_op jit(solution)/shard_map/ppermute | solution.py:42
  24.7 2.2 %copy-start = (bf16[256,16,512]{2,1,0:T(8,128)(2,1)S(1)}, bf16[256,16,512]{2,1,0:T(8,128)(2,1)}, u32[]{:S(2)}) copy-start(bf16[256,16,512]{2,1,0:T(8,128)(2,1)} %head.2) | copy-start | bytes 12582916
  26.9 2.6 %copy-start.1 = (bf16[256,16,512]{2,1,0:T(8,128)(2,1)S(1)}, bf16[256,16,512]{2,1,0:T(8,128)(2,1)}, u32[]{:S(2)}) copy-start(bf16[256,16,512]{2,1,0:T(8,128)(2,1)} %head.3) | copy-start | bytes 12582916
  28.8 2.2 %collective-permute-start.3 = (bf16[256,1024]{1,0:T(8,128)(2,1)S(1)}, bf16[256,1024]{1,0:T(8,128)(2,1)S(1)}, u32[]{:S(2)}, u32[]{:S(2)}) collective-permute-start(bf16[256,1024]{1,0:T(8,128)(2,1)S(1)} %constant_dynamic-update-slice_fusion.refs_0_), channel_id=1, source_target_pairs={{0,16},{1,17},{2,18},{3,19},{4,20},{5,21},{6,22},{7,23},{8,24},{9,... | collective-permute-start | bytes 1572872 | tf_op jit(solution)/shard_map/ppermute | solution.py:42
  32.4 14.9 %collective-permute-start.7 = (bf16[4,512,256]{2,1,0:T(8,128)(2,1)S(1)}, bf16[4,512,256]{2,1,0:T(8,128)(2,1)S(1)}, u32[]{:S(2)}, u32[]{:S(2)}) collective-permute-start(bf16[4,512,256]{2,1,0:T(8,128)(2,1)S(1)} %shard_map.129), channel_id=1, source_target_pairs={{0,1},{1,0},{2,3},{3,2},{4,5},{5,4},{6,7},{7,6},{8,9},{9,8},{10,11... | collective-permute-start | bytes 3145736 | tf_op jit(solution)/shard_map/ppermute | solution.py:42
  34.3 18.7 %collective-permute-start.4 = (bf16[4,512,256]{2,1,0:T(8,128)(2,1)S(1)}, bf16[4,512,256]{2,1,0:T(8,128)(2,1)S(1)}, u32[]{:S(2)}, u32[]{:S(2)}) collective-permute-start(bf16[4,512,256]{2,1,0:T(8,128)(2,1)S(1)} %shard_map.130), channel_id=1, source_target_pairs={{0,4},{1,5},{2,6},{3,7},{4,0},{5,1},{6,2},{7,3},{8,12},{9,13},{10,... | collective-permute-start | bytes 3145736 | tf_op jit(solution)/shard_map/ppermute | solution.py:42
  36.2 29.6 %collective-permute-start.5 = (bf16[4,512,256]{2,1,0:T(8,128)(2,1)S(1)}, bf16[4,512,256]{2,1,0:T(8,128)(2,1)S(1)}, u32[]{:S(2)}, u32[]{:S(2)}) collective-permute-start(bf16[4,512,256]{2,1,0:T(8,128)(2,1)S(1)} %shard_map.131), channel_id=1, source_target_pairs={{0,1},{1,0},{2,3},{3,2},{4,5},{5,4},{6,7},{7,6},{8,9},{9,8},{10,11... | collective-permute-start | bytes 3145736 | tf_op jit(solution)/shard_map/ppermute | solution.py:42
  39.1 27.0 %collective-permute-start.6 = (bf16[4,512,256]{2,1,0:T(8,128)(2,1)S(1)}, bf16[4,512,256]{2,1,0:T(8,128)(2,1)S(1)}, u32[]{:S(2)}, u32[]{:S(2)}) collective-permute-start(bf16[4,512,256]{2,1,0:T(8,128)(2,1)S(1)} %shard_map.132), channel_id=1, source_target_pairs={{0,4},{1,5},{2,6},{3,7},{4,0},{5,1},{6,2},{7,3},{8,12},{9,13},{10,... | collective-permute-start | bytes 3145736 | tf_op jit(solution)/shard_map/ppermute | solution.py:42
  47.7 22.8 %collective-permute-start.8 = (f16[4,512,256]{2,1,0:T(8,128)(2,1)S(1)}, f16[4,512,256]{2,1,0:T(8,128)(2,1)S(1)}, u32[]{:S(2)}, u32[]{:S(2)}) collective-permute-start(f16[4,512,256]{2,1,0:T(8,128)(2,1)S(1)} %multiply_convert_fusion), channel_id=1, source_target_pairs={{0,3},{1,2},{2,1},{3,0},{4,7},{5,6},{6,5},{7,4},{8,11},{9,10},{10,... | collective-permute-start | bytes 3145736 | tf_op jit(solution)/shard_map/ppermute | solution.py:42
  53.5 19.3 %collective-permute-start.12 = (f16[4,512,256]{2,1,0:T(8,128)(2,1)S(1)}, f16[4,512,256]{2,1,0:T(8,128)(2,1)S(1)}, u32[]{:S(2)}, u32[]{:S(2)}) collective-permute-start(f16[4,512,256]{2,1,0:T(8,128)(2,1)S(1)} %multiply_convert_fusion.1), channel_id=1, source_target_pairs={{0,12},{1,13},{2,14},{3,15},{4,8},{5,9},{6,10},{7,11},{8,4},{9,5},... | collective-permute-start | bytes 3145736 | tf_op jit(solution)/shard_map/ppermute | solution.py:42
  70.9 6.5 %collective-permute-start.10 = (f16[512,256]{1,0:T(8,128)(2,1)S(1)}, f16[512,256]{1,0:T(8,128)(2,1)S(1)}, u32[]{:S(2)}, u32[]{:S(2)}) collective-permute-start(f16[512,256]{1,0:T(8,128)(2,1)S(1)} %get-tuple-element.79), channel_id=1, source_target_pairs={{0,4},{1,5},{2,6},{3,7},{4,0},{5,1},{6,2},{7,3},{8,12},{9,13},{10,... | collective-permute-start | bytes 786440 | tf_op jit(solution)/shard_map/ppermute | solution.py:42
  73.1 6.5 %collective-permute-start.14 = (f16[512,256]{1,0:T(8,128)(2,1)S(1)}, f16[512,256]{1,0:T(8,128)(2,1)S(1)}, u32[]{:S(2)}, u32[]{:S(2)}) collective-permute-start(f16[512,256]{1,0:T(8,128)(2,1)S(1)} %get-tuple-element.81), channel_id=1, source_target_pairs={{0,1},{1,0},{2,3},{3,2},{4,5},{5,4},{6,7},{7,6},{8,9},{9,8},{10,11... | collective-permute-start | bytes 786440 | tf_op jit(solution)/shard_map/ppermute | solution.py:42
  73.3 8.5 %collective-permute-start.9 = (f16[512,256]{1,0:T(8,128)(2,1)S(1)}, f16[512,256]{1,0:T(8,128)(2,1)S(1)}, u32[]{:S(2)}, u32[]{:S(2)}) collective-permute-start(f16[512,256]{1,0:T(8,128)(2,1)S(1)} %get-tuple-element.78), channel_id=1, source_target_pairs={{0,4},{1,5},{2,6},{3,7},{4,0},{5,1},{6,2},{7,3},{8,12},{9,13},{10,... | collective-permute-start | bytes 786440 | tf_op jit(solution)/shard_map/ppermute | solution.py:42
  77.5 7.7 %collective-permute-start.11 = (f16[512,256]{1,0:T(8,128)(2,1)S(1)}, f16[512,256]{1,0:T(8,128)(2,1)S(1)}, u32[]{:S(2)}, u32[]{:S(2)}) collective-permute-start(f16[512,256]{1,0:T(8,128)(2,1)S(1)} %fusion.12), channel_id=1, source_target_pairs={{0,12},{1,13},{2,14},{3,15},{4,8},{5,9},{6,10},{7,11},{8,4},{9,5},... | collective-permute-start | bytes 786440 | tf_op jit(solution)/shard_map/ppermute | solution.py:42
  78.7 8.4 %collective-permute-start.13 = (f16[512,256]{1,0:T(8,128)(2,1)S(1)}, f16[512,256]{1,0:T(8,128)(2,1)S(1)}, u32[]{:S(2)}, u32[]{:S(2)}) collective-permute-start(f16[512,256]{1,0:T(8,128)(2,1)S(1)} %get-tuple-element.80), channel_id=1, source_target_pairs={{0,1},{1,0},{2,3},{3,2},{4,5},{5,4},{6,7},{7,6},{8,9},{9,8},{10,11... | collective-permute-start | bytes 786440 | tf_op jit(solution)/shard_map/ppermute | solution.py:42
  79.7 7.7 %collective-permute-start.15 = (f16[512,256]{1,0:T(8,128)(2,1)S(1)}, f16[512,256]{1,0:T(8,128)(2,1)S(1)}, u32[]{:S(2)}, u32[]{:S(2)}) collective-permute-start(f16[512,256]{1,0:T(8,128)(2,1)S(1)} %fusion.3), channel_id=1, source_target_pairs={{0,3},{1,2},{2,1},{3,0},{4,7},{5,6},{6,5},{7,4},{8,11},{9,10},{10,... | collective-permute-start | bytes 786440 | tf_op jit(solution)/shard_map/ppermute | solution.py:42
  87.7 1.6 %collective-permute-start.16 = (f16[4,64,512]{2,1,0:T(8,128)(2,1)S(1)}, f16[4,64,512]{2,1,0:T(8,128)(2,1)S(1)}, u32[]{:S(2)}, u32[]{:S(2)}) collective-permute-start(f16[4,64,512]{2,1,0:T(8,128)(2,1)S(1)} %bitcast.61), channel_id=1, source_target_pairs={{0,16},{1,17},{2,18},{3,19},{4,20},{5,21},{6,22},{7,23},{8,24},{9,... | collective-permute-start | bytes 786440 | tf_op jit(solution)/shard_map/ppermute | solution.py:42
  89.4 7.9 %collective-permute-start.17 = (f16[2,64,512]{2,1,0:T(8,128)(2,1)S(1)}, f16[2,64,512]{2,1,0:T(8,128)(2,1)S(1)}, u32[]{:S(2)}, u32[]{:S(2)}) collective-permute-start(f16[2,64,512]{2,1,0:T(8,128)(2,1)S(1)} %pad_maximum_fusion.1), channel_id=1, source_target_pairs={{0,64},{1,65},{2,66},{3,67},{4,68},{5,69},{6,70},{7,71},{8,72},{9,... | collective-permute-start | bytes 393224 | tf_op jit(solution)/shard_map/ppermute | solution.py:42
  91.6 7.3 %collective-permute-start.18 = (f16[2,64,512]{2,1,0:T(8,128)(2,1)S(1)}, f16[2,64,512]{2,1,0:T(8,128)(2,1)S(1)}, u32[]{:S(2)}, u32[]{:S(2)}) collective-permute-start(f16[2,64,512]{2,1,0:T(8,128)(2,1)S(1)} %pad_maximum_fusion.2), channel_id=1, source_target_pairs={{0,32},{1,33},{2,34},{3,35},{4,36},{5,37},{6,38},{7,39},{8,40},{9,... | collective-permute-start | bytes 393224 | tf_op jit(solution)/shard_map/ppermute | solution.py:42
  92.8 6.8 %collective-permute-start.19 = (f16[2,64,512]{2,1,0:T(8,128)(2,1)S(1)}, f16[2,64,512]{2,1,0:T(8,128)(2,1)S(1)}, u32[]{:S(2)}, u32[]{:S(2)}) collective-permute-start(f16[2,64,512]{2,1,0:T(8,128)(2,1)S(1)} %pad_maximum_fusion.3), channel_id=1, source_target_pairs={{0,96},{1,97},{2,98},{3,99},{4,100},{5,101},{6,102},{7,103},{8,104... | collective-permute-start | bytes 393224 | tf_op jit(solution)/shard_map/ppermute | solution.py:42

commit v10 on v9

--- a/solution.py
+++ b/solution.py
@@ -261,7 +261,7 @@
         for half in range(2):
             kind = BF if i < 2 else F32
             part = project(strength, acts, heads, i, half, kind)
-            strength, part = together(strength, part)
+            acts, part = together(acts, part)
             if i < 2:
                 moved[half].append(exchange(part, axes[half][0], 0))
             else:
@@ -269,7 +269,7 @@
         if i == 2:
             totals = [narrow(kept[h][0] + wide(moved[h][0])) for h in range(2)]
             second_step = [exchange(totals[h], axes[h][0], 1) for h in range(2)]
-            strength, _ = together(strength, totals[1])
+            acts, _ = together(acts, totals[1])
     own = together(kept[0][1], kept[1][1])
     sums = together(*[own[h] + wide(moved[h][1]) for h in range(2)])
     sums = [sums[h] + wide(second_step[h]) for h in range(2)]

time: 114 us -> 114 us (level)
  transfers between devices with their start and end apart: 20 -> 20, of which waited for: 14 -> 15; matrix products, arithmetic and copies ran while one was open for 2% -> 3% of each run, Pallas kernels for 13% -> 13%
where the time goes in v10:
time: 114 us; the launch traced here: 113 us
  waiting for transfers between devices  39.2 us (34%)
  blocking collectives  26.3 us (23%)
  starting transfers between devices  21.1 us (19%)
  Pallas kernels  20.7 us (18%)
  other arithmetic  3.34 us (3%)
  between operations  1.62 us (1%)
    ppermute x20, waiting for transfers between devices, exchange(): return lax.ppermute(value, AXES, pairs)  39.2 us
    ppermute x20, starting transfers between devices, exchange(): return lax.ppermute(value, AXES, pairs)  21.1 us
    all_to_all x1, blocking collectives, shards(): sums = lax.all_to_all(sums, 'tensor', 0, 0, tiled=True)  14.8 us
    all_to_all x1, blocking collectives, shards(): stats = lax.all_to_all(stats, 'tensor', 0, 0, tiled=True)  11.5 us
    pallas_call x8, Pallas kernels, project(): pl.pallas_call(functools.partial(matmul_kernel, step, half), in_specs=[sm...  10.4 us
    pallas_call x4, Pallas kernels, relay(): pl.pallas_call(relay_kernel, grid=(count // step,), in_specs=[pl.BlockSpe...  5.57 us
    pallas_call x5, Pallas kernels, call(): pl.pallas_call(kernel, in_specs=[pl.BlockSpec() for _ in args], out_specs...  4.74 us
  transfers between devices with their start and end apart: 20, of which 15 were waited for; matrix products, arithmetic and copies ran while one was open for 3% of the time, Pallas kernels for 13%

profile of v10, /device:TPU:0, one launch (start us, length us, event | category | flops | bytes accessed | tf_op | source)
XLA Modules:
  0.0 113.3 jit_solution(12667941321475052330)
XLA Ops:
  0.6 1.0 shard_map.122
  1.6 14.8 %all_to_all.10.refs_6_ = f32[16,8,128]{2,1,0:T(8,128)S(1)} all-to-all(f32[16,8,128]{2,1,0:T(8,128)S(1)} %shard_map.122), channel_id=1, replica_groups=mesh['rows'=8,'tensor'=16] {'tensor'}, dimensions={0} | all-to-all | bytes 131072 | tf_op jit(solution)/shard_map/all_to_all | solution.py:240
  16.5 1.2 %shard_map.123 = bf16[64,1024]{1,0:T(8,128)(2,1)S(1)} custom-call(bf16[64,512]{1,0:T(8,128)(2,1)} %refs_0_.3, bf16[64,256]{1,0:T(8,128)(2,1)} %refs_1_.3, bf16[64,256]{1,0:T(8,128)(2,1)} %refs_2_.3, bf16[512]{0:T(512)(128)(2,1)} %refs_3_.1, bf16[256]{0:T(256)(128)(2,1)} %refs_4_.1, bf16[256]{0:T(256)(128)(2,1)} %refs_5_.1, f32[16,8,128]{2,1,0:T(8,128)S(1)} %all_to_all.10.refs_6_), custom_call_target="tpu_custom_call" | custom-call | flops 10000000000 | bytes 16777216 | tf_op jit(solution)/shard_map/pallas_call | solution.py:198
  17.7 4.0 %collective-permute-start.2 = (bf16[64,1024]{1,0:T(8,128)(2,1)S(1)}, bf16[64,1024]{1,0:T(8,128)(2,1)S(1)}, u32[]{:S(2)}, u32[]{:S(2)}) collective-permute-start(bf16[64,1024]{1,0:T(8,128)(2,1)S(1)} %shard_map.123), channel_id=1, source_target_pairs={{0,64},{1,65},{2,66},{3,67},{4,68},{5,69},{6,70},{7,71},{8,72},{9,... | collective-permute-start | bytes 393224 | tf_op jit(solution)/shard_map/ppermute | solution.py:42
  21.7 0.7 collective-permute-start.1
  22.4 0.3 collective-permute-start
  22.7 1.4 %shard_map.124.wb0 = bf16[16,256,512]{2,1,0:T(8,128)(2,1)S(1)} custom-call(bf16[512,16,512]{2,1,0:T(8,128)(2,1)S(1)} %bitcast.58), custom_call_target="tpu_custom_call" | custom-call | bytes 8388608 | tf_op jit(solution)/shard_map/pallas_call | solution.py:61
  24.1 1.4 %shard_map.125.wb1 = bf16[16,256,512]{2,1,0:T(8,128)(2,1)S(1)} custom-call(bf16[512,16,512]{2,1,0:T(8,128)(2,1)S(1)} %bitcast.58), custom_call_target="tpu_custom_call" | custom-call | bytes 8388608 | tf_op jit(solution)/shard_map/pallas_call | solution.py:61
  25.5 0.8 copy-done
  26.3 1.4 %shard_map.126.we = bf16[16,256,512]{2,1,0:T(8,128)(2,1)S(1)} custom-call(bf16[256,16,512]{2,1,0:T(8,128)(2,1)S(1)} %copy-done), custom_call_target="tpu_custom_call" | custom-call | bytes 8388608 | tf_op jit(solution)/shard_map/pallas_call | solution.py:61
  27.7 0.1 collective-permute-done.1
  28.7 1.4 %shard_map.127.wa = bf16[16,256,512]{2,1,0:T(8,128)(2,1)S(1)} custom-call(bf16[256,16,512]{2,1,0:T(8,128)(2,1)S(1)} %copy-done.1), custom_call_target="tpu_custom_call" | custom-call | bytes 8388608 | tf_op jit(solution)/shard_map/pallas_call | solution.py:61
  30.2 1.3 %shard_map.129 = bf16[4,512,256]{2,1,0:T(8,128)(2,1)S(1)} custom-call(f32[1]{0:T(128)S(6)} %copy.20.alpha, bf16[512,1024]{1,0:T(8,128)(2,1)S(1)} %shard_map.128.acts, bf16[16,256,512]{2,1,0:T(8,128)(2,1)S(1)} %shard_map.124.wb0, bf16[16,256,512]{2,1,0:T(8,128)(2,1)S(1)} %shard_map.125.wb1, bf16[16,256,512]{2,1,0:T(8,128)(2,1)S(1)} %shard_map.126.we, ...), custom_call_target="tpu_custom_call" | custom-call | flops 1 | bytes 1 | tf_op jit(solution)/shard_map/pallas_call | solution.py:95
  31.5 0.6 collective-permute-start.7
  32.2 1.3 %shard_map.130 = bf16[4,512,256]{2,1,0:T(8,128)(2,1)S(1)} custom-call(f32[1]{0:T(128)S(6)} %copy.20.alpha, bf16[512,1024]{1,0:T(8,128)(2,1)S(1)} %shard_map.128.acts, bf16[16,256,512]{2,1,0:T(8,128)(2,1)S(1)} %shard_map.124.wb0, bf16[16,256,512]{2,1,0:T(8,128)(2,1)S(1)} %shard_map.125.wb1, bf16[16,256,512]{2,1,0:T(8,128)(2,1)S(1)} %shard_map.126.we, ...), custom_call_target="tpu_custom_call" | custom-call | flops 1 | bytes 1 | tf_op jit(solution)/shard_map/pallas_call | solution.py:95
  33.5 0.6 collective-permute-start.4
  34.1 1.3 %shard_map.131 = bf16[4,512,256]{2,1,0:T(8,128)(2,1)S(1)} custom-call(f32[1]{0:T(128)S(6)} %copy.20.alpha, bf16[512,1024]{1,0:T(8,128)(2,1)S(1)} %shard_map.128.acts, bf16[16,256,512]{2,1,0:T(8,128)(2,1)S(1)} %shard_map.124.wb0, bf16[16,256,512]{2,1,0:T(8,128)(2,1)S(1)} %shard_map.125.wb1, bf16[16,256,512]{2,1,0:T(8,128)(2,1)S(1)} %shard_map.126.we, ...), custom_call_target="tpu_custom_call" | custom-call | flops 1 | bytes 1 | tf_op jit(solution)/shard_map/pallas_call | solution.py:95
  35.4 1.5 %collective-permute-start.5 = (bf16[4,512,256]{2,1,0:T(8,128)(2,1)S(1)}, bf16[4,512,256]{2,1,0:T(8,128)(2,1)S(1)}, u32[]{:S(2)}, u32[]{:S(2)}) collective-permute-start(bf16[4,512,256]{2,1,0:T(8,128)(2,1)S(1)} %shard_map.131), channel_id=1, source_target_pairs={{0,1},{1,0},{2,3},{3,2},{4,5},{5,4},{6,7},{7,6},{8,9},{9,8},{10,11... | collective-permute-start | bytes 3145736 | tf_op jit(solution)/shard_map/ppermute | solution.py:42
  36.9 1.3 %shard_map.132 = bf16[4,512,256]{2,1,0:T(8,128)(2,1)S(1)} custom-call(f32[1]{0:T(128)S(6)} %copy.20.alpha, bf16[512,1024]{1,0:T(8,128)(2,1)S(1)} %shard_map.128.acts, bf16[16,256,512]{2,1,0:T(8,128)(2,1)S(1)} %shard_map.124.wb0, bf16[16,256,512]{2,1,0:T(8,128)(2,1)S(1)} %shard_map.125.wb1, bf16[16,256,512]{2,1,0:T(8,128)(2,1)S(1)} %shard_map.126.we, ...), custom_call_target="tpu_custom_call" | custom-call | flops 1 | bytes 1 | tf_op jit(solution)/shard_map/pallas_call | solution.py:95
  38.2 1.6 %collective-permute-start.6 = (bf16[4,512,256]{2,1,0:T(8,128)(2,1)S(1)}, bf16[4,512,256]{2,1,0:T(8,128)(2,1)S(1)}, u32[]{:S(2)}, u32[]{:S(2)}) collective-permute-start(bf16[4,512,256]{2,1,0:T(8,128)(2,1)S(1)} %shard_map.132), channel_id=1, source_target_pairs={{0,4},{1,5},{2,6},{3,7},{4,0},{5,1},{6,2},{7,3},{8,12},{9,13},{10,... | collective-permute-start | bytes 3145736 | tf_op jit(solution)/shard_map/ppermute | solution.py:42
  39.8 1.3 %shard_map.133 = f32[4,512,256]{2,1,0:T(8,128)S(1)} custom-call(f32[1]{0:T(128)S(6)} %copy.20.alpha, bf16[512,1024]{1,0:T(8,128)(2,1)S(1)} %shard_map.128.acts, bf16[16,256,512]{2,1,0:T(8,128)(2,1)S(1)} %shard_map.124.wb0, bf16[16,256,512]{2,1,0:T(8,128)(2,1)S(1)} %shard_map.125.wb1, bf16[16,256,512]{2,1,0:T(8,128)(2,1)S(1)} %shard_map.126.we, ...), custom_call_target="tpu_custom_call" | custom-call | flops 1 | bytes 1 | tf_op jit(solution)/shard_map/pallas_call | solution.py:95
  41.1 5.3 %collective-permute-done.7 = bf16[4,512,256]{2,1,0:T(8,128)(2,1)S(1)} collective-permute-done((bf16[4,512,256]{2,1,0:T(8,128)(2,1)S(1)}, bf16[4,512,256]{2,1,0:T(8,128)(2,1)S(1)}, u32[]{:S(2)}, u32[]{:S(2)}) %collective-permute-start.7) | collective-permute-done | bytes 1048608 | tf_op jit(solution)/shard_map/ppermute | solution.py:42
  46.4 0.4 multiply_convert_fusion
  46.8 1.4 %collective-permute-start.8 = (f16[4,512,256]{2,1,0:T(8,128)(2,1)S(1)}, f16[4,512,256]{2,1,0:T(8,128)(2,1)S(1)}, u32[]{:S(2)}, u32[]{:S(2)}) collective-permute-start(f16[4,512,256]{2,1,0:T(8,128)(2,1)S(1)} %multiply_convert_fusion), channel_id=1, source_target_pairs={{0,3},{1,2},{2,1},{3,0},{4,7},{5,6},{6,5},{7,4},{8,11},{9,10},{10,... | collective-permute-start | bytes 3145736 | tf_op jit(solution)/shard_map/ppermute | solution.py:42
  48.3 1.3 %shard_map.134 = f32[4,512,256]{2,1,0:T(8,128)S(1)} custom-call(f32[1]{0:T(128)S(6)} %copy.20.alpha, bf16[512,1024]{1,0:T(8,128)(2,1)S(1)} %shard_map.128.acts, bf16[16,256,512]{2,1,0:T(8,128)(2,1)S(1)} %shard_map.124.wb0, bf16[16,256,512]{2,1,0:T(8,128)(2,1)S(1)} %shard_map.125.wb1, bf16[16,256,512]{2,1,0:T(8,128)(2,1)S(1)} %shard_map.126.we, ...), custom_call_target="tpu_custom_call" | custom-call | flops 1 | bytes 1 | tf_op jit(solution)/shard_map/pallas_call | solution.py:95
  49.6 0.4 multiply_convert_fusion.1
  50.0 1.2 %collective-permute-start.12 = (f16[4,512,256]{2,1,0:T(8,128)(2,1)S(1)}, f16[4,512,256]{2,1,0:T(8,128)(2,1)S(1)}, u32[]{:S(2)}, u32[]{:S(2)}) collective-permute-start(f16[4,512,256]{2,1,0:T(8,128)(2,1)S(1)} %multiply_convert_fusion.1), channel_id=1, source_target_pairs={{0,12},{1,13},{2,14},{3,15},{4,8},{5,9},{6,10},{7,11},{8,4},{9,5},... | collective-permute-start | bytes 3145736 | tf_op jit(solution)/shard_map/ppermute | solution.py:42
  51.2 1.3 %shard_map.135 = f32[4,512,256]{2,1,0:T(8,128)S(1)} custom-call(f32[1]{0:T(128)S(6)} %copy.20.alpha, bf16[512,1024]{1,0:T(8,128)(2,1)S(1)} %shard_map.128.acts, bf16[16,256,512]{2,1,0:T(8,128)(2,1)S(1)} %shard_map.124.wb0, bf16[16,256,512]{2,1,0:T(8,128)(2,1)S(1)} %shard_map.125.wb1, bf16[16,256,512]{2,1,0:T(8,128)(2,1)S(1)} %shard_map.126.we, ...), custom_call_target="tpu_custom_call" | custom-call | flops 1 | bytes 1 | tf_op jit(solution)/shard_map/pallas_call | solution.py:95
  52.5 1.3 %shard_map.136 = f32[4,512,256]{2,1,0:T(8,128)S(1)} custom-call(f32[1]{0:T(128)S(6)} %copy.20.alpha, bf16[512,1024]{1,0:T(8,128)(2,1)S(1)} %shard_map.128.acts, bf16[16,256,512]{2,1,0:T(8,128)(2,1)S(1)} %shard_map.124.wb0, bf16[16,256,512]{2,1,0:T(8,128)(2,1)S(1)} %shard_map.125.wb1, bf16[16,256,512]{2,1,0:T(8,128)(2,1)S(1)} %shard_map.126.we, ...), custom_call_target="tpu_custom_call" | custom-call | flops 1 | bytes 1 | tf_op jit(solution)/shard_map/pallas_call | solution.py:95
  53.9 11.1 %collective-permute-done.5 = bf16[4,512,256]{2,1,0:T(8,128)(2,1)S(1)} collective-permute-done((bf16[4,512,256]{2,1,0:T(8,128)(2,1)S(1)}, bf16[4,512,256]{2,1,0:T(8,128)(2,1)S(1)}, u32[]{:S(2)}, u32[]{:S(2)}) %collective-permute-start.5) | collective-permute-done | bytes 1048608 | tf_op jit(solution)/shard_map/ppermute | solution.py:42
  65.0 0.3 convert_add_fusion.1
  65.2 1.5 %collective-permute-done.6 = bf16[4,512,256]{2,1,0:T(8,128)(2,1)S(1)} collective-permute-done((bf16[4,512,256]{2,1,0:T(8,128)(2,1)S(1)}, bf16[4,512,256]{2,1,0:T(8,128)(2,1)S(1)}, u32[]{:S(2)}, u32[]{:S(2)}) %collective-permute-start.6) | collective-permute-done | bytes 1048608 | tf_op jit(solution)/shard_map/ppermute | solution.py:42
  66.8 0.3 convert_add_fusion
  67.0 2.6 %collective-permute-done.8 = f16[4,512,256]{2,1,0:T(8,128)(2,1)S(1)} collective-permute-done((f16[4,512,256]{2,1,0:T(8,128)(2,1)S(1)}, f16[4,512,256]{2,1,0:T(8,128)(2,1)S(1)}, u32[]{:S(2)}, u32[]{:S(2)}) %collective-permute-start.8) | collective-permute-done | bytes 1048608 | tf_op jit(solution)/shard_map/ppermute | solution.py:42
  69.6 0.3 multiply_add_fusion.1
  69.9 0.1 fusion.18
  70.1 0.6 collective-permute-start.10
  70.7 1.2 %collective-permute-done.12 = f16[4,512,256]{2,1,0:T(8,128)(2,1)S(1)} collective-permute-done((f16[4,512,256]{2,1,0:T(8,128)(2,1)S(1)}, f16[4,512,256]{2,1,0:T(8,128)(2,1)S(1)}, u32[]{:S(2)}, u32[]{:S(2)}) %collective-permute-start.12) | collective-permute-done | bytes 1048608 | tf_op jit(solution)/shard_map/ppermute | solution.py:42
  71.9 0.3 multiply_add_fusion
  72.2 0.1 fusion.20
  72.3 0.2 collective-permute-start.14
  72.5 0.3 collective-permute-start.9
  72.8 3.7 %collective-permute-done.10 = f16[512,256]{1,0:T(8,128)(2,1)S(1)} collective-permute-done((f16[512,256]{1,0:T(8,128)(2,1)S(1)}, f16[512,256]{1,0:T(8,128)(2,1)S(1)}, u32[]{:S(2)}, u32[]{:S(2)}) %collective-permute-start.10) | collective-permute-done | bytes 262176 | tf_op jit(solution)/shard_map/ppermute | solution.py:42
  76.5 0.1 fusion.12
  76.6 1.2 %collective-permute-start.11 = (f16[512,256]{1,0:T(8,128)(2,1)S(1)}, f16[512,256]{1,0:T(8,128)(2,1)S(1)}, u32[]{:S(2)}, u32[]{:S(2)}) collective-permute-start(f16[512,256]{1,0:T(8,128)(2,1)S(1)} %fusion.12), channel_id=1, source_target_pairs={{0,12},{1,13},{2,14},{3,15},{4,8},{5,9},{6,10},{7,11},{8,4},{9,5},... | collective-permute-start | bytes 786440 | tf_op jit(solution)/shard_map/ppermute | solution.py:42
  77.8 0.9 collective-permute-done.14
  78.8 0.1 fusion.3
  78.9 2.1 %collective-permute-start.15 = (f16[512,256]{1,0:T(8,128)(2,1)S(1)}, f16[512,256]{1,0:T(8,128)(2,1)S(1)}, u32[]{:S(2)}, u32[]{:S(2)}) collective-permute-start(f16[512,256]{1,0:T(8,128)(2,1)S(1)} %fusion.3), channel_id=1, source_target_pairs={{0,3},{1,2},{2,1},{3,0},{4,7},{5,6},{6,5},{7,4},{8,11},{9,10},{10,... | collective-permute-start | bytes 786440 | tf_op jit(solution)/shard_map/ppermute | solution.py:42
  81.1 3.2 %collective-permute-done.11 = f16[512,256]{1,0:T(8,128)(2,1)S(1)} collective-permute-done((f16[512,256]{1,0:T(8,128)(2,1)S(1)}, f16[512,256]{1,0:T(8,128)(2,1)S(1)}, u32[]{:S(2)}, u32[]{:S(2)}) %collective-permute-start.11) | collective-permute-done | bytes 262176 | tf_op jit(solution)/shard_map/ppermute | solution.py:42
  84.3 0.2 fusion.17
  84.5 1.8 %collective-permute-done.13 = f16[512,256]{1,0:T(8,128)(2,1)S(1)} collective-permute-done((f16[512,256]{1,0:T(8,128)(2,1)S(1)}, f16[512,256]{1,0:T(8,128)(2,1)S(1)}, u32[]{:S(2)}, u32[]{:S(2)}) %collective-permute-start.13) | collective-permute-done | bytes 262176 | tf_op jit(solution)/shard_map/ppermute | solution.py:42
  86.3 0.3 collective-permute-done.15
  86.6 0.2 fusion.8
  86.8 0.1 pad_maximum_fusion
  87.1 1.5 %collective-permute-done.16 = f16[4,64,512]{2,1,0:T(8,128)(2,1)S(1)} collective-permute-done((f16[4,64,512]{2,1,0:T(8,128)(2,1)S(1)}, f16[4,64,512]{2,1,0:T(8,128)(2,1)S(1)}, u32[]{:S(2)}, u32[]{:S(2)}) %collective-permute-start.16) | collective-permute-done | bytes 262176 | tf_op jit(solution)/shard_map/ppermute | solution.py:42
  88.7 3.6 %collective-permute-start.17 = (f16[2,64,512]{2,1,0:T(8,128)(2,1)S(1)}, f16[2,64,512]{2,1,0:T(8,128)(2,1)S(1)}, u32[]{:S(2)}, u32[]{:S(2)}) collective-permute-start(f16[2,64,512]{2,1,0:T(8,128)(2,1)S(1)} %pad_maximum_fusion.1), channel_id=1, source_target_pairs={{0,64},{1,65},{2,66},{3,67},{4,68},{5,69},{6,70},{7,71},{8,72},{9,... | collective-permute-start | bytes 393224 | tf_op jit(solution)/shard_map/ppermute | solution.py:42
  92.5 0.8 collective-permute-start.19
  93.2 3.3 %collective-permute-done.17 = f16[2,64,512]{2,1,0:T(8,128)(2,1)S(1)} collective-permute-done((f16[2,64,512]{2,1,0:T(8,128)(2,1)S(1)}, f16[2,64,512]{2,1,0:T(8,128)(2,1)S(1)}, u32[]{:S(2)}, u32[]{:S(2)}) %collective-permute-start.17) | collective-permute-done | bytes 131104 | tf_op jit(solution)/shard_map/ppermute | solution.py:42
  96.6 1.8 %collective-permute-done.18 = f16[2,64,512]{2,1,0:T(8,128)(2,1)S(1)} collective-permute-done((f16[2,64,512]{2,1,0:T(8,128)(2,1)S(1)}, f16[2,64,512]{2,1,0:T(8,128)(2,1)S(1)}, u32[]{:S(2)}, u32[]{:S(2)}) %collective-permute-start.18) | collective-permute-done | bytes 131104 | tf_op jit(solution)/shard_map/ppermute | solution.py:42
  98.4 0.8 collective-permute-done.19
  99.2 0.1 convert_multiply_fusion.home
  99.4 1.2 %shard_map.137 = f32[16,8,128]{2,1,0:T(8,128)S(1)} custom-call(f32[8,64,512]{2,1,0:T(8,128)S(1)} %convert_multiply_fusion.home, s32[64]{0:T(128)} %ids.1), custom_call_target="tpu_custom_call" | custom-call | tf_op jit(solution)/shard_map/pallas_call | solution.py:198
  100.5 11.5 %all_to_all.11.stats = f32[16,8,128]{2,1,0:T(8,128)S(1)} all-to-all(f32[16,8,128]{2,1,0:T(8,128)S(1)} %shard_map.137), channel_id=1, replica_groups=mesh['rows'=8,'tensor'=16] {'tensor'}, dimensions={0} | all-to-all | bytes 131072 | tf_op jit(solution)/shard_map/all_to_all | solution.py:294
  112.0 1.2 %shard_map.138 = (f32[64,4096]{1,0:T(8,128)}, f32[1,64]{1,0:T(1,128)}) custom-call(f32[8,64,512]{2,1,0:T(8,128)S(1)} %convert_multiply_fusion.home, f32[16,8,128]{2,1,0:T(8,128)S(1)} %all_to_all.11.stats), custom_call_target="tpu_custom_call" | custom-call | tf_op jit(solution)/shard_map/pallas_call | solution.py:198
  (32 shorter events, 0.7 us)
Async XLA Ops:
  1.6 21.1 %slice-start = ((s8[8388608]{0:T(1024)(128)(4,1)}), s8[4194304]{0:T(1024)(128)(4,1)S(1)}, s32[]{:S(2)}) async-start(s8[8388608]{0:T(1024)(128)(4,1)} %bitcast.57), calls=%async_computation.2 | async-start | bytes 8388608
  16.5 6.2 %slice-start.1 = ((s8[8388608]{0:T(1024)(128)(4,1)}), s8[4194304]{0:T(1024)(128)(4,1)S(1)}, s32[]{:S(2)}) async-start(s8[8388608]{0:T(1024)(128)(4,1)} %bitcast.57), calls=%async_computation.3 | async-start | bytes 8388608
  17.7 10.0 %collective-permute-start.2 = (bf16[64,1024]{1,0:T(8,128)(2,1)S(1)}, bf16[64,1024]{1,0:T(8,128)(2,1)S(1)}, u32[]{:S(2)}, u32[]{:S(2)}) collective-permute-start(bf16[64,1024]{1,0:T(8,128)(2,1)S(1)} %shard_map.123), channel_id=1, source_target_pairs={{0,64},{1,65},{2,66},{3,67},{4,68},{5,69},{6,70},{7,71},{8,72},{9,... | collective-permute-start | bytes 393224 | tf_op jit(solution)/shard_map/ppermute | solution.py:42
  21.7 6.2 %collective-permute-start.1 = (bf16[64,1024]{1,0:T(8,128)(2,1)S(1)}, bf16[64,1024]{1,0:T(8,128)(2,1)S(1)}, u32[]{:S(2)}, u32[]{:S(2)}) collective-permute-start(bf16[64,1024]{1,0:T(8,128)(2,1)S(1)} %shard_map.123), channel_id=1, source_target_pairs={{0,96},{1,97},{2,98},{3,99},{4,100},{5,101},{6,102},{7,103},{8,104... | collective-permute-start | bytes 393224 | tf_op jit(solution)/shard_map/ppermute | solution.py:42
  22.4 5.5 %collective-permute-start = (bf16[64,1024]{1,0:T(8,128)(2,1)S(1)}, bf16[64,1024]{1,0:T(8,128)(2,1)S(1)}, u32[]{:S(2)}, u32[]{:S(2)}) collective-permute-start(bf16[64,1024]{1,0:T(8,128)(2,1)S(1)} %shard_map.123), channel_id=1, source_target_pairs={{0,32},{1,33},{2,34},{3,35},{4,36},{5,37},{6,38},{7,39},{8,40},{9,... | collective-permute-start | bytes 393224 | tf_op jit(solution)/shard_map/ppermute | solution.py:42
  24.1 2.2 %copy-start = (bf16[256,16,512]{2,1,0:T(8,128)(2,1)S(1)}, bf16[256,16,512]{2,1,0:T(8,128)(2,1)}, u32[]{:S(2)}) copy-start(bf16[256,16,512]{2,1,0:T(8,128)(2,1)} %head.2) | copy-start | bytes 12582916
  26.3 2.4 %copy-start.1 = (bf16[256,16,512]{2,1,0:T(8,128)(2,1)S(1)}, bf16[256,16,512]{2,1,0:T(8,128)(2,1)}, u32[]{:S(2)}) copy-start(bf16[256,16,512]{2,1,0:T(8,128)(2,1)} %head.3) | copy-start | bytes 12582916
  27.9 2.2 %collective-permute-start.3 = (bf16[256,1024]{1,0:T(8,128)(2,1)S(1)}, bf16[256,1024]{1,0:T(8,128)(2,1)S(1)}, u32[]{:S(2)}, u32[]{:S(2)}) collective-permute-start(bf16[256,1024]{1,0:T(8,128)(2,1)S(1)} %constant_dynamic-update-slice_fusion.refs_0_), channel_id=1, source_target_pairs={{0,16},{1,17},{2,18},{3,19},{4,20},{5,21},{6,22},{7,23},{8,24},{9,... | collective-permute-start | bytes 1572872 | tf_op jit(solution)/shard_map/ppermute | solution.py:42
  31.5 14.9 %collective-permute-start.7 = (bf16[4,512,256]{2,1,0:T(8,128)(2,1)S(1)}, bf16[4,512,256]{2,1,0:T(8,128)(2,1)S(1)}, u32[]{:S(2)}, u32[]{:S(2)}) collective-permute-start(bf16[4,512,256]{2,1,0:T(8,128)(2,1)S(1)} %shard_map.129), channel_id=1, source_target_pairs={{0,1},{1,0},{2,3},{3,2},{4,5},{5,4},{6,7},{7,6},{8,9},{9,8},{10,11... | collective-permute-start | bytes 3145736 | tf_op jit(solution)/shard_map/ppermute | solution.py:42
  33.5 16.1 %collective-permute-start.4 = (bf16[4,512,256]{2,1,0:T(8,128)(2,1)S(1)}, bf16[4,512,256]{2,1,0:T(8,128)(2,1)S(1)}, u32[]{:S(2)}, u32[]{:S(2)}) collective-permute-start(bf16[4,512,256]{2,1,0:T(8,128)(2,1)S(1)} %shard_map.130), channel_id=1, source_target_pairs={{0,4},{1,5},{2,6},{3,7},{4,0},{5,1},{6,2},{7,3},{8,12},{9,13},{10,... | collective-permute-start | bytes 3145736 | tf_op jit(solution)/shard_map/ppermute | solution.py:42
  35.4 29.6 %collective-permute-start.5 = (bf16[4,512,256]{2,1,0:T(8,128)(2,1)S(1)}, bf16[4,512,256]{2,1,0:T(8,128)(2,1)S(1)}, u32[]{:S(2)}, u32[]{:S(2)}) collective-permute-start(bf16[4,512,256]{2,1,0:T(8,128)(2,1)S(1)} %shard_map.131), channel_id=1, source_target_pairs={{0,1},{1,0},{2,3},{3,2},{4,5},{5,4},{6,7},{7,6},{8,9},{9,8},{10,11... | collective-permute-start | bytes 3145736 | tf_op jit(solution)/shard_map/ppermute | solution.py:42
  38.2 28.5 %collective-permute-start.6 = (bf16[4,512,256]{2,1,0:T(8,128)(2,1)S(1)}, bf16[4,512,256]{2,1,0:T(8,128)(2,1)S(1)}, u32[]{:S(2)}, u32[]{:S(2)}) collective-permute-start(bf16[4,512,256]{2,1,0:T(8,128)(2,1)S(1)} %shard_map.132), channel_id=1, source_target_pairs={{0,4},{1,5},{2,6},{3,7},{4,0},{5,1},{6,2},{7,3},{8,12},{9,13},{10,... | collective-permute-start | bytes 3145736 | tf_op jit(solution)/shard_map/ppermute | solution.py:42
  46.8 22.8 %collective-permute-start.8 = (f16[4,512,256]{2,1,0:T(8,128)(2,1)S(1)}, f16[4,512,256]{2,1,0:T(8,128)(2,1)S(1)}, u32[]{:S(2)}, u32[]{:S(2)}) collective-permute-start(f16[4,512,256]{2,1,0:T(8,128)(2,1)S(1)} %multiply_convert_fusion), channel_id=1, source_target_pairs={{0,3},{1,2},{2,1},{3,0},{4,7},{5,6},{6,5},{7,4},{8,11},{9,10},{10,... | collective-permute-start | bytes 3145736 | tf_op jit(solution)/shard_map/ppermute | solution.py:42
  50.0 21.9 %collective-permute-start.12 = (f16[4,512,256]{2,1,0:T(8,128)(2,1)S(1)}, f16[4,512,256]{2,1,0:T(8,128)(2,1)S(1)}, u32[]{:S(2)}, u32[]{:S(2)}) collective-permute-start(f16[4,512,256]{2,1,0:T(8,128)(2,1)S(1)} %multiply_convert_fusion.1), channel_id=1, source_target_pairs={{0,12},{1,13},{2,14},{3,15},{4,8},{5,9},{6,10},{7,11},{8,4},{9,5},... | collective-permute-start | bytes 3145736 | tf_op jit(solution)/shard_map/ppermute | solution.py:42
  70.1 6.5 %collective-permute-start.10 = (f16[512,256]{1,0:T(8,128)(2,1)S(1)}, f16[512,256]{1,0:T(8,128)(2,1)S(1)}, u32[]{:S(2)}, u32[]{:S(2)}) collective-permute-start(f16[512,256]{1,0:T(8,128)(2,1)S(1)} %get-tuple-element.79), channel_id=1, source_target_pairs={{0,4},{1,5},{2,6},{3,7},{4,0},{5,1},{6,2},{7,3},{8,12},{9,13},{10,... | collective-permute-start | bytes 786440 | tf_op jit(solution)/shard_map/ppermute | solution.py:42
  72.3 6.5 %collective-permute-start.14 = (f16[512,256]{1,0:T(8,128)(2,1)S(1)}, f16[512,256]{1,0:T(8,128)(2,1)S(1)}, u32[]{:S(2)}, u32[]{:S(2)}) collective-permute-start(f16[512,256]{1,0:T(8,128)(2,1)S(1)} %get-tuple-element.81), channel_id=1, source_target_pairs={{0,1},{1,0},{2,3},{3,2},{4,5},{5,4},{6,7},{7,6},{8,9},{9,8},{10,11... | collective-permute-start | bytes 786440 | tf_op jit(solution)/shard_map/ppermute | solution.py:42
  72.5 8.5 %collective-permute-start.9 = (f16[512,256]{1,0:T(8,128)(2,1)S(1)}, f16[512,256]{1,0:T(8,128)(2,1)S(1)}, u32[]{:S(2)}, u32[]{:S(2)}) collective-permute-start(f16[512,256]{1,0:T(8,128)(2,1)S(1)} %get-tuple-element.78), channel_id=1, source_target_pairs={{0,4},{1,5},{2,6},{3,7},{4,0},{5,1},{6,2},{7,3},{8,12},{9,13},{10,... | collective-permute-start | bytes 786440 | tf_op jit(solution)/shard_map/ppermute | solution.py:42
  76.6 7.7 %collective-permute-start.11 = (f16[512,256]{1,0:T(8,128)(2,1)S(1)}, f16[512,256]{1,0:T(8,128)(2,1)S(1)}, u32[]{:S(2)}, u32[]{:S(2)}) collective-permute-start(f16[512,256]{1,0:T(8,128)(2,1)S(1)} %fusion.12), channel_id=1, source_target_pairs={{0,12},{1,13},{2,14},{3,15},{4,8},{5,9},{6,10},{7,11},{8,4},{9,5},... | collective-permute-start | bytes 786440 | tf_op jit(solution)/shard_map/ppermute | solution.py:42
  77.8 8.5 %collective-permute-start.13 = (f16[512,256]{1,0:T(8,128)(2,1)S(1)}, f16[512,256]{1,0:T(8,128)(2,1)S(1)}, u32[]{:S(2)}, u32[]{:S(2)}) collective-permute-start(f16[512,256]{1,0:T(8,128)(2,1)S(1)} %get-tuple-element.80), channel_id=1, source_target_pairs={{0,1},{1,0},{2,3},{3,2},{4,5},{5,4},{6,7},{7,6},{8,9},{9,8},{10,11... | collective-permute-start | bytes 786440 | tf_op jit(solution)/shard_map/ppermute | solution.py:42
  78.9 7.7 %collective-permute-start.15 = (f16[512,256]{1,0:T(8,128)(2,1)S(1)}, f16[512,256]{1,0:T(8,128)(2,1)S(1)}, u32[]{:S(2)}, u32[]{:S(2)}) collective-permute-start(f16[512,256]{1,0:T(8,128)(2,1)S(1)} %fusion.3), channel_id=1, source_target_pairs={{0,3},{1,2},{2,1},{3,0},{4,7},{5,6},{6,5},{7,4},{8,11},{9,10},{10,... | collective-permute-start | bytes 786440 | tf_op jit(solution)/shard_map/ppermute | solution.py:42
  86.9 1.6 %collective-permute-start.16 = (f16[4,64,512]{2,1,0:T(8,128)(2,1)S(1)}, f16[4,64,512]{2,1,0:T(8,128)(2,1)S(1)}, u32[]{:S(2)}, u32[]{:S(2)}) collective-permute-start(f16[4,64,512]{2,1,0:T(8,128)(2,1)S(1)} %bitcast.61), channel_id=1, source_target_pairs={{0,16},{1,17},{2,18},{3,19},{4,20},{5,21},{6,22},{7,23},{8,24},{9,... | collective-permute-start | bytes 786440 | tf_op jit(solution)/shard_map/ppermute | solution.py:42
  88.7 7.9 %collective-permute-start.17 = (f16[2,64,512]{2,1,0:T(8,128)(2,1)S(1)}, f16[2,64,512]{2,1,0:T(8,128)(2,1)S(1)}, u32[]{:S(2)}, u32[]{:S(2)}) collective-permute-start(f16[2,64,512]{2,1,0:T(8,128)(2,1)S(1)} %pad_maximum_fusion.1), channel_id=1, source_target_pairs={{0,64},{1,65},{2,66},{3,67},{4,68},{5,69},{6,70},{7,71},{8,72},{9,... | collective-permute-start | bytes 393224 | tf_op jit(solution)/shard_map/ppermute | solution.py:42
  92.3 6.1 %collective-permute-start.18 = (f16[2,64,512]{2,1,0:T(8,128)(2,1)S(1)}, f16[2,64,512]{2,1,0:T(8,128)(2,1)S(1)}, u32[]{:S(2)}, u32[]{:S(2)}) collective-permute-start(f16[2,64,512]{2,1,0:T(8,128)(2,1)S(1)} %pad_maximum_fusion.2), channel_id=1, source_target_pairs={{0,32},{1,33},{2,34},{3,35},{4,36},{5,37},{6,38},{7,39},{8,40},{9,... | collective-permute-start | bytes 393224 | tf_op jit(solution)/shard_map/ppermute | solution.py:42
  92.5 6.7 %collective-permute-start.19 = (f16[2,64,512]{2,1,0:T(8,128)(2,1)S(1)}, f16[2,64,512]{2,1,0:T(8,128)(2,1)S(1)}, u32[]{:S(2)}, u32[]{:S(2)}) collective-permute-start(f16[2,64,512]{2,1,0:T(8,128)(2,1)S(1)} %pad_maximum_fusion.3), channel_id=1, source_target_pairs={{0,96},{1,97},{2,98},{3,99},{4,100},{5,101},{6,102},{7,103},{8,104... | collective-permute-start | bytes 393224 | tf_op jit(solution)/shard_map/ppermute | solution.py:42

commit v11 on v10

--- a/solution.py
+++ b/solution.py
@@ -147,13 +147,6 @@
         value = h[...].astype(F32) * scale * gains[i][...].astype(F32)[None]
         out[:, at : at + h.shape[1]] = value.astype(out.dtype)
         at += h.shape[1]
-
-
-def join_kernel(*refs):
-    at = 0
-    for ref in refs[:-1]:
-        refs[-1][at : at + ref.shape[0]] = ref[...]
-        at += ref.shape[0]
 
 
 def stats_kernel(home, ids, out):
@@ -251,7 +244,7 @@
     got = swap(normed, along_z, (base_head, 0), (base_head, quarter), (expert_head, 0))
     mine = jnp.concatenate([normed, *got])
     (other,) = swap(mine, [("core",)], (anti_head, 0))
-    acts = call(join_kernel, [((NZ * NC * rows, width), BF)], mine, other)
+    acts = jnp.concatenate([mine, other])
 
     axes = (("x", "y"), ("y", "x"))
     kept = [[], []]

time: 114 us -> 114 us (level)
    pallas_call x5 -> x4, Pallas kernels: 4.74 us -> 4.67 us  [call(): pl.pallas_call(kernel, in_specs=[pl.BlockSpec() for _ in args], out_specs...]
where the time goes in v11:
time: 114 us; the launch traced here: 113 us
  waiting for transfers between devices  39.2 us (34%)
  blocking collectives  26.3 us (23%)
  starting transfers between devices  21.1 us (19%)
  Pallas kernels  20.6 us (18%)
  other arithmetic  3.38 us (3%)
  between operations  1.63 us (1%)
    ppermute x20, waiting for transfers between devices, exchange(): return lax.ppermute(value, AXES, pairs)  39.2 us
    ppermute x20, starting transfers between devices, exchange(): return lax.ppermute(value, AXES, pairs)  21.1 us
    all_to_all x1, blocking collectives, shards(): sums = lax.all_to_all(sums, 'tensor', 0, 0, tiled=True)  14.8 us
    all_to_all x1, blocking collectives, shards(): stats = lax.all_to_all(stats, 'tensor', 0, 0, tiled=True)  11.5 us
    pallas_call x8, Pallas kernels, project(): pl.pallas_call(functools.partial(matmul_kernel, step, half), in_specs=[sm...  10.4 us
    pallas_call x4, Pallas kernels, relay(): pl.pallas_call(relay_kernel, grid=(count // step,), in_specs=[pl.BlockSpe...  5.57 us
    pallas_call x4, Pallas kernels, call(): pl.pallas_call(kernel, in_specs=[pl.BlockSpec() for _ in args], out_specs...  4.67 us
  transfers between devices with their start and end apart: 20, of which 15 were waited for; matrix products, arithmetic and copies ran while one was open for 3% of the time, Pallas kernels for 13%

profile of v11, /device:TPU:0, one launch (start us, length us, event | category | flops | bytes accessed | tf_op | source)
XLA Modules:
  0.0 113.3 jit_solution(15896883483833482264)
XLA Ops:
  0.6 1.0 shard_map.122
  1.6 14.8 %all_to_all.10.refs_6_ = f32[16,8,128]{2,1,0:T(8,128)S(1)} all-to-all(f32[16,8,128]{2,1,0:T(8,128)S(1)} %shard_map.122), channel_id=1, replica_groups=mesh['rows'=8,'tensor'=16] {'tensor'}, dimensions={0} | all-to-all | bytes 131072 | tf_op jit(solution)/shard_map/all_to_all | solution.py:233
  16.5 1.2 %shard_map.123 = bf16[64,1024]{1,0:T(8,128)(2,1)S(1)} custom-call(bf16[64,512]{1,0:T(8,128)(2,1)} %refs_0_.3, bf16[64,256]{1,0:T(8,128)(2,1)} %refs_1_.3, bf16[64,256]{1,0:T(8,128)(2,1)} %refs_2_.3, bf16[512]{0:T(512)(128)(2,1)} %refs_3_.1, bf16[256]{0:T(256)(128)(2,1)} %refs_4_.1, bf16[256]{0:T(256)(128)(2,1)} %refs_5_.1, f32[16,8,128]{2,1,0:T(8,128)S(1)} %all_to_all.10.refs_6_), custom_call_target="tpu_custom_call" | custom-call | flops 10000000000 | bytes 16777216 | tf_op jit(solution)/shard_map/pallas_call | solution.py:191
  17.7 4.0 %collective-permute-start.2 = (bf16[64,1024]{1,0:T(8,128)(2,1)S(1)}, bf16[64,1024]{1,0:T(8,128)(2,1)S(1)}, u32[]{:S(2)}, u32[]{:S(2)}) collective-permute-start(bf16[64,1024]{1,0:T(8,128)(2,1)S(1)} %shard_map.123), channel_id=1, source_target_pairs={{0,64},{1,65},{2,66},{3,67},{4,68},{5,69},{6,70},{7,71},{8,72},{9,... | collective-permute-start | bytes 393224 | tf_op jit(solution)/shard_map/ppermute | solution.py:42
  21.7 0.7 collective-permute-start.1
  22.4 0.3 collective-permute-start
  22.7 1.4 %shard_map.124.wb0 = bf16[16,256,512]{2,1,0:T(8,128)(2,1)S(1)} custom-call(bf16[512,16,512]{2,1,0:T(8,128)(2,1)S(1)} %bitcast.58), custom_call_target="tpu_custom_call" | custom-call | bytes 8388608 | tf_op jit(solution)/shard_map/pallas_call | solution.py:61
  24.1 1.4 %shard_map.125.wb1 = bf16[16,256,512]{2,1,0:T(8,128)(2,1)S(1)} custom-call(bf16[512,16,512]{2,1,0:T(8,128)(2,1)S(1)} %bitcast.58), custom_call_target="tpu_custom_call" | custom-call | bytes 8388608 | tf_op jit(solution)/shard_map/pallas_call | solution.py:61
  25.5 0.8 copy-done
  26.3 1.4 %shard_map.126.we = bf16[16,256,512]{2,1,0:T(8,128)(2,1)S(1)} custom-call(bf16[256,16,512]{2,1,0:T(8,128)(2,1)S(1)} %copy-done), custom_call_target="tpu_custom_call" | custom-call | bytes 8388608 | tf_op jit(solution)/shard_map/pallas_call | solution.py:61
  27.7 0.2 collective-permute-done.1
  28.7 1.4 %shard_map.127.wa = bf16[16,256,512]{2,1,0:T(8,128)(2,1)S(1)} custom-call(bf16[256,16,512]{2,1,0:T(8,128)(2,1)S(1)} %copy-done.1), custom_call_target="tpu_custom_call" | custom-call | bytes 8388608 | tf_op jit(solution)/shard_map/pallas_call | solution.py:61
  30.2 1.3 %shard_map.128 = bf16[4,512,256]{2,1,0:T(8,128)(2,1)S(1)} custom-call(f32[1]{0:T(128)S(6)} %copy.21.alpha, bf16[512,1024]{1,0:T(8,128)(2,1)S(1)} %constant_dynamic-update-slice_fusion.acts, bf16[16,256,512]{2,1,0:T(8,128)(2,1)S(1)} %shard_map.124.wb0, bf16[16,256,512]{2,1,0:T(8,128)(2,1)S(1)} %shard_map.125.wb1, bf16[16,256,512]{2,1,0:T(8,128)(2,1)S(1)} %shard_map.126.we, ...), custom_call_target="tpu_custom_call" | custom-call | flops 1 | bytes 1 | tf_op jit(solution)/shard_map/pallas_call | solution.py:95
  31.5 0.6 collective-permute-start.7
  32.2 1.3 %shard_map.129 = bf16[4,512,256]{2,1,0:T(8,128)(2,1)S(1)} custom-call(f32[1]{0:T(128)S(6)} %copy.21.alpha, bf16[512,1024]{1,0:T(8,128)(2,1)S(1)} %constant_dynamic-update-slice_fusion.acts, bf16[16,256,512]{2,1,0:T(8,128)(2,1)S(1)} %shard_map.124.wb0, bf16[16,256,512]{2,1,0:T(8,128)(2,1)S(1)} %shard_map.125.wb1, bf16[16,256,512]{2,1,0:T(8,128)(2,1)S(1)} %shard_map.126.we, ...), custom_call_target="tpu_custom_call" | custom-call | flops 1 | bytes 1 | tf_op jit(solution)/shard_map/pallas_call | solution.py:95
  33.5 0.6 collective-permute-start.4
  34.1 1.3 %shard_map.130 = bf16[4,512,256]{2,1,0:T(8,128)(2,1)S(1)} custom-call(f32[1]{0:T(128)S(6)} %copy.21.alpha, bf16[512,1024]{1,0:T(8,128)(2,1)S(1)} %constant_dynamic-update-slice_fusion.acts, bf16[16,256,512]{2,1,0:T(8,128)(2,1)S(1)} %shard_map.124.wb0, bf16[16,256,512]{2,1,0:T(8,128)(2,1)S(1)} %shard_map.125.wb1, bf16[16,256,512]{2,1,0:T(8,128)(2,1)S(1)} %shard_map.126.we, ...), custom_call_target="tpu_custom_call" | custom-call | flops 1 | bytes 1 | tf_op jit(solution)/shard_map/pallas_call | solution.py:95
  35.4 1.5 %collective-permute-start.5 = (bf16[4,512,256]{2,1,0:T(8,128)(2,1)S(1)}, bf16[4,512,256]{2,1,0:T(8,128)(2,1)S(1)}, u32[]{:S(2)}, u32[]{:S(2)}) collective-permute-start(bf16[4,512,256]{2,1,0:T(8,128)(2,1)S(1)} %shard_map.130), channel_id=1, source_target_pairs={{0,1},{1,0},{2,3},{3,2},{4,5},{5,4},{6,7},{7,6},{8,9},{9,8},{10,11... | collective-permute-start | bytes 3145736 | tf_op jit(solution)/shard_map/ppermute | solution.py:42
  37.0 1.3 %shard_map.131 = bf16[4,512,256]{2,1,0:T(8,128)(2,1)S(1)} custom-call(f32[1]{0:T(128)S(6)} %copy.21.alpha, bf16[512,1024]{1,0:T(8,128)(2,1)S(1)} %constant_dynamic-update-slice_fusion.acts, bf16[16,256,512]{2,1,0:T(8,128)(2,1)S(1)} %shard_map.124.wb0, bf16[16,256,512]{2,1,0:T(8,128)(2,1)S(1)} %shard_map.125.wb1, bf16[16,256,512]{2,1,0:T(8,128)(2,1)S(1)} %shard_map.126.we, ...), custom_call_target="tpu_custom_call" | custom-call | flops 1 | bytes 1 | tf_op jit(solution)/shard_map/pallas_call | solution.py:95
  38.3 1.6 %collective-permute-start.6 = (bf16[4,512,256]{2,1,0:T(8,128)(2,1)S(1)}, bf16[4,512,256]{2,1,0:T(8,128)(2,1)S(1)}, u32[]{:S(2)}, u32[]{:S(2)}) collective-permute-start(bf16[4,512,256]{2,1,0:T(8,128)(2,1)S(1)} %shard_map.131), channel_id=1, source_target_pairs={{0,4},{1,5},{2,6},{3,7},{4,0},{5,1},{6,2},{7,3},{8,12},{9,13},{10,... | collective-permute-start | bytes 3145736 | tf_op jit(solution)/shard_map/ppermute | solution.py:42
  39.8 1.3 %shard_map.132 = f32[4,512,256]{2,1,0:T(8,128)S(1)} custom-call(f32[1]{0:T(128)S(6)} %copy.21.alpha, bf16[512,1024]{1,0:T(8,128)(2,1)S(1)} %constant_dynamic-update-slice_fusion.acts, bf16[16,256,512]{2,1,0:T(8,128)(2,1)S(1)} %shard_map.124.wb0, bf16[16,256,512]{2,1,0:T(8,128)(2,1)S(1)} %shard_map.125.wb1, bf16[16,256,512]{2,1,0:T(8,128)(2,1)S(1)} %shard_map.126.we, ...), custom_call_target="tpu_custom_call" | custom-call | flops 1 | bytes 1 | tf_op jit(solution)/shard_map/pallas_call | solution.py:95
  41.1 5.3 %collective-permute-done.7 = bf16[4,512,256]{2,1,0:T(8,128)(2,1)S(1)} collective-permute-done((bf16[4,512,256]{2,1,0:T(8,128)(2,1)S(1)}, bf16[4,512,256]{2,1,0:T(8,128)(2,1)S(1)}, u32[]{:S(2)}, u32[]{:S(2)}) %collective-permute-start.7) | collective-permute-done | bytes 1048608 | tf_op jit(solution)/shard_map/ppermute | solution.py:42
  46.4 0.4 multiply_convert_fusion
  46.9 1.4 %collective-permute-start.8 = (f16[4,512,256]{2,1,0:T(8,128)(2,1)S(1)}, f16[4,512,256]{2,1,0:T(8,128)(2,1)S(1)}, u32[]{:S(2)}, u32[]{:S(2)}) collective-permute-start(f16[4,512,256]{2,1,0:T(8,128)(2,1)S(1)} %multiply_convert_fusion), channel_id=1, source_target_pairs={{0,3},{1,2},{2,1},{3,0},{4,7},{5,6},{6,5},{7,4},{8,11},{9,10},{10,... | collective-permute-start | bytes 3145736 | tf_op jit(solution)/shard_map/ppermute | solution.py:42
  48.3 1.3 %shard_map.133 = f32[4,512,256]{2,1,0:T(8,128)S(1)} custom-call(f32[1]{0:T(128)S(6)} %copy.21.alpha, bf16[512,1024]{1,0:T(8,128)(2,1)S(1)} %constant_dynamic-update-slice_fusion.acts, bf16[16,256,512]{2,1,0:T(8,128)(2,1)S(1)} %shard_map.124.wb0, bf16[16,256,512]{2,1,0:T(8,128)(2,1)S(1)} %shard_map.125.wb1, bf16[16,256,512]{2,1,0:T(8,128)(2,1)S(1)} %shard_map.126.we, ...), custom_call_target="tpu_custom_call" | custom-call | flops 1 | bytes 1 | tf_op jit(solution)/shard_map/pallas_call | solution.py:95
  49.6 0.4 multiply_convert_fusion.1
  50.0 1.2 %collective-permute-start.12 = (f16[4,512,256]{2,1,0:T(8,128)(2,1)S(1)}, f16[4,512,256]{2,1,0:T(8,128)(2,1)S(1)}, u32[]{:S(2)}, u32[]{:S(2)}) collective-permute-start(f16[4,512,256]{2,1,0:T(8,128)(2,1)S(1)} %multiply_convert_fusion.1), channel_id=1, source_target_pairs={{0,12},{1,13},{2,14},{3,15},{4,8},{5,9},{6,10},{7,11},{8,4},{9,5},... | collective-permute-start | bytes 3145736 | tf_op jit(solution)/shard_map/ppermute | solution.py:42
  51.3 1.3 %shard_map.134 = f32[4,512,256]{2,1,0:T(8,128)S(1)} custom-call(f32[1]{0:T(128)S(6)} %copy.21.alpha, bf16[512,1024]{1,0:T(8,128)(2,1)S(1)} %constant_dynamic-update-slice_fusion.acts, bf16[16,256,512]{2,1,0:T(8,128)(2,1)S(1)} %shard_map.124.wb0, bf16[16,256,512]{2,1,0:T(8,128)(2,1)S(1)} %shard_map.125.wb1, bf16[16,256,512]{2,1,0:T(8,128)(2,1)S(1)} %shard_map.126.we, ...), custom_call_target="tpu_custom_call" | custom-call | flops 1 | bytes 1 | tf_op jit(solution)/shard_map/pallas_call | solution.py:95
  52.6 1.3 %shard_map.135 = f32[4,512,256]{2,1,0:T(8,128)S(1)} custom-call(f32[1]{0:T(128)S(6)} %copy.21.alpha, bf16[512,1024]{1,0:T(8,128)(2,1)S(1)} %constant_dynamic-update-slice_fusion.acts, bf16[16,256,512]{2,1,0:T(8,128)(2,1)S(1)} %shard_map.124.wb0, bf16[16,256,512]{2,1,0:T(8,128)(2,1)S(1)} %shard_map.125.wb1, bf16[16,256,512]{2,1,0:T(8,128)(2,1)S(1)} %shard_map.126.we, ...), custom_call_target="tpu_custom_call" | custom-call | flops 1 | bytes 1 | tf_op jit(solution)/shard_map/pallas_call | solution.py:95
  53.9 11.1 %collective-permute-done.5 = bf16[4,512,256]{2,1,0:T(8,128)(2,1)S(1)} collective-permute-done((bf16[4,512,256]{2,1,0:T(8,128)(2,1)S(1)}, bf16[4,512,256]{2,1,0:T(8,128)(2,1)S(1)}, u32[]{:S(2)}, u32[]{:S(2)}) %collective-permute-start.5) | collective-permute-done | bytes 1048608 | tf_op jit(solution)/shard_map/ppermute | solution.py:42
  65.0 0.3 convert_add_fusion.1
  65.3 1.5 %collective-permute-done.6 = bf16[4,512,256]{2,1,0:T(8,128)(2,1)S(1)} collective-permute-done((bf16[4,512,256]{2,1,0:T(8,128)(2,1)S(1)}, bf16[4,512,256]{2,1,0:T(8,128)(2,1)S(1)}, u32[]{:S(2)}, u32[]{:S(2)}) %collective-permute-start.6) | collective-permute-done | bytes 1048608 | tf_op jit(solution)/shard_map/ppermute | solution.py:42
  66.8 0.3 convert_add_fusion
  67.1 2.6 %collective-permute-done.8 = f16[4,512,256]{2,1,0:T(8,128)(2,1)S(1)} collective-permute-done((f16[4,512,256]{2,1,0:T(8,128)(2,1)S(1)}, f16[4,512,256]{2,1,0:T(8,128)(2,1)S(1)}, u32[]{:S(2)}, u32[]{:S(2)}) %collective-permute-start.8) | collective-permute-done | bytes 1048608 | tf_op jit(solution)/shard_map/ppermute | solution.py:42
  69.6 0.3 multiply_add_fusion.1
  70.0 0.1 fusion.18
  70.1 0.6 collective-permute-start.10
  70.7 1.2 %collective-permute-done.12 = f16[4,512,256]{2,1,0:T(8,128)(2,1)S(1)} collective-permute-done((f16[4,512,256]{2,1,0:T(8,128)(2,1)S(1)}, f16[4,512,256]{2,1,0:T(8,128)(2,1)S(1)}, u32[]{:S(2)}, u32[]{:S(2)}) %collective-permute-start.12) | collective-permute-done | bytes 1048608 | tf_op jit(solution)/shard_map/ppermute | solution.py:42
  71.9 0.3 multiply_add_fusion
  72.2 0.1 fusion.20
  72.4 0.2 collective-permute-start.14
  72.5 0.3 collective-permute-start.9
  72.8 3.7 %collective-permute-done.10 = f16[512,256]{1,0:T(8,128)(2,1)S(1)} collective-permute-done((f16[512,256]{1,0:T(8,128)(2,1)S(1)}, f16[512,256]{1,0:T(8,128)(2,1)S(1)}, u32[]{:S(2)}, u32[]{:S(2)}) %collective-permute-start.10) | collective-permute-done | bytes 262176 | tf_op jit(solution)/shard_map/ppermute | solution.py:42
  76.5 0.1 fusion.12
  76.7 1.2 %collective-permute-start.11 = (f16[512,256]{1,0:T(8,128)(2,1)S(1)}, f16[512,256]{1,0:T(8,128)(2,1)S(1)}, u32[]{:S(2)}, u32[]{:S(2)}) collective-permute-start(f16[512,256]{1,0:T(8,128)(2,1)S(1)} %fusion.12), channel_id=1, source_target_pairs={{0,12},{1,13},{2,14},{3,15},{4,8},{5,9},{6,10},{7,11},{8,4},{9,5},... | collective-permute-start | bytes 786440 | tf_op jit(solution)/shard_map/ppermute | solution.py:42
  77.9 0.9 collective-permute-done.14
  78.8 0.1 fusion.3
  78.9 2.1 %collective-permute-start.15 = (f16[512,256]{1,0:T(8,128)(2,1)S(1)}, f16[512,256]{1,0:T(8,128)(2,1)S(1)}, u32[]{:S(2)}, u32[]{:S(2)}) collective-permute-start(f16[512,256]{1,0:T(8,128)(2,1)S(1)} %fusion.3), channel_id=1, source_target_pairs={{0,3},{1,2},{2,1},{3,0},{4,7},{5,6},{6,5},{7,4},{8,11},{9,10},{10,... | collective-permute-start | bytes 786440 | tf_op jit(solution)/shard_map/ppermute | solution.py:42
  81.1 3.2 %collective-permute-done.11 = f16[512,256]{1,0:T(8,128)(2,1)S(1)} collective-permute-done((f16[512,256]{1,0:T(8,128)(2,1)S(1)}, f16[512,256]{1,0:T(8,128)(2,1)S(1)}, u32[]{:S(2)}, u32[]{:S(2)}) %collective-permute-start.11) | collective-permute-done | bytes 262176 | tf_op jit(solution)/shard_map/ppermute | solution.py:42
  84.3 0.2 fusion.17
  84.5 1.8 %collective-permute-done.13 = f16[512,256]{1,0:T(8,128)(2,1)S(1)} collective-permute-done((f16[512,256]{1,0:T(8,128)(2,1)S(1)}, f16[512,256]{1,0:T(8,128)(2,1)S(1)}, u32[]{:S(2)}, u32[]{:S(2)}) %collective-permute-start.13) | collective-permute-done | bytes 262176 | tf_op jit(solution)/shard_map/ppermute | solution.py:42
  86.3 0.3 collective-permute-done.15
  86.6 0.2 fusion.8
  86.8 0.1 pad_maximum_fusion
  87.1 1.5 %collective-permute-done.16 = f16[4,64,512]{2,1,0:T(8,128)(2,1)S(1)} collective-permute-done((f16[4,64,512]{2,1,0:T(8,128)(2,1)S(1)}, f16[4,64,512]{2,1,0:T(8,128)(2,1)S(1)}, u32[]{:S(2)}, u32[]{:S(2)}) %collective-permute-start.16) | collective-permute-done | bytes 262176 | tf_op jit(solution)/shard_map/ppermute | solution.py:42
  88.7 3.6 %collective-permute-start.17 = (f16[2,64,512]{2,1,0:T(8,128)(2,1)S(1)}, f16[2,64,512]{2,1,0:T(8,128)(2,1)S(1)}, u32[]{:S(2)}, u32[]{:S(2)}) collective-permute-start(f16[2,64,512]{2,1,0:T(8,128)(2,1)S(1)} %pad_maximum_fusion.2), channel_id=1, source_target_pairs={{0,64},{1,65},{2,66},{3,67},{4,68},{5,69},{6,70},{7,71},{8,72},{9,... | collective-permute-start | bytes 393224 | tf_op jit(solution)/shard_map/ppermute | solution.py:42
  92.5 0.8 collective-permute-start.19
  93.3 3.3 %collective-permute-done.17 = f16[2,64,512]{2,1,0:T(8,128)(2,1)S(1)} collective-permute-done((f16[2,64,512]{2,1,0:T(8,128)(2,1)S(1)}, f16[2,64,512]{2,1,0:T(8,128)(2,1)S(1)}, u32[]{:S(2)}, u32[]{:S(2)}) %collective-permute-start.17) | collective-permute-done | bytes 131104 | tf_op jit(solution)/shard_map/ppermute | solution.py:42
  96.6 1.8 %collective-permute-done.18 = f16[2,64,512]{2,1,0:T(8,128)(2,1)S(1)} collective-permute-done((f16[2,64,512]{2,1,0:T(8,128)(2,1)S(1)}, f16[2,64,512]{2,1,0:T(8,128)(2,1)S(1)}, u32[]{:S(2)}, u32[]{:S(2)}) %collective-permute-start.18) | collective-permute-done | bytes 131104 | tf_op jit(solution)/shard_map/ppermute | solution.py:42
  98.5 0.8 collective-permute-done.19
  99.2 0.1 convert_multiply_fusion.home
  99.4 1.2 %shard_map.136 = f32[16,8,128]{2,1,0:T(8,128)S(1)} custom-call(f32[8,64,512]{2,1,0:T(8,128)S(1)} %convert_multiply_fusion.home, s32[64]{0:T(128)} %ids.1), custom_call_target="tpu_custom_call" | custom-call | tf_op jit(solution)/shard_map/pallas_call | solution.py:191
  100.6 11.5 %all_to_all.11.stats = f32[16,8,128]{2,1,0:T(8,128)S(1)} all-to-all(f32[16,8,128]{2,1,0:T(8,128)S(1)} %shard_map.136), channel_id=1, replica_groups=mesh['rows'=8,'tensor'=16] {'tensor'}, dimensions={0} | all-to-all | bytes 131072 | tf_op jit(solution)/shard_map/all_to_all | solution.py:287
  112.0 1.2 %shard_map.137 = (f32[64,4096]{1,0:T(8,128)}, f32[1,64]{1,0:T(1,128)}) custom-call(f32[8,64,512]{2,1,0:T(8,128)S(1)} %convert_multiply_fusion.home, f32[16,8,128]{2,1,0:T(8,128)S(1)} %all_to_all.11.stats), custom_call_target="tpu_custom_call" | custom-call | tf_op jit(solution)/shard_map/pallas_call | solution.py:191
  (33 shorter events, 0.7 us)
Async XLA Ops:
  1.6 21.1 %slice-start = ((s8[8388608]{0:T(1024)(128)(4,1)}), s8[4194304]{0:T(1024)(128)(4,1)S(1)}, s32[]{:S(2)}) async-start(s8[8388608]{0:T(1024)(128)(4,1)} %bitcast.57), calls=%async_computation.2 | async-start | bytes 8388608
  16.5 6.2 %slice-start.1 = ((s8[8388608]{0:T(1024)(128)(4,1)}), s8[4194304]{0:T(1024)(128)(4,1)S(1)}, s32[]{:S(2)}) async-start(s8[8388608]{0:T(1024)(128)(4,1)} %bitcast.57), calls=%async_computation.3 | async-start | bytes 8388608
  17.7 10.0 %collective-permute-start.2 = (bf16[64,1024]{1,0:T(8,128)(2,1)S(1)}, bf16[64,1024]{1,0:T(8,128)(2,1)S(1)}, u32[]{:S(2)}, u32[]{:S(2)}) collective-permute-start(bf16[64,1024]{1,0:T(8,128)(2,1)S(1)} %shard_map.123), channel_id=1, source_target_pairs={{0,64},{1,65},{2,66},{3,67},{4,68},{5,69},{6,70},{7,71},{8,72},{9,... | collective-permute-start | bytes 393224 | tf_op jit(solution)/shard_map/ppermute | solution.py:42
  21.7 6.2 %collective-permute-start.1 = (bf16[64,1024]{1,0:T(8,128)(2,1)S(1)}, bf16[64,1024]{1,0:T(8,128)(2,1)S(1)}, u32[]{:S(2)}, u32[]{:S(2)}) collective-permute-start(bf16[64,1024]{1,0:T(8,128)(2,1)S(1)} %shard_map.123), channel_id=1, source_target_pairs={{0,96},{1,97},{2,98},{3,99},{4,100},{5,101},{6,102},{7,103},{8,104... | collective-permute-start | bytes 393224 | tf_op jit(solution)/shard_map/ppermute | solution.py:42
  22.4 5.5 %collective-permute-start = (bf16[64,1024]{1,0:T(8,128)(2,1)S(1)}, bf16[64,1024]{1,0:T(8,128)(2,1)S(1)}, u32[]{:S(2)}, u32[]{:S(2)}) collective-permute-start(bf16[64,1024]{1,0:T(8,128)(2,1)S(1)} %shard_map.123), channel_id=1, source_target_pairs={{0,32},{1,33},{2,34},{3,35},{4,36},{5,37},{6,38},{7,39},{8,40},{9,... | collective-permute-start | bytes 393224 | tf_op jit(solution)/shard_map/ppermute | solution.py:42
  24.1 2.2 %copy-start = (bf16[256,16,512]{2,1,0:T(8,128)(2,1)S(1)}, bf16[256,16,512]{2,1,0:T(8,128)(2,1)}, u32[]{:S(2)}) copy-start(bf16[256,16,512]{2,1,0:T(8,128)(2,1)} %head.2) | copy-start | bytes 12582916
  26.3 2.4 %copy-start.1 = (bf16[256,16,512]{2,1,0:T(8,128)(2,1)S(1)}, bf16[256,16,512]{2,1,0:T(8,128)(2,1)}, u32[]{:S(2)}) copy-start(bf16[256,16,512]{2,1,0:T(8,128)(2,1)} %head.3) | copy-start | bytes 12582916
  27.9 2.2 %collective-permute-start.3 = (bf16[256,1024]{1,0:T(8,128)(2,1)S(1)}, bf16[256,1024]{1,0:T(8,128)(2,1)S(1)}, u32[]{:S(2)}, u32[]{:S(2)}) collective-permute-start(bf16[256,1024]{1,0:T(8,128)(2,1)S(1)} %pad_maximum_fusion.1), channel_id=1, source_target_pairs={{0,16},{1,17},{2,18},{3,19},{4,20},{5,21},{6,22},{7,23},{8,24},{9,... | collective-permute-start | bytes 1572872 | tf_op jit(solution)/shard_map/ppermute | solution.py:42
  31.5 14.9 %collective-permute-start.7 = (bf16[4,512,256]{2,1,0:T(8,128)(2,1)S(1)}, bf16[4,512,256]{2,1,0:T(8,128)(2,1)S(1)}, u32[]{:S(2)}, u32[]{:S(2)}) collective-permute-start(bf16[4,512,256]{2,1,0:T(8,128)(2,1)S(1)} %shard_map.128), channel_id=1, source_target_pairs={{0,1},{1,0},{2,3},{3,2},{4,5},{5,4},{6,7},{7,6},{8,9},{9,8},{10,11... | collective-permute-start | bytes 3145736 | tf_op jit(solution)/shard_map/ppermute | solution.py:42
  33.5 16.1 %collective-permute-start.4 = (bf16[4,512,256]{2,1,0:T(8,128)(2,1)S(1)}, bf16[4,512,256]{2,1,0:T(8,128)(2,1)S(1)}, u32[]{:S(2)}, u32[]{:S(2)}) collective-permute-start(bf16[4,512,256]{2,1,0:T(8,128)(2,1)S(1)} %shard_map.129), channel_id=1, source_target_pairs={{0,4},{1,5},{2,6},{3,7},{4,0},{5,1},{6,2},{7,3},{8,12},{9,13},{10,... | collective-permute-start | bytes 3145736 | tf_op jit(solution)/shard_map/ppermute | solution.py:42
  35.4 29.6 %collective-permute-start.5 = (bf16[4,512,256]{2,1,0:T(8,128)(2,1)S(1)}, bf16[4,512,256]{2,1,0:T(8,128)(2,1)S(1)}, u32[]{:S(2)}, u32[]{:S(2)}) collective-permute-start(bf16[4,512,256]{2,1,0:T(8,128)(2,1)S(1)} %shard_map.130), channel_id=1, source_target_pairs={{0,1},{1,0},{2,3},{3,2},{4,5},{5,4},{6,7},{7,6},{8,9},{9,8},{10,11... | collective-permute-start | bytes 3145736 | tf_op jit(solution)/shard_map/ppermute | solution.py:42
  38.3 28.5 %collective-permute-start.6 = (bf16[4,512,256]{2,1,0:T(8,128)(2,1)S(1)}, bf16[4,512,256]{2,1,0:T(8,128)(2,1)S(1)}, u32[]{:S(2)}, u32[]{:S(2)}) collective-permute-start(bf16[4,512,256]{2,1,0:T(8,128)(2,1)S(1)} %shard_map.131), channel_id=1, source_target_pairs={{0,4},{1,5},{2,6},{3,7},{4,0},{5,1},{6,2},{7,3},{8,12},{9,13},{10,... | collective-permute-start | bytes 3145736 | tf_op jit(solution)/shard_map/ppermute | solution.py:42
  46.9 22.8 %collective-permute-start.8 = (f16[4,512,256]{2,1,0:T(8,128)(2,1)S(1)}, f16[4,512,256]{2,1,0:T(8,128)(2,1)S(1)}, u32[]{:S(2)}, u32[]{:S(2)}) collective-permute-start(f16[4,512,256]{2,1,0:T(8,128)(2,1)S(1)} %multiply_convert_fusion), channel_id=1, source_target_pairs={{0,3},{1,2},{2,1},{3,0},{4,7},{5,6},{6,5},{7,4},{8,11},{9,10},{10,... | collective-permute-start | bytes 3145736 | tf_op jit(solution)/shard_map/ppermute | solution.py:42
  50.0 21.9 %collective-permute-start.12 = (f16[4,512,256]{2,1,0:T(8,128)(2,1)S(1)}, f16[4,512,256]{2,1,0:T(8,128)(2,1)S(1)}, u32[]{:S(2)}, u32[]{:S(2)}) collective-permute-start(f16[4,512,256]{2,1,0:T(8,128)(2,1)S(1)} %multiply_convert_fusion.1), channel_id=1, source_target_pairs={{0,12},{1,13},{2,14},{3,15},{4,8},{5,9},{6,10},{7,11},{8,4},{9,5},... | collective-permute-start | bytes 3145736 | tf_op jit(solution)/shard_map/ppermute | solution.py:42
  70.1 6.5 %collective-permute-start.10 = (f16[512,256]{1,0:T(8,128)(2,1)S(1)}, f16[512,256]{1,0:T(8,128)(2,1)S(1)}, u32[]{:S(2)}, u32[]{:S(2)}) collective-permute-start(f16[512,256]{1,0:T(8,128)(2,1)S(1)} %get-tuple-element.79), channel_id=1, source_target_pairs={{0,4},{1,5},{2,6},{3,7},{4,0},{5,1},{6,2},{7,3},{8,12},{9,13},{10,... | collective-permute-start | bytes 786440 | tf_op jit(solution)/shard_map/ppermute | solution.py:42
  72.4 6.5 %collective-permute-start.14 = (f16[512,256]{1,0:T(8,128)(2,1)S(1)}, f16[512,256]{1,0:T(8,128)(2,1)S(1)}, u32[]{:S(2)}, u32[]{:S(2)}) collective-permute-start(f16[512,256]{1,0:T(8,128)(2,1)S(1)} %get-tuple-element.81), channel_id=1, source_target_pairs={{0,1},{1,0},{2,3},{3,2},{4,5},{5,4},{6,7},{7,6},{8,9},{9,8},{10,11... | collective-permute-start | bytes 786440 | tf_op jit(solution)/shard_map/ppermute | solution.py:42
  72.5 8.5 %collective-permute-start.9 = (f16[512,256]{1,0:T(8,128)(2,1)S(1)}, f16[512,256]{1,0:T(8,128)(2,1)S(1)}, u32[]{:S(2)}, u32[]{:S(2)}) collective-permute-start(f16[512,256]{1,0:T(8,128)(2,1)S(1)} %get-tuple-element.78), channel_id=1, source_target_pairs={{0,4},{1,5},{2,6},{3,7},{4,0},{5,1},{6,2},{7,3},{8,12},{9,13},{10,... | collective-permute-start | bytes 786440 | tf_op jit(solution)/shard_map/ppermute | solution.py:42
  76.7 7.7 %collective-permute-start.11 = (f16[512,256]{1,0:T(8,128)(2,1)S(1)}, f16[512,256]{1,0:T(8,128)(2,1)S(1)}, u32[]{:S(2)}, u32[]{:S(2)}) collective-permute-start(f16[512,256]{1,0:T(8,128)(2,1)S(1)} %fusion.12), channel_id=1, source_target_pairs={{0,12},{1,13},{2,14},{3,15},{4,8},{5,9},{6,10},{7,11},{8,4},{9,5},... | collective-permute-start | bytes 786440 | tf_op jit(solution)/shard_map/ppermute | solution.py:42
  77.9 8.5 %collective-permute-start.13 = (f16[512,256]{1,0:T(8,128)(2,1)S(1)}, f16[512,256]{1,0:T(8,128)(2,1)S(1)}, u32[]{:S(2)}, u32[]{:S(2)}) collective-permute-start(f16[512,256]{1,0:T(8,128)(2,1)S(1)} %get-tuple-element.80), channel_id=1, source_target_pairs={{0,1},{1,0},{2,3},{3,2},{4,5},{5,4},{6,7},{7,6},{8,9},{9,8},{10,11... | collective-permute-start | bytes 786440 | tf_op jit(solution)/shard_map/ppermute | solution.py:42
  78.9 7.7 %collective-permute-start.15 = (f16[512,256]{1,0:T(8,128)(2,1)S(1)}, f16[512,256]{1,0:T(8,128)(2,1)S(1)}, u32[]{:S(2)}, u32[]{:S(2)}) collective-permute-start(f16[512,256]{1,0:T(8,128)(2,1)S(1)} %fusion.3), channel_id=1, source_target_pairs={{0,3},{1,2},{2,1},{3,0},{4,7},{5,6},{6,5},{7,4},{8,11},{9,10},{10,... | collective-permute-start | bytes 786440 | tf_op jit(solution)/shard_map/ppermute | solution.py:42
  87.0 1.6 %collective-permute-start.16 = (f16[4,64,512]{2,1,0:T(8,128)(2,1)S(1)}, f16[4,64,512]{2,1,0:T(8,128)(2,1)S(1)}, u32[]{:S(2)}, u32[]{:S(2)}) collective-permute-start(f16[4,64,512]{2,1,0:T(8,128)(2,1)S(1)} %bitcast.61), channel_id=1, source_target_pairs={{0,16},{1,17},{2,18},{3,19},{4,20},{5,21},{6,22},{7,23},{8,24},{9,... | collective-permute-start | bytes 786440 | tf_op jit(solution)/shard_map/ppermute | solution.py:42
  88.7 7.9 %collective-permute-start.17 = (f16[2,64,512]{2,1,0:T(8,128)(2,1)S(1)}, f16[2,64,512]{2,1,0:T(8,128)(2,1)S(1)}, u32[]{:S(2)}, u32[]{:S(2)}) collective-permute-start(f16[2,64,512]{2,1,0:T(8,128)(2,1)S(1)} %pad_maximum_fusion.2), channel_id=1, source_target_pairs={{0,64},{1,65},{2,66},{3,67},{4,68},{5,69},{6,70},{7,71},{8,72},{9,... | collective-permute-start | bytes 393224 | tf_op jit(solution)/shard_map/ppermute | solution.py:42
  92.3 6.1 %collective-permute-start.18 = (f16[2,64,512]{2,1,0:T(8,128)(2,1)S(1)}, f16[2,64,512]{2,1,0:T(8,128)(2,1)S(1)}, u32[]{:S(2)}, u32[]{:S(2)}) collective-permute-start(f16[2,64,512]{2,1,0:T(8,128)(2,1)S(1)} %pad_maximum_fusion.3), channel_id=1, source_target_pairs={{0,32},{1,33},{2,34},{3,35},{4,36},{5,37},{6,38},{7,39},{8,40},{9,... | collective-permute-start | bytes 393224 | tf_op jit(solution)/shard_map/ppermute | solution.py:42
  92.5 6.7 %collective-permute-start.19 = (f16[2,64,512]{2,1,0:T(8,128)(2,1)S(1)}, f16[2,64,512]{2,1,0:T(8,128)(2,1)S(1)}, u32[]{:S(2)}, u32[]{:S(2)}) collective-permute-start(f16[2,64,512]{2,1,0:T(8,128)(2,1)S(1)} %pad_maximum_fusion.4), channel_id=1, source_target_pairs={{0,96},{1,97},{2,98},{3,99},{4,100},{5,101},{6,102},{7,103},{8,104... | collective-permute-start | bytes 393224 | tf_op jit(solution)/shard_map/ppermute | solution.py:42
